TPU v7x, 32 devices: a whole 2x2x4 slice. The times are simulated.
32 devices in a mesh: fsdp: 8 (over z, x), tp: 4 (over y, core).
Axes of the slice: x: 2, y: 2, z: 4, core: 2. Of those that a mesh axis runs over, the one named last changes fastest.
Arguments:
- inputs: bfloat16 [2, 8, 1024, 2048], P(None, 'fsdp', 'tp'), may hold values from -6 to 6
- ln_gain: bfloat16 [2048], P(('fsdp', 'tp')), may hold values from 0.099609375 to 1.8984375
- ln_bias: bfloat16 [2048], P(('fsdp', 'tp')), may hold values from -3 to 3
- qkv_weight: bfloat16 [2048, 3, 2048], P('fsdp', None, 'tp'), may hold values from -0.125 to 0.125
- qkv_bias: bfloat16 [3, 32, 64], P(None, 'tp', 'fsdp'), may hold values from -3 to 3
- out_weight: bfloat16 [2048, 2048], P('tp', 'fsdp'), may hold values from -1.5 to 1.5
- out_bias: bfloat16 [2048], P(('fsdp', 'tp')), may hold values from -3 to 3
- up_weight: bfloat16 [2048, 8192], P('fsdp', 'tp'), may hold values from -0.125 to 0.125
- up_bias: bfloat16 [128, 64], P('tp', 'fsdp'), may hold values from -3 to 3
- down_weight: bfloat16 [8192, 2048], P('tp', 'fsdp'), may hold values from -0.0625 to 0.0625
- down_bias: bfloat16 [2048], P(('fsdp', 'tp')), may hold values from -3 to 3
- cotangent: bfloat16 [2, 8, 1024, 2048], P(None, 'fsdp', 'tp'), may hold values from -40 to 40
Outputs:
- output: bfloat16 [2, 8, 1024, 2048], P(None, 'fsdp', 'tp')
- input_grad: bfloat16 [2, 8, 1024, 2048], P(None, 'fsdp', 'tp')
- ln_gain_grad: float32 [2048], P(('fsdp', 'tp'))
- ln_bias_grad: float32 [2048], P(('fsdp', 'tp'))
- qkv_weight_grad: float32 [2048, 3, 2048], P('fsdp', None, 'tp')
- qkv_bias_grad: float32 [3, 32, 64], P(None, 'tp', 'fsdp')
- out_weight_grad: float32 [2048, 2048], P('tp', 'fsdp')
- out_bias_grad: float32 [2048], P(('fsdp', 'tp'))
- up_weight_grad: float32 [2048, 8192], P('fsdp', 'tp')
- up_bias_grad: float32 [128, 64], P('tp', 'fsdp')
- down_weight_grad: float32 [8192, 2048], P('tp', 'fsdp')
- down_bias_grad: float32 [2048], P(('fsdp', 'tp'))
All inputs are finite; a program needn't handle non-finite values.
Results may differ from a plain program's by a relative error of at most 0.014.
Values may be sent and summed in bfloat16 or wider, within the bound.
No kernel may reach another device: no remote copies, remote signals or barrier semaphores. Data moves between devices by JAX's collectives and lax.ppermute only.
A program may use at most 320 MiB of HBM per device.

v0:
```python
import math

import jax
import jax.numpy as jnp
from jax import lax
from jax.sharding import PartitionSpec as P

ROT = 32


norm_epsilon = 1e-05
gelu_factor = 0.7978845608028654
mask_fill = -1e30


def layer_norm(resid_rows, gain_vec, shift_vec):
    row_mean = jnp.mean(resid_rows, axis=-1, keepdims=True)
    centred = resid_rows - row_mean
    row_var = jnp.mean(centred * centred, axis=-1, keepdims=True)
    return centred * lax.rsqrt(row_var + norm_epsilon) * gain_vec + shift_vec


def gelu_tanh(inner):
    return 0.5 * inner * (1.0 + jnp.tanh(gelu_factor * (inner + 0.044715 * inner * inner * inner)))


def rotary_tables(length, head_dim, rot_dim):
    half_rot = rot_dim // 2
    inv_freq = 10000.0 ** (-2.0 * jnp.arange(half_rot, dtype=jnp.float32) / rot_dim)
    angles = jnp.arange(length, dtype=jnp.float32)[:, None] * inv_freq[None, :]
    rest_ones = jnp.ones((length, head_dim - rot_dim), jnp.float32)
    cosine_table = jnp.concatenate([jnp.cos(angles), jnp.cos(angles), rest_ones], axis=1)
    sine_table = jnp.concatenate([jnp.sin(angles), jnp.sin(angles), 0.0 * rest_ones], axis=1)
    return (cosine_table, sine_table)


def rotate(head_vals, cosine_table, sine_table, rot_dim):
    half_rot = rot_dim // 2
    turned = jnp.concatenate(
        [
            -head_vals[..., half_rot:rot_dim],
            head_vals[..., :half_rot],
            0.0 * head_vals[..., rot_dim:],
        ],
        axis=-1,
    )
    return head_vals * cosine_table[:, None, :] + turned * sine_table[:, None, :]


def causal_mask(first_row, block_rows, key_count):
    row_ids = first_row + lax.broadcasted_iota(jnp.int32, (block_rows, key_count), 0)
    col_ids = lax.broadcasted_iota(jnp.int32, (block_rows, key_count), 1)
    return col_ids <= row_ids


def dot_rows(left, right):
    return lax.dot_general(
        left, right, (((0,), (0,)), ((), ())), preferred_element_type=jnp.float32
    )


def dot_cols(left, right):
    return lax.dot_general(
        left, right, (((1,), (1,)), ((), ())), preferred_element_type=jnp.float32
    )


def attend_forward(queries, keys_rot, values_low, score_scale):
    length = queries.shape[0]
    block_rows = min(512, length)
    out_blocks, lse_blocks = ([], [])
    for first_row in range(0, length, block_rows):
        last_row = first_row + block_rows
        scores = (
            jnp.einsum(
                "qhd,khd->hqk",
                queries[first_row:last_row],
                keys_rot[:last_row],
                preferred_element_type=jnp.float32,
            )
            * score_scale
        )
        scores = jnp.where(causal_mask(first_row, block_rows, last_row)[None], scores, mask_fill)
        row_max = jnp.max(scores, axis=-1, keepdims=True)
        exp_scores = jnp.exp(scores - row_max)
        denom_sum = jnp.sum(exp_scores, axis=-1, keepdims=True)
        prob_low = (exp_scores / denom_sum).astype(jnp.bfloat16)
        attn_block = jnp.einsum(
            "hqk,khd->qhd", prob_low, values_low[:last_row], preferred_element_type=jnp.float32
        )
        out_blocks.append(attn_block.astype(jnp.bfloat16))
        lse_blocks.append((row_max + jnp.log(denom_sum))[..., 0])
    return (jnp.concatenate(out_blocks, axis=0), jnp.concatenate(lse_blocks, axis=1))


def attend_backward(queries, keys_rot, values_low, lse_rows, attn_grad, score_scale):
    length = queries.shape[0]
    block_rows = min(512, length)
    key_grad = jnp.zeros(queries.shape, jnp.float32)
    value_grad = jnp.zeros(queries.shape, jnp.float32)
    query_blocks = []
    for first_row in range(0, length, block_rows):
        last_row = first_row + block_rows
        query_block = queries[first_row:last_row]
        grad_block = attn_grad[first_row:last_row]
        scores = (
            jnp.einsum(
                "qhd,khd->hqk", query_block, keys_rot[:last_row], preferred_element_type=jnp.float32
            )
            * score_scale
        )
        scores = jnp.where(causal_mask(first_row, block_rows, last_row)[None], scores, mask_fill)
        probs = jnp.exp(scores - lse_rows[:, first_row:last_row, None])
        prob_low = probs.astype(jnp.bfloat16)
        value_grad = value_grad.at[:last_row].add(
            jnp.einsum("hqk,qhd->khd", prob_low, grad_block, preferred_element_type=jnp.float32)
        )
        prob_grad = jnp.einsum(
            "qhd,khd->hqk", grad_block, values_low[:last_row], preferred_element_type=jnp.float32
        )
        inner_sum = jnp.sum(probs * prob_grad, axis=-1, keepdims=True)
        score_grad = (probs * (prob_grad - inner_sum)).astype(jnp.bfloat16)
        query_blocks.append(
            jnp.einsum(
                "hqk,khd->qhd", score_grad, keys_rot[:last_row], preferred_element_type=jnp.float32
            )
            * score_scale
        )
        key_grad = key_grad.at[:last_row].add(
            jnp.einsum("hqk,qhd->khd", score_grad, query_block, preferred_element_type=jnp.float32)
            * score_scale
        )
    return (jnp.concatenate(query_blocks, axis=0), key_grad, value_grad)


def shards(
    inputs,
    ln_gain,
    ln_bias,
    qkv_weight,
    qkv_bias,
    out_weight,
    out_bias,
    up_weight,
    up_bias,
    down_weight,
    down_bias,
    cotangent,
):
    micro_count = inputs.shape[0]
    seq_count = inputs.shape[1]
    model_width = inputs.shape[3]
    length = inputs.shape[2] * lax.axis_size("tp")
    local_heads = qkv_bias.shape[1]
    head_dim = qkv_bias.shape[2] * lax.axis_size("fsdp")
    score_scale = 1.0 / math.sqrt(head_dim)
    cosine_table, sine_table = rotary_tables(length, head_dim, ROT)
    gain_full, shift_full, bias_out_full, bias_down_full = (
        lax.all_gather(ln_gain, ("fsdp", "tp"), axis=0, tiled=True),
        lax.all_gather(ln_bias, ("fsdp", "tp"), axis=0, tiled=True),
        lax.all_gather(out_bias, ("fsdp", "tp"), axis=0, tiled=True),
        lax.all_gather(down_bias, ("fsdp", "tp"), axis=0, tiled=True),
    )
    gain_vec = gain_full.astype(jnp.float32)
    shift_vec = shift_full.astype(jnp.float32)
    bias_both = bias_out_full.astype(jnp.float32) + bias_down_full.astype(jnp.float32)
    gain_total = jnp.zeros((model_width,), jnp.float32)
    shift_total = jnp.zeros((model_width,), jnp.float32)
    bias_total = jnp.zeros((model_width,), jnp.float32)
    grad_totals = None
    outputs, input_grads = ([], [])

    def rot_back(head_grads):
        pull_back = jax.vjp(
            lambda head_vals: rotate(head_vals, cosine_table, sine_table, ROT),
            jnp.zeros_like(head_grads),
        )[1]
        return pull_back(head_grads)[0]

    for batch_index in range(micro_count):
        w_qkv, b_qkv, w_out, w_up, b_up, w_down = (
            lax.all_gather(qkv_weight, "fsdp", axis=0, tiled=True),
            lax.all_gather(qkv_bias, "fsdp", axis=2, tiled=True),
            lax.all_gather(out_weight, "fsdp", axis=1, tiled=True),
            lax.all_gather(up_weight, "fsdp", axis=0, tiled=True),
            lax.all_gather(up_bias, "fsdp", axis=1, tiled=True),
            lax.all_gather(down_weight, "fsdp", axis=1, tiled=True),
        )
        w_qkv_flat = w_qkv.reshape(model_width, -1)
        resid_rows = inputs[batch_index].astype(jnp.float32)
        normed_low = layer_norm(resid_rows, gain_vec, shift_vec).astype(jnp.bfloat16)
        normed_full = lax.all_gather(normed_low, "tp", axis=1, tiled=True)
        flat_normed = normed_full.reshape(-1, model_width)
        qkv_proj = jnp.dot(
            flat_normed, w_qkv_flat, preferred_element_type=jnp.float32
        ) + b_qkv.reshape(-1).astype(jnp.float32)
        qkv_proj = qkv_proj.reshape(seq_count, length, 3, local_heads, head_dim)
        queries = rotate(qkv_proj[:, :, 0], cosine_table, sine_table, ROT).astype(jnp.bfloat16)
        keys_rot = rotate(qkv_proj[:, :, 1], cosine_table, sine_table, ROT).astype(jnp.bfloat16)
        values_low = qkv_proj[:, :, 2].astype(jnp.bfloat16)
        attn_low, lse_rows = lax.map(
            lambda seq_args: attend_forward(seq_args[0], seq_args[1], seq_args[2], score_scale),
            (queries, keys_rot, values_low),
        )
        attn_flat = attn_low.reshape(-1, local_heads * head_dim)
        pre_act = jnp.dot(flat_normed, w_up, preferred_element_type=jnp.float32) + b_up.reshape(
            -1
        ).astype(jnp.float32)
        act_low = gelu_tanh(pre_act).astype(jnp.bfloat16)
        branch_terms = jnp.dot(attn_flat, w_out, preferred_element_type=jnp.float32) + jnp.dot(
            act_low, w_down, preferred_element_type=jnp.float32
        )
        branch_local = lax.psum_scatter(
            branch_terms.reshape(seq_count, length, model_width).astype(jnp.bfloat16),
            "tp",
            scatter_dimension=1,
            tiled=True,
        ).astype(jnp.float32)
        outputs.append((resid_rows + branch_local + bias_both).astype(jnp.bfloat16))
        w_qkv, w_out, w_up, w_down = (
            lax.all_gather(qkv_weight, "fsdp", axis=0, tiled=True),
            lax.all_gather(out_weight, "fsdp", axis=1, tiled=True),
            lax.all_gather(up_weight, "fsdp", axis=0, tiled=True),
            lax.all_gather(down_weight, "fsdp", axis=1, tiled=True),
        )
        w_qkv_flat = w_qkv.reshape(model_width, -1)
        cot_local = cotangent[batch_index]
        cot_full = lax.all_gather(cot_local, "tp", axis=1, tiled=True)
        cot_flat = cot_full.reshape(-1, model_width)
        bias_total = bias_total + jnp.sum(cot_local.astype(jnp.float32), axis=(0, 1))
        out_w_grad = dot_rows(attn_flat, cot_flat)
        down_w_grad = dot_rows(act_low, cot_flat)
        attn_grad = dot_cols(cot_flat, w_out).astype(jnp.bfloat16)
        act_grad = dot_cols(cot_flat, w_down)
        pre_grad = jax.vjp(gelu_tanh, pre_act)[1](act_grad)[0].astype(jnp.bfloat16)
        up_w_grad = dot_rows(flat_normed, pre_grad)
        up_b_grad = jnp.sum(pre_grad.astype(jnp.float32), axis=0).reshape(b_up.shape)
        attn_grad_heads = attn_grad.reshape(seq_count, length, local_heads, head_dim)
        query_grad, key_grad, value_grad = lax.map(
            lambda seq_args: attend_backward(
                seq_args[0], seq_args[1], seq_args[2], seq_args[3], seq_args[4], score_scale
            ),
            (queries, keys_rot, values_low, lse_rows, attn_grad_heads),
        )
        qkv_grad = jnp.stack([rot_back(query_grad), rot_back(key_grad), value_grad], axis=2).astype(
            jnp.bfloat16
        )
        qkv_grad = qkv_grad.reshape(-1, 3 * local_heads * head_dim)
        qkv_w_grad = dot_rows(flat_normed, qkv_grad).reshape(w_qkv.shape)
        qkv_b_grad = jnp.sum(qkv_grad.astype(jnp.float32), axis=0).reshape(3, local_heads, head_dim)
        normed_grad = dot_cols(qkv_grad, w_qkv_flat) + dot_cols(pre_grad, w_up)
        normed_local = lax.psum_scatter(
            normed_grad.reshape(seq_count, length, model_width).astype(jnp.bfloat16),
            "tp",
            scatter_dimension=1,
            tiled=True,
        ).astype(jnp.float32)
        norm_back = jax.vjp(layer_norm, resid_rows, gain_vec, shift_vec)[1]
        rows_grad, gain_grad, shift_grad = norm_back(normed_local)
        input_grads.append((cot_local.astype(jnp.float32) + rows_grad).astype(jnp.bfloat16))
        gain_total = gain_total + gain_grad
        shift_total = shift_total + shift_grad
        big_grads = (qkv_w_grad, qkv_b_grad, out_w_grad, up_w_grad, up_b_grad, down_w_grad)
        big_grads = (
            lax.psum_scatter(
                big_grads[0].astype(jnp.bfloat16), "fsdp", scatter_dimension=0, tiled=True
            ).astype(jnp.float32),
            lax.psum_scatter(
                big_grads[1].astype(jnp.bfloat16), "fsdp", scatter_dimension=2, tiled=True
            ).astype(jnp.float32),
            lax.psum_scatter(
                big_grads[2].astype(jnp.bfloat16), "fsdp", scatter_dimension=1, tiled=True
            ).astype(jnp.float32),
            lax.psum_scatter(
                big_grads[3].astype(jnp.bfloat16), "fsdp", scatter_dimension=0, tiled=True
            ).astype(jnp.float32),
            lax.psum_scatter(
                big_grads[4].astype(jnp.bfloat16), "fsdp", scatter_dimension=1, tiled=True
            ).astype(jnp.float32),
            lax.psum_scatter(
                big_grads[5].astype(jnp.bfloat16), "fsdp", scatter_dimension=1, tiled=True
            ).astype(jnp.float32),
        )
        if grad_totals is None:
            grad_totals = big_grads
        else:
            grad_totals = tuple((earlier + later for earlier, later in zip(grad_totals, big_grads)))
    gain_sum, shift_sum, bias_sum = (
        lax.psum_scatter(gain_total, ("fsdp", "tp"), scatter_dimension=0, tiled=True),
        lax.psum_scatter(shift_total, ("fsdp", "tp"), scatter_dimension=0, tiled=True),
        lax.psum_scatter(bias_total, ("fsdp", "tp"), scatter_dimension=0, tiled=True),
    )
    return (
        jnp.stack(outputs, axis=0),
        jnp.stack(input_grads, axis=0),
        gain_sum,
        shift_sum,
        grad_totals[0],
        grad_totals[1],
        grad_totals[2],
        bias_sum,
        grad_totals[3],
        grad_totals[4],
        grad_totals[5],
        bias_sum,
    )


def solution(mesh):
    return jax.shard_map(
        shards,
        mesh=mesh,
        in_specs=(
            P(None, "fsdp", "tp", None),
            P(("fsdp", "tp")),
            P(("fsdp", "tp")),
            P("fsdp", None, "tp"),
            P(None, "tp", "fsdp"),
            P("tp", "fsdp"),
            P(("fsdp", "tp")),
            P("fsdp", "tp"),
            P("tp", "fsdp"),
            P("tp", "fsdp"),
            P(("fsdp", "tp")),
            P(None, "fsdp", "tp", None),
        ),
        out_specs=(
            P(None, "fsdp", "tp", None),
            P(None, "fsdp", "tp", None),
            P(("fsdp", "tp")),
            P(("fsdp", "tp")),
            P("fsdp", None, "tp"),
            P(None, "tp", "fsdp"),
            P("tp", "fsdp"),
            P(("fsdp", "tp")),
            P("fsdp", "tp"),
            P("tp", "fsdp"),
            P("tp", "fsdp"),
            P(("fsdp", "tp")),
        ),
        check_vma=False,
    )
```

profile of v0, /device:TPU:0, one launch (start us, length us, event | category | flops | bytes accessed | tf_op | source)
XLA Modules:
  0.0 1753.6 jit_solution(16200274292250818931)
XLA Ops:
  13.0 42.9 %all-reduce.28 = (bf16[2048]{0:T(1024)(128)(2,1)S(1)}, bf16[2048]{0:T(1024)(128)(2,1)S(1)}, bf16[2048]{0:T(1024)(128)(2,1)}, bf16[2048]{0:T(1024)(128)(2,1)}) all-reduce(bf16[2048]{0:T(1024)(128)(2,1)S(1)} %dynamic-update-slice.25, bf16[2048]{0:T(1024)(128)(2,1)S(1)} %dynamic-update-slice.24, ...), channel_id=1, replica_groups=mesh['fsdp'=8,'tp'=4] {'fsdp','tp'}, use_global_device_ids=true, to_apply=%add.17 | all-reduce | flops 8192 | bytes 32768
  64.3 26.0 %all_gather.63 = bf16[32,64]{0,1:T(8,128)(2,1)S(1)} all-gather(bf16[32,8]{0,1:T(8,128)(2,1)S(1)} %copy-done.84), channel_id=1, replica_groups=mesh['fsdp'=8,'tp'=4] {'fsdp'}, dimensions={1}, use_global_device_ids=true | all-gather | bytes 4608 | tf_op jit(solution)/shard_map/all_gather | solution.py:186
  91.0 30.5 %all_gather.60 = bf16[3,8,64]{1,0,2:T(4,128)(2,1)S(1)} all-gather(bf16[3,8,8]{1,0,2:T(4,128)(2,1)S(1)} %copy.106), channel_id=1, replica_groups=mesh['fsdp'=8,'tp'=4] {'fsdp'}, dimensions={2}, use_global_device_ids=true | all-gather | bytes 3456 | tf_op jit(solution)/shard_map/all_gather | solution.py:183
  142.0 30.9 %all-gather.21.cloned.1.call-done = bf16[1,1024,2048]{2,1,0:T(8,128)(2,1)} async-done(((bf16[1,256,2048]{2,1,0:T(8,128)(2,1)}), bf16[1,1024,2048]{2,1,0:T(8,128)(2,1)}) %all-gather.21.cloned.1.call-update) | async-done | bytes 4194320 | tf_op jit(solution)/shard_map/all_gather | solution.py:192
  172.9 102.4 %all-gather.13.cloned.1.call-done = bf16[2048,3,512]{0,2,1:T(8,128)(2,1)} async-done(((bf16[256,3,512]{0,2,1:T(8,128)(2,1)}), bf16[2048,3,512]{0,2,1:T(8,128)(2,1)}) %all-gather.13.cloned.1.call-update) | async-done | bytes 6291472 | tf_op jit(solution)/shard_map/all_gather | solution.py:182
  391.6 12.1 multiply_reduce_fusion.1
  404.8 12.1 multiply_convert_fusion.1
  419.6 12.3 multiply_reduce_fusion
  531.3 14.4 fusion.53
  545.7 17.0 all-gather.19.cloned.1.call-done
  562.8 20.6 %fusion.205 = (bf16[2048]{0:T(1024)(128)(2,1)}, bf16[1024,2048]{1,0:T(8,128)(2,1)S(1)}) fusion(bf16[2048,2048]{1,0:T(8,128)(2,1)} %all-gather.19.cloned.1.call-done, bf16[1,1,1024,2048]{3,2,1,0:T(8,128)(2,1)} %all-gather.25.cloned.1.call-done, f32[1024,2048]{1,0:T(8,128)} %fusion.53, f32[2048]{0:T(1024)S(1)} %copy-done.78), kind=kOutput, calls=%fused_computation.335 | convolution fusion | flops 8644458496 | bytes 25178112 | tf_op jit(solution)/shard_map/dot_general | solution.py:63
  594.7 12.6 fusion.35
  607.3 15.1 fusion.57
  622.5 20.8 %fusion.206 = (bf16[2048]{0:T(1024)(128)(2,1)}, bf16[1024,2048]{1,0:T(8,128)(2,1)}) fusion(bf16[2048,2048]{1,0:T(8,128)(2,1)} %all-gather.19.cloned.1.call-done, bf16[1,1,1024,2048]{3,2,1,0:T(8,128)(2,1)S(1)} %copy-done.87, f32[1024,2048]{1,0:T(8,128)} %fusion.57, f32[2048]{0:T(1024)S(1)} %copy-done.78), kind=kOutput, calls=%fused_computation.336 | convolution fusion | flops 8644458496 | bytes 25178112 | tf_op jit(solution)/shard_map/dot_general | solution.py:63
  643.3 12.9 fusion.207
  656.2 12.6 fusion.34
  668.8 15.5 fusion.190
  688.9 15.7 fusion.191
  709.0 12.2 convolution_convert_fusion.4
  733.0 14.1 convolution_convert_fusion.3
  747.2 14.6 convolution_convert_fusion.2
  761.9 16.2 convolution_convert_fusion
  778.2 16.2 convolution_convert_fusion.1
  798.5 34.4 %all-reduce.29 = (bf16[3,8,64]{2,1,0:T(8,128)(2,1)S(1)}, bf16[3,8,64]{2,1,0:T(8,128)(2,1)S(1)}, bf16[32,64]{1,0:T(8,128)(2,1)S(1)}, bf16[32,64]{1,0:T(8,128)(2,1)S(1)}) all-reduce(bf16[3,8,64]{2,1,0:T(8,128)(2,1)S(1)} %copy-done.69, bf16[3,8,64]{2,1,0:T(8,128)(2,1)S(1)} %copy-done.68, ...), channel_id=13, replica_groups=mesh['fsdp'=8,'tp'=4] {'fsdp'}, use_global_device_ids=true, to_apply=%region_35.36.clone | all-reduce | flops 7168 | bytes 28672
  843.8 47.1 %reduce-scatter.19.cloned.1.call-done = bf16[1,256,2048]{2,1,0:T(8,128)(2,1)} async-done(((bf16[1,1024,2048]{2,1,0:T(8,128)(2,1)}), bf16[1,256,2048]{2,1,0:T(8,128)(2,1)}) %reduce-scatter.19.cloned.1.call-update) | async-done | bytes 1048592 | tf_op jit(solution)/shard_map/reduce_scatter | solution.py:213
  895.7 43.0 %all-reduce.27 = (f32[2048]{0:T(1024)S(1)}, f32[2048]{0:T(1024)S(1)}, f32[2048]{0:T(1024)S(1)}) all-reduce(f32[2048]{0:T(1024)S(1)} %add.457, f32[2048]{0:T(1024)S(1)} %add.458, f32[2048]{0:T(1024)S(1)} %add.462), channel_id=8, replica_groups=mesh['fsdp'=8,'tp'=4] {'fsdp','tp'}, use_global_device_ids=true, to_apply=%region_26.27.clone | all-reduce | flops 6144 | bytes 49152
  947.1 66.8 %reduce-scatter.27.cloned.1.call-done = bf16[256,3,512]{2,0,1:T(8,128)(2,1)} async-done(((bf16[2048,3,512]{2,0,1:T(8,128)(2,1)}), bf16[256,3,512]{2,0,1:T(8,128)(2,1)}) %reduce-scatter.27.cloned.1.call-update) | async-done | bytes 786448 | tf_op jit(solution)/shard_map/reduce_scatter | solution.py:265
  1013.8 121.0 %reduce-scatter.25.cloned.1.call-done = bf16[256,3,512]{2,0,1:T(8,128)(2,1)} async-done(((bf16[2048,3,512]{2,0,1:T(8,128)(2,1)}), bf16[256,3,512]{2,0,1:T(8,128)(2,1)}) %reduce-scatter.25.cloned.1.call-update) | async-done | bytes 786448 | tf_op jit(solution)/shard_map/reduce_scatter | solution.py:265
  1137.6 148.9 %reduce-scatter.33.cloned.1.call-done = bf16[256,2048]{1,0:T(8,128)(2,1)} async-done(((bf16[2048,2048]{1,0:T(8,128)(2,1)}), bf16[256,2048]{1,0:T(8,128)(2,1)}) %reduce-scatter.33.cloned.1.call-update) | async-done | bytes 1048592 | tf_op jit(solution)/shard_map/reduce_scatter | solution.py:274
  1286.5 152.0 %reduce-scatter.35.cloned.1.call-done = bf16[256,2048]{1,0:T(8,128)(2,1)} async-done(((bf16[2048,2048]{1,0:T(8,128)(2,1)}), bf16[256,2048]{1,0:T(8,128)(2,1)}) %reduce-scatter.35.cloned.1.call-update) | async-done | bytes 1048592 | tf_op jit(solution)/shard_map/reduce_scatter | solution.py:274
  1441.7 148.8 %reduce-scatter.39.cloned.1.call-done = bf16[2048,256]{1,0:T(8,128)(2,1)} async-done(((bf16[2048,2048]{1,0:T(8,128)(2,1)}), bf16[2048,256]{1,0:T(8,128)(2,1)}) %reduce-scatter.39.cloned.1.call-update) | async-done | bytes 1048592 | tf_op jit(solution)/shard_map/reduce_scatter | solution.py:280
  1590.6 152.4 %reduce-scatter.37.cloned.1.call-done = bf16[2048,256]{1,0:T(8,128)(2,1)} async-done(((bf16[2048,2048]{1,0:T(8,128)(2,1)}), bf16[2048,256]{1,0:T(8,128)(2,1)}) %reduce-scatter.37.cloned.1.call-update) | async-done | bytes 1048592 | tf_op jit(solution)/shard_map/reduce_scatter | solution.py:280
  (406 shorter events, 323.1 us)
Async XLA Ops:
  7.2 48.7 %copy-start.4 = (bf16[2,1,256,2048]{3,2,1,0:T(8,128)(2,1)S(1)}, bf16[2,1,256,2048]{3,2,1,0:T(8,128)(2,1)}, u32[]{:S(2)}) copy-start(bf16[2,1,256,2048]{3,2,1,0:T(8,128)(2,1)} %param.36) | copy-start | bytes 6291460
  7.2 116.9 %all-gather.15.cloned.1.call-start = ((), (), s32[]{:S(2)}) async-start(), calls=%async_computation.14 | async-start | bytes 2359296 | tf_op jit(solution)/shard_map/all_gather | solution.py:184
  8.0 116.2 %all-gather.25.cloned.1.call-start = ((), (), s32[]{:S(2)}) async-start(), calls=%async_computation.31 | async-start | bytes 5242880 | tf_op jit(solution)/shard_map/all_gather | solution.py:228
  11.1 125.2 %all-gather.23.cloned.1.call-start = ((), (), s32[]{:S(2)}) async-start(), calls=%async_computation.30 | async-start | bytes 5242880 | tf_op jit(solution)/shard_map/all_gather | solution.py:228
  11.9 161.0 %all-gather.21.cloned.1.call-start = ((), (), s32[]{:S(2)}) async-start(), calls=%async_computation.18 | async-start | bytes 5242880 | tf_op jit(solution)/shard_map/all_gather | solution.py:192
  59.8 215.5 %all-gather.13.cloned.1.call-start = ((), (), s32[]{:S(2)}) async-start(), calls=%async_computation.13 | async-start | bytes 7077888 | tf_op jit(solution)/shard_map/all_gather | solution.py:182
  61.1 249.0 %all-gather.11.cloned.1.call-start = ((), (), s32[]{:S(2)}) async-start(), calls=%async_computation.12 | async-start | bytes 5242880 | tf_op jit(solution)/shard_map/all_gather | solution.py:192
  61.6 469.7 %all-gather.17.cloned.1.call-start = ((), (), s32[]{:S(2)}) async-start(), calls=%async_computation.15 | async-start | bytes 9437184 | tf_op jit(solution)/shard_map/all_gather | solution.py:185
  62.4 500.4 %all-gather.19.cloned.1.call-start = ((), (), s32[]{:S(2)}) async-start(), calls=%async_computation.16 | async-start | bytes 9437184 | tf_op jit(solution)/shard_map/all_gather | solution.py:187
  63.1 771.1 %reduce-scatter.29.cloned.1.call-start = ((), (), s32[]{:S(2)}) async-start(), calls=%async_computation.24 | async-start | bytes 2359296 | tf_op jit(solution)/shard_map/reduce_scatter | solution.py:271
  122.9 217.3 %copy-start.25 = (f32[1024,64]{0,1:T(8,128)}, f32[1024,64]{0,1:T(8,128)S(1)}, u32[]{:S(2)}) copy-start(f32[1024,64]{0,1:T(8,128)S(1)} %maximum_maximum_fusion.1) | copy-start | bytes 786436
  482.7 351.5 %reduce-scatter.31.cloned.1.call-start = ((), (), s32[]{:S(2)}) async-start(), calls=%async_computation.25 | async-start | bytes 2359296 | tf_op jit(solution)/shard_map/reduce_scatter | solution.py:271
  522.0 314.2 %reduce-scatter.23.cloned.1.call-start = ((), (), s32[]{:S(2)}) async-start(), calls=%async_computation.21 | async-start | bytes 5242880 | tf_op jit(solution)/shard_map/reduce_scatter | solution.py:252
  607.3 228.9 %reduce-scatter.21.cloned.1.call-start = ((), (), s32[]{:S(2)}) async-start(), calls=%async_computation.20 | async-start | bytes 5242880 | tf_op jit(solution)/shard_map/reduce_scatter | solution.py:252
  668.7 175.1 %reduce-scatter.17.cloned.1.call-start = ((), (), s32[]{:S(2)}) async-start(), calls=%async_computation.17 | async-start | bytes 5242880 | tf_op jit(solution)/shard_map/reduce_scatter | solution.py:213
  688.8 202.1 %reduce-scatter.19.cloned.1.call-start = ((), (), s32[]{:S(2)}) async-start(), calls=%async_computation.19 | async-start | bytes 5242880 | tf_op jit(solution)/shard_map/reduce_scatter | solution.py:213
  708.9 304.9 %reduce-scatter.27.cloned.1.call-start = ((), (), s32[]{:S(2)}) async-start(), calls=%async_computation.23 | async-start | bytes 7077888 | tf_op jit(solution)/shard_map/reduce_scatter | solution.py:265
  721.2 413.6 %reduce-scatter.25.cloned.1.call-start = ((), (), s32[]{:S(2)}) async-start(), calls=%async_computation.22 | async-start | bytes 7077888 | tf_op jit(solution)/shard_map/reduce_scatter | solution.py:265
  733.0 553.5 %reduce-scatter.33.cloned.1.call-start = ((), (), s32[]{:S(2)}) async-start(), calls=%async_computation.26 | async-start | bytes 9437184 | tf_op jit(solution)/shard_map/reduce_scatter | solution.py:274
  747.2 691.3 %reduce-scatter.35.cloned.1.call-start = ((), (), s32[]{:S(2)}) async-start(), calls=%async_computation.27 | async-start | bytes 9437184 | tf_op jit(solution)/shard_map/reduce_scatter | solution.py:274
  761.9 828.7 %reduce-scatter.39.cloned.1.call-start = ((), (), s32[]{:S(2)}) async-start(), calls=%async_computation.29 | async-start | bytes 9437184 | tf_op jit(solution)/shard_map/reduce_scatter | solution.py:280
  778.1 964.8 %reduce-scatter.37.cloned.1.call-start = ((), (), s32[]{:S(2)}) async-start(), calls=%async_computation.28 | async-start | bytes 9437184 | tf_op jit(solution)/shard_map/reduce_scatter | solution.py:280
  794.5 41.7 %copy-start.5 = (bf16[2,1,256,2048]{3,2,1,0:T(8,128)(2,1)S(1)}, bf16[2,1,256,2048]{3,2,1,0:T(8,128)(2,1)}, u32[]{:S(2)}) copy-start(bf16[2,1,256,2048]{3,2,1,0:T(8,128)(2,1)} %param.36) | copy-start | bytes 6291460
  794.5 41.7 %copy-start.63 = (f32[2048]{0:T(1024)S(1)}, f32[2048]{0:T(1024)}, u32[]{:S(2)}) copy-start(f32[2048]{0:T(1024)} %copy-done.62) | copy-start | bytes 24580
  794.5 41.7 %copy-start.65 = (f32[256]{0:T(256)S(1)}, f32[256]{0:T(256)}, u32[]{:S(2)}) copy-start(f32[256]{0:T(256)} %copy-done.64) | copy-start | bytes 3076
  794.5 41.7 %copy-start.67 = (f32[256]{0:T(256)S(1)}, f32[256]{0:T(256)}, u32[]{:S(2)}) copy-start(f32[256]{0:T(256)} %copy-done.66) | copy-start | bytes 3076
  794.5 44.4 %copy-start.77 = (f32[256]{0:T(256)S(1)}, f32[256]{0:T(256)}, u32[]{:S(2)}) copy-start(f32[256]{0:T(256)} %copy-done.76) | copy-start | bytes 3076
  794.5 44.4 %copy-start.75 = (f32[256]{0:T(256)S(1)}, f32[256]{0:T(256)}, u32[]{:S(2)}) copy-start(f32[256]{0:T(256)} %copy-done.74) | copy-start | bytes 3076
  794.5 96.4 %copy-start.71 = (f32[256]{0:T(256)S(1)}, f32[256]{0:T(256)}, u32[]{:S(2)}) copy-start(f32[256]{0:T(256)} %copy-done.70) | copy-start | bytes 3076
  794.6 96.4 %copy-start.73 = (f32[256]{0:T(256)S(1)}, f32[256]{0:T(256)}, u32[]{:S(2)}) copy-start(f32[256]{0:T(256)} %copy-done.72) | copy-start | bytes 3076
  836.1 54.8 %copy-start.13 = (bf16[1,256,2048]{2,1,0:T(8,128)(2,1)S(1)}, bf16[1,256,2048]{2,1,0:T(8,128)(2,1)}, u32[]{:S(2)}) copy-start(bf16[1,256,2048]{2,1,0:T(8,128)(2,1)} %reduce-scatter.23.cloned.1.call-done) | copy-start | bytes 3145732
  939.4 806.7 %copy-start.97 = (f32[64]{0:T(128)}, f32[64]{0:T(128)S(1)}, u32[]{:S(2)}) copy-start(f32[64]{0:T(128)S(1)} %dynamic-slice.70) | copy-start | bytes 772
  (95 other events, 614.5 us)
Sparse Core Ops, SparseCore 0:
  10.1 54.6 all-gather.14
  67.0 32.7 all-gather.24
  101.8 34.4 all-gather.22
  138.4 34.4 all-gather.20
  175.3 99.9 all-gather.12
  277.3 32.6 all-gather.10
  312.1 124.9 all-gather.16
  439.1 123.5 all-gather.18
  566.3 66.2 reduce-scatter.28
  636.5 67.0 reduce-scatter.30
  706.1 43.5 reduce-scatter.22
  752.2 44.4 reduce-scatter.20
  799.3 44.5 reduce-scatter.16
  846.4 44.4 reduce-scatter.18
  894.4 119.4 reduce-scatter.26
  1017.3 117.5 reduce-scatter.24
  1138.3 148.1 reduce-scatter.32
  1290.4 147.9 reduce-scatter.34
  1442.1 148.4 reduce-scatter.38
  1594.5 148.4 reduce-scatter.36
where the time goes:
time: 1760 us; the launch traced here: 1750 us
  waiting for transfers between devices  1010 us (57%)
  matrix products  388 us (22%)
  blocking collectives  177 us (10%)
  other arithmetic  111 us (6%)
  local copies, waits for them, and re-layouts  52.3 us (3%)
    reduce_scatter x2, waiting for transfers between devices, shards(): lax.psum_scatter(big_grads[5].astype(jnp.bfloat16), 'fsdp', scatter_dimen...  301 us
    reduce_scatter x2, waiting for transfers between devices, shards(): lax.psum_scatter(big_grads[3].astype(jnp.bfloat16), 'fsdp', scatter_dimen...  301 us
    reduce_scatter x2, waiting for transfers between devices, shards(): lax.psum_scatter(big_grads[0].astype(jnp.bfloat16), 'fsdp', scatter_dimen...  188 us
    unnamed x3, blocking collectives  120 us
    all_gather x1, waiting for transfers between devices, shards(): lax.all_gather(qkv_weight, 'fsdp', axis=0, tiled=True)  102 us
    dot_general x8, matrix products, dot_cols(): lax.dot_general(left, right, (((1,), (1,)), ((), ())), preferred_element_...  101 us
    dot_general x8, matrix products, dot_rows(): lax.dot_general(left, right, (((0,), (0,)), ((), ())), preferred_element_...  92.4 us
    reduce_scatter x2, waiting for transfers between devices, shards(): lax.psum_scatter(branch_terms.reshape(seq_count, length, model_width).ast...  51.9 us
  transfers between devices with their start and end apart: 20, of which 13 were waited for; matrix products, arithmetic and copies ran while one was open for 30% of the time, Pallas kernels for 0%

commit v1 on v0

v1 whole, which is shorter than its diff:
```python
import functools
import math

import jax
import jax.numpy as jnp
from jax import lax
from jax.experimental import pallas as pl
from jax.experimental.pallas import tpu as pltpu
from jax.sharding import PartitionSpec as P

ROT = 32
LANES = 128

norm_epsilon = 1e-05
gelu_factor = 0.7978845608028654
mask_fill = -1e30
BF = jnp.bfloat16
F32 = jnp.float32
VMEM_LIMIT = 48 * 1024 * 1024


def layer_norm(resid_rows, gain_vec, shift_vec):
    row_mean = jnp.mean(resid_rows, axis=-1, keepdims=True)
    centred = resid_rows - row_mean
    row_var = jnp.mean(centred * centred, axis=-1, keepdims=True)
    return centred * lax.rsqrt(row_var + norm_epsilon) * gain_vec + shift_vec


def gelu_tanh(inner):
    return 0.5 * inner * (1.0 + jnp.tanh(gelu_factor * (inner + 0.044715 * inner * inner * inner)))


def rotary_tables(length, head_dim, rot_dim):
    half_rot = rot_dim // 2
    inv_freq = 10000.0 ** (-2.0 * jnp.arange(half_rot, dtype=F32) / rot_dim)
    angles = jnp.arange(length, dtype=F32)[:, None] * inv_freq[None, :]
    cos, sin = jnp.cos(angles), jnp.sin(angles)
    rest = jnp.ones((length, head_dim - rot_dim), F32)
    cosine = jnp.concatenate([cos, cos, rest], axis=1)
    lower = jnp.concatenate([-sin, 0.0 * sin, 0.0 * rest], axis=1)
    upper = jnp.concatenate([0.0 * sin, sin, 0.0 * rest], axis=1)
    copies = LANES // head_dim
    return tuple(jnp.tile(table, (1, copies)) for table in (cosine, lower, upper))


def turn(vals, cosine, lower, upper):
    half_rot = ROT // 2
    ahead = pltpu.roll(vals, LANES - half_rot, 1)
    behind = pltpu.roll(vals, half_rot, 1)
    return vals * cosine + ahead * lower + behind * upper


def dot_rows(left, right):
    return lax.dot_general(left, right, (((0,), (0,)), ((), ())), preferred_element_type=F32)


def dot_cols(left, right):
    return lax.dot_general(left, right, (((1,), (1,)), ((), ())), preferred_element_type=F32)


def dot_plain(left, right):
    return lax.dot_general(left, right, (((1,), (0,)), ((), ())), preferred_element_type=F32)


def causal_fill(scores, first, fill):
    keys, cols = scores.shape
    key_ids = lax.broadcasted_iota(jnp.int32, (keys, cols), 0)
    query_ids = lax.broadcasted_iota(jnp.int32, (keys, cols), 1) + first
    return jnp.where(key_ids <= query_ids, scores, fill)


def head_lanes(vals, head, head_dim):
    lane_ids = lax.broadcasted_iota(jnp.int32, vals.shape, 1)
    return jnp.where(lane_ids // head_dim == head, vals, jnp.zeros_like(vals))


def attend_kernel(head_dim, block, qkv_ref, cos_ref, low_ref, up_ref, rot_ref, attn_ref, lse_ref):
    length = qkv_ref.shape[0]
    scale = 1.0 / math.sqrt(head_dim)
    tables = (cos_ref[...], low_ref[...], up_ref[...])
    queries = turn(qkv_ref[:, :LANES], *tables).astype(BF)
    keys = turn(qkv_ref[:, LANES : 2 * LANES], *tables).astype(BF)
    values = qkv_ref[:, 2 * LANES :].astype(BF)
    rot_ref[:, :LANES] = queries
    rot_ref[:, LANES : 2 * LANES] = keys
    rot_ref[:, 2 * LANES :] = values
    heads = LANES // head_dim
    for first in range(0, length, block):
        last = first + block
        total = jnp.zeros((block, LANES), F32)
        for head in range(heads):
            query_block = head_lanes(queries[first:last], head, head_dim)
            scores = dot_cols(keys[:last], query_block) * scale
            scores = causal_fill(scores, first, mask_fill)
            col_max = jnp.max(scores, axis=0, keepdims=True)
            exp_scores = jnp.exp(scores - col_max)
            denom = jnp.sum(exp_scores, axis=0, keepdims=True)
            prob_low = (exp_scores * (1.0 / denom)).astype(BF)
            total += dot_rows(prob_low, head_lanes(values[:last], head, head_dim))
            lse_ref[0, head : head + 1, first:last] = col_max + jnp.log(denom)
        attn_ref[first:last, :] = total.astype(BF)


def attend_back_kernel(head_dim, block, rot_ref, grad_ref, lse_ref, cos_ref, low_ref, up_ref, out_ref, key_acc, value_acc):
    length = rot_ref.shape[0]
    scale = 1.0 / math.sqrt(head_dim)
    tables = (cos_ref[...], -low_ref[...], -up_ref[...])
    heads = LANES // head_dim
    key_acc[...] = jnp.zeros_like(key_acc)
    value_acc[...] = jnp.zeros_like(value_acc)
    for first in range(0, length, block):
        last = first + block
        total = jnp.zeros((block, LANES), F32)
        for head in range(heads):
            query_block = head_lanes(rot_ref[first:last, :LANES], head, head_dim)
            grad_block = head_lanes(grad_ref[first:last, :], head, head_dim)
            keys = rot_ref[:last, LANES : 2 * LANES]
            scores = dot_cols(keys, query_block) * scale
            probs = jnp.exp(scores - lse_ref[0, head : head + 1, first:last])
            probs = causal_fill(probs, first, 0.0)
            value_acc[:last, :] += dot_plain(probs.astype(BF), grad_block)
            prob_grad = dot_cols(rot_ref[:last, 2 * LANES :], grad_block)
            inner_sum = jnp.sum(probs * prob_grad, axis=0, keepdims=True)
            score_grad = (probs * (prob_grad - inner_sum)).astype(BF)
            total += dot_rows(score_grad, head_lanes(keys, head, head_dim))
            key_acc[:last, :] += dot_plain(score_grad, query_block)
        out_ref[first:last, :LANES] = turn(total * scale, *(table[first:last] for table in tables)).astype(BF)
    out_ref[:, LANES : 2 * LANES] = turn(key_acc[...] * scale, *tables).astype(BF)
    out_ref[:, 2 * LANES :] = value_acc[...].astype(BF)


def attention_cost(seqs, pairs, length, matmuls):
    flops = seqs * pairs * matmuls * 2 * 2 * length * length * LANES
    return pl.CostEstimate(flops=flops, bytes_accessed=seqs * pairs * length * LANES * 16, transcendentals=0)


def attend(qkv, tables, length, head_dim):
    tokens, width = qkv.shape
    seqs, pairs = tokens // length, width // (3 * LANES)
    heads = LANES // head_dim
    block = min(256, length)
    table_spec = pl.BlockSpec((length, LANES), lambda s, h: (0, 0))
    return pl.pallas_call(
        functools.partial(attend_kernel, head_dim, block),
        grid=(seqs, pairs),
        in_specs=[pl.BlockSpec((length, 3 * LANES), lambda s, h: (s, h))] + [table_spec] * 3,
        out_specs=[
            pl.BlockSpec((length, 3 * LANES), lambda s, h: (s, h)),
            pl.BlockSpec((length, LANES), lambda s, h: (s, h)),
            pl.BlockSpec((1, heads, length), lambda s, h: (s * pairs + h, 0, 0)),
        ],
        out_shape=[
            jax.ShapeDtypeStruct((tokens, width), BF),
            jax.ShapeDtypeStruct((tokens, pairs * LANES), BF),
            jax.ShapeDtypeStruct((seqs * pairs, heads, length), F32),
        ],
        compiler_params=pltpu.CompilerParams(vmem_limit_bytes=VMEM_LIMIT),
        cost_estimate=attention_cost(seqs, pairs, length, 3),
    )(qkv, *tables)


def attend_back(rot, attn_grad, lse, tables, length, head_dim):
    tokens, width = rot.shape
    seqs, pairs = tokens // length, width // (3 * LANES)
    heads = LANES // head_dim
    block = min(256, length)
    table_spec = pl.BlockSpec((length, LANES), lambda s, h: (0, 0))
    return pl.pallas_call(
        functools.partial(attend_back_kernel, head_dim, block),
        grid=(seqs, pairs),
        in_specs=[
            pl.BlockSpec((length, 3 * LANES), lambda s, h: (s, h)),
            pl.BlockSpec((length, LANES), lambda s, h: (s, h)),
            pl.BlockSpec((1, heads, length), lambda s, h: (s * pairs + h, 0, 0)),
        ]
        + [table_spec] * 3,
        out_specs=pl.BlockSpec((length, 3 * LANES), lambda s, h: (s, h)),
        out_shape=jax.ShapeDtypeStruct((tokens, width), BF),
        scratch_shapes=[pltpu.VMEM((length, LANES), F32), pltpu.VMEM((length, LANES), F32)],
        compiler_params=pltpu.CompilerParams(vmem_limit_bytes=VMEM_LIMIT),
        cost_estimate=attention_cost(seqs, pairs, length, 6),
    )(rot, attn_grad, lse, *tables)


def shards(
    inputs,
    ln_gain,
    ln_bias,
    qkv_weight,
    qkv_bias,
    out_weight,
    out_bias,
    up_weight,
    up_bias,
    down_weight,
    down_bias,
    cotangent,
):
    micro_count, _, token_rows, model_width = inputs.shape
    fsdp_size, tp_size = lax.axis_size("fsdp"), lax.axis_size("tp")
    line = fsdp_size // 2
    fsdp_at, tp_at = lax.axis_index("fsdp"), lax.axis_index("tp")
    line_at, pair_at = fsdp_at // 2, fsdp_at % 2
    plane_size = 2 * tp_size
    planes = [[plane * plane_size + i for i in range(plane_size)] for plane in range(line)]
    ring = [(f, ((f // 2 + 1) % line) * 2 + f % 2) for f in range(fsdp_size)]
    length = token_rows * tp_size
    head_dim = qkv_bias.shape[2] * fsdp_size
    shard_rows = model_width // fsdp_size
    line_rows = 2 * shard_rows
    attn_cols = out_weight.shape[0] // 2
    qkv_cols = 3 * attn_cols
    pairs = attn_cols // LANES
    mlp_cols = up_weight.shape[1] // 2
    both_axes = ("fsdp", "tp")

    def swap_pair(vals):
        return lax.ppermute(vals, "fsdp", [(f, f ^ 1) for f in range(fsdp_size)])

    def gather_plane(vals):
        return lax.all_gather(vals, both_axes, axis=0, tiled=True, axis_index_groups=planes)

    def scatter_plane(vals):
        return lax.psum_scatter(vals, both_axes, scatter_dimension=0, tiled=True, axis_index_groups=planes)

    def after(vals, *others):
        return lax.optimization_barrier((vals,) + others)[0]

    def gather_small(vals):
        cur = vals[None]
        bit = 1
        while bit < tp_size:
            other = lax.ppermute(cur, "tp", [(t, t ^ bit) for t in range(tp_size)])
            upper = (tp_at & bit) != 0
            cur = jnp.where(upper, jnp.concatenate([other, cur]), jnp.concatenate([cur, other]))
            bit *= 2
        bit = 1
        while bit < fsdp_size:
            other = lax.ppermute(cur, "fsdp", [(f, f ^ bit) for f in range(fsdp_size)])
            upper = (fsdp_at & bit) != 0
            cur = jnp.where(upper, jnp.concatenate([other, cur]), jnp.concatenate([cur, other]))
            bit *= 2
        return cur

    def sum_small(everywhere, over_fsdp):
        cur = everywhere
        bit = 1
        while bit < tp_size:
            cur = cur + lax.ppermute(cur, "tp", [(t, t ^ bit) for t in range(tp_size)])
            bit *= 2
        cur = jnp.concatenate([cur, over_fsdp])
        bit = 1
        while bit < fsdp_size:
            cur = cur + lax.ppermute(cur, "fsdp", [(f, f ^ bit) for f in range(fsdp_size)])
            bit *= 2
        return cur[: everywhere.shape[0]], cur[everywhere.shape[0] :]

    small = jnp.concatenate(
        [vec.reshape(-1) for vec in (ln_gain, ln_bias, out_bias, down_bias, qkv_bias, up_bias)]
    )
    small_all = gather_small(small)
    vec_size = ln_gain.shape[0]
    gain_vec, shift_vec, bias_out, bias_down = (
        small_all[:, i * vec_size : (i + 1) * vec_size].reshape(-1).astype(F32) for i in range(4)
    )
    bias_both = bias_out + bias_down
    mine = lax.dynamic_slice_in_dim(
        small_all.reshape(fsdp_size, tp_size, -1), tp_at, 1, axis=1
    )[:, 0].astype(F32)
    at = 4 * vec_size
    qkv_b = mine[:, at : at + qkv_bias.size].reshape(fsdp_size, 3, 2, pairs, -1, qkv_bias.shape[2])
    qkv_b = lax.dynamic_slice_in_dim(qkv_b, pair_at, 1, axis=2)[:, :, 0]
    qkv_b = qkv_b.transpose(2, 1, 3, 0, 4).reshape(1, qkv_cols)
    at += qkv_bias.size
    up_b = mine[:, at:].reshape(fsdp_size, up_bias.shape[0], up_bias.shape[1])
    up_b = up_b.transpose(1, 0, 2).reshape(2, mlp_cols)
    up_b = lax.dynamic_slice_in_dim(up_b, pair_at, 1, axis=0)

    def attn_half(half):
        qkv_part = lax.dynamic_slice_in_dim(qkv_weight, half * attn_cols, attn_cols, axis=2)
        qkv_part = qkv_part.reshape(shard_rows, 3, pairs, LANES).transpose(0, 2, 1, 3)
        out_part = lax.dynamic_slice_in_dim(out_weight, half * attn_cols, attn_cols, axis=0)
        return jnp.concatenate([qkv_part.reshape(shard_rows, qkv_cols), out_part.T], axis=1)

    def up_half(half):
        return lax.dynamic_slice_in_dim(up_weight, half * mlp_cols, mlp_cols, axis=1)

    def down_half(half):
        return lax.dynamic_slice_in_dim(down_weight, half * mlp_cols, mlp_cols, axis=0).T

    def pair_shard(half_of):
        own = half_of(pair_at)
        other = swap_pair(half_of(1 - pair_at))
        return jnp.where(
            pair_at == 0, jnp.concatenate([own, other]), jnp.concatenate([other, own])
        )

    def gather_line(shard):
        whole = jnp.zeros((line * line_rows, shard.shape[1]), BF)
        whole = lax.dynamic_update_slice_in_dim(whole, shard, line_at * line_rows, axis=0)
        moving = shard
        for step in range(1, line):
            moving = lax.ppermute(moving, "fsdp", ring)
            at_line = (line_at - step) % line
            whole = lax.dynamic_update_slice_in_dim(whole, moving, at_line * line_rows, axis=0)
        return whole, moving

    attn_shard = pair_shard(attn_half)
    w_attn, last_moved = gather_line(attn_shard)
    up_shard = pair_shard(up_half)
    up_shard = after(up_shard, last_moved)
    w_up, last_moved = gather_line(up_shard)
    down_shard = pair_shard(down_half)
    down_shard = after(down_shard, last_moved)
    w_down, _ = gather_line(down_shard)
    w_qkv, w_out = w_attn[:, :qkv_cols], w_attn[:, qkv_cols:]

    resid, cots, plane_rows, plane_cots = [], [], [], []
    for micro in range(micro_count):
        resid.append(inputs[micro].reshape(token_rows, model_width))
        cots.append(cotangent[micro].reshape(token_rows, model_width))
    before = None
    for micro in range(micro_count):
        sent = resid[micro] if before is None else after(resid[micro], before)
        before = gather_plane(sent)
        plane_rows.append(before)
    for micro in range(micro_count):
        before = gather_plane(after(cots[micro], before))
        plane_cots.append(before)

    tables = rotary_tables(length, head_dim, ROT)
    normed, rots, attns, lses, acts, pre_acts, outputs = ([] for _ in range(7))
    for micro in range(micro_count):
        normed.append(layer_norm(plane_rows[micro].astype(F32), gain_vec, shift_vec).astype(BF))
        qkv = dot_plain(normed[micro], w_qkv) + qkv_b
        rot, attn, lse = attend(qkv, tables, length, head_dim)
        rots.append(rot)
        attns.append(attn)
        lses.append(lse)
    for micro in range(micro_count):
        pre = dot_plain(normed[micro], w_up) + up_b
        pre_acts.append(pre)
        acts.append(gelu_tanh(pre).astype(BF))
    for micro in range(micro_count):
        branch = dot_cols(
            jnp.concatenate([attns[micro], acts[micro]], axis=1), jnp.concatenate([w_out, w_down], axis=1)
        ).astype(BF)
        branch = scatter_plane(branch).astype(F32)
        outputs.append((resid[micro].astype(F32) + branch + bias_both).astype(BF))

    def scatter_line(part):
        def own(step):
            at_line = (line_at - step) % line
            return lax.dynamic_slice_in_dim(part, at_line * line_rows, line_rows, axis=0).astype(F32)

        moving = own(1)
        for step in range(2, line + 1):
            moving = lax.ppermute(moving.astype(BF), "fsdp", ring).astype(F32) + own(step)
        keep = lax.dynamic_slice_in_dim(moving, pair_at * shard_rows, shard_rows, axis=0)
        give = lax.dynamic_slice_in_dim(moving, (1 - pair_at) * shard_rows, shard_rows, axis=0)
        got = swap_pair(give.astype(BF)).astype(F32)
        return jnp.where(pair_at == 0, keep, got), jnp.where(pair_at == 0, got, keep)

    down_part = sum(dot_rows(plane_cots[m], acts[m]) for m in range(micro_count)).astype(BF)
    down_grads = scatter_line(down_part)
    pre_grads = []
    for micro in range(micro_count):
        act_grad = dot_plain(plane_cots[micro], w_down)
        pre_grads.append(jax.vjp(gelu_tanh, pre_acts[micro])[1](act_grad)[0].astype(BF))
    up_part = sum(dot_rows(normed[m], pre_grads[m]) for m in range(micro_count)).astype(BF)
    up_grads = scatter_line(up_part)
    qkv_grads = []
    for micro in range(micro_count):
        attn_grad = dot_plain(plane_cots[micro], w_out).astype(BF)
        qkv_grads.append(attend_back(rots[micro], attn_grad, lses[micro], tables, length, head_dim))
    attn_part = jnp.concatenate(
        [
            sum(dot_rows(normed[m], qkv_grads[m]) for m in range(micro_count)).astype(BF),
            sum(dot_rows(plane_cots[m], attns[m]) for m in range(micro_count)).astype(BF),
        ],
        axis=1,
    )
    attn_grads = scatter_line(attn_part)
    input_grads = []
    gain_total = jnp.zeros((model_width,), F32)
    shift_total = jnp.zeros((model_width,), F32)
    bias_total = jnp.zeros((model_width,), F32)
    for micro in range(micro_count):
        normed_grad = dot_cols(
            jnp.concatenate([qkv_grads[micro], pre_grads[micro]], axis=1),
            jnp.concatenate([w_qkv, w_up], axis=1),
        ).astype(BF)
        normed_grad = scatter_plane(normed_grad).astype(F32)
        norm_back = jax.vjp(layer_norm, resid[micro].astype(F32), gain_vec, shift_vec)[1]
        rows_grad, gain_grad, shift_grad = norm_back(normed_grad)
        cot = cots[micro].astype(F32)
        input_grads.append((cot + rows_grad).astype(BF))
        gain_total += gain_grad
        shift_total += shift_grad
        bias_total += jnp.sum(cot, axis=0)

    up_b_grad = sum(jnp.sum(pre_grads[m].astype(F32), axis=0) for m in range(micro_count))
    qkv_b_grad = sum(jnp.sum(qkv_grads[m].astype(F32), axis=0) for m in range(micro_count))
    qkv_b_grad = qkv_b_grad.reshape(pairs, 3, -1).transpose(1, 0, 2).reshape(3, attn_cols)

    def in_half(vals):
        blank = jnp.zeros_like(vals)
        return jnp.where(
            pair_at == 0, jnp.concatenate([vals, blank], axis=-1), jnp.concatenate([blank, vals], axis=-1)
        )

    small_sums, bias_sums = sum_small(
        jnp.concatenate([gain_total, shift_total, bias_total]),
        jnp.concatenate([in_half(up_b_grad), in_half(qkv_b_grad).reshape(-1)]),
    )
    small_sums = small_sums.reshape(3, fsdp_size * tp_size, vec_size)
    small_sums = lax.dynamic_slice_in_dim(small_sums, fsdp_at * tp_size + tp_at, 1, axis=1)[:, 0]
    gain_sum, shift_sum, bias_sum = small_sums[0], small_sums[1], small_sums[2]
    up_b_sum = bias_sums[: 2 * mlp_cols].reshape(up_bias.shape[0], -1)
    up_b_sum = lax.dynamic_slice_in_dim(up_b_sum, fsdp_at * up_bias.shape[1], up_bias.shape[1], axis=1)
    qkv_b_sum = bias_sums[2 * mlp_cols :].reshape(3, qkv_bias.shape[1], -1)
    qkv_b_sum = lax.dynamic_slice_in_dim(qkv_b_sum, fsdp_at * qkv_bias.shape[2], qkv_bias.shape[2], axis=2)

    def qkv_columns(vals):
        return vals[:, :qkv_cols].reshape(shard_rows, pairs, 3, LANES).transpose(0, 2, 1, 3).reshape(
            shard_rows, 3, attn_cols
        )

    qkv_w_grad = jnp.concatenate([qkv_columns(half) for half in attn_grads], axis=2)
    out_w_grad = jnp.concatenate([half[:, qkv_cols:].T for half in attn_grads], axis=0)
    up_w_grad = jnp.concatenate(up_grads, axis=1)
    down_w_grad = jnp.concatenate([half.T for half in down_grads], axis=0)
    return (
        jnp.stack(outputs, axis=0)[:, None],
        jnp.stack(input_grads, axis=0)[:, None],
        gain_sum,
        shift_sum,
        qkv_w_grad,
        qkv_b_sum,
        out_w_grad,
        bias_sum,
        up_w_grad,
        up_b_sum,
        down_w_grad,
        bias_sum,
    )


def solution(mesh):
    return jax.shard_map(
        shards,
        mesh=mesh,
        in_specs=(
            P(None, "fsdp", "tp", None),
            P(("fsdp", "tp")),
            P(("fsdp", "tp")),
            P("fsdp", None, "tp"),
            P(None, "tp", "fsdp"),
            P("tp", "fsdp"),
            P(("fsdp", "tp")),
            P("fsdp", "tp"),
            P("tp", "fsdp"),
            P("tp", "fsdp"),
            P(("fsdp", "tp")),
            P(None, "fsdp", "tp", None),
        ),
        out_specs=(
            P(None, "fsdp", "tp", None),
            P(None, "fsdp", "tp", None),
            P(("fsdp", "tp")),
            P(("fsdp", "tp")),
            P("fsdp", None, "tp"),
            P(None, "tp", "fsdp"),
            P("tp", "fsdp"),
            P(("fsdp", "tp")),
            P("fsdp", "tp"),
            P("tp", "fsdp"),
            P("tp", "fsdp"),
            P(("fsdp", "tp")),
        ),
        check_vma=False,
    )
```

time: 1760 us -> 946 us (0.54)
  waiting for transfers between devices: 1010 us -> 406 us
  blocking collectives: 177 us -> 0 us
  matrix products: 388 us -> 275 us
  Pallas kernels: 0 us -> 77.2 us
  other arithmetic: 111 us -> 75.3 us
  local copies, waits for them, and re-layouts: 52.3 us -> 71.6 us
  starting transfers between devices: 1.39 us -> 19.4 us
    reduce_scatter x12 -> x4, waiting for transfers between devices: 842 us -> 0.04 us  [scatter_plane(): lax.psum_scatter(vals, both_axes, scatter_dimension=0, tiled=True, axis_i...]
    ppermute x0 -> x34, waiting for transfers between devices: none -> 349 us  [the longest x9 134 us: scatter_line(): lax.ppermute(moving.astype(BF), 'fsdp', ring).astype(F32) + own(step)]
    unnamed x3 -> x0, blocking collectives: 120 us -> none
    all_gather x8 -> x4, waiting for transfers between devices: 162 us -> 55.8 us  [gather_plane(): lax.all_gather(vals, both_axes, axis=0, tiled=True, axis_index_groups=pla...]
    dot_general x32 -> x8, matrix products: 195 us -> 113 us  [dot_plain(): lax.dot_general(left, right, (((1,), (0,)), ((), ())), preferred_element_...]
    pallas_call x0 -> x4, Pallas kernels: none -> 77.2 us  [the longest x2 46.5 us: attend_back(): pl.pallas_call(functools.partial(attend_back_kernel, head_dim, block), gr...]
    all_gather x2 -> x0, blocking collectives: 56.5 us -> none  [the longest x1 30.5 us: shards(): lax.all_gather(qkv_bias, 'fsdp', axis=2, tiled=True)]
    dot_general x8 -> x4, matrix products: 101 us -> 74.6 us  [dot_cols(): lax.dot_general(left, right, (((1,), (1,)), ((), ())), preferred_element_...]
  transfers between devices with their start and end apart: 20 -> 42, of which waited for: 13 -> 28; matrix products, arithmetic and copies ran while one was open for 30% -> 33% of each run, Pallas kernels for 0% -> 6%
where the time goes in v1:
time: 946 us; the launch traced here: 940 us
  waiting for transfers between devices  406 us (43%)
  matrix products  275 us (29%)
  Pallas kernels  77.2 us (8%)
  other arithmetic  75.3 us (8%)
  local copies, waits for them, and re-layouts  71.6 us (8%)
  starting transfers between devices  19.4 us (2%)
  between operations  16.1 us (2%)
    ppermute x9, waiting for transfers between devices, scatter_line(): lax.ppermute(moving.astype(BF), 'fsdp', ring).astype(F32) + own(step)  134 us
    ppermute x9, waiting for transfers between devices, gather_line(): moving = lax.ppermute(moving, 'fsdp', ring)  121 us
    dot_general x8, matrix products, dot_plain(): lax.dot_general(left, right, (((1,), (0,)), ((), ())), preferred_element_...  113 us
    dot_general x8, matrix products, dot_rows(): lax.dot_general(left, right, (((0,), (0,)), ((), ())), preferred_element_...  86.6 us
    dot_general x4, matrix products, dot_cols(): lax.dot_general(left, right, (((1,), (1,)), ((), ())), preferred_element_...  74.6 us
    all_gather x4, waiting for transfers between devices, gather_plane(): lax.all_gather(vals, both_axes, axis=0, tiled=True, axis_index_groups=pla...  55.8 us
    ppermute x6, waiting for transfers between devices, swap_pair(): return lax.ppermute(vals, 'fsdp', [(f, f ^ 1) for f in range(fsdp_size)])  51.3 us
    pallas_call x2, Pallas kernels, attend_back(): pl.pallas_call(functools.partial(attend_back_kernel, head_dim, block), gr...  46.5 us
  transfers between devices with their start and end apart: 42, of which 28 were waited for; matrix products, arithmetic and copies ran while one was open for 33% of the time, Pallas kernels for 6%

profile of v1, /device:TPU:0, one launch (start us, length us, event | category | flops | bytes accessed | tf_op | source)
XLA Modules:
  0.0 940.1 jit_solution(16138745190179352264)
XLA Ops:
  12.0 55.7 %all-gather.6.cloned.1.call-done = bf16[2048,2048]{1,0:T(8,128)(2,1)} async-done(((bf16[256,2048]{1,0:T(8,128)(2,1)}), bf16[2048,2048]{1,0:T(8,128)(2,1)}) %all-gather.6.cloned.1.call-update) | async-done | bytes 8388624 | tf_op jit(solution)/shard_map/all_gather | solution.py:221
  70.7 15.4 %collective-permute-done.5 = bf16[256,1024]{0,1:T(8,128)(2,1)S(1)} collective-permute-done((bf16[256,1024]{0,1:T(8,128)(2,1)S(1)}, bf16[256,1024]{0,1:T(8,128)(2,1)S(1)}, u32[]{:S(2)}, u32[]{:S(2)}) %collective-permute-start.5) | collective-permute-done | bytes 524320 | tf_op jit(solution)/shard_map/ppermute | solution.py:218
  91.3 23.6 %collective-permute-done.6 = bf16[512,1024]{0,1:T(8,128)(2,1)S(1)} collective-permute-done((bf16[512,1024]{0,1:T(8,128)(2,1)S(1)}, bf16[512,1024]{0,1:T(8,128)(2,1)S(1)}, u32[]{:S(2)}, u32[]{:S(2)}) %collective-permute-start.6) | collective-permute-done | bytes 1048608 | tf_op jit(solution)/shard_map/ppermute | solution.py:303
  115.9 24.1 %collective-permute-done.7 = bf16[512,1024]{0,1:T(8,128)(2,1)} collective-permute-done((bf16[512,1024]{0,1:T(8,128)(2,1)S(1)}, bf16[512,1024]{0,1:T(8,128)(2,1)}, u32[]{:S(2)}, u32[]{:S(2)}) %collective-permute-start.7) | collective-permute-done | bytes 1048608 | tf_op jit(solution)/shard_map/ppermute | solution.py:303
  143.4 18.6 %collective-permute-done.9 = bf16[256,1024]{0,1:T(8,128)(2,1)S(1)} collective-permute-done((bf16[256,1024]{0,1:T(8,128)(2,1)S(1)}, bf16[256,1024]{0,1:T(8,128)(2,1)S(1)}, u32[]{:S(2)}, u32[]{:S(2)}) %collective-permute-start.9) | collective-permute-done | bytes 524320 | tf_op jit(solution)/shard_map/ppermute | solution.py:218
  163.5 24.3 %collective-permute-done.10 = bf16[512,1024]{0,1:T(8,128)(2,1)S(1)} collective-permute-done((bf16[512,1024]{0,1:T(8,128)(2,1)S(1)}, bf16[512,1024]{0,1:T(8,128)(2,1)S(1)}, u32[]{:S(2)}, u32[]{:S(2)}) %collective-permute-start.10) | collective-permute-done | bytes 1048608 | tf_op jit(solution)/shard_map/ppermute | solution.py:303
  187.8 23.4 %collective-permute-done.11 = bf16[512,1024]{0,1:T(8,128)(2,1)S(1)} collective-permute-done((bf16[512,1024]{0,1:T(8,128)(2,1)S(1)}, bf16[512,1024]{0,1:T(8,128)(2,1)S(1)}, u32[]{:S(2)}, u32[]{:S(2)}) %collective-permute-start.11) | collective-permute-done | bytes 1048608 | tf_op jit(solution)/shard_map/ppermute | solution.py:303
  222.7 11.8 %collective-permute-done.12 = bf16[512,1024]{0,1:T(8,128)(2,1)} collective-permute-done((bf16[512,1024]{0,1:T(8,128)(2,1)S(1)}, bf16[512,1024]{0,1:T(8,128)(2,1)}, u32[]{:S(2)}, u32[]{:S(2)}) %collective-permute-start.12) | collective-permute-done | bytes 1048608 | tf_op jit(solution)/shard_map/ppermute | solution.py:303
  260.1 19.7 %collective-permute-done.4 = bf16[16,704]{1,0:T(8,128)(2,1)S(1)} collective-permute-done((bf16[16,704]{1,0:T(8,128)(2,1)S(1)}, bf16[16,704]{1,0:T(8,128)(2,1)S(1)}, u32[]{:S(2)}, u32[]{:S(2)}) %collective-permute-start.4) | collective-permute-done | bytes 22560 | tf_op jit(solution)/shard_map/ppermute | solution.py:239
  300.6 12.7 %collective-permute-done.16 = bf16[512,1024]{0,1:T(8,128)(2,1)S(1)} collective-permute-done((bf16[512,1024]{0,1:T(8,128)(2,1)}, bf16[512,1024]{0,1:T(8,128)(2,1)S(1)}, u32[]{:S(2)}, u32[]{:S(2)}) %collective-permute-start.16) | collective-permute-done | bytes 1048608 | tf_op jit(solution)/shard_map/ppermute | solution.py:303
  351.1 15.4 %shard_map.212 = (bf16[2048,768]{1,0:T(8,128)(2,1)S(1)}, bf16[2048,256]{1,0:T(8,128)(2,1)S(1)}, f32[4,2,1024]{2,1,0:T(2,128)S(1)}) custom-call(f32[2048,768]{1,0:T(8,128)} %broadcast_add_fusion.qkv_ref, f32[1024,128]{1,0:T(8,128)S(1)} %copy.78.cos_ref, f32[1024,128]{1,0:T(8,128)S(1)} %copy.79.low_ref, f32[1024,128]{1,0:T(8,128)S(1)} %copy.80.up_ref), custom_call_target="tpu_custom_call" | custom-call | flops 6442450944 | bytes 8388608 | tf_op jit(solution)/shard_map/pallas_call | solution.py:143
  366.5 14.1 %fusion.96 = f32[2048,1024]{0,1:T(8,128)} fusion(bf16[2048,2048]{1,0:T(8,128)(2,1)S(1)} %copy-done.33, bf16[2048,1024]{0,1:T(8,128)(2,1)} %copy-done.44), kind=kOutput, calls=%fused_computation.245 | convolution fusion | flops 8589934592 | bytes 20971520 | tf_op jit(solution)/shard_map/dot_general | solution.py:62
  380.6 13.5 %fusion.95 = f32[2048,1024]{0,1:T(8,128)} fusion(bf16[2048,2048]{1,0:T(8,128)(2,1)} %get-tuple-element.125, bf16[2048,1024]{0,1:T(8,128)(2,1)S(1)} %copy-done.45), kind=kOutput, calls=%fused_computation.244 | convolution fusion | flops 8589934592 | bytes 20971520 | tf_op jit(solution)/shard_map/dot_general | solution.py:62
  400.3 23.1 %shard_map.214 = bf16[2048,768]{1,0:T(8,128)(2,1)S(1)} custom-call(bf16[2048,768]{1,0:T(8,128)(2,1)} %copy-done.19, bf16[2048,256]{1,0:T(8,128)(2,1)S(1)} %convolution_convert_fusion.4.grad_ref, f32[4,2,1024]{2,1,0:T(2,128)S(1)} %get-tuple-element.33.lse_ref, f32[1024,128]{1,0:T(8,128)S(1)} %copy-done.8, f32[1024,128]{1,0:T(8,128)S(1)} %copy-done.12, ...), custom_call_target="tpu_custom_call" | custom-call | flops 12884901888 | bytes 8388608 | tf_op jit(solution)/shard_map/pallas_call | solution.py:168
  426.8 15.9 %fusion.97 = f32[2048,1024]{0,1:T(8,128)} fusion(bf16[2048,2048]{1,0:T(8,128)(2,1)} %all-gather.10.cloned.1.call-done, bf16[2048,1024]{0,1:T(8,128)(2,1)} %copy-done.41), kind=kOutput, calls=%fused_computation.246 | convolution fusion | flops 8589934592 | bytes 20971520 | tf_op jit(solution)/shard_map/dot_general | solution.py:62
  442.7 33.8 %convert_reduce_fusion.3 = (f32[1024]{0:T(1024)}, bf16[2048,1024]{0,1:T(8,128)(2,1)}, bf16[2048,1024]{0,1:T(8,128)(2,1)}, bf16[2048,1024]{0,1:T(8,128)(2,1)}, f32[1024]{0:T(1024)}, /*index=5*/bf16[2048,1024]{0,1:T(8,128)(2,1)}) fusion(f32[2048,1024]{0,1:T(8,128)} %fusion.95, f32[1024]{0:T(1024)S(1)} %bitcast.190, f32[2048,1024]{0,1:T(8,128)} %fusion.96, ...), kind=kOutput, calls=%fused_computation.39 | convolution fusion | flops 8711567360 | bytes 54538240 | tf_op jit(solution)/shard_map/dot_general | solution.py:62
  476.5 20.4 %convolution_convert_fusion.2 = bf16[2048,2048]{1,0:T(8,128)(2,1)} fusion(bf16[2048,1024]{0,1:T(8,128)(2,1)} %get-tuple-element.129, bf16[2048,768]{0,1:T(8,128)(2,1)} %copy.100, bf16[2048,1024]{0,1:T(8,128)(2,1)S(1)} %copy-done.46, bf16[2048,768]{0,1:T(8,128)(2,1)S(1)} %copy-done.52), kind=kOutput, calls=%fused_computation.44 | convolution fusion | flops 15065939968 | bytes 23068672 | tf_op jit(solution)/shard_map/dot_general | solution.py:58
  497.0 12.8 %broadcast_add_fusion.1.qkv_ref = f32[2048,768]{1,0:T(8,128)} fusion(f32[768]{0:T(1024)S(1)} %add.351, bf16[2048,2048]{1,0:T(8,128)(2,1)} %get-tuple-element.125, bf16[2048,1024]{0,1:T(8,128)(2,1)} %constant_dynamic-update-slice_fusion.8), kind=kOutput, calls=%fused_computation.87 | convolution fusion | flops 6444023808 | bytes 17828864 | tf_op jit(solution)/shard_map/dot_general | solution.py:62
  509.8 15.3 %shard_map.211 = (bf16[2048,768]{1,0:T(8,128)(2,1)S(1)}, bf16[2048,256]{1,0:T(8,128)(2,1)S(1)}, f32[4,2,1024]{2,1,0:T(2,128)S(1)}) custom-call(f32[2048,768]{1,0:T(8,128)} %broadcast_add_fusion.1.qkv_ref, f32[1024,128]{1,0:T(8,128)S(1)} %copy-done.9, f32[1024,128]{1,0:T(8,128)S(1)} %copy-done.13, f32[1024,128]{1,0:T(8,128)S(1)} %copy-done.17), custom_call_target="tpu_custom_call" | custom-call | flops 6442450944 | bytes 8388608 | tf_op jit(solution)/shard_map/pallas_call | solution.py:143
  533.5 23.4 %shard_map.213 = bf16[2048,768]{1,0:T(8,128)(2,1)S(1)} custom-call(bf16[2048,768]{1,0:T(8,128)(2,1)} %copy-done.20, bf16[2048,256]{1,0:T(8,128)(2,1)S(1)} %convolution_convert_fusion.5.grad_ref, f32[4,2,1024]{2,1,0:T(2,128)S(1)} %get-tuple-element.30.lse_ref, f32[1024,128]{1,0:T(8,128)S(1)} %copy-done.10, f32[1024,128]{1,0:T(8,128)S(1)} %copy-done.14, ...), custom_call_target="tpu_custom_call" | custom-call | flops 12884901888 | bytes 8388608 | tf_op jit(solution)/shard_map/pallas_call | solution.py:168
  560.3 22.4 %convolution_convert_fusion.3 = bf16[2048,2048]{1,0:T(8,128)(2,1)} fusion(bf16[2048,1024]{0,1:T(8,128)(2,1)} %get-tuple-element.87, bf16[2048,768]{0,1:T(8,128)(2,1)} %copy.94, bf16[2048,1024]{0,1:T(8,128)(2,1)} %copy-done.44, bf16[2048,768]{0,1:T(8,128)(2,1)} %slice.118), kind=kOutput, calls=%fused_computation.45 | convolution fusion | flops 15065939968 | bytes 23068672 | tf_op jit(solution)/shard_map/dot_general | solution.py:58
  587.9 18.0 %convolution_convert_fusion.1 = bf16[2048,2048]{1,0:T(8,128)(2,1)} fusion(bf16[2048,1024]{0,1:T(8,128)(2,1)} %get-tuple-element.90, bf16[2048,256]{0,1:T(8,128)(2,1)} %copy.84, bf16[2048,1024]{0,1:T(8,128)(2,1)} %copy-done.41, bf16[2048,256]{0,1:T(8,128)(2,1)} %slice.121), kind=kOutput, calls=%fused_computation.43 | convolution fusion | flops 10762584064 | bytes 18874368 | tf_op jit(solution)/shard_map/dot_general | solution.py:58
  654.6 13.8 %convolution_convert_fusion = bf16[2048,2048]{1,0:T(8,128)(2,1)} fusion(bf16[2048,1024]{0,1:T(8,128)(2,1)S(1)} %copy-done.76, bf16[2048,256]{0,1:T(8,128)(2,1)S(1)} %copy-done.59, bf16[2048,1024]{0,1:T(8,128)(2,1)S(1)} %copy-done.43, bf16[2048,256]{0,1:T(8,128)(2,1)S(1)} %copy-done.58), kind=kOutput, calls=%fused_computation.42 | convolution fusion | flops 10762584064 | bytes 18874368 | tf_op jit(solution)/shard_map/dot_general | solution.py:58
  689.5 14.5 %fusion.100 = f32[2048,1024]{0,1:T(8,128)} fusion(bf16[2048,1024]{0,1:T(8,128)(2,1)S(1)} %copy-done.78, bf16[2048,2048]{1,0:T(8,128)(2,1)} %get-tuple-element.125), kind=kOutput, calls=%fused_computation.249 | convolution fusion | flops 8589934592 | bytes 20971520 | tf_op jit(solution)/shard_map/dot_general | solution.py:54
  704.0 11.9 %add_convert_fusion.1 = bf16[2048,1024]{0,1:T(8,128)(2,1)S(1)} fusion(f32[2048,1024]{0,1:T(8,128)} %fusion.100, bf16[2048,1024]{0,1:T(8,128)(2,1)} %get-tuple-element.129, bf16[2048,2048]{1,0:T(8,128)(2,1)S(1)} %bitcast.175), kind=kOutput, calls=%fused_computation.37 | convolution fusion | flops 8594128896 | bytes 25165824 | tf_op jit(solution)/shard_map/dot_general | solution.py:54
  727.6 17.7 %collective-permute-done.26 = bf16[512,1024]{0,1:T(8,128)(2,1)} collective-permute-done((bf16[512,1024]{0,1:T(8,128)(2,1)}, bf16[512,1024]{0,1:T(8,128)(2,1)}, u32[]{:S(2)}, u32[]{:S(2)}) %collective-permute-start.26) | collective-permute-done | bytes 1048608 | tf_op jit(solution)/shard_map/ppermute | solution.py:358
  748.2 19.6 %collective-permute-done.31 = bf16[512,1024]{0,1:T(8,128)(2,1)} collective-permute-done((bf16[512,1024]{0,1:T(8,128)(2,1)}, bf16[512,1024]{0,1:T(8,128)(2,1)}, u32[]{:S(2)}, u32[]{:S(2)}) %collective-permute-start.31) | collective-permute-done | bytes 1048608 | tf_op jit(solution)/shard_map/ppermute | solution.py:358
  771.2 19.1 %collective-permute-done.23 = bf16[512,1024]{0,1:T(8,128)(2,1)} collective-permute-done((bf16[512,1024]{0,1:T(8,128)(2,1)}, bf16[512,1024]{0,1:T(8,128)(2,1)}, u32[]{:S(2)}, u32[]{:S(2)}) %collective-permute-start.23) | collective-permute-done | bytes 1048608 | tf_op jit(solution)/shard_map/ppermute | solution.py:358
  793.4 19.3 %collective-permute-done.27 = bf16[512,1024]{0,1:T(8,128)(2,1)} collective-permute-done((bf16[512,1024]{0,1:T(8,128)(2,1)}, bf16[512,1024]{0,1:T(8,128)(2,1)}, u32[]{:S(2)}, u32[]{:S(2)}) %collective-permute-start.27) | collective-permute-done | bytes 1048608 | tf_op jit(solution)/shard_map/ppermute | solution.py:358
  815.8 19.4 %collective-permute-done.32 = bf16[512,1024]{0,1:T(8,128)(2,1)} collective-permute-done((bf16[512,1024]{0,1:T(8,128)(2,1)}, bf16[512,1024]{0,1:T(8,128)(2,1)}, u32[]{:S(2)}, u32[]{:S(2)}) %collective-permute-start.32) | collective-permute-done | bytes 1048608 | tf_op jit(solution)/shard_map/ppermute | solution.py:358
  837.2 20.4 %collective-permute-done.24 = bf16[512,1024]{0,1:T(8,128)(2,1)} collective-permute-done((bf16[512,1024]{0,1:T(8,128)(2,1)}, bf16[512,1024]{0,1:T(8,128)(2,1)}, u32[]{:S(2)}, u32[]{:S(2)}) %collective-permute-start.24) | collective-permute-done | bytes 1048608 | tf_op jit(solution)/shard_map/ppermute | solution.py:358
  859.5 18.9 %collective-permute-done.28 = bf16[512,1024]{0,1:T(8,128)(2,1)} collective-permute-done((bf16[512,1024]{0,1:T(8,128)(2,1)}, bf16[512,1024]{0,1:T(8,128)(2,1)}, u32[]{:S(2)}, u32[]{:S(2)}) %collective-permute-start.28) | collective-permute-done | bytes 1048608 | tf_op jit(solution)/shard_map/ppermute | solution.py:358
  (425 shorter events, 291.7 us)
Async XLA Ops:
  7.2 60.6 %all-gather.6.cloned.1.call-start = ((), (), s32[]{:S(2)}) async-start(), calls=%async_computation.5 | async-start | bytes 9437184 | tf_op jit(solution)/shard_map/all_gather | solution.py:221
  10.5 269.4 %all-gather.8.cloned.1.call-start = ((), (), s32[]{:S(2)}) async-start(), calls=%async_computation.7 | async-start | bytes 9437184 | tf_op jit(solution)/shard_map/all_gather | solution.py:221
  67.8 250.1 %all-gather.12.cloned.1.call-start = ((), (), s32[]{:S(2)}) async-start(), calls=%async_computation.11 | async-start | bytes 9437184 | tf_op jit(solution)/shard_map/all_gather | solution.py:221
  68.5 325.6 %all-gather.10.cloned.1.call-start = ((), (), s32[]{:S(2)}) async-start(), calls=%async_computation.9 | async-start | bytes 9437184 | tf_op jit(solution)/shard_map/all_gather | solution.py:221
  69.0 17.2 %collective-permute-start.5 = (bf16[256,1024]{0,1:T(8,128)(2,1)S(1)}, bf16[256,1024]{0,1:T(8,128)(2,1)S(1)}, u32[]{:S(2)}, u32[]{:S(2)}) collective-permute-start(bf16[256,1024]{0,1:T(8,128)(2,1)S(1)} %pad_maximum_fusion.9), channel_id=1, source_target_pairs={{0,4},{4,0},{8,12},{12,8},{16,20},{20,16},{24,28},{28,24},{1,5},{5... | collective-permute-start | bytes 1572872 | tf_op jit(solution)/shard_map/ppermute | solution.py:218
  89.9 25.0 %collective-permute-start.6 = (bf16[512,1024]{0,1:T(8,128)(2,1)S(1)}, bf16[512,1024]{0,1:T(8,128)(2,1)S(1)}, u32[]{:S(2)}, u32[]{:S(2)}) collective-permute-start(bf16[512,1024]{0,1:T(8,128)(2,1)S(1)} %get-tuple-element.89), channel_id=1, source_target_pairs={{0,8},{4,12},{8,16},{12,20},{16,24},{20,28},{24,0},{28,4},{1,9},{5... | collective-permute-start | bytes 3145736 | tf_op jit(solution)/shard_map/ppermute | solution.py:303
  115.9 24.2 %collective-permute-start.7 = (bf16[512,1024]{0,1:T(8,128)(2,1)S(1)}, bf16[512,1024]{0,1:T(8,128)(2,1)}, u32[]{:S(2)}, u32[]{:S(2)}) collective-permute-start(bf16[512,1024]{0,1:T(8,128)(2,1)S(1)} %collective-permute-done.6), channel_id=1, source_target_pairs={{0,8},{4,12},{8,16},{12,20},{16,24},{20,28},{24,0},{28,4},{1,9},{5... | collective-permute-start | bytes 3145736 | tf_op jit(solution)/shard_map/ppermute | solution.py:303
  140.0 23.4 %collective-permute-start.8 = (bf16[512,1024]{0,1:T(8,128)(2,1)}, bf16[512,1024]{0,1:T(8,128)(2,1)}, u32[]{:S(2)}, u32[]{:S(2)}) collective-permute-start(bf16[512,1024]{0,1:T(8,128)(2,1)} %collective-permute-done.7), channel_id=1, source_target_pairs={{0,8},{4,12},{8,16},{12,20},{16,24},{20,28},{24,0},{28,4},{1,9},{5... | collective-permute-start | bytes 3145736 | tf_op jit(solution)/shard_map/ppermute | solution.py:303
  140.4 21.6 %collective-permute-start.9 = (bf16[256,1024]{0,1:T(8,128)(2,1)S(1)}, bf16[256,1024]{0,1:T(8,128)(2,1)S(1)}, u32[]{:S(2)}, u32[]{:S(2)}) collective-permute-start(bf16[256,1024]{0,1:T(8,128)(2,1)S(1)} %copy.113), channel_id=1, source_target_pairs={{0,4},{4,0},{8,12},{12,8},{16,20},{20,16},{24,28},{28,24},{1,5},{5... | collective-permute-start | bytes 1572872 | tf_op jit(solution)/shard_map/ppermute | solution.py:218
  163.5 24.3 %collective-permute-start.10 = (bf16[512,1024]{0,1:T(8,128)(2,1)S(1)}, bf16[512,1024]{0,1:T(8,128)(2,1)S(1)}, u32[]{:S(2)}, u32[]{:S(2)}) collective-permute-start(bf16[512,1024]{0,1:T(8,128)(2,1)S(1)} %maximum_select_fusion.1), channel_id=1, source_target_pairs={{0,8},{4,12},{8,16},{12,20},{16,24},{20,28},{24,0},{28,4},{1,9},{5... | collective-permute-start | bytes 3145736 | tf_op jit(solution)/shard_map/ppermute | solution.py:303
  187.8 23.4 %collective-permute-start.11 = (bf16[512,1024]{0,1:T(8,128)(2,1)S(1)}, bf16[512,1024]{0,1:T(8,128)(2,1)S(1)}, u32[]{:S(2)}, u32[]{:S(2)}) collective-permute-start(bf16[512,1024]{0,1:T(8,128)(2,1)S(1)} %collective-permute-done.10), channel_id=1, source_target_pairs={{0,8},{4,12},{8,16},{12,20},{16,24},{20,28},{24,0},{28,4},{1,9},{5... | collective-permute-start | bytes 3145736 | tf_op jit(solution)/shard_map/ppermute | solution.py:303
  211.2 23.3 %collective-permute-start.12 = (bf16[512,1024]{0,1:T(8,128)(2,1)S(1)}, bf16[512,1024]{0,1:T(8,128)(2,1)}, u32[]{:S(2)}, u32[]{:S(2)}) collective-permute-start(bf16[512,1024]{0,1:T(8,128)(2,1)S(1)} %collective-permute-done.11), channel_id=1, source_target_pairs={{0,8},{4,12},{8,16},{12,20},{16,24},{20,28},{24,0},{28,4},{1,9},{5... | collective-permute-start | bytes 3145736 | tf_op jit(solution)/shard_map/ppermute | solution.py:303
  234.6 24.0 %collective-permute-start.14 = (bf16[512,1024]{0,1:T(8,128)(2,1)S(1)}, bf16[512,1024]{0,1:T(8,128)(2,1)}, u32[]{:S(2)}, u32[]{:S(2)}) collective-permute-start(bf16[512,1024]{0,1:T(8,128)(2,1)S(1)} %maximum_select_fusion.2), channel_id=1, source_target_pairs={{0,8},{4,12},{8,16},{12,20},{16,24},{20,28},{24,0},{28,4},{1,9},{5... | collective-permute-start | bytes 3145736 | tf_op jit(solution)/shard_map/ppermute | solution.py:303
  253.5 26.3 %collective-permute-start.4 = (bf16[16,704]{1,0:T(8,128)(2,1)S(1)}, bf16[16,704]{1,0:T(8,128)(2,1)S(1)}, u32[]{:S(2)}, u32[]{:S(2)}) collective-permute-start(bf16[16,704]{1,0:T(8,128)(2,1)S(1)} %maximum_select_fusion.4), channel_id=1, source_target_pairs={{0,16},{4,20},{8,24},{12,28},{16,0},{20,4},{24,8},{28,12},{1,17},{... | collective-permute-start | bytes 67592 | tf_op jit(solution)/shard_map/ppermute | solution.py:239
  258.6 27.4 %collective-permute-start.15 = (bf16[512,1024]{0,1:T(8,128)(2,1)}, bf16[512,1024]{0,1:T(8,128)(2,1)}, u32[]{:S(2)}, u32[]{:S(2)}) collective-permute-start(bf16[512,1024]{0,1:T(8,128)(2,1)} %collective-permute-done.14), channel_id=1, source_target_pairs={{0,8},{4,12},{8,16},{12,20},{16,24},{20,28},{24,0},{28,4},{1,9},{5... | collective-permute-start | bytes 3145736 | tf_op jit(solution)/shard_map/ppermute | solution.py:303
  280.0 614.2 %reduce-scatter.11.cloned.1.call-start = ((), (), s32[]{:S(2)}) async-start(), calls=%async_computation.10 | async-start | bytes 9437184 | tf_op jit(solution)/shard_map/reduce_scatter | solution.py:224
  285.9 27.4 %collective-permute-start.16 = (bf16[512,1024]{0,1:T(8,128)(2,1)}, bf16[512,1024]{0,1:T(8,128)(2,1)S(1)}, u32[]{:S(2)}, u32[]{:S(2)}) collective-permute-start(bf16[512,1024]{0,1:T(8,128)(2,1)} %collective-permute-done.15), channel_id=1, source_target_pairs={{0,8},{4,12},{8,16},{12,20},{16,24},{20,28},{24,0},{28,4},{1,9},{5... | collective-permute-start | bytes 3145736 | tf_op jit(solution)/shard_map/ppermute | solution.py:303
  496.9 397.2 %reduce-scatter.9.cloned.1.call-start = ((), (), s32[]{:S(2)}) async-start(), calls=%async_computation.8 | async-start | bytes 9437184 | tf_op jit(solution)/shard_map/reduce_scatter | solution.py:224
  582.7 314.5 %reduce-scatter.5.cloned.1.call-start = ((), (), s32[]{:S(2)}) async-start(), calls=%async_computation.4 | async-start | bytes 9437184 | tf_op jit(solution)/shard_map/reduce_scatter | solution.py:224
  605.9 291.4 %reduce-scatter.7.cloned.1.call-start = ((), (), s32[]{:S(2)}) async-start(), calls=%async_computation.6 | async-start | bytes 9437184 | tf_op jit(solution)/shard_map/reduce_scatter | solution.py:224
  654.6 62.6 %collective-permute-start.30 = (bf16[512,1024]{0,1:T(8,128)(2,1)}, bf16[512,1024]{0,1:T(8,128)(2,1)}, u32[]{:S(2)}, u32[]{:S(2)}) collective-permute-start(bf16[512,1024]{0,1:T(8,128)(2,1)} %constant_dynamic-slice_fusion.2), channel_id=1, source_target_pairs={{0,8},{4,12},{8,16},{12,20},{16,24},{20,28},{24,0},{28,4},{1,9},{5... | collective-permute-start | bytes 3145736 | tf_op jit(solution)/shard_map/ppermute | solution.py:358
  689.4 34.5 %collective-permute-start.22 = (bf16[512,1024]{0,1:T(8,128)(2,1)S(1)}, bf16[512,1024]{0,1:T(8,128)(2,1)S(1)}, u32[]{:S(2)}, u32[]{:S(2)}) collective-permute-start(bf16[512,1024]{0,1:T(8,128)(2,1)S(1)} %fusion.70), channel_id=1, source_target_pairs={{0,8},{4,12},{8,16},{12,20},{16,24},{20,28},{24,0},{28,4},{1,9},{5... | collective-permute-start | bytes 3145736 | tf_op jit(solution)/shard_map/ppermute | solution.py:358
  717.1 28.2 %collective-permute-start.26 = (bf16[512,1024]{0,1:T(8,128)(2,1)}, bf16[512,1024]{0,1:T(8,128)(2,1)}, u32[]{:S(2)}, u32[]{:S(2)}) collective-permute-start(bf16[512,1024]{0,1:T(8,128)(2,1)} %constant_dynamic-slice_fusion.4), channel_id=1, source_target_pairs={{0,8},{4,12},{8,16},{12,20},{16,24},{20,28},{24,0},{28,4},{1,9},{5... | collective-permute-start | bytes 3145736 | tf_op jit(solution)/shard_map/ppermute | solution.py:358
  721.4 46.5 %collective-permute-start.31 = (bf16[512,1024]{0,1:T(8,128)(2,1)}, bf16[512,1024]{0,1:T(8,128)(2,1)}, u32[]{:S(2)}, u32[]{:S(2)}) collective-permute-start(bf16[512,1024]{0,1:T(8,128)(2,1)} %add_convert_fusion.4), channel_id=1, source_target_pairs={{0,8},{4,12},{8,16},{12,20},{16,24},{20,28},{24,0},{28,4},{1,9},{5... | collective-permute-start | bytes 3145736 | tf_op jit(solution)/shard_map/ppermute | solution.py:358
  725.3 65.0 %collective-permute-start.23 = (bf16[512,1024]{0,1:T(8,128)(2,1)}, bf16[512,1024]{0,1:T(8,128)(2,1)}, u32[]{:S(2)}, u32[]{:S(2)}) collective-permute-start(bf16[512,1024]{0,1:T(8,128)(2,1)} %add_convert_fusion.8), channel_id=1, source_target_pairs={{0,8},{4,12},{8,16},{12,20},{16,24},{20,28},{24,0},{28,4},{1,9},{5... | collective-permute-start | bytes 3145736 | tf_op jit(solution)/shard_map/ppermute | solution.py:358
  748.2 64.5 %collective-permute-start.27 = (bf16[512,1024]{0,1:T(8,128)(2,1)}, bf16[512,1024]{0,1:T(8,128)(2,1)}, u32[]{:S(2)}, u32[]{:S(2)}) collective-permute-start(bf16[512,1024]{0,1:T(8,128)(2,1)} %add_convert_fusion.6), channel_id=1, source_target_pairs={{0,8},{4,12},{8,16},{12,20},{16,24},{20,28},{24,0},{28,4},{1,9},{5... | collective-permute-start | bytes 3145736 | tf_op jit(solution)/shard_map/ppermute | solution.py:358
  770.6 64.6 %collective-permute-start.32 = (bf16[512,1024]{0,1:T(8,128)(2,1)}, bf16[512,1024]{0,1:T(8,128)(2,1)}, u32[]{:S(2)}, u32[]{:S(2)}) collective-permute-start(bf16[512,1024]{0,1:T(8,128)(2,1)} %add_convert_fusion.3), channel_id=1, source_target_pairs={{0,8},{4,12},{8,16},{12,20},{16,24},{20,28},{24,0},{28,4},{1,9},{5... | collective-permute-start | bytes 3145736 | tf_op jit(solution)/shard_map/ppermute | solution.py:358
  792.9 64.8 %collective-permute-start.24 = (bf16[512,1024]{0,1:T(8,128)(2,1)}, bf16[512,1024]{0,1:T(8,128)(2,1)}, u32[]{:S(2)}, u32[]{:S(2)}) collective-permute-start(bf16[512,1024]{0,1:T(8,128)(2,1)} %add_convert_fusion.7), channel_id=1, source_target_pairs={{0,8},{4,12},{8,16},{12,20},{16,24},{20,28},{24,0},{28,4},{1,9},{5... | collective-permute-start | bytes 3145736 | tf_op jit(solution)/shard_map/ppermute | solution.py:358
  815.5 62.8 %collective-permute-start.28 = (bf16[512,1024]{0,1:T(8,128)(2,1)}, bf16[512,1024]{0,1:T(8,128)(2,1)}, u32[]{:S(2)}, u32[]{:S(2)}) collective-permute-start(bf16[512,1024]{0,1:T(8,128)(2,1)} %add_convert_fusion.5), channel_id=1, source_target_pairs={{0,8},{4,12},{8,16},{12,20},{16,24},{20,28},{24,0},{28,4},{1,9},{5... | collective-permute-start | bytes 3145736 | tf_op jit(solution)/shard_map/ppermute | solution.py:358
  837.2 43.2 %collective-permute-start.33 = (bf16[256,1024]{0,1:T(8,128)(2,1)S(1)}, bf16[256,1024]{0,1:T(8,128)(2,1)S(1)}, u32[]{:S(2)}, u32[]{:S(2)}) collective-permute-start(bf16[256,1024]{0,1:T(8,128)(2,1)S(1)} %dynamic-slice_convert_fusion), channel_id=1, source_target_pairs={{0,4},{4,0},{8,12},{12,8},{16,20},{20,16},{24,28},{28,24},{1,5},{5... | collective-permute-start | bytes 1572872 | tf_op jit(solution)/shard_map/ppermute | solution.py:218
  859.4 21.2 %collective-permute-start.25 = (bf16[256,1024]{0,1:T(8,128)(2,1)S(1)}, bf16[256,1024]{0,1:T(8,128)(2,1)S(1)}, u32[]{:S(2)}, u32[]{:S(2)}) collective-permute-start(bf16[256,1024]{0,1:T(8,128)(2,1)S(1)} %dynamic-slice_convert_fusion.2), channel_id=1, source_target_pairs={{0,4},{4,0},{8,12},{12,8},{16,20},{20,16},{24,28},{28,24},{1,5},{5... | collective-permute-start | bytes 1572872 | tf_op jit(solution)/shard_map/ppermute | solution.py:218
  880.3 12.2 %collective-permute-start.29 = (bf16[256,1024]{0,1:T(8,128)(2,1)S(1)}, bf16[256,1024]{0,1:T(8,128)(2,1)S(1)}, u32[]{:S(2)}, u32[]{:S(2)}) collective-permute-start(bf16[256,1024]{0,1:T(8,128)(2,1)S(1)} %dynamic-slice_convert_fusion.1), channel_id=1, source_target_pairs={{0,4},{4,0},{8,12},{12,8},{16,20},{20,16},{24,28},{28,24},{1,5},{5... | collective-permute-start | bytes 1572872 | tf_op jit(solution)/shard_map/ppermute | solution.py:218
  (99 other events, 2283.3 us)
Sparse Core Ops, SparseCore 0:
  10.6 57.0 all-gather.5
  70.2 56.2 all-gather.7
  129.0 63.4 all-gather.11
  280.1 51.2 all-gather.9
  497.0 67.9 reduce-scatter.10
  582.9 67.5 reduce-scatter.8
  653.9 71.2 reduce-scatter.4
  729.1 71.2 reduce-scatter.6

commit v2 on v1

--- a/solution.py
+++ b/solution.py
@@ -16,7 +16,7 @@
 mask_fill = -1e30
 BF = jnp.bfloat16
 F32 = jnp.float32
-VMEM_LIMIT = 48 * 1024 * 1024
+VMEM_LIMIT = 56 * 1024 * 1024
 
 
 def layer_norm(resid_rows, gain_vec, shift_vec):
@@ -131,7 +131,7 @@
 
 def attention_cost(seqs, pairs, length, matmuls):
     flops = seqs * pairs * matmuls * 2 * 2 * length * length * LANES
-    return pl.CostEstimate(flops=flops, bytes_accessed=seqs * pairs * length * LANES * 16, transcendentals=0)
+    return estimate(flops, seqs * pairs * length * LANES * 16)
 
 
 def attend(qkv, tables, length, head_dim):
@@ -182,6 +182,256 @@
     )(rot, attn_grad, lse, *tables)
 
 
+def spec_rows(tile, width):
+    return pl.BlockSpec((tile, width), lambda i, s: (i, 0))
+
+
+def spec_whole(array):
+    return pl.BlockSpec(array.shape, lambda i, s: (0,) * array.ndim)
+
+
+def estimate(flops, moved):
+    return pl.CostEstimate(flops=int(flops) // 64, bytes_accessed=int(moved) // 64, transcendentals=0)
+
+
+def lined_dot(slots_ref, rows_ref, parts, cols):
+    depth = parts[0].shape[0]
+    total = None
+    for at, part in enumerate(parts):
+        first = pl.multiple_of(slots_ref[at] * depth, depth)
+        piece = dot_plain(rows_ref[:, pl.ds(first, depth)], part[:, cols])
+        total = piece if total is None else total + piece
+    return total
+
+
+def rows_call(kernel, slots, ins, in_specs, outs, tile, cost, out_specs=None):
+    tokens = outs[0].shape[0]
+    return pl.pallas_call(
+        kernel,
+        grid_spec=pltpu.PrefetchScalarGridSpec(
+            num_scalar_prefetch=1,
+            grid=(tokens // tile,),
+            in_specs=in_specs,
+            out_specs=out_specs or [spec_rows(tile, out.shape[1]) for out in outs],
+        ),
+        out_shape=outs,
+        compiler_params=pltpu.CompilerParams(vmem_limit_bytes=VMEM_LIMIT),
+        cost_estimate=cost,
+    )(slots, *ins)
+
+
+def norm_qkv(slots, rows, gain, shift, parts, bias):
+    tokens, width = rows.shape
+    cols, tile = bias.shape[1], 256
+
+    def kernel(slots_ref, rows_ref, gain_ref, shift_ref, bias_ref, *refs):
+        parts, (normed_ref, qkv_ref, stat_ref) = refs[:-3], refs[-3:]
+        vals = rows_ref[...].astype(F32)
+        mean = jnp.mean(vals, axis=-1, keepdims=True)
+        centred = vals - mean
+        var = jnp.mean(centred * centred, axis=-1, keepdims=True)
+        scale = lax.rsqrt(var + norm_epsilon)
+        normed_ref[...] = (centred * scale * gain_ref[...] + shift_ref[...]).astype(BF)
+        lane_ids = lax.broadcasted_iota(jnp.int32, (tile, LANES), 1)
+        stat_ref[...] = jnp.where(lane_ids == 0, mean, scale)
+        qkv_ref[...] = lined_dot(slots_ref, normed_ref, parts, slice(0, cols)) + bias_ref[...]
+
+    return rows_call(
+        kernel,
+        slots,
+        [rows, gain, shift, bias, *parts],
+        [spec_rows(tile, width)] + [spec_whole(array) for array in (gain, shift, bias, *parts)],
+        [
+            jax.ShapeDtypeStruct((tokens, width), BF),
+            jax.ShapeDtypeStruct((tokens, cols), F32),
+            jax.ShapeDtypeStruct((tokens, LANES), F32),
+        ],
+        tile,
+        estimate(2 * tokens * width * cols, tokens * (4 * width + 4 * cols)),
+    )
+
+
+def up_act(slots, rows, parts, bias):
+    tokens, width = rows.shape
+    cols, tile, chunk = bias.shape[1], 512, 512
+
+    def kernel(slots_ref, rows_ref, bias_ref, *refs):
+        parts, (act_ref, slope_ref) = refs[:-2], refs[-2:]
+        for at in range(0, cols, chunk):
+            span = slice(at, at + chunk)
+            pre = lined_dot(slots_ref, rows_ref, parts, span) + bias_ref[:, span]
+            square = pre * pre
+            tanh = jnp.tanh(gelu_factor * (pre * (1.0 + 0.044715 * square)))
+            half = 0.5 * (1.0 + tanh)
+            act_ref[:, span] = (pre * half).astype(BF)
+            inner = gelu_factor * (1.0 + 3 * 0.044715 * square)
+            slope_ref[:, span] = (half + 0.5 * pre * (1.0 - tanh * tanh) * inner).astype(BF)
+
+    return rows_call(
+        kernel,
+        slots,
+        [rows, bias, *parts],
+        [spec_rows(tile, width)] + [spec_whole(array) for array in (bias, *parts)],
+        [jax.ShapeDtypeStruct((tokens, cols), BF)] * 2,
+        tile,
+        estimate(2 * tokens * width * cols, tokens * (2 * width + 4 * cols)),
+    )
+
+
+def pre_grad_rows(slots, rows, parts, slope):
+    tokens, width = rows.shape
+    cols, tile = slope.shape[1], 512
+
+    def kernel(slots_ref, rows_ref, slope_ref, *refs):
+        parts, out_ref = refs[:-1], refs[-1]
+        act_grad = lined_dot(slots_ref, rows_ref, parts, slice(0, cols))
+        out_ref[...] = (act_grad * slope_ref[...].astype(F32)).astype(BF)
+
+    return rows_call(
+        kernel,
+        slots,
+        [rows, slope, *parts],
+        [spec_rows(tile, width), spec_rows(tile, cols)] + [spec_whole(part) for part in parts],
+        [jax.ShapeDtypeStruct((tokens, cols), BF)],
+        tile,
+        estimate(2 * tokens * width * cols, tokens * (2 * width + 4 * cols)),
+    )[0]
+
+
+def head_grad_rows(slots, rows, parts, first):
+    tokens, width = rows.shape
+    cols, tile = parts[0].shape[1] - first, 1024
+
+    def kernel(slots_ref, rows_ref, *refs):
+        parts, out_ref = refs[:-1], refs[-1]
+        out_ref[...] = lined_dot(slots_ref, rows_ref, parts, slice(first, first + cols)).astype(BF)
+
+    return rows_call(
+        kernel,
+        slots,
+        [rows, *parts],
+        [spec_rows(tile, width)] + [spec_whole(part) for part in parts],
+        [jax.ShapeDtypeStruct((tokens, cols), BF)],
+        tile,
+        estimate(2 * tokens * width * cols, tokens * (2 * width + 2 * cols)),
+    )[0]
+
+
+def branch_rows(slots, one, one_parts, first, two, two_parts):
+    tokens, cols = one.shape
+    count, depth, tile = len(one_parts), one_parts[0].shape[0], 512
+    width = count * depth
+
+    def kernel(slots_ref, one_ref, two_ref, *refs):
+        out_ref = refs[-1]
+        for at in range(count):
+            where = pl.multiple_of(slots_ref[at] * depth, depth)
+            total = dot_cols(one_ref[...], refs[at][:, first : first + cols])
+            total += dot_cols(two_ref[...], refs[count + at][...])
+            out_ref[:, pl.ds(where, depth)] = total.astype(BF)
+
+    return rows_call(
+        kernel,
+        slots,
+        [one, two, *one_parts, *two_parts],
+        [spec_rows(tile, cols), spec_rows(tile, two.shape[1])]
+        + [spec_whole(part) for part in (*one_parts, *two_parts)],
+        [jax.ShapeDtypeStruct((tokens, width), BF)],
+        tile,
+        estimate(2 * tokens * width * (cols + two.shape[1]), 2 * tokens * (width + cols + two.shape[1])),
+    )[0]
+
+
+def normed_grad_rows(slots, one, one_parts, two, two_parts, rows, stats):
+    tokens, cols = one.shape
+    count, depth, tile = len(one_parts), one_parts[0].shape[0], 512
+    width = count * depth
+
+    def kernel(slots_ref, one_ref, two_ref, rows_ref, stat_ref, *refs):
+        out_ref, sum_ref = refs[-2:]
+
+        @pl.when(pl.program_id(0) == 0)
+        def _():
+            sum_ref[...] = jnp.zeros_like(sum_ref)
+
+        for at in range(count):
+            where = pl.multiple_of(slots_ref[at] * depth, depth)
+            span = pl.ds(where, depth)
+            total = dot_cols(one_ref[...], refs[at][:, :cols])
+            total += dot_cols(two_ref[...], refs[count + at][...])
+            out_ref[:, span] = total.astype(BF)
+            scaled = (rows_ref[:, span].astype(F32) - stat_ref[:, 0:1]) * stat_ref[:, 1:2]
+            sum_ref[0:1, span] += jnp.sum(total * scaled, axis=0, keepdims=True)
+            sum_ref[1:2, span] += jnp.sum(total, axis=0, keepdims=True)
+
+    return rows_call(
+        kernel,
+        slots,
+        [one, two, rows, stats, *one_parts, *two_parts],
+        [spec_rows(tile, cols), spec_rows(tile, two.shape[1]), spec_rows(tile, width), spec_rows(tile, LANES)]
+        + [spec_whole(part) for part in (*one_parts, *two_parts)],
+        [jax.ShapeDtypeStruct((tokens, width), BF), jax.ShapeDtypeStruct((8, width), F32)],
+        tile,
+        estimate(2 * tokens * width * (cols + two.shape[1]), 2 * tokens * (2 * width + cols + two.shape[1])),
+        [spec_rows(tile, width), pl.BlockSpec((8, width), lambda i, s: (0, 0))],
+    )
+
+
+def weight_grad(groups):
+    tile, chunk = 512, 512
+    micro_count = len(groups[0][0])
+    tokens, width = groups[0][0][0].shape
+    widths = [rights[0].shape[1] for _, rights in groups]
+    cols, steps = sum(widths), tokens // tile
+    arrays = [array for lefts, rights in groups for array in (*lefts, *rights)]
+
+    def kernel(*refs):
+        ins, out_ref, acc_ref = refs[: len(arrays)], refs[-2], refs[-1]
+        step = pl.program_id(0)
+
+        @pl.when(step == 0)
+        def _():
+            acc_ref[...] = jnp.zeros_like(acc_ref)
+
+        for micro in range(micro_count):
+
+            @pl.when(step // steps == micro)
+            def _():
+                first = 0
+                for at, span in enumerate(widths):
+                    left = ins[2 * micro_count * at + micro]
+                    right = ins[2 * micro_count * at + micro_count + micro]
+                    for row in range(0, width, chunk):
+                        acc_ref[row : row + chunk, first : first + span] += dot_rows(
+                            left[:, row : row + chunk], right[...]
+                        )
+                    first += span
+
+        @pl.when(step == micro_count * steps - 1)
+        def _():
+            out_ref[...] = acc_ref[...].astype(BF)
+
+    def side(micro, span):
+        return pl.BlockSpec((tile, span), lambda i: (jnp.clip(i - micro * steps, 0, steps - 1), 0))
+
+    in_specs = []
+    for span in widths:
+        in_specs += [side(micro, width) for micro in range(micro_count)]
+        in_specs += [side(micro, span) for micro in range(micro_count)]
+    return pl.pallas_call(
+        kernel,
+        grid=(micro_count * steps,),
+        in_specs=in_specs,
+        out_specs=pl.BlockSpec((width, cols), lambda i: (0, 0)),
+        out_shape=jax.ShapeDtypeStruct((width, cols), BF),
+        scratch_shapes=[pltpu.VMEM((width, cols), F32)],
+        compiler_params=pltpu.CompilerParams(vmem_limit_bytes=VMEM_LIMIT),
+        cost_estimate=estimate(
+            2 * micro_count * tokens * width * cols, 2 * micro_count * tokens * (len(groups) * width + cols)
+        ),
+    )(*arrays)
+
+
 def shards(
     inputs,
     ln_gain,
@@ -200,7 +450,7 @@
     fsdp_size, tp_size = lax.axis_size("fsdp"), lax.axis_size("tp")
     line = fsdp_size // 2
     fsdp_at, tp_at = lax.axis_index("fsdp"), lax.axis_index("tp")
-    line_at, pair_at = fsdp_at // 2, fsdp_at % 2
+    line_at, pair_at = fsdp_at >> 1, fsdp_at & 1
     plane_size = 2 * tp_size
     planes = [[plane * plane_size + i for i in range(plane_size)] for plane in range(line)]
     ring = [(f, ((f // 2 + 1) % line) * 2 + f % 2) for f in range(fsdp_size)]
@@ -226,21 +476,10 @@
     def after(vals, *others):
         return lax.optimization_barrier((vals,) + others)[0]
 
-    def gather_small(vals):
-        cur = vals[None]
-        bit = 1
-        while bit < tp_size:
-            other = lax.ppermute(cur, "tp", [(t, t ^ bit) for t in range(tp_size)])
-            upper = (tp_at & bit) != 0
-            cur = jnp.where(upper, jnp.concatenate([other, cur]), jnp.concatenate([cur, other]))
-            bit *= 2
-        bit = 1
-        while bit < fsdp_size:
-            other = lax.ppermute(cur, "fsdp", [(f, f ^ bit) for f in range(fsdp_size)])
-            upper = (fsdp_at & bit) != 0
-            cur = jnp.where(upper, jnp.concatenate([other, cur]), jnp.concatenate([cur, other]))
-            bit *= 2
-        return cur
+    def doubled(cur, axis, size, at, bit):
+        other = lax.ppermute(cur, axis, [(i, i ^ bit) for i in range(size)])
+        upper = (at & bit) != 0
+        return jnp.where(upper, jnp.concatenate([other, cur]), jnp.concatenate([cur, other]))
 
     def sum_small(everywhere, over_fsdp):
         cur = everywhere
@@ -258,7 +497,155 @@
     small = jnp.concatenate(
         [vec.reshape(-1) for vec in (ln_gain, ln_bias, out_bias, down_bias, qkv_bias, up_bias)]
     )
-    small_all = gather_small(small)
+    small_all = small[None]
+    for bit in range(tp_size.bit_length() - 1):
+        small_all = doubled(small_all, "tp", tp_size, tp_at, 1 << bit)
+    small_near = small_all
+    def attn_half(half):
+        qkv_part = lax.dynamic_slice_in_dim(qkv_weight, half * attn_cols, attn_cols, axis=2)
+        qkv_part = qkv_part.reshape(shard_rows, 3, pairs, LANES).transpose(0, 2, 1, 3)
+        out_part = lax.dynamic_slice_in_dim(out_weight, half * attn_cols, attn_cols, axis=0)
+        return jnp.concatenate([qkv_part.reshape(shard_rows, qkv_cols), out_part.T], axis=1)
+
+    def up_half(half):
+        return lax.dynamic_slice_in_dim(up_weight, half * mlp_cols, mlp_cols, axis=1)
+
+    def down_half(half):
+        return lax.dynamic_slice_in_dim(down_weight, half * mlp_cols, mlp_cols, axis=0).T
+
+    def pair_join(own, other):
+        return jnp.where(pair_at == 0, jnp.concatenate([own, other]), jnp.concatenate([other, own]))
+
+    def pair_shard(half_of, *behind):
+        own = half_of(pair_at)
+        other = swap_pair(after(half_of(1 - pair_at), *behind))
+        return pair_join(own, other)
+
+    class Box:
+        def __init__(self, val):
+            self.val = val
+
+    class Line:
+        tokens = []
+
+        def tie(self, *boxes):
+            held = []
+            for box in (*boxes, *self.tokens):
+                if box not in held:
+                    held.append(box)
+            if len(held) > 1:
+                for box, val in zip(held, lax.optimization_barrier(tuple(box.val for box in held))):
+                    box.val = val
+
+        def run(self, piece, *boxes):
+            self.tie(*boxes)
+            results = [Box(val) for val in piece(*(box.val for box in boxes))]
+            self.tokens = [results[0]]
+            return results
+
+        def sync(self, box):
+            self.tokens = self.tokens + [box]
+
+    order = Line()
+
+    class Gather:
+        def __init__(self, shard):
+            self.parts = [shard]
+
+        def move(self):
+            if len(self.parts) < line:
+                order.tie(self.parts[-1])
+                self.parts.append(Box(lax.ppermute(self.parts[-1].val, "fsdp", ring)))
+
+        def sync(self):
+            order.sync(self.parts[-1])
+
+        def finish(self):
+            while len(self.parts) < line:
+                self.move()
+            self.sync()
+
+        def vals(self):
+            return [part.val for part in self.parts]
+
+    class Scatter:
+        def __init__(self, part):
+            self.part, self.step = part, 1
+            self.moving = Box(self.own().astype(BF))
+
+        def own(self):
+            at_line = lax.rem(line_at + line - self.step, line)
+            return lax.dynamic_slice_in_dim(self.part.val, at_line * line_rows, line_rows, axis=0).astype(F32)
+
+        def move(self):
+            if self.step < line:
+                self.step += 1
+                order.tie(self.moving)
+                came = lax.ppermute(self.moving.val, "fsdp", ring).astype(F32) + self.own()
+                self.moving = Box(came.astype(BF) if self.step < line else came)
+
+        def sync(self):
+            order.sync(self.moving)
+
+        def swap(self):
+            while self.step < line:
+                self.move()
+            order.tie(self.moving)
+            total = self.moving.val
+            self.keep = lax.dynamic_slice_in_dim(total, pair_at * shard_rows, shard_rows, axis=0)
+            give = lax.dynamic_slice_in_dim(total, (1 - pair_at) * shard_rows, shard_rows, axis=0)
+            self.got = Box(swap_pair(give.astype(BF)))
+
+        def halves(self):
+            got = self.got.val.astype(F32)
+            return jnp.where(pair_at == 0, self.keep, got), jnp.where(pair_at == 0, got, self.keep)
+
+    resid = [inputs[m].reshape(token_rows, model_width) for m in range(micro_count)]
+    cots = [cotangent[m].reshape(token_rows, model_width) for m in range(micro_count)]
+    micros = range(micro_count)
+    plane_rows, plane_cots = [None] * micro_count, [None] * micro_count
+
+    def gather_behind(rows):
+        sent = Box(rows)
+        order.tie(sent)
+        return Box(gather_plane(sent.val))
+
+    def small_step(small_all, bit):
+        if bit < fsdp_size.bit_length() - 1:
+            order.tie(small_all)
+            return Box(doubled(small_all.val, "fsdp", fsdp_size, fsdp_at, 1 << bit))
+        return small_all
+
+    small_all = Box(small_near)
+    order.tokens = [small_all]
+    plane_rows[0] = gather_behind(resid[0])
+    attn_shard = Box(pair_shard(attn_half))
+    order.tokens = [attn_shard]
+    plane_rows[1] = gather_behind(resid[1])
+    attn_ring = Gather(attn_shard)
+    attn_ring.move()
+    small_all = small_step(small_all, 0)
+    attn_ring.sync()
+    order.sync(small_all)
+    up_send = Box(up_half(1 - pair_at))
+    order.tie(up_send)
+    up_shard = Box(pair_join(up_half(pair_at), swap_pair(up_send.val)))
+    attn_ring.move()
+    small_all = small_step(small_all, 1)
+    attn_ring.sync()
+    order.sync(small_all)
+    order.sync(up_shard)
+    plane_cots[0] = gather_behind(cots[0])
+    down_send = Box(down_half(1 - pair_at))
+    order.tie(down_send)
+    down_shard = Box(pair_join(down_half(pair_at), swap_pair(down_send.val)))
+    attn_ring.move()
+    for bit in range(2, fsdp_size.bit_length() - 1):
+        small_all = small_step(small_all, bit)
+    attn_ring.finish()
+    order.sync(small_all)
+    order.tie()
+    small_all = small_all.val
     vec_size = ln_gain.shape[0]
     gain_vec, shift_vec, bias_out, bias_down = (
         small_all[:, i * vec_size : (i + 1) * vec_size].reshape(-1).astype(F32) for i in range(4)
@@ -276,131 +663,158 @@
     up_b = up_b.transpose(1, 0, 2).reshape(2, mlp_cols)
     up_b = lax.dynamic_slice_in_dim(up_b, pair_at, 1, axis=0)
 
-    def attn_half(half):
-        qkv_part = lax.dynamic_slice_in_dim(qkv_weight, half * attn_cols, attn_cols, axis=2)
-        qkv_part = qkv_part.reshape(shard_rows, 3, pairs, LANES).transpose(0, 2, 1, 3)
-        out_part = lax.dynamic_slice_in_dim(out_weight, half * attn_cols, attn_cols, axis=0)
-        return jnp.concatenate([qkv_part.reshape(shard_rows, qkv_cols), out_part.T], axis=1)
-
-    def up_half(half):
-        return lax.dynamic_slice_in_dim(up_weight, half * mlp_cols, mlp_cols, axis=1)
-
-    def down_half(half):
-        return lax.dynamic_slice_in_dim(down_weight, half * mlp_cols, mlp_cols, axis=0).T
-
-    def pair_shard(half_of):
-        own = half_of(pair_at)
-        other = swap_pair(half_of(1 - pair_at))
-        return jnp.where(
-            pair_at == 0, jnp.concatenate([own, other]), jnp.concatenate([other, own])
+    slots = jnp.stack([lax.rem(line_at + line - step, line) for step in range(line)]).astype(jnp.int32)
+    tables = rotary_tables(length, head_dim, ROT)
+    gain_row, shift_row = gain_vec[None], shift_vec[None]
+    normed, qkvs, stats, rots, attns, lses, acts, slopes = ([None] * micro_count for _ in range(8))
+    pre_grads, qkv_grads, back, sums, branches, attn_heads = ([None] * micro_count for _ in range(6))
+
+    def norm_piece(m):
+        normed[m], qkvs[m], stats[m] = order.run(
+            lambda rows: norm_qkv(slots, rows, gain_row, shift_row, attn_ring.vals(), qkv_b), plane_rows[m]
         )
 
-    def gather_line(shard):
-        whole = jnp.zeros((line * line_rows, shard.shape[1]), BF)
-        whole = lax.dynamic_update_slice_in_dim(whole, shard, line_at * line_rows, axis=0)
-        moving = shard
-        for step in range(1, line):
-            moving = lax.ppermute(moving, "fsdp", ring)
-            at_line = (line_at - step) % line
-            whole = lax.dynamic_update_slice_in_dim(whole, moving, at_line * line_rows, axis=0)
-        return whole, moving
-
-    attn_shard = pair_shard(attn_half)
-    w_attn, last_moved = gather_line(attn_shard)
-    up_shard = pair_shard(up_half)
-    up_shard = after(up_shard, last_moved)
-    w_up, last_moved = gather_line(up_shard)
-    down_shard = pair_shard(down_half)
-    down_shard = after(down_shard, last_moved)
-    w_down, _ = gather_line(down_shard)
-    w_qkv, w_out = w_attn[:, :qkv_cols], w_attn[:, qkv_cols:]
-
-    resid, cots, plane_rows, plane_cots = [], [], [], []
-    for micro in range(micro_count):
-        resid.append(inputs[micro].reshape(token_rows, model_width))
-        cots.append(cotangent[micro].reshape(token_rows, model_width))
-    before = None
-    for micro in range(micro_count):
-        sent = resid[micro] if before is None else after(resid[micro], before)
-        before = gather_plane(sent)
-        plane_rows.append(before)
-    for micro in range(micro_count):
-        before = gather_plane(after(cots[micro], before))
-        plane_cots.append(before)
-
-    tables = rotary_tables(length, head_dim, ROT)
-    normed, rots, attns, lses, acts, pre_acts, outputs = ([] for _ in range(7))
-    for micro in range(micro_count):
-        normed.append(layer_norm(plane_rows[micro].astype(F32), gain_vec, shift_vec).astype(BF))
-        qkv = dot_plain(normed[micro], w_qkv) + qkv_b
-        rot, attn, lse = attend(qkv, tables, length, head_dim)
-        rots.append(rot)
-        attns.append(attn)
-        lses.append(lse)
-    for micro in range(micro_count):
-        pre = dot_plain(normed[micro], w_up) + up_b
-        pre_acts.append(pre)
-        acts.append(gelu_tanh(pre).astype(BF))
-    for micro in range(micro_count):
-        branch = dot_cols(
-            jnp.concatenate([attns[micro], acts[micro]], axis=1), jnp.concatenate([w_out, w_down], axis=1)
-        ).astype(BF)
-        branch = scatter_plane(branch).astype(F32)
-        outputs.append((resid[micro].astype(F32) + branch + bias_both).astype(BF))
-
-    def scatter_line(part):
-        def own(step):
-            at_line = (line_at - step) % line
-            return lax.dynamic_slice_in_dim(part, at_line * line_rows, line_rows, axis=0).astype(F32)
-
-        moving = own(1)
-        for step in range(2, line + 1):
-            moving = lax.ppermute(moving.astype(BF), "fsdp", ring).astype(F32) + own(step)
-        keep = lax.dynamic_slice_in_dim(moving, pair_at * shard_rows, shard_rows, axis=0)
-        give = lax.dynamic_slice_in_dim(moving, (1 - pair_at) * shard_rows, shard_rows, axis=0)
-        got = swap_pair(give.astype(BF)).astype(F32)
-        return jnp.where(pair_at == 0, keep, got), jnp.where(pair_at == 0, got, keep)
-
-    down_part = sum(dot_rows(plane_cots[m], acts[m]) for m in range(micro_count)).astype(BF)
-    down_grads = scatter_line(down_part)
-    pre_grads = []
-    for micro in range(micro_count):
-        act_grad = dot_plain(plane_cots[micro], w_down)
-        pre_grads.append(jax.vjp(gelu_tanh, pre_acts[micro])[1](act_grad)[0].astype(BF))
-    up_part = sum(dot_rows(normed[m], pre_grads[m]) for m in range(micro_count)).astype(BF)
-    up_grads = scatter_line(up_part)
-    qkv_grads = []
-    for micro in range(micro_count):
-        attn_grad = dot_plain(plane_cots[micro], w_out).astype(BF)
-        qkv_grads.append(attend_back(rots[micro], attn_grad, lses[micro], tables, length, head_dim))
-    attn_part = jnp.concatenate(
-        [
-            sum(dot_rows(normed[m], qkv_grads[m]) for m in range(micro_count)).astype(BF),
-            sum(dot_rows(plane_cots[m], attns[m]) for m in range(micro_count)).astype(BF),
-        ],
-        axis=1,
-    )
-    attn_grads = scatter_line(attn_part)
-    input_grads = []
-    gain_total = jnp.zeros((model_width,), F32)
-    shift_total = jnp.zeros((model_width,), F32)
+    def attend_piece(m):
+        rots[m], attns[m], lses[m] = order.run(
+            lambda vals: attend(vals, tables, length, head_dim), qkvs[m]
+        )
+
+    def up_piece(m):
+        acts[m], slopes[m] = order.run(lambda rows: up_act(slots, rows, up_ring.vals(), up_b), normed[m])
+
+    def head_grad_piece(m):
+        (attn_heads[m],) = order.run(
+            lambda cot: [head_grad_rows(slots, cot, attn_ring.vals(), qkv_cols)], plane_cots[m]
+        )
+
+    def attend_back_piece(m):
+        (qkv_grads[m],) = order.run(
+            lambda rot, grad, lse: [attend_back(rot, grad, lse, tables, length, head_dim)],
+            rots[m],
+            attn_heads[m],
+            lses[m],
+        )
+
+    def pre_grad_piece(m):
+        (pre_grads[m],) = order.run(
+            lambda cot, slope: [pre_grad_rows(slots, cot, down_ring.vals(), slope)], plane_cots[m], slopes[m]
+        )
+
+    def weight_piece(*groups):
+        flat = [box for lefts, rights in groups for box in (*lefts, *rights)]
+
+        def piece(*flat):
+            count = 2 * micro_count
+            return [
+                weight_grad(
+                    [
+                        (flat[at : at + micro_count], flat[at + micro_count : at + count])
+                        for at in range(0, len(flat), count)
+                    ]
+                )
+            ]
+
+        return Scatter(order.run(piece, *flat)[0])
+
+    def branch_piece(m):
+        (branches[m],) = order.run(
+            lambda attn, act: [branch_rows(slots, attn, attn_ring.vals(), qkv_cols, act, down_ring.vals())],
+            attns[m],
+            acts[m],
+        )
+
+    def normed_grad_piece(m):
+        back[m], sums[m] = order.run(
+            lambda one, two, rows, stat: normed_grad_rows(
+                slots, one, attn_ring.vals(), two, up_ring.vals(), rows, stat
+            ),
+            qkv_grads[m],
+            pre_grads[m],
+            plane_rows[m],
+            stats[m],
+        )
+
+    def scatter_behind(box):
+        order.tie(box)
+        return Box(scatter_plane(box.val))
+
+    up_ring, down_ring = Gather(up_shard), Gather(down_shard)
+    order.sync(down_shard)
+    up_ring.move()
+    norm_piece(0)
+    up_ring.sync()
+    plane_cots[1] = gather_behind(cots[1])
+    up_ring.move()
+    attend_piece(0)
+    norm_piece(1)
+    up_ring.sync()
+    up_ring.move()
+    attend_piece(1)
+    head_grad_piece(0)
+    up_ring.finish()
+    down_ring.move()
+    up_piece(0)
+    down_ring.sync()
+    down_ring.move()
+    up_piece(1)
+    down_ring.sync()
+    down_ring.move()
+    attend_back_piece(0)
+    down_ring.finish()
+
+    down_scatter = weight_piece((plane_cots, acts))
+    down_scatter.move()
+    pre_grad_piece(0)
+    branch_piece(0)
+    down_scatter.sync()
+    branch_sums = [scatter_behind(branches[0])]
+    down_scatter.move()
+    pre_grad_piece(1)
+    branch_piece(1)
+    down_scatter.sync()
+    branch_sums.append(scatter_behind(branches[1]))
+    down_scatter.move()
+    up_scatter = weight_piece((normed, pre_grads))
+    down_scatter.sync()
+    order.sync(branch_sums[0])
+    down_scatter.swap()
+    up_scatter.move()
+    head_grad_piece(1)
+    normed_grad_piece(0)
+    up_scatter.sync()
+    back_sums = [scatter_behind(back[0])]
+    up_scatter.move()
+    attend_back_piece(1)
+    up_scatter.sync()
+    order.sync(down_scatter.got)
+    up_scatter.move()
+    attn_scatter = weight_piece((normed, qkv_grads), (plane_cots, attns))
+    up_scatter.sync()
+    order.sync(branch_sums[1])
+    up_scatter.swap()
+    attn_scatter.move()
+    normed_grad_piece(1)
+    attn_scatter.sync()
+    back_sums.append(scatter_behind(back[1]))
+    attn_scatter.move()
+    order.sync(up_scatter.got)
+    attn_scatter.sync()
+    attn_scatter.move()
+    attn_scatter.swap()
+    attn_grads, up_grads, down_grads = attn_scatter.halves(), up_scatter.halves(), down_scatter.halves()
+
+    outputs, input_grads = [], []
     bias_total = jnp.zeros((model_width,), F32)
-    for micro in range(micro_count):
-        normed_grad = dot_cols(
-            jnp.concatenate([qkv_grads[micro], pre_grads[micro]], axis=1),
-            jnp.concatenate([w_qkv, w_up], axis=1),
-        ).astype(BF)
-        normed_grad = scatter_plane(normed_grad).astype(F32)
-        norm_back = jax.vjp(layer_norm, resid[micro].astype(F32), gain_vec, shift_vec)[1]
-        rows_grad, gain_grad, shift_grad = norm_back(normed_grad)
-        cot = cots[micro].astype(F32)
-        input_grads.append((cot + rows_grad).astype(BF))
-        gain_total += gain_grad
-        shift_total += shift_grad
+    for m in micros:
+        outputs.append((resid[m].astype(F32) + branch_sums[m].val.astype(F32) + bias_both).astype(BF))
+        vals, cot = resid[m].astype(F32), cots[m].astype(F32)
+        pull_back = jax.vjp(lambda vals: layer_norm(vals, gain_vec, shift_vec), vals)[1]
+        input_grads.append((cot + pull_back(back_sums[m].val.astype(F32))[0]).astype(BF))
         bias_total += jnp.sum(cot, axis=0)
-
-    up_b_grad = sum(jnp.sum(pre_grads[m].astype(F32), axis=0) for m in range(micro_count))
-    qkv_b_grad = sum(jnp.sum(qkv_grads[m].astype(F32), axis=0) for m in range(micro_count))
+    gain_total, shift_total = (sum(part.val[i] for part in sums) for i in range(2))
+
+    up_b_grad = sum(jnp.sum(pre_grads[m].val.astype(F32), axis=0) for m in micros)
+    qkv_b_grad = sum(jnp.sum(qkv_grads[m].val.astype(F32), axis=0) for m in micros)
     qkv_b_grad = qkv_b_grad.reshape(pairs, 3, -1).transpose(1, 0, 2).reshape(3, attn_cols)
 
     def in_half(vals):

time: 946 us -> 716 us (0.76)
  Pallas kernels: 77.2 us -> 371 us
  matrix products: 275 us -> 0 us
  waiting for transfers between devices: 406 us -> 178 us
  local copies, waits for them, and re-layouts: 71.6 us -> 48.6 us
  starting transfers between devices: 19.4 us -> 41 us
  other arithmetic: 75.3 us -> 55.8 us
    pallas_call x0 -> x15, Pallas kernels: none -> 289 us  [the longest x12 210 us: rows_call(): pl.pallas_call(kernel, grid_spec=pltpu.PrefetchScalarGridSpec(num_scalar_...]
    dot_general x20 -> x0, matrix products: 275 us -> none  [the longest x8 113 us: dot_plain(): lax.dot_general(left, right, (((1,), (0,)), ((), ())), preferred_element_...]
    ppermute x23, waiting for transfers between devices: 293 us -> 101 us  [the longest x9 36 us: move(): came = lax.ppermute(self.moving.val, 'fsdp', ring).astype(F32) + self.own()]
    all_gather x4, waiting for transfers between devices: 55.8 us -> 0.04 us  [gather_plane(): lax.all_gather(vals, both_axes, axis=0, tiled=True, axis_index_groups=pla...]
    reduce_scatter x4, waiting for transfers between devices: 0.04 us -> 45.4 us  [scatter_plane(): lax.psum_scatter(vals, both_axes, scatter_dimension=0, tiled=True, axis_i...]
    ppermute x6, waiting for transfers between devices: 51.3 us -> 28.7 us  [swap_pair(): return lax.ppermute(vals, 'fsdp', [(f, f ^ 1) for f in range(fsdp_size)])]
    ppermute x23, starting transfers between devices: 12.2 us -> 26.7 us  [the longest x9 12.2 us: move(): came = lax.ppermute(self.moving.val, 'fsdp', ring).astype(F32) + self.own()]
    convert_element_type x7 -> x6, other arithmetic: 24.6 us -> 10.2 us  [move(): self.moving = Box(came.astype(BF) if self.step < line else came)]
  transfers between devices with their start and end apart: 42 -> 42, of which waited for: 28 -> 18; matrix products, arithmetic and copies ran while one was open for 33% -> 12% of each run, Pallas kernels for 6% -> 49%
where the time goes in v2:
time: 716 us; the launch traced here: 709 us
  Pallas kernels  371 us (52%)
  waiting for transfers between devices  178 us (25%)
  other arithmetic  55.8 us (8%)
  local copies, waits for them, and re-layouts  48.6 us (7%)
  starting transfers between devices  41 us (6%)
  between operations  15.2 us (2%)
    pallas_call x12, Pallas kernels, rows_call(): pl.pallas_call(kernel, grid_spec=pltpu.PrefetchScalarGridSpec(num_scalar_...  210 us
    pallas_call x3, Pallas kernels, weight_grad(): pl.pallas_call(kernel, grid=(micro_count * steps,), in_specs=in_specs, ou...  79.2 us
    pallas_call x2, Pallas kernels, attend_back(): pl.pallas_call(functools.partial(attend_back_kernel, head_dim, block), gr...  49.5 us
    reduce_scatter x4, waiting for transfers between devices, scatter_plane(): lax.psum_scatter(vals, both_axes, scatter_dimension=0, tiled=True, axis_i...  45.4 us
    ppermute x9, waiting for transfers between devices, move(): came = lax.ppermute(self.moving.val, 'fsdp', ring).astype(F32) + self.own()  36 us
    ppermute x9, waiting for transfers between devices, move(): self.parts.append(Box(lax.ppermute(self.parts[-1].val, 'fsdp', ring)))  33.7 us
    pallas_call x2, Pallas kernels, attend(): pl.pallas_call(functools.partial(attend_kernel, head_dim, block), grid=(s...  32.1 us
    ppermute x5, waiting for transfers between devices, doubled(): other = lax.ppermute(cur, axis, [(i, i ^ bit) for i in range(size)])  30.9 us
  transfers between devices with their start and end apart: 42, of which 18 were waited for; matrix products, arithmetic and copies ran while one was open for 12% of the time, Pallas kernels for 49%

profile of v2, /device:TPU:0, one launch (start us, length us, event | category | flops | bytes accessed | tf_op | source)
XLA Modules:
  0.0 709.3 jit_solution(5978405120672489697)
XLA Ops:
  21.9 16.5 %collective-permute-done.2 = bf16[256,1024]{1,0:T(8,128)(2,1)S(1)} collective-permute-done((bf16[256,1024]{1,0:T(8,128)(2,1)S(1)}, bf16[256,1024]{1,0:T(8,128)(2,1)S(1)}, u32[]{:S(2)}, u32[]{:S(2)}) %collective-permute-start.2) | collective-permute-done | bytes 524320 | tf_op jit(solution)/shard_map/ppermute | solution.py:468
  45.1 17.9 %collective-permute-done.3.refs_1_ = bf16[512,1024]{1,0:T(8,128)(2,1)S(1)} collective-permute-done((bf16[512,1024]{1,0:T(8,128)(2,1)S(1)}, bf16[512,1024]{1,0:T(8,128)(2,1)S(1)}, u32[]{:S(2)}, u32[]{:S(2)}) %collective-permute-start.3) | collective-permute-done | bytes 1048608 | tf_op jit(solution)/shard_map/ppermute | solution.py:558
  70.9 11.8 %collective-permute-done.6 = bf16[8,704]{1,0:T(8,128)(2,1)S(1)} collective-permute-done((bf16[8,704]{1,0:T(8,128)(2,1)S(1)}, bf16[8,704]{1,0:T(8,128)(2,1)S(1)}, u32[]{:S(2)}, u32[]{:S(2)}) %collective-permute-start.6) | collective-permute-done | bytes 11296 | tf_op jit(solution)/shard_map/ppermute | solution.py:480
  82.7 4.1 collective-permute-done.7
  98.6 18.3 %collective-permute-done.9 = bf16[16,704]{1,0:T(8,128)(2,1)S(1)} collective-permute-done((bf16[16,704]{1,0:T(8,128)(2,1)S(1)}, bf16[16,704]{1,0:T(8,128)(2,1)S(1)}, u32[]{:S(2)}, u32[]{:S(2)}) %collective-permute-start.9) | collective-permute-done | bytes 22560 | tf_op jit(solution)/shard_map/ppermute | solution.py:480
  123.2 20.4 %shard_map.211 = (bf16[2048,2048]{1,0:T(8,128)(2,1)}, f32[2048,768]{1,0:T(8,128)}, f32[2048,128]{1,0:T(8,128)}) custom-call(s32[4]{0:T(128)} %pad_add_fusion.slots_ref, bf16[2048,2048]{1,0:T(8,128)(2,1)} %all-gather.9.cloned.1.call-done.rows_ref, f32[1,2048]{1,0:T(1,128)} %reshape.238.gain_ref, f32[1,2048]{1,0:T(1,128)} %reshape.239.shift_ref, ...), custom_call_target="tpu_custom_call" | custom-call | flops 100663296 | bytes 360448 | tf_op jit(solution)/shard_map/pallas_call | solution.py:209
  151.0 16.0 %shard_map.212 = (bf16[2048,768]{1,0:T(8,128)(2,1)}, bf16[2048,256]{1,0:T(8,128)(2,1)}, f32[4,2,1024]{2,1,0:T(2,128)}) custom-call(f32[2048,768]{1,0:T(8,128)} %get-tuple-element.265.qkv_ref, f32[1024,128]{1,0:T(8,128)} %copy.78.cos_ref, f32[1024,128]{1,0:T(8,128)} %copy.79.low_ref, f32[1024,128]{1,0:T(8,128)} %copy.80.up_ref), custom_call_target="tpu_custom_call" | custom-call | flops 100663296 | bytes 131072 | tf_op jit(solution)/shard_map/pallas_call | solution.py:143
  167.1 20.4 %shard_map.213 = (bf16[2048,2048]{1,0:T(8,128)(2,1)}, f32[2048,768]{1,0:T(8,128)}, f32[2048,128]{1,0:T(8,128)}) custom-call(s32[4]{0:T(128)} %pad_add_fusion.slots_ref, bf16[2048,2048]{1,0:T(8,128)(2,1)} %all-gather.7.cloned.1.call-done.rows_ref, f32[1,2048]{1,0:T(1,128)} %reshape.238.gain_ref, f32[1,2048]{1,0:T(1,128)} %reshape.239.shift_ref, ...), custom_call_target="tpu_custom_call" | custom-call | flops 100663296 | bytes 360448 | tf_op jit(solution)/shard_map/pallas_call | solution.py:209
  187.8 16.1 %shard_map.214 = (bf16[2048,768]{1,0:T(8,128)(2,1)}, bf16[2048,256]{1,0:T(8,128)(2,1)}, f32[4,2,1024]{2,1,0:T(2,128)}) custom-call(f32[2048,768]{1,0:T(8,128)} %get-tuple-element.272.qkv_ref, f32[1024,128]{1,0:T(8,128)} %copy.78.cos_ref, f32[1024,128]{1,0:T(8,128)} %copy.79.low_ref, f32[1024,128]{1,0:T(8,128)} %copy.80.up_ref), custom_call_target="tpu_custom_call" | custom-call | flops 100663296 | bytes 131072 | tf_op jit(solution)/shard_map/pallas_call | solution.py:143
  203.9 7.6 %shard_map.215.grad_ref = bf16[2048,256]{1,0:T(8,128)(2,1)} custom-call(s32[4]{0:T(128)} %pad_add_fusion.slots_ref, bf16[2048,2048]{1,0:T(8,128)(2,1)} %all-gather.5.cloned.1.call-done.rows_ref.refs_0_.refs_4_, bf16[512,1024]{1,0:T(8,128)(2,1)} %copy-done, bf16[512,1024]{1,0:T(8,128)(2,1)} %copy-done.1, bf16[512,1024]{1,0:T(8,128)(2,1)} %copy-done.2, ...), custom_call_target="tpu_custom_call" | custom-call | flops 33554432 | bytes 147456 | tf_op jit(solution)/shard_map/pallas_call | solution.py:209
  214.7 18.9 %shard_map.216 = (bf16[2048,1024]{1,0:T(8,128)(2,1)}, bf16[2048,1024]{1,0:T(8,128)(2,1)}) custom-call(s32[4]{0:T(128)} %pad_add_fusion.slots_ref, bf16[2048,2048]{1,0:T(8,128)(2,1)} %get-tuple-element.366.rows_ref.refs_0_, f32[1,1024]{1,0:T(1,128)} %constant_dynamic-slice_fusion.8.bias_ref, bf16[512,1024]{1,0:T(8,128)(2,1)} %maximum_select_fusion.1.refs_0_.refs_4_, ...), custom_call_target="tpu_custom_call" | custom-call | flops 134217728 | bytes 262144 | tf_op jit(solution)/shard_map/pallas_call | solution.py:209
  233.6 5.2 collective-permute-done.14.refs_1_.refs_5_
  238.8 18.9 %shard_map.217 = (bf16[2048,1024]{1,0:T(8,128)(2,1)}, bf16[2048,1024]{1,0:T(8,128)(2,1)}) custom-call(s32[4]{0:T(128)} %pad_add_fusion.slots_ref, bf16[2048,2048]{1,0:T(8,128)(2,1)} %get-tuple-element.367.rows_ref.refs_1_, f32[1,1024]{1,0:T(1,128)} %constant_dynamic-slice_fusion.8.bias_ref, bf16[512,1024]{1,0:T(8,128)(2,1)} %maximum_select_fusion.1.refs_0_.refs_4_, ...), custom_call_target="tpu_custom_call" | custom-call | flops 134217728 | bytes 262144 | tf_op jit(solution)/shard_map/pallas_call | solution.py:209
  257.8 5.3 collective-permute-done.15.refs_2_.refs_6_
  263.0 24.7 %shard_map.218.one_ref.refs_2_ = bf16[2048,768]{1,0:T(8,128)(2,1)} custom-call(bf16[2048,768]{1,0:T(8,128)(2,1)} %get-tuple-element.299.rot_ref, bf16[2048,256]{1,0:T(8,128)(2,1)} %shard_map.215.grad_ref, f32[4,2,1024]{2,1,0:T(2,128)} %get-tuple-element.301.lse_ref, f32[1024,128]{1,0:T(8,128)} %copy.78.cos_ref, f32[1024,128]{1,0:T(8,128)} %copy.79.low_ref, ...), custom_call_target="tpu_custom_call" | custom-call | flops 201326592 | bytes 131072 | tf_op jit(solution)/shard_map/pallas_call | solution.py:168
  287.8 25.7 %shard_map.219 = bf16[2048,1024]{1,0:T(8,128)(2,1)} custom-call(bf16[2048,2048]{1,0:T(8,128)(2,1)} %all-gather.5.cloned.1.call-done.rows_ref.refs_0_.refs_4_, bf16[2048,2048]{1,0:T(8,128)(2,1)} %all-gather.11.cloned.1.call-done.refs_1_.rows_ref.refs_5_, bf16[2048,1024]{1,0:T(8,128)(2,1)} %get-tuple-element.316.refs_2_.two_ref, ...), custom_call_target="tpu_custom_call" | custom-call | flops 268435456 | bytes 393216 | tf_op jit(solution)/shard_map/pallas_call | solution.py:421
  315.3 14.2 %shard_map.220.refs_2_.two_ref = bf16[2048,1024]{1,0:T(8,128)(2,1)} custom-call(s32[4]{0:T(128)} %pad_add_fusion.slots_ref, bf16[2048,2048]{1,0:T(8,128)(2,1)} %all-gather.5.cloned.1.call-done.rows_ref.refs_0_.refs_4_, bf16[2048,1024]{1,0:T(8,128)(2,1)} %get-tuple-element.311.slope_ref, bf16[512,1024]{1,0:T(8,128)(2,1)} %maximum_select_fusion.2.refs_0_.refs_4_, ...), custom_call_target="tpu_custom_call" | custom-call | flops 134217728 | bytes 262144 | tf_op jit(solution)/shard_map/pallas_call | solution.py:209
  329.5 17.6 %shard_map.221 = bf16[2048,2048]{1,0:T(8,128)(2,1)} custom-call(s32[4]{0:T(128)} %pad_add_fusion.slots_ref, bf16[2048,256]{1,0:T(8,128)(2,1)} %get-tuple-element.371.one_ref.refs_6_, bf16[2048,1024]{1,0:T(8,128)(2,1)} %get-tuple-element.316.refs_2_.two_ref, bf16[512,1024]{1,0:T(8,128)(2,1)} %copy-done, bf16[512,1024]{1,0:T(8,128)(2,1)} %copy-done.1, ...), custom_call_target="tpu_custom_call" | custom-call | flops 167772160 | bytes 212992 | tf_op jit(solution)/shard_map/pallas_call | solution.py:209
  349.2 14.8 %shard_map.222.refs_3_.two_ref = bf16[2048,1024]{1,0:T(8,128)(2,1)} custom-call(s32[4]{0:T(128)} %pad_add_fusion.slots_ref, bf16[2048,2048]{1,0:T(8,128)(2,1)} %all-gather.11.cloned.1.call-done.refs_1_.rows_ref.refs_5_, bf16[2048,1024]{1,0:T(8,128)(2,1)} %get-tuple-element.324.slope_ref, bf16[512,1024]{1,0:T(8,128)(2,1)} %maximum_select_fusion.2.refs_0_.refs_4_, ...), custom_call_target="tpu_custom_call" | custom-call | flops 134217728 | bytes 262144 | tf_op jit(solution)/shard_map/pallas_call | solution.py:209
  364.0 17.8 %shard_map.223 = bf16[2048,2048]{1,0:T(8,128)(2,1)} custom-call(s32[4]{0:T(128)} %pad_add_fusion.slots_ref, bf16[2048,256]{1,0:T(8,128)(2,1)} %get-tuple-element.372.one_ref.refs_7_, bf16[2048,1024]{1,0:T(8,128)(2,1)} %get-tuple-element.327.refs_3_.two_ref, bf16[512,1024]{1,0:T(8,128)(2,1)} %copy-done, bf16[512,1024]{1,0:T(8,128)(2,1)} %copy-done.1, ...), custom_call_target="tpu_custom_call" | custom-call | flops 167772160 | bytes 212992 | tf_op jit(solution)/shard_map/pallas_call | solution.py:209
  383.5 4.7 collective-permute-start.19
  388.2 25.7 %shard_map.224 = bf16[2048,1024]{1,0:T(8,128)(2,1)} custom-call(bf16[2048,2048]{1,0:T(8,128)(2,1)} %get-tuple-element.366.rows_ref.refs_0_, bf16[2048,2048]{1,0:T(8,128)(2,1)} %get-tuple-element.367.rows_ref.refs_1_, bf16[2048,1024]{1,0:T(8,128)(2,1)} %shard_map.220.refs_2_.two_ref, bf16[2048,1024]{1,0:T(8,128)(2,1)} %shard_map.222.refs_3_.two_ref), custom_call_target="tpu_custom_call" | custom-call | flops 268435456 | bytes 393216 | tf_op jit(solution)/shard_map/pallas_call | solution.py:421
  422.1 7.4 %shard_map.225.grad_ref = bf16[2048,256]{1,0:T(8,128)(2,1)} custom-call(s32[4]{0:T(128)} %pad_add_fusion.slots_ref, bf16[2048,2048]{1,0:T(8,128)(2,1)} %all-gather.11.cloned.1.call-done.refs_1_.rows_ref.refs_5_, bf16[512,1024]{1,0:T(8,128)(2,1)} %copy-done, bf16[512,1024]{1,0:T(8,128)(2,1)} %copy-done.1, bf16[512,1024]{1,0:T(8,128)(2,1)} %copy-done.2, ...), custom_call_target="tpu_custom_call" | custom-call | flops 33554432 | bytes 147456 | tf_op jit(solution)/shard_map/pallas_call | solution.py:209
  429.5 26.1 %shard_map.226 = (bf16[2048,2048]{1,0:T(8,128)(2,1)}, f32[8,2048]{1,0:T(8,128)}) custom-call(s32[4]{0:T(128)} %pad_add_fusion.slots_ref, bf16[2048,768]{1,0:T(8,128)(2,1)} %shard_map.218.one_ref.refs_2_, bf16[2048,1024]{1,0:T(8,128)(2,1)} %shard_map.220.refs_2_.two_ref, bf16[2048,2048]{1,0:T(8,128)(2,1)} %all-gather.9.cloned.1.call-done.rows_ref, ...), custom_call_target="tpu_custom_call" | custom-call | flops 234881024 | bytes 376832 | tf_op jit(solution)/shard_map/pallas_call | solution.py:209
  460.9 24.7 %shard_map.227.refs_3_.one_ref = bf16[2048,768]{1,0:T(8,128)(2,1)} custom-call(bf16[2048,768]{1,0:T(8,128)(2,1)} %get-tuple-element.358.rot_ref, bf16[2048,256]{1,0:T(8,128)(2,1)} %shard_map.225.grad_ref, f32[4,2,1024]{2,1,0:T(2,128)} %get-tuple-element.360.lse_ref, f32[1024,128]{1,0:T(8,128)} %copy.78.cos_ref, f32[1024,128]{1,0:T(8,128)} %copy.79.low_ref, ...), custom_call_target="tpu_custom_call" | custom-call | flops 201326592 | bytes 131072 | tf_op jit(solution)/shard_map/pallas_call | solution.py:168
  488.8 27.8 %shard_map.228 = bf16[2048,1024]{1,0:T(8,128)(2,1)} custom-call(bf16[2048,2048]{1,0:T(8,128)(2,1)} %get-tuple-element.366.rows_ref.refs_0_, bf16[2048,2048]{1,0:T(8,128)(2,1)} %get-tuple-element.367.rows_ref.refs_1_, bf16[2048,768]{1,0:T(8,128)(2,1)} %shard_map.218.one_ref.refs_2_, bf16[2048,768]{1,0:T(8,128)(2,1)} %shard_map.227.refs_3_.one_ref, ...), custom_call_target="tpu_custom_call" | custom-call | flops 268435456 | bytes 655360 | tf_op jit(solution)/shard_map/pallas_call | solution.py:421
  519.9 25.8 %shard_map.229 = (bf16[2048,2048]{1,0:T(8,128)(2,1)}, f32[8,2048]{1,0:T(8,128)}) custom-call(s32[4]{0:T(128)} %pad_add_fusion.slots_ref, bf16[2048,768]{1,0:T(8,128)(2,1)} %shard_map.227.refs_3_.one_ref, bf16[2048,1024]{1,0:T(8,128)(2,1)} %shard_map.222.refs_3_.two_ref, bf16[2048,2048]{1,0:T(8,128)(2,1)} %all-gather.7.cloned.1.call-done.rows_ref, ...), custom_call_target="tpu_custom_call" | custom-call | flops 234881024 | bytes 376832 | tf_op jit(solution)/shard_map/pallas_call | solution.py:209
  557.9 17.1 %collective-permute-done.30 = bf16[512,1024]{1,0:T(8,128)(2,1)} collective-permute-done((bf16[512,1024]{1,0:T(8,128)(2,1)S(1)}, bf16[512,1024]{1,0:T(8,128)(2,1)}, u32[]{:S(2)}, u32[]{:S(2)}) %collective-permute-start.30) | collective-permute-done | bytes 1048608 | tf_op jit(solution)/shard_map/ppermute | solution.py:584
  577.1 5.2 convert_reduce_fusion
  583.3 18.9 %collective-permute-done.32 = bf16[512,1024]{1,0:T(8,128)(2,1)S(1)} collective-permute-done((bf16[512,1024]{1,0:T(8,128)(2,1)S(1)}, bf16[512,1024]{1,0:T(8,128)(2,1)S(1)}, u32[]{:S(2)}, u32[]{:S(2)}) %collective-permute-start.32) | collective-permute-done | bytes 1048608 | tf_op jit(solution)/shard_map/ppermute | solution.py:584
  607.2 8.1 %collective-permute-done.33 = bf16[256,1024]{1,0:T(8,128)(2,1)S(1)} collective-permute-done((bf16[256,1024]{1,0:T(8,128)(2,1)S(1)}, bf16[256,1024]{1,0:T(8,128)(2,1)S(1)}, u32[]{:S(2)}, u32[]{:S(2)}) %collective-permute-start.33) | collective-permute-done | bytes 524320 | tf_op jit(solution)/shard_map/ppermute | solution.py:468
  620.4 42.6 %reduce-scatter.11.cloned.1.call-done = bf16[256,2048]{1,0:T(8,128)(2,1)} async-done(((bf16[2048,2048]{1,0:T(8,128)(2,1)}), bf16[256,2048]{1,0:T(8,128)(2,1)}) %reduce-scatter.11.cloned.1.call-update) | async-done | bytes 1048592 | tf_op jit(solution)/shard_map/reduce_scatter | solution.py:474
  (284 shorter events, 147.9 us)
Async XLA Ops:
  7.2 116.0 %all-gather.9.cloned.1.call-start = ((), (), s32[]{:S(2)}) async-start(), calls=%async_computation.6 | async-start | bytes 9437184 | tf_op jit(solution)/shard_map/all_gather | solution.py:471
  19.1 148.0 %all-gather.7.cloned.1.call-start = ((), (), s32[]{:S(2)}) async-start(), calls=%async_computation.5 | async-start | bytes 9437184 | tf_op jit(solution)/shard_map/all_gather | solution.py:471
  38.8 165.0 %all-gather.5.cloned.1.call-start = ((), (), s32[]{:S(2)}) async-start(), calls=%async_computation.4 | async-start | bytes 9437184 | tf_op jit(solution)/shard_map/all_gather | solution.py:471
  38.9 24.1 %collective-permute-start.3 = (bf16[512,1024]{1,0:T(8,128)(2,1)S(1)}, bf16[512,1024]{1,0:T(8,128)(2,1)S(1)}, u32[]{:S(2)}, u32[]{:S(2)}) collective-permute-start(bf16[512,1024]{1,0:T(8,128)(2,1)S(1)} %maximum_select_fusion.refs_0_), channel_id=1, source_target_pairs={{0,8},{4,12},{8,16},{12,20},{16,24},{20,28},{24,0},{28,4},{1,9},{5... | collective-permute-start | bytes 3145736 | tf_op jit(solution)/shard_map/ppermute | solution.py:558
  63.0 26.9 %collective-permute-start.5 = (bf16[512,1024]{1,0:T(8,128)(2,1)S(1)}, bf16[512,1024]{1,0:T(8,128)(2,1)S(1)}, u32[]{:S(2)}, u32[]{:S(2)}) collective-permute-start(bf16[512,1024]{1,0:T(8,128)(2,1)S(1)} %collective-permute-done.3.refs_1_), channel_id=1, source_target_pairs={{0,8},{4,12},{8,16},{12,20},{16,24},{20,28},{24,0},{28,4},{1,9},{5... | collective-permute-start | bytes 3145736 | tf_op jit(solution)/shard_map/ppermute | solution.py:558
  63.0 19.7 %collective-permute-start.6 = (bf16[8,704]{1,0:T(8,128)(2,1)S(1)}, bf16[8,704]{1,0:T(8,128)(2,1)S(1)}, u32[]{:S(2)}, u32[]{:S(2)}) collective-permute-start(bf16[8,704]{1,0:T(8,128)(2,1)S(1)} %maximum_select_fusion.5), channel_id=1, source_target_pairs={{0,8},{4,12},{8,0},{12,4},{16,24},{20,28},{24,16},{28,20},{1,9},{5... | collective-permute-start | bytes 33800 | tf_op jit(solution)/shard_map/ppermute | solution.py:480
  65.3 21.5 %collective-permute-start.7 = (bf16[256,1024]{1,0:T(8,128)(2,1)}, bf16[256,1024]{1,0:T(8,128)(2,1)}, u32[]{:S(2)}, u32[]{:S(2)}) collective-permute-start(bf16[256,1024]{1,0:T(8,128)(2,1)} %get-tuple-element.217), channel_id=1, source_target_pairs={{0,4},{4,0},{8,12},{12,8},{16,20},{20,16},{24,28},{28,24},{1,5},{5... | collective-permute-start | bytes 1572872 | tf_op jit(solution)/shard_map/ppermute | solution.py:468
  89.9 197.9 %all-gather.11.cloned.1.call-start = ((), (), s32[]{:S(2)}) async-start(), calls=%async_computation.7 | async-start | bytes 9437184 | tf_op jit(solution)/shard_map/all_gather | solution.py:471
  92.1 27.8 %collective-permute-start.8 = (bf16[512,1024]{1,0:T(8,128)(2,1)S(1)}, bf16[512,1024]{1,0:T(8,128)(2,1)S(1)}, u32[]{:S(2)}, u32[]{:S(2)}) collective-permute-start(bf16[512,1024]{1,0:T(8,128)(2,1)S(1)} %collective-permute-done.5.refs_2_), channel_id=1, source_target_pairs={{0,8},{4,12},{8,16},{12,20},{16,24},{20,28},{24,0},{28,4},{1,9},{5... | collective-permute-start | bytes 3145736 | tf_op jit(solution)/shard_map/ppermute | solution.py:558
  93.5 23.4 %collective-permute-start.10 = (bf16[256,1024]{1,0:T(8,128)(2,1)}, bf16[256,1024]{1,0:T(8,128)(2,1)}, u32[]{:S(2)}, u32[]{:S(2)}) collective-permute-start(bf16[256,1024]{1,0:T(8,128)(2,1)} %bitcast.126), channel_id=1, source_target_pairs={{0,4},{4,0},{8,12},{12,8},{16,20},{20,16},{24,28},{28,24},{1,5},{5... | collective-permute-start | bytes 1572872 | tf_op jit(solution)/shard_map/ppermute | solution.py:468
  94.1 22.8 %collective-permute-start.9 = (bf16[16,704]{1,0:T(8,128)(2,1)S(1)}, bf16[16,704]{1,0:T(8,128)(2,1)S(1)}, u32[]{:S(2)}, u32[]{:S(2)}) collective-permute-start(bf16[16,704]{1,0:T(8,128)(2,1)S(1)} %maximum_select_fusion.4), channel_id=1, source_target_pairs={{0,16},{4,20},{8,24},{12,28},{16,0},{20,4},{24,8},{28,12},{1,17},{... | collective-permute-start | bytes 67592 | tf_op jit(solution)/shard_map/ppermute | solution.py:480
  119.9 26.9 %collective-permute-start.11 = (bf16[512,1024]{1,0:T(8,128)(2,1)S(1)}, bf16[512,1024]{1,0:T(8,128)(2,1)S(1)}, u32[]{:S(2)}, u32[]{:S(2)}) collective-permute-start(bf16[512,1024]{1,0:T(8,128)(2,1)S(1)} %copy-done.5), channel_id=1, source_target_pairs={{0,8},{4,12},{8,16},{12,20},{16,24},{20,28},{24,0},{28,4},{1,9},{5... | collective-permute-start | bytes 3145736 | tf_op jit(solution)/shard_map/ppermute | solution.py:558
  146.9 273.8 %reduce-scatter.5.cloned.1.call-start = ((), (), s32[]{:S(2)}) async-start(), calls=%async_computation.8 | async-start | bytes 9437184 | tf_op jit(solution)/shard_map/reduce_scatter | solution.py:474
  146.9 40.5 %collective-permute-start.12 = (bf16[512,1024]{1,0:T(8,128)(2,1)S(1)}, bf16[512,1024]{1,0:T(8,128)(2,1)S(1)}, u32[]{:S(2)}, u32[]{:S(2)}) collective-permute-start(bf16[512,1024]{1,0:T(8,128)(2,1)S(1)} %collective-permute-done.11.refs_1_.refs_5_), channel_id=1, source_target_pairs={{0,8},{4,12},{8,16},{12,20},{16,24},{20,28},{24,0},{28,4},{1,9},{5... | collective-permute-start | bytes 3145736 | tf_op jit(solution)/shard_map/ppermute | solution.py:558
  187.4 26.1 %collective-permute-start.13 = (bf16[512,1024]{1,0:T(8,128)(2,1)S(1)}, bf16[512,1024]{1,0:T(8,128)(2,1)S(1)}, u32[]{:S(2)}, u32[]{:S(2)}) collective-permute-start(bf16[512,1024]{1,0:T(8,128)(2,1)S(1)} %collective-permute-done.12.refs_2_.refs_6_), channel_id=1, source_target_pairs={{0,8},{4,12},{8,16},{12,20},{16,24},{20,28},{24,0},{28,4},{1,9},{5... | collective-permute-start | bytes 3145736 | tf_op jit(solution)/shard_map/ppermute | solution.py:558
  213.5 25.3 %collective-permute-start.14 = (bf16[512,1024]{1,0:T(8,128)(2,1)S(1)}, bf16[512,1024]{1,0:T(8,128)(2,1)S(1)}, u32[]{:S(2)}, u32[]{:S(2)}) collective-permute-start(bf16[512,1024]{1,0:T(8,128)(2,1)S(1)} %copy-done.6), channel_id=1, source_target_pairs={{0,8},{4,12},{8,16},{12,20},{16,24},{20,28},{24,0},{28,4},{1,9},{5... | collective-permute-start | bytes 3145736 | tf_op jit(solution)/shard_map/ppermute | solution.py:558
  238.8 24.2 %collective-permute-start.15 = (bf16[512,1024]{1,0:T(8,128)(2,1)S(1)}, bf16[512,1024]{1,0:T(8,128)(2,1)S(1)}, u32[]{:S(2)}, u32[]{:S(2)}) collective-permute-start(bf16[512,1024]{1,0:T(8,128)(2,1)S(1)} %collective-permute-done.14.refs_1_.refs_5_), channel_id=1, source_target_pairs={{0,8},{4,12},{8,16},{12,20},{16,24},{20,28},{24,0},{28,4},{1,9},{5... | collective-permute-start | bytes 3145736 | tf_op jit(solution)/shard_map/ppermute | solution.py:558
  263.0 24.7 %collective-permute-start.16 = (bf16[512,1024]{1,0:T(8,128)(2,1)S(1)}, bf16[512,1024]{1,0:T(8,128)(2,1)S(1)}, u32[]{:S(2)}, u32[]{:S(2)}) collective-permute-start(bf16[512,1024]{1,0:T(8,128)(2,1)S(1)} %collective-permute-done.15.refs_2_.refs_6_), channel_id=1, source_target_pairs={{0,8},{4,12},{8,16},{12,20},{16,24},{20,28},{24,0},{28,4},{1,9},{5... | collective-permute-start | bytes 3145736 | tf_op jit(solution)/shard_map/ppermute | solution.py:558
  314.8 32.3 %collective-permute-start.17 = (bf16[512,1024]{1,0:T(8,128)(2,1)S(1)}, bf16[512,1024]{1,0:T(8,128)(2,1)S(1)}, u32[]{:S(2)}, u32[]{:S(2)}) collective-permute-start(bf16[512,1024]{1,0:T(8,128)(2,1)S(1)} %constant_dynamic-slice_fusion.7), channel_id=1, source_target_pairs={{0,8},{4,12},{8,16},{12,20},{16,24},{20,28},{24,0},{28,4},{1,9},{5... | collective-permute-start | bytes 3145736 | tf_op jit(solution)/shard_map/ppermute | solution.py:584
  348.7 170.8 %reduce-scatter.7.cloned.1.call-start = ((), (), s32[]{:S(2)}) async-start(), calls=%async_computation.9 | async-start | bytes 9437184 | tf_op jit(solution)/shard_map/reduce_scatter | solution.py:474
  348.8 33.0 %collective-permute-start.18 = (bf16[512,1024]{1,0:T(8,128)(2,1)S(1)}, bf16[512,1024]{1,0:T(8,128)(2,1)S(1)}, u32[]{:S(2)}, u32[]{:S(2)}) collective-permute-start(bf16[512,1024]{1,0:T(8,128)(2,1)S(1)} %add_convert_fusion.5), channel_id=1, source_target_pairs={{0,8},{4,12},{8,16},{12,20},{16,24},{20,28},{24,0},{28,4},{1,9},{5... | collective-permute-start | bytes 3145736 | tf_op jit(solution)/shard_map/ppermute | solution.py:584
  383.5 237.0 %reduce-scatter.9.cloned.1.call-start = ((), (), s32[]{:S(2)}) async-start(), calls=%async_computation.10 | async-start | bytes 9437184 | tf_op jit(solution)/shard_map/reduce_scatter | solution.py:474
  383.5 32.7 %collective-permute-start.19 = (bf16[512,1024]{1,0:T(8,128)(2,1)S(1)}, bf16[512,1024]{1,0:T(8,128)(2,1)S(1)}, u32[]{:S(2)}, u32[]{:S(2)}) collective-permute-start(bf16[512,1024]{1,0:T(8,128)(2,1)S(1)} %add_convert_fusion.4), channel_id=1, source_target_pairs={{0,8},{4,12},{8,16},{12,20},{16,24},{20,28},{24,0},{28,4},{1,9},{5... | collective-permute-start | bytes 3145736 | tf_op jit(solution)/shard_map/ppermute | solution.py:584
  420.6 35.0 %collective-permute-start.20 = (bf16[512,1024]{1,0:T(8,128)(2,1)}, bf16[512,1024]{1,0:T(8,128)(2,1)S(1)}, u32[]{:S(2)}, u32[]{:S(2)}) collective-permute-start(bf16[512,1024]{1,0:T(8,128)(2,1)} %constant_dynamic-slice_fusion.6), channel_id=1, source_target_pairs={{0,8},{4,12},{8,16},{12,20},{16,24},{20,28},{24,0},{28,4},{1,9},{5... | collective-permute-start | bytes 3145736 | tf_op jit(solution)/shard_map/ppermute | solution.py:584
  457.4 205.7 %reduce-scatter.11.cloned.1.call-start = ((), (), s32[]{:S(2)}) async-start(), calls=%async_computation.11 | async-start | bytes 9437184 | tf_op jit(solution)/shard_map/reduce_scatter | solution.py:474
  457.4 28.1 %collective-permute-start.21 = (bf16[512,1024]{1,0:T(8,128)(2,1)S(1)}, bf16[512,1024]{1,0:T(8,128)(2,1)}, u32[]{:S(2)}, u32[]{:S(2)}) collective-permute-start(bf16[512,1024]{1,0:T(8,128)(2,1)S(1)} %add_convert_fusion.3), channel_id=1, source_target_pairs={{0,8},{4,12},{8,16},{12,20},{16,24},{20,28},{24,0},{28,4},{1,9},{5... | collective-permute-start | bytes 3145736 | tf_op jit(solution)/shard_map/ppermute | solution.py:584
  459.4 27.9 %collective-permute-start.22 = (bf16[256,1024]{1,0:T(8,128)(2,1)S(1)}, bf16[256,1024]{1,0:T(8,128)(2,1)}, u32[]{:S(2)}, u32[]{:S(2)}) collective-permute-start(bf16[256,1024]{1,0:T(8,128)(2,1)S(1)} %dynamic-slice_convert_fusion.2), channel_id=1, source_target_pairs={{0,4},{4,0},{8,12},{12,8},{16,20},{20,16},{24,28},{28,24},{1,5},{5... | collective-permute-start | bytes 1572872 | tf_op jit(solution)/shard_map/ppermute | solution.py:468
  487.3 30.5 %collective-permute-start.23 = (bf16[512,1024]{1,0:T(8,128)(2,1)S(1)}, bf16[512,1024]{1,0:T(8,128)(2,1)S(1)}, u32[]{:S(2)}, u32[]{:S(2)}) collective-permute-start(bf16[512,1024]{1,0:T(8,128)(2,1)S(1)} %add_convert_fusion.2), channel_id=1, source_target_pairs={{0,8},{4,12},{8,16},{12,20},{16,24},{20,28},{24,0},{28,4},{1,9},{5... | collective-permute-start | bytes 3145736 | tf_op jit(solution)/shard_map/ppermute | solution.py:584
  519.5 26.2 %collective-permute-start.24 = (bf16[512,1024]{1,0:T(8,128)(2,1)S(1)}, bf16[512,1024]{1,0:T(8,128)(2,1)S(1)}, u32[]{:S(2)}, u32[]{:S(2)}) collective-permute-start(bf16[512,1024]{1,0:T(8,128)(2,1)S(1)} %constant_dynamic-slice_fusion.5), channel_id=1, source_target_pairs={{0,8},{4,12},{8,16},{12,20},{16,24},{20,28},{24,0},{28,4},{1,9},{5... | collective-permute-start | bytes 3145736 | tf_op jit(solution)/shard_map/ppermute | solution.py:584
  549.4 25.7 %collective-permute-start.30 = (bf16[512,1024]{1,0:T(8,128)(2,1)S(1)}, bf16[512,1024]{1,0:T(8,128)(2,1)}, u32[]{:S(2)}, u32[]{:S(2)}) collective-permute-start(bf16[512,1024]{1,0:T(8,128)(2,1)S(1)} %add_convert_fusion.1), channel_id=1, source_target_pairs={{0,8},{4,12},{8,16},{12,20},{16,24},{20,28},{24,0},{28,4},{1,9},{5... | collective-permute-start | bytes 3145736 | tf_op jit(solution)/shard_map/ppermute | solution.py:584
  553.0 24.0 %collective-permute-start.31 = (bf16[256,1024]{1,0:T(8,128)(2,1)}, bf16[256,1024]{1,0:T(8,128)(2,1)}, u32[]{:S(2)}, u32[]{:S(2)}) collective-permute-start(bf16[256,1024]{1,0:T(8,128)(2,1)} %dynamic-slice_convert_fusion.1), channel_id=1, source_target_pairs={{0,4},{4,0},{8,12},{12,8},{16,20},{20,16},{24,28},{28,24},{1,5},{5... | collective-permute-start | bytes 1572872 | tf_op jit(solution)/shard_map/ppermute | solution.py:468
  577.0 25.1 %collective-permute-start.32 = (bf16[512,1024]{1,0:T(8,128)(2,1)S(1)}, bf16[512,1024]{1,0:T(8,128)(2,1)S(1)}, u32[]{:S(2)}, u32[]{:S(2)}) collective-permute-start(bf16[512,1024]{1,0:T(8,128)(2,1)S(1)} %add_convert_fusion), channel_id=1, source_target_pairs={{0,8},{4,12},{8,16},{12,20},{16,24},{20,28},{24,0},{28,4},{1,9},{5... | collective-permute-start | bytes 3145736 | tf_op jit(solution)/shard_map/ppermute | solution.py:584
  (45 other events, 426.6 us)
Sparse Core Ops, SparseCore 0:
  19.2 67.6 all-gather.8
  89.3 57.1 all-gather.6
  148.5 54.3 all-gather.4
  204.6 54.3 all-gather.10
  348.8 71.7 reduce-scatter.4
  424.3 82.3 reduce-scatter.6
  510.2 77.6 reduce-scatter.8
  591.8 71.2 reduce-scatter.10

commit v3 on v2

--- a/solution.py
+++ b/solution.py
@@ -62,71 +62,89 @@
     return lax.dot_general(left, right, (((1,), (0,)), ((), ())), preferred_element_type=F32)
 
 
-def causal_fill(scores, first, fill):
-    keys, cols = scores.shape
-    key_ids = lax.broadcasted_iota(jnp.int32, (keys, cols), 0)
-    query_ids = lax.broadcasted_iota(jnp.int32, (keys, cols), 1) + first
-    return jnp.where(key_ids <= query_ids, scores, fill)
-
-
 def head_lanes(vals, head, head_dim):
     lane_ids = lax.broadcasted_iota(jnp.int32, vals.shape, 1)
     return jnp.where(lane_ids // head_dim == head, vals, jnp.zeros_like(vals))
+
+
+def seen_keys(block):
+    key_ids = lax.broadcasted_iota(jnp.int32, (block, block), 0)
+    return key_ids <= lax.broadcasted_iota(jnp.int32, (block, block), 1)
 
 
 def attend_kernel(head_dim, block, qkv_ref, cos_ref, low_ref, up_ref, rot_ref, attn_ref, lse_ref):
     length = qkv_ref.shape[0]
     scale = 1.0 / math.sqrt(head_dim)
     tables = (cos_ref[...], low_ref[...], up_ref[...])
-    queries = turn(qkv_ref[:, :LANES], *tables).astype(BF)
-    keys = turn(qkv_ref[:, LANES : 2 * LANES], *tables).astype(BF)
-    values = qkv_ref[:, 2 * LANES :].astype(BF)
-    rot_ref[:, :LANES] = queries
-    rot_ref[:, LANES : 2 * LANES] = keys
-    rot_ref[:, 2 * LANES :] = values
+    rot_ref[:, :LANES] = turn(qkv_ref[:, :LANES], *tables).astype(BF) * BF(scale)
+    rot_ref[:, LANES : 2 * LANES] = turn(qkv_ref[:, LANES : 2 * LANES], *tables).astype(BF)
+    rot_ref[:, 2 * LANES :] = qkv_ref[:, 2 * LANES :].astype(BF)
     heads = LANES // head_dim
+    seen = seen_keys(block)
     for first in range(0, length, block):
         last = first + block
         total = jnp.zeros((block, LANES), F32)
         for head in range(heads):
-            query_block = head_lanes(queries[first:last], head, head_dim)
-            scores = dot_cols(keys[:last], query_block) * scale
-            scores = causal_fill(scores, first, mask_fill)
+            query_block = head_lanes(rot_ref[first:last, :LANES], head, head_dim)
+            scores = jnp.where(seen, dot_cols(rot_ref[first:last, LANES : 2 * LANES], query_block), mask_fill)
             col_max = jnp.max(scores, axis=0, keepdims=True)
-            exp_scores = jnp.exp(scores - col_max)
-            denom = jnp.sum(exp_scores, axis=0, keepdims=True)
-            prob_low = (exp_scores * (1.0 / denom)).astype(BF)
-            total += dot_rows(prob_low, head_lanes(values[:last], head, head_dim))
+            if first:
+                before = dot_cols(rot_ref[:first, LANES : 2 * LANES], query_block)
+                col_max = jnp.maximum(col_max, jnp.max(before, axis=0, keepdims=True))
+            probs = jnp.exp(scores - col_max)
+            denom = jnp.sum(probs, axis=0, keepdims=True)
+            part = dot_rows(probs.astype(BF), head_lanes(rot_ref[first:last, 2 * LANES :], head, head_dim))
+            if first:
+                probs = jnp.exp(before - col_max)
+                denom += jnp.sum(probs, axis=0, keepdims=True)
+                part += dot_rows(probs.astype(BF), head_lanes(rot_ref[:first, 2 * LANES :], head, head_dim))
+            total += part * jnp.broadcast_to(1.0 / denom, (LANES, block)).T
             lse_ref[0, head : head + 1, first:last] = col_max + jnp.log(denom)
         attn_ref[first:last, :] = total.astype(BF)
 
 
-def attend_back_kernel(head_dim, block, rot_ref, grad_ref, lse_ref, cos_ref, low_ref, up_ref, out_ref, key_acc, value_acc):
+def attend_back_kernel(head_dim, block, rot_ref, grad_ref, attn_ref, lse_ref, cos_ref, low_ref, up_ref, out_ref, sum_ref, key_acc, value_acc):
     length = rot_ref.shape[0]
     scale = 1.0 / math.sqrt(head_dim)
-    tables = (cos_ref[...], -low_ref[...], -up_ref[...])
     heads = LANES // head_dim
+    seen = seen_keys(block)
+
+    def back(vals, span):
+        return turn(vals, cos_ref[span, :], -low_ref[span, :], -up_ref[span, :])
+
+    query_sum = jnp.zeros((1, LANES), F32)
     key_acc[...] = jnp.zeros_like(key_acc)
     value_acc[...] = jnp.zeros_like(value_acc)
     for first in range(0, length, block):
         last = first + block
         total = jnp.zeros((block, LANES), F32)
+        inner = (grad_ref[first:last, :].astype(F32) * attn_ref[first:last, :].astype(F32)).T
         for head in range(heads):
             query_block = head_lanes(rot_ref[first:last, :LANES], head, head_dim)
             grad_block = head_lanes(grad_ref[first:last, :], head, head_dim)
-            keys = rot_ref[:last, LANES : 2 * LANES]
-            scores = dot_cols(keys, query_block) * scale
-            probs = jnp.exp(scores - lse_ref[0, head : head + 1, first:last])
-            probs = causal_fill(probs, first, 0.0)
-            value_acc[:last, :] += dot_plain(probs.astype(BF), grad_block)
-            prob_grad = dot_cols(rot_ref[:last, 2 * LANES :], grad_block)
-            inner_sum = jnp.sum(probs * prob_grad, axis=0, keepdims=True)
-            score_grad = (probs * (prob_grad - inner_sum)).astype(BF)
-            total += dot_rows(score_grad, head_lanes(keys, head, head_dim))
-            key_acc[:last, :] += dot_plain(score_grad, query_block)
-        out_ref[first:last, :LANES] = turn(total * scale, *(table[first:last] for table in tables)).astype(BF)
-    out_ref[:, LANES : 2 * LANES] = turn(key_acc[...] * scale, *tables).astype(BF)
+            lse = lse_ref[0, head : head + 1, first:last]
+            inner_sum = jnp.sum(inner[head * head_dim : (head + 1) * head_dim], axis=0, keepdims=True)
+            for start, stop in ((0, first), (first, last)):
+                if start == stop:
+                    continue
+                keys = rot_ref[start:stop, LANES : 2 * LANES]
+                probs = jnp.exp(dot_cols(keys, query_block) - lse)
+                if start == first:
+                    probs = jnp.where(seen, probs, 0.0)
+                value_acc[start:stop, :] += dot_plain(probs.astype(BF), grad_block)
+                prob_grad = dot_cols(rot_ref[start:stop, 2 * LANES :], grad_block)
+                score_grad = (probs * (prob_grad - inner_sum)).astype(BF)
+                total += dot_rows(score_grad, head_lanes(keys, head, head_dim))
+                key_acc[start:stop, :] += dot_plain(score_grad, query_block)
+        turned = back(total * scale, slice(first, last))
+        query_sum += jnp.sum(turned, axis=0, keepdims=True)
+        out_ref[first:last, :LANES] = turned.astype(BF)
+    turned = back(key_acc[...], slice(0, length))
+    out_ref[:, LANES : 2 * LANES] = turned.astype(BF)
     out_ref[:, 2 * LANES :] = value_acc[...].astype(BF)
+    sum_ref[0:1, :LANES] = query_sum
+    sum_ref[0:1, LANES : 2 * LANES] = jnp.sum(turned, axis=0, keepdims=True)
+    sum_ref[0:1, 2 * LANES :] = jnp.sum(value_acc[...], axis=0, keepdims=True)
 
 
 def attention_cost(seqs, pairs, length, matmuls):
@@ -138,7 +156,7 @@
     tokens, width = qkv.shape
     seqs, pairs = tokens // length, width // (3 * LANES)
     heads = LANES // head_dim
-    block = min(256, length)
+    block = min(512, length)
     table_spec = pl.BlockSpec((length, LANES), lambda s, h: (0, 0))
     return pl.pallas_call(
         functools.partial(attend_kernel, head_dim, block),
@@ -159,11 +177,11 @@
     )(qkv, *tables)
 
 
-def attend_back(rot, attn_grad, lse, tables, length, head_dim):
+def attend_back(rot, attn_grad, attn, lse, tables, length, head_dim):
     tokens, width = rot.shape
     seqs, pairs = tokens // length, width // (3 * LANES)
     heads = LANES // head_dim
-    block = min(256, length)
+    block = min(512, length)
     table_spec = pl.BlockSpec((length, LANES), lambda s, h: (0, 0))
     return pl.pallas_call(
         functools.partial(attend_back_kernel, head_dim, block),
@@ -171,15 +189,19 @@
         in_specs=[
             pl.BlockSpec((length, 3 * LANES), lambda s, h: (s, h)),
             pl.BlockSpec((length, LANES), lambda s, h: (s, h)),
+            pl.BlockSpec((length, LANES), lambda s, h: (s, h)),
             pl.BlockSpec((1, heads, length), lambda s, h: (s * pairs + h, 0, 0)),
         ]
         + [table_spec] * 3,
-        out_specs=pl.BlockSpec((length, 3 * LANES), lambda s, h: (s, h)),
-        out_shape=jax.ShapeDtypeStruct((tokens, width), BF),
+        out_specs=[
+            pl.BlockSpec((length, 3 * LANES), lambda s, h: (s, h)),
+            pl.BlockSpec((8, 3 * LANES), lambda s, h: (s, h)),
+        ],
+        out_shape=[jax.ShapeDtypeStruct((tokens, width), BF), jax.ShapeDtypeStruct((8 * seqs, width), F32)],
         scratch_shapes=[pltpu.VMEM((length, LANES), F32), pltpu.VMEM((length, LANES), F32)],
         compiler_params=pltpu.CompilerParams(vmem_limit_bytes=VMEM_LIMIT),
         cost_estimate=attention_cost(seqs, pairs, length, 6),
-    )(rot, attn_grad, lse, *tables)
+    )(rot, attn_grad, attn, lse, *tables)
 
 
 def spec_rows(tile, width):
@@ -204,13 +226,12 @@
     return total
 
 
-def rows_call(kernel, slots, ins, in_specs, outs, tile, cost, out_specs=None):
-    tokens = outs[0].shape[0]
+def rows_call(kernel, slots, ins, in_specs, outs, tile, cost, out_specs=None, steps=None):
     return pl.pallas_call(
         kernel,
         grid_spec=pltpu.PrefetchScalarGridSpec(
             num_scalar_prefetch=1,
-            grid=(tokens // tile,),
+            grid=(steps or outs[0].shape[0] // tile,),
             in_specs=in_specs,
             out_specs=out_specs or [spec_rows(tile, out.shape[1]) for out in outs],
         ),
@@ -251,51 +272,85 @@
     )
 
 
+def micro_spec(micro, steps, tile, width):
+    return pl.BlockSpec((tile, width), lambda i, s: (jnp.clip(i - micro * steps, 0, steps - 1), 0))
+
+
 def up_act(slots, rows, parts, bias):
-    tokens, width = rows.shape
+    count = len(rows)
+    tokens, width = rows[0].shape
     cols, tile, chunk = bias.shape[1], 512, 512
-
-    def kernel(slots_ref, rows_ref, bias_ref, *refs):
-        parts, (act_ref, slope_ref) = refs[:-2], refs[-2:]
-        for at in range(0, cols, chunk):
-            span = slice(at, at + chunk)
-            pre = lined_dot(slots_ref, rows_ref, parts, span) + bias_ref[:, span]
-            square = pre * pre
-            tanh = jnp.tanh(gelu_factor * (pre * (1.0 + 0.044715 * square)))
-            half = 0.5 * (1.0 + tanh)
-            act_ref[:, span] = (pre * half).astype(BF)
-            inner = gelu_factor * (1.0 + 3 * 0.044715 * square)
-            slope_ref[:, span] = (half + 0.5 * pre * (1.0 - tanh * tanh) * inner).astype(BF)
+    steps = tokens // tile
+
+    def kernel(slots_ref, bias_ref, *refs):
+        ins, parts, outs = refs[:count], refs[count : -2 * count], refs[-2 * count :]
+        for micro in range(count):
+
+            @pl.when(pl.program_id(0) // steps == micro)
+            def _():
+                for at in range(0, cols, chunk):
+                    span = slice(at, at + chunk)
+                    pre = lined_dot(slots_ref, ins[micro], parts, span) + bias_ref[:, span]
+                    square = pre * pre
+                    tanh = jnp.tanh(gelu_factor * (pre * (1.0 + 0.044715 * square)))
+                    half = 0.5 * (1.0 + tanh)
+                    outs[micro][:, span] = (pre * half).astype(BF)
+                    inner = gelu_factor * (1.0 + 3 * 0.044715 * square)
+                    slope = half + 0.5 * pre * (1.0 - tanh * tanh) * inner
+                    outs[count + micro][:, span] = slope.astype(BF)
+
+    outs = rows_call(
+        kernel,
+        slots,
+        [bias, *rows, *parts],
+        [spec_whole(bias)]
+        + [micro_spec(m, steps, tile, width) for m in range(count)]
+        + [spec_whole(part) for part in parts],
+        [jax.ShapeDtypeStruct((tokens, cols), BF)] * (2 * count),
+        tile,
+        estimate(2 * count * tokens * width * cols, count * tokens * (2 * width + 4 * cols)),
+        [micro_spec(m, steps, tile, cols) for m in range(count)] * 2,
+        count * steps,
+    )
+    return outs[:count], outs[count:]
+
+
+def pre_grad_rows(slots, rows, parts, slopes):
+    count = len(rows)
+    tokens, width = rows[0].shape
+    cols, tile = slopes[0].shape[1], 512
+    steps = tokens // tile
+
+    def kernel(slots_ref, *refs):
+        ins, slopes, parts = refs[:count], refs[count : 2 * count], refs[2 * count : -count - 1]
+        outs, sum_ref = refs[-count - 1 : -1], refs[-1]
+
+        @pl.when(pl.program_id(0) == 0)
+        def _():
+            sum_ref[...] = jnp.zeros_like(sum_ref)
+
+        for micro in range(count):
+
+            @pl.when(pl.program_id(0) // steps == micro)
+            def _():
+                act_grad = lined_dot(slots_ref, ins[micro], parts, slice(0, cols))
+                grad = act_grad * slopes[micro][...].astype(F32)
+                outs[micro][...] = grad.astype(BF)
+                sum_ref[0:1, :] += jnp.sum(grad, axis=0, keepdims=True)
 
     return rows_call(
         kernel,
         slots,
-        [rows, bias, *parts],
-        [spec_rows(tile, width)] + [spec_whole(array) for array in (bias, *parts)],
-        [jax.ShapeDtypeStruct((tokens, cols), BF)] * 2,
+        [*rows, *slopes, *parts],
+        [micro_spec(m, steps, tile, width) for m in range(count)]
+        + [micro_spec(m, steps, tile, cols) for m in range(count)]
+        + [spec_whole(part) for part in parts],
+        [jax.ShapeDtypeStruct((tokens, cols), BF)] * count + [jax.ShapeDtypeStruct((8, cols), F32)],
         tile,
-        estimate(2 * tokens * width * cols, tokens * (2 * width + 4 * cols)),
+        estimate(2 * count * tokens * width * cols, count * tokens * (2 * width + 4 * cols)),
+        [micro_spec(m, steps, tile, cols) for m in range(count)] + [pl.BlockSpec((8, cols), lambda i, s: (0, 0))],
+        count * steps,
     )
-
-
-def pre_grad_rows(slots, rows, parts, slope):
-    tokens, width = rows.shape
-    cols, tile = slope.shape[1], 512
-
-    def kernel(slots_ref, rows_ref, slope_ref, *refs):
-        parts, out_ref = refs[:-1], refs[-1]
-        act_grad = lined_dot(slots_ref, rows_ref, parts, slice(0, cols))
-        out_ref[...] = (act_grad * slope_ref[...].astype(F32)).astype(BF)
-
-    return rows_call(
-        kernel,
-        slots,
-        [rows, slope, *parts],
-        [spec_rows(tile, width), spec_rows(tile, cols)] + [spec_whole(part) for part in parts],
-        [jax.ShapeDtypeStruct((tokens, cols), BF)],
-        tile,
-        estimate(2 * tokens * width * cols, tokens * (2 * width + 4 * cols)),
-    )[0]
 
 
 def head_grad_rows(slots, rows, parts, first):
@@ -317,28 +372,39 @@
     )[0]
 
 
-def branch_rows(slots, one, one_parts, first, two, two_parts):
-    tokens, cols = one.shape
-    count, depth, tile = len(one_parts), one_parts[0].shape[0], 512
-    width = count * depth
-
-    def kernel(slots_ref, one_ref, two_ref, *refs):
-        out_ref = refs[-1]
-        for at in range(count):
-            where = pl.multiple_of(slots_ref[at] * depth, depth)
-            total = dot_cols(one_ref[...], refs[at][:, first : first + cols])
-            total += dot_cols(two_ref[...], refs[count + at][...])
-            out_ref[:, pl.ds(where, depth)] = total.astype(BF)
+def branch_rows(slots, ones, one_parts, first, twos, two_parts, block):
+    micros = len(ones)
+    tokens, cols = ones[0].shape
+    count, depth = len(one_parts), one_parts[0].shape[0]
+    held = 2
+    tile = held * block
+    width, steps = count * depth, tokens // tile
+
+    def kernel(slots_ref, *refs):
+        ones, twos, out_ref = refs[:micros], refs[micros : 2 * micros], refs[-1]
+        parts = refs[2 * micros : -1]
+        for micro in range(micros):
+
+            @pl.when(pl.program_id(0) // steps == micro)
+            def _():
+                for at in range(count):
+                    where = pl.multiple_of(slots_ref[at] * depth, depth)
+                    total = dot_cols(ones[micro][...], parts[at][:, first : first + cols])
+                    total += dot_cols(twos[micro][...], parts[count + at][...])
+                    out_ref[:, 0, :, pl.ds(where, depth)] = total.astype(BF).reshape(held, block, depth)
 
     return rows_call(
         kernel,
         slots,
-        [one, two, *one_parts, *two_parts],
-        [spec_rows(tile, cols), spec_rows(tile, two.shape[1])]
+        [*ones, *twos, *one_parts, *two_parts],
+        [micro_spec(m, steps, tile, cols) for m in range(micros)]
+        + [micro_spec(m, steps, tile, twos[0].shape[1]) for m in range(micros)]
         + [spec_whole(part) for part in (*one_parts, *two_parts)],
-        [jax.ShapeDtypeStruct((tokens, width), BF)],
+        [jax.ShapeDtypeStruct((tokens // block, micros, block, width), BF)],
         tile,
-        estimate(2 * tokens * width * (cols + two.shape[1]), 2 * tokens * (width + cols + two.shape[1])),
+        estimate(2 * micros * tokens * width * (cols + twos[0].shape[1]), 2 * micros * tokens * (width + cols)),
+        [pl.BlockSpec((held, 1, block, width), lambda i, s: (lax.rem(i, steps), i // steps, 0, 0))],
+        micros * steps,
     )[0]
 
 
@@ -481,19 +547,6 @@
         upper = (at & bit) != 0
         return jnp.where(upper, jnp.concatenate([other, cur]), jnp.concatenate([cur, other]))
 
-    def sum_small(everywhere, over_fsdp):
-        cur = everywhere
-        bit = 1
-        while bit < tp_size:
-            cur = cur + lax.ppermute(cur, "tp", [(t, t ^ bit) for t in range(tp_size)])
-            bit *= 2
-        cur = jnp.concatenate([cur, over_fsdp])
-        bit = 1
-        while bit < fsdp_size:
-            cur = cur + lax.ppermute(cur, "fsdp", [(f, f ^ bit) for f in range(fsdp_size)])
-            bit *= 2
-        return cur[: everywhere.shape[0]], cur[everywhere.shape[0] :]
-
     small = jnp.concatenate(
         [vec.reshape(-1) for vec in (ln_gain, ln_bias, out_bias, down_bias, qkv_bias, up_bias)]
     )
@@ -600,6 +653,27 @@
             got = self.got.val.astype(F32)
             return jnp.where(pair_at == 0, self.keep, got), jnp.where(pair_at == 0, got, self.keep)
 
+    class SmallSum:
+        def __init__(self, everywhere, over_fsdp):
+            self.cur, self.rest = Box(everywhere), over_fsdp
+            self.size = everywhere.shape[0]
+            bits = [("tp", tp_size, bit) for bit in range(tp_size.bit_length() - 1)]
+            self.steps = bits + [("fsdp", fsdp_size, bit) for bit in range(fsdp_size.bit_length() - 1)]
+
+        def move(self):
+            if self.steps:
+                axis, size, bit = self.steps.pop(0)
+                if axis == "fsdp" and bit == 0:
+                    self.cur = Box(jnp.concatenate([self.cur.val, self.rest]))
+                order.tie(self.cur)
+                other = lax.ppermute(self.cur.val, axis, [(i, i ^ (1 << bit)) for i in range(size)])
+                self.cur = Box(self.cur.val + other)
+
+        def split(self):
+            while self.steps:
+                self.move()
+            return self.cur.val[: self.size], self.cur.val[self.size :]
+
     resid = [inputs[m].reshape(token_rows, model_width) for m in range(micro_count)]
     cots = [cotangent[m].reshape(token_rows, model_width) for m in range(micro_count)]
     micros = range(micro_count)
@@ -627,6 +701,8 @@
     small_all = small_step(small_all, 0)
     attn_ring.sync()
     order.sync(small_all)
+    bias_total = Box(sum(jnp.sum(cots[m].astype(F32), axis=0) for m in micros))
+    order.sync(bias_total)
     up_send = Box(up_half(1 - pair_at))
     order.tie(up_send)
     up_shard = Box(pair_join(up_half(pair_at), swap_pair(up_send.val)))
@@ -667,7 +743,7 @@
     tables = rotary_tables(length, head_dim, ROT)
     gain_row, shift_row = gain_vec[None], shift_vec[None]
     normed, qkvs, stats, rots, attns, lses, acts, slopes = ([None] * micro_count for _ in range(8))
-    pre_grads, qkv_grads, back, sums, branches, attn_heads = ([None] * micro_count for _ in range(6))
+    pre_grads, qkv_grads, qkv_sums, back, sums, attn_heads = ([None] * micro_count for _ in range(6))
 
     def norm_piece(m):
         normed[m], qkvs[m], stats[m] = order.run(
@@ -679,8 +755,12 @@
             lambda vals: attend(vals, tables, length, head_dim), qkvs[m]
         )
 
-    def up_piece(m):
-        acts[m], slopes[m] = order.run(lambda rows: up_act(slots, rows, up_ring.vals(), up_b), normed[m])
+    def up_piece():
+        def piece(*rows):
+            return [val for vals in up_act(slots, rows, up_ring.vals(), up_b) for val in vals]
+
+        results = order.run(piece, *normed)
+        acts[:], slopes[:] = results[:micro_count], results[micro_count:]
 
     def head_grad_piece(m):
         (attn_heads[m],) = order.run(
@@ -688,17 +768,20 @@
         )
 
     def attend_back_piece(m):
-        (qkv_grads[m],) = order.run(
-            lambda rot, grad, lse: [attend_back(rot, grad, lse, tables, length, head_dim)],
+        qkv_grads[m], qkv_sums[m] = order.run(
+            lambda rot, grad, attn, lse: attend_back(rot, grad, attn, lse, tables, length, head_dim),
             rots[m],
             attn_heads[m],
+            attns[m],
             lses[m],
         )
 
-    def pre_grad_piece(m):
-        (pre_grads[m],) = order.run(
-            lambda cot, slope: [pre_grad_rows(slots, cot, down_ring.vals(), slope)], plane_cots[m], slopes[m]
-        )
+    def pre_grad_piece():
+        def piece(*vals):
+            return pre_grad_rows(slots, vals[:micro_count], down_ring.vals(), vals[micro_count:])
+
+        *pre_grads[:], up_sums = order.run(piece, *plane_cots, *slopes)
+        return up_sums
 
     def weight_piece(*groups):
         flat = [box for lefts, rights in groups for box in (*lefts, *rights)]
@@ -716,12 +799,20 @@
 
         return Scatter(order.run(piece, *flat)[0])
 
-    def branch_piece(m):
-        (branches[m],) = order.run(
-            lambda attn, act: [branch_rows(slots, attn, attn_ring.vals(), qkv_cols, act, down_ring.vals())],
-            attns[m],
-            acts[m],
-        )
+    def branch_piece():
+        def piece(*vals):
+            rows = branch_rows(
+                slots,
+                vals[:micro_count],
+                attn_ring.vals(),
+                qkv_cols,
+                vals[micro_count:],
+                down_ring.vals(),
+                token_rows,
+            )
+            return [rows.reshape(-1, model_width)]
+
+        return order.run(piece, *attns, *acts)[0]
 
     def normed_grad_piece(m):
         back[m], sums[m] = order.run(
@@ -753,68 +844,49 @@
     head_grad_piece(0)
     up_ring.finish()
     down_ring.move()
-    up_piece(0)
-    down_ring.sync()
-    down_ring.move()
-    up_piece(1)
+    up_piece()
     down_ring.sync()
     down_ring.move()
     attend_back_piece(0)
+    down_ring.sync()
+    down_ring.move()
+
+    down_scatter = weight_piece((plane_cots, acts))
     down_ring.finish()
-
-    down_scatter = weight_piece((plane_cots, acts))
     down_scatter.move()
-    pre_grad_piece(0)
-    branch_piece(0)
+    branch = branch_piece()
     down_scatter.sync()
-    branch_sums = [scatter_behind(branches[0])]
+    branch_sum = scatter_behind(branch)
     down_scatter.move()
-    pre_grad_piece(1)
-    branch_piece(1)
+    up_sums = pre_grad_piece()
     down_scatter.sync()
-    branch_sums.append(scatter_behind(branches[1]))
     down_scatter.move()
     up_scatter = weight_piece((normed, pre_grads))
     down_scatter.sync()
-    order.sync(branch_sums[0])
     down_scatter.swap()
     up_scatter.move()
-    head_grad_piece(1)
     normed_grad_piece(0)
     up_scatter.sync()
+    order.sync(down_scatter.got)
     back_sums = [scatter_behind(back[0])]
     up_scatter.move()
+    head_grad_piece(1)
     attend_back_piece(1)
     up_scatter.sync()
-    order.sync(down_scatter.got)
     up_scatter.move()
     attn_scatter = weight_piece((normed, qkv_grads), (plane_cots, attns))
     up_scatter.sync()
-    order.sync(branch_sums[1])
+    order.sync(branch_sum)
     up_scatter.swap()
     attn_scatter.move()
     normed_grad_piece(1)
     attn_scatter.sync()
+    order.sync(up_scatter.got)
     back_sums.append(scatter_behind(back[1]))
+
     attn_scatter.move()
-    order.sync(up_scatter.got)
-    attn_scatter.sync()
-    attn_scatter.move()
-    attn_scatter.swap()
-    attn_grads, up_grads, down_grads = attn_scatter.halves(), up_scatter.halves(), down_scatter.halves()
-
-    outputs, input_grads = [], []
-    bias_total = jnp.zeros((model_width,), F32)
-    for m in micros:
-        outputs.append((resid[m].astype(F32) + branch_sums[m].val.astype(F32) + bias_both).astype(BF))
-        vals, cot = resid[m].astype(F32), cots[m].astype(F32)
-        pull_back = jax.vjp(lambda vals: layer_norm(vals, gain_vec, shift_vec), vals)[1]
-        input_grads.append((cot + pull_back(back_sums[m].val.astype(F32))[0]).astype(BF))
-        bias_total += jnp.sum(cot, axis=0)
-    gain_total, shift_total = (sum(part.val[i] for part in sums) for i in range(2))
-
-    up_b_grad = sum(jnp.sum(pre_grads[m].val.astype(F32), axis=0) for m in micros)
-    qkv_b_grad = sum(jnp.sum(qkv_grads[m].val.astype(F32), axis=0) for m in micros)
+    up_b_grad = up_sums.val[0]
+    qkv_b_grad = sum(jnp.sum(part.val.reshape(-1, 8, qkv_cols)[:, 0], axis=0) for part in qkv_sums)
     qkv_b_grad = qkv_b_grad.reshape(pairs, 3, -1).transpose(1, 0, 2).reshape(3, attn_cols)
 
     def in_half(vals):
@@ -823,10 +895,36 @@
             pair_at == 0, jnp.concatenate([vals, blank], axis=-1), jnp.concatenate([blank, vals], axis=-1)
         )
 
-    small_sums, bias_sums = sum_small(
-        jnp.concatenate([gain_total, shift_total, bias_total]),
+    gain_total, shift_total = (sum(part.val[i] for part in sums) for i in range(2))
+    tail = SmallSum(
+        jnp.concatenate([gain_total, shift_total, bias_total.val]),
         jnp.concatenate([in_half(up_b_grad), in_half(qkv_b_grad).reshape(-1)]),
     )
+    tail.move()
+    tail.move()
+    attn_scatter.sync()
+    attn_scatter.move()
+    tail.move()
+    down_w_grad = Box(jnp.concatenate([half.T for half in down_scatter.halves()], axis=0))
+    up_w_grad = Box(jnp.concatenate(up_scatter.halves(), axis=1))
+    order.sync(down_w_grad)
+    order.sync(up_w_grad)
+    attn_scatter.sync()
+    attn_scatter.swap()
+    tail.move()
+    tail.move()
+    order.sync(tail.cur)
+    small_sums, bias_sums = tail.split()
+    attn_grads = attn_scatter.halves()
+
+    outputs, input_grads = [], []
+    for m in micros:
+        outputs.append((resid[m].astype(F32) + branch_sum.val.reshape(micro_count, token_rows, -1)[m].astype(F32) + bias_both).astype(BF))
+        order.tie(back_sums[m])
+        vals, cot = resid[m].astype(F32), cots[m].astype(F32)
+        pull_back = jax.vjp(lambda vals: layer_norm(vals, gain_vec, shift_vec), vals)[1]
+        input_grads.append((cot + pull_back(back_sums[m].val.astype(F32))[0]).astype(BF))
+
     small_sums = small_sums.reshape(3, fsdp_size * tp_size, vec_size)
     small_sums = lax.dynamic_slice_in_dim(small_sums, fsdp_at * tp_size + tp_at, 1, axis=1)[:, 0]
     gain_sum, shift_sum, bias_sum = small_sums[0], small_sums[1], small_sums[2]
@@ -842,8 +940,6 @@
 
     qkv_w_grad = jnp.concatenate([qkv_columns(half) for half in attn_grads], axis=2)
     out_w_grad = jnp.concatenate([half[:, qkv_cols:].T for half in attn_grads], axis=0)
-    up_w_grad = jnp.concatenate(up_grads, axis=1)
-    down_w_grad = jnp.concatenate([half.T for half in down_grads], axis=0)
     return (
         jnp.stack(outputs, axis=0)[:, None],
         jnp.stack(input_grads, axis=0)[:, None],
@@ -853,9 +949,9 @@
         qkv_b_sum,
         out_w_grad,
         bias_sum,
-        up_w_grad,
+        up_w_grad.val,
         up_b_sum,
-        down_w_grad,
+        down_w_grad.val,
         bias_sum,
     )
 

time: 716 us -> 655 us (0.915)
  waiting for transfers between devices: 178 us -> 129 us
  Pallas kernels: 371 us -> 350 us
  local copies, waits for them, and re-layouts: 48.6 us -> 60.2 us
    reduce_scatter x4 -> x3, waiting for transfers between devices: 45.4 us -> 10.5 us  [scatter_plane(): lax.psum_scatter(vals, both_axes, scatter_dimension=0, tiled=True, axis_i...]
    pallas_call x12 -> x9, Pallas kernels: 210 us -> 196 us  [rows_call(): pl.pallas_call(kernel, grid_spec=pltpu.PrefetchScalarGridSpec(num_scalar_...]
    ppermute x9, waiting for transfers between devices: 33.7 us -> 22.6 us  [move(): self.parts.append(Box(lax.ppermute(self.parts[-1].val, 'fsdp', ring)))]
    ppermute x9, waiting for transfers between devices: 36 us -> 25.4 us  [move(): came = lax.ppermute(self.moving.val, 'fsdp', ring).astype(F32) + self.own()]
    reduce_sum x3, other arithmetic: 12.9 us -> 3.75 us  [the longest x1 1.92 us: shards(): jnp.sum(cots[m].astype(F32), axis=0)]
    unnamed x83 -> x81, local copies, waits for them, and re-layouts: 15.3 us -> 22.2 us
  transfers between devices with their start and end apart: 42 -> 41, of which waited for: 18 -> 18; matrix products, arithmetic and copies ran while one was open for 12% -> 12% of each run, Pallas kernels for 49% -> 54%
where the time goes in v3:
time: 655 us; the launch traced here: 647 us
  Pallas kernels  350 us (53%)
  waiting for transfers between devices  129 us (20%)
  local copies, waits for them, and re-layouts  60.2 us (9%)
  other arithmetic  49.7 us (8%)
  starting transfers between devices  43.2 us (7%)
  between operations  15.4 us (2%)
    pallas_call x9, Pallas kernels, rows_call(): pl.pallas_call(kernel, grid_spec=pltpu.PrefetchScalarGridSpec(num_scalar_...  196 us
    pallas_call x3, Pallas kernels, weight_grad(): pl.pallas_call(kernel, grid=(micro_count * steps,), in_specs=in_specs, ou...  79.1 us
    pallas_call x2, Pallas kernels, attend_back(): pl.pallas_call(functools.partial(attend_back_kernel, head_dim, block), gr...  42.4 us
    pallas_call x2, Pallas kernels, attend(): pl.pallas_call(functools.partial(attend_kernel, head_dim, block), grid=(s...  32.6 us
    ppermute x5, waiting for transfers between devices, doubled(): other = lax.ppermute(cur, axis, [(i, i ^ bit) for i in range(size)])  31.6 us
    ppermute x6, waiting for transfers between devices, swap_pair(): return lax.ppermute(vals, 'fsdp', [(f, f ^ 1) for f in range(fsdp_size)])  30.8 us
    ppermute x9, waiting for transfers between devices, move(): came = lax.ppermute(self.moving.val, 'fsdp', ring).astype(F32) + self.own()  25.4 us
    ppermute x9, waiting for transfers between devices, move(): self.parts.append(Box(lax.ppermute(self.parts[-1].val, 'fsdp', ring)))  22.6 us
  transfers between devices with their start and end apart: 41, of which 18 were waited for; matrix products, arithmetic and copies ran while one was open for 12% of the time, Pallas kernels for 54%

profile of v3, /device:TPU:0, one launch (start us, length us, event | category | flops | bytes accessed | tf_op | source)
XLA Modules:
  0.0 647.5 jit_solution(16915644416313548718)
XLA Ops:
  15.9 3.1 slice_bitcast_fusion.1
  21.9 16.5 %collective-permute-done.2 = bf16[256,1024]{1,0:T(8,128)(2,1)S(1)} collective-permute-done((bf16[256,1024]{1,0:T(8,128)(2,1)S(1)}, bf16[256,1024]{1,0:T(8,128)(2,1)S(1)}, u32[]{:S(2)}, u32[]{:S(2)}) %collective-permute-start.2) | collective-permute-done | bytes 524320 | tf_op jit(solution)/shard_map/ppermute | solution.py:534
  46.5 16.5 %collective-permute-done.3.refs_1_.refs_5_ = bf16[512,1024]{1,0:T(8,128)(2,1)S(1)} collective-permute-done((bf16[512,1024]{1,0:T(8,128)(2,1)S(1)}, bf16[512,1024]{1,0:T(8,128)(2,1)S(1)}, u32[]{:S(2)}, u32[]{:S(2)}) %collective-permute-start.3) | collective-permute-done | bytes 1048608 | tf_op jit(solution)/shard_map/ppermute | solution.py:611
  67.8 3.2 slice_bitcast_fusion
  70.9 11.8 %collective-permute-done.6 = bf16[8,704]{1,0:T(8,128)(2,1)S(1)} collective-permute-done((bf16[8,704]{1,0:T(8,128)(2,1)S(1)}, bf16[8,704]{1,0:T(8,128)(2,1)S(1)}, u32[]{:S(2)}, u32[]{:S(2)}) %collective-permute-start.6) | collective-permute-done | bytes 11296 | tf_op jit(solution)/shard_map/ppermute | solution.py:546
  82.7 3.9 collective-permute-done.7
  99.8 18.4 %collective-permute-done.9 = bf16[16,704]{1,0:T(8,128)(2,1)S(1)} collective-permute-done((bf16[16,704]{1,0:T(8,128)(2,1)S(1)}, bf16[16,704]{1,0:T(8,128)(2,1)S(1)}, u32[]{:S(2)}, u32[]{:S(2)}) %collective-permute-start.9) | collective-permute-done | bytes 22560 | tf_op jit(solution)/shard_map/ppermute | solution.py:546
  124.6 20.3 %shard_map.211 = (bf16[2048,2048]{1,0:T(8,128)(2,1)}, f32[2048,768]{1,0:T(8,128)}, f32[2048,128]{1,0:T(8,128)}) custom-call(s32[4]{0:T(128)} %pad_add_fusion.slots_ref, bf16[2048,2048]{1,0:T(8,128)(2,1)} %all-gather.5.cloned.1.call-done.rows_ref, f32[1,2048]{1,0:T(1,128)} %reshape.284.gain_ref, f32[1,2048]{1,0:T(1,128)} %reshape.285.shift_ref, ...), custom_call_target="tpu_custom_call" | custom-call | flops 100663296 | bytes 360448 | tf_op jit(solution)/shard_map/pallas_call | solution.py:230
  144.9 3.3 collective-permute-done.11.refs_3_.refs_5_
  152.6 16.3 %shard_map.212 = (bf16[2048,768]{1,0:T(8,128)(2,1)}, bf16[2048,256]{1,0:T(8,128)(2,1)}, f32[4,2,1024]{2,1,0:T(2,128)}) custom-call(f32[2048,768]{1,0:T(8,128)} %get-tuple-element.308.qkv_ref, f32[1024,128]{1,0:T(8,128)} %copy.78.cos_ref, f32[1024,128]{1,0:T(8,128)} %copy.79.low_ref, f32[1024,128]{1,0:T(8,128)} %copy.80.up_ref), custom_call_target="tpu_custom_call" | custom-call | flops 100663296 | bytes 131072 | tf_op jit(solution)/shard_map/pallas_call | solution.py:161
  168.9 20.4 %shard_map.213 = (bf16[2048,2048]{1,0:T(8,128)(2,1)}, f32[2048,768]{1,0:T(8,128)}, f32[2048,128]{1,0:T(8,128)}) custom-call(s32[4]{0:T(128)} %pad_add_fusion.slots_ref, bf16[2048,2048]{1,0:T(8,128)(2,1)} %all-gather.7.cloned.1.call-done.rows_ref, f32[1,2048]{1,0:T(1,128)} %reshape.284.gain_ref, f32[1,2048]{1,0:T(1,128)} %reshape.285.shift_ref, ...), custom_call_target="tpu_custom_call" | custom-call | flops 100663296 | bytes 360448 | tf_op jit(solution)/shard_map/pallas_call | solution.py:230
  189.6 16.3 %shard_map.214 = (bf16[2048,768]{1,0:T(8,128)(2,1)}, bf16[2048,256]{1,0:T(8,128)(2,1)}, f32[4,2,1024]{2,1,0:T(2,128)}) custom-call(f32[2048,768]{1,0:T(8,128)} %get-tuple-element.318.qkv_ref, f32[1024,128]{1,0:T(8,128)} %copy.78.cos_ref, f32[1024,128]{1,0:T(8,128)} %copy.79.low_ref, f32[1024,128]{1,0:T(8,128)} %copy.80.up_ref), custom_call_target="tpu_custom_call" | custom-call | flops 100663296 | bytes 131072 | tf_op jit(solution)/shard_map/pallas_call | solution.py:161
  206.0 7.8 %shard_map.215.grad_ref = bf16[2048,256]{1,0:T(8,128)(2,1)} custom-call(s32[4]{0:T(128)} %pad_add_fusion.slots_ref, bf16[2048,2048]{1,0:T(8,128)(2,1)} %all-gather.9.cloned.1.call-done.rows_ref.refs_0_.refs_4_, bf16[512,1024]{1,0:T(8,128)(2,1)} %copy-done, bf16[512,1024]{1,0:T(8,128)(2,1)} %copy-done.2, bf16[512,1024]{1,0:T(8,128)(2,1)} %copy-done.3, ...), custom_call_target="tpu_custom_call" | custom-call | flops 33554432 | bytes 147456 | tf_op jit(solution)/shard_map/pallas_call | solution.py:230
  216.6 34.6 %shard_map.216 = (bf16[2048,1024]{1,0:T(8,128)(2,1)}, bf16[2048,1024]{1,0:T(8,128)(2,1)}, bf16[2048,1024]{1,0:T(8,128)(2,1)}, bf16[2048,1024]{1,0:T(8,128)(2,1)}) custom-call(s32[4]{0:T(128)} %pad_add_fusion.slots_ref, f32[1,1024]{1,0:T(1,128)} %constant_dynamic-slice_fusion.8.bias_ref, bf16[2048,2048]{1,0:T(8,128)(2,1)} %get-tuple-element.409.refs_0_, ...), custom_call_target="tpu_custom_call" | custom-call | flops 268435456 | bytes 524288 | tf_op jit(solution)/shard_map/pallas_call | solution.py:230
  251.1 3.4 collective-permute-start.15
  254.6 21.0 %shard_map.217 = (bf16[2048,768]{1,0:T(8,128)(2,1)}, f32[16,768]{1,0:T(8,128)}) custom-call(bf16[2048,768]{1,0:T(8,128)(2,1)} %get-tuple-element.342.rot_ref, bf16[2048,256]{1,0:T(8,128)(2,1)} %shard_map.215.grad_ref, bf16[2048,256]{1,0:T(8,128)(2,1)} %get-tuple-element.414.attn_ref.refs_0_.refs_6_, f32[4,2,1024]{2,1,0:T(2,128)} %get-tuple-element.344.lse_ref, ...), custom_call_target="tpu_custom_call" | custom-call | flops 201326592 | bytes 131072 | tf_op jit(solution)/shard_map/pallas_call | solution.py:186
  278.0 25.4 %shard_map.218 = bf16[2048,1024]{1,0:T(8,128)(2,1)} custom-call(bf16[2048,2048]{1,0:T(8,128)(2,1)} %all-gather.9.cloned.1.call-done.rows_ref.refs_0_.refs_4_, bf16[2048,2048]{1,0:T(8,128)(2,1)} %all-gather.11.cloned.1.call-done.refs_1_.rows_ref.refs_5_, bf16[2048,1024]{1,0:T(8,128)(2,1)} %get-tuple-element.356.refs_2_, ...), custom_call_target="tpu_custom_call" | custom-call | flops 268435456 | bytes 393216 | tf_op jit(solution)/shard_map/pallas_call | solution.py:487
  305.6 30.2 %shard_map.219 = bf16[8,2,256,2048]{3,2,1,0:T(8,128)(2,1)} custom-call(s32[4]{0:T(128)} %pad_add_fusion.slots_ref, bf16[2048,256]{1,0:T(8,128)(2,1)} %get-tuple-element.414.attn_ref.refs_0_.refs_6_, bf16[2048,256]{1,0:T(8,128)(2,1)} %get-tuple-element.415.refs_1_.attn_ref.refs_7_, bf16[2048,1024]{1,0:T(8,128)(2,1)} %get-tuple-element.356.refs_2_, ...), custom_call_target="tpu_custom_call" | custom-call | flops 335544320 | bytes 294912 | tf_op jit(solution)/shard_map/pallas_call | solution.py:230
  338.9 27.0 %shard_map.220 = (bf16[2048,1024]{1,0:T(8,128)(2,1)}, bf16[2048,1024]{1,0:T(8,128)(2,1)}, f32[8,1024]{1,0:T(8,128)}) custom-call(s32[4]{0:T(128)} %pad_add_fusion.slots_ref, bf16[2048,2048]{1,0:T(8,128)(2,1)} %all-gather.9.cloned.1.call-done.rows_ref.refs_0_.refs_4_, bf16[2048,2048]{1,0:T(8,128)(2,1)} %all-gather.11.cloned.1.call-done.refs_1_.rows_ref.refs_5_, ...), custom_call_target="tpu_custom_call" | custom-call | flops 268435456 | bytes 524288 | tf_op jit(solution)/shard_map/pallas_call | solution.py:230
  369.8 25.3 %shard_map.221 = bf16[2048,1024]{1,0:T(8,128)(2,1)} custom-call(bf16[2048,2048]{1,0:T(8,128)(2,1)} %get-tuple-element.409.refs_0_, bf16[2048,2048]{1,0:T(8,128)(2,1)} %get-tuple-element.410.refs_1_, bf16[2048,1024]{1,0:T(8,128)(2,1)} %get-tuple-element.386.refs_2_.two_ref, bf16[2048,1024]{1,0:T(8,128)(2,1)} %get-tuple-element.424.refs_3_.two_ref), custom_call_target="tpu_custom_call" | custom-call | flops 268435456 | bytes 393216 | tf_op jit(solution)/shard_map/pallas_call | solution.py:487
  400.9 24.3 %shard_map.222 = (bf16[2048,2048]{1,0:T(8,128)(2,1)}, f32[8,2048]{1,0:T(8,128)}) custom-call(s32[4]{0:T(128)} %pad_add_fusion.slots_ref, bf16[2048,768]{1,0:T(8,128)(2,1)} %get-tuple-element.411.one_ref.refs_2_, bf16[2048,1024]{1,0:T(8,128)(2,1)} %get-tuple-element.386.refs_2_.two_ref, bf16[2048,2048]{1,0:T(8,128)(2,1)} %all-gather.5.cloned.1.call-done.rows_ref, ...), custom_call_target="tpu_custom_call" | custom-call | flops 234881024 | bytes 376832 | tf_op jit(solution)/shard_map/pallas_call | solution.py:230
  428.7 7.6 %shard_map.223.grad_ref = bf16[2048,256]{1,0:T(8,128)(2,1)} custom-call(s32[4]{0:T(128)} %pad_add_fusion.slots_ref, bf16[2048,2048]{1,0:T(8,128)(2,1)} %all-gather.11.cloned.1.call-done.refs_1_.rows_ref.refs_5_, bf16[512,1024]{1,0:T(8,128)(2,1)} %copy-done, bf16[512,1024]{1,0:T(8,128)(2,1)} %copy-done.2, bf16[512,1024]{1,0:T(8,128)(2,1)} %copy-done.3, ...), custom_call_target="tpu_custom_call" | custom-call | flops 33554432 | bytes 147456 | tf_op jit(solution)/shard_map/pallas_call | solution.py:230
  436.3 21.4 %shard_map.224 = (bf16[2048,768]{1,0:T(8,128)(2,1)}, f32[16,768]{1,0:T(8,128)}) custom-call(bf16[2048,768]{1,0:T(8,128)(2,1)} %get-tuple-element.400.rot_ref, bf16[2048,256]{1,0:T(8,128)(2,1)} %shard_map.223.grad_ref, bf16[2048,256]{1,0:T(8,128)(2,1)} %get-tuple-element.415.refs_1_.attn_ref.refs_7_, f32[4,2,1024]{2,1,0:T(2,128)} %get-tuple-element.403.lse_ref, ...), custom_call_target="tpu_custom_call" | custom-call | flops 201326592 | bytes 131072 | tf_op jit(solution)/shard_map/pallas_call | solution.py:186
  458.7 28.4 %shard_map.225 = bf16[2048,1024]{1,0:T(8,128)(2,1)} custom-call(bf16[2048,2048]{1,0:T(8,128)(2,1)} %get-tuple-element.409.refs_0_, bf16[2048,2048]{1,0:T(8,128)(2,1)} %get-tuple-element.410.refs_1_, bf16[2048,768]{1,0:T(8,128)(2,1)} %get-tuple-element.411.one_ref.refs_2_, bf16[2048,768]{1,0:T(8,128)(2,1)} %get-tuple-element.423.refs_3_.one_ref, ...), custom_call_target="tpu_custom_call" | custom-call | flops 268435456 | bytes 655360 | tf_op jit(solution)/shard_map/pallas_call | solution.py:487
  493.2 24.1 %shard_map.226 = (bf16[2048,2048]{1,0:T(8,128)(2,1)}, f32[8,2048]{1,0:T(8,128)}) custom-call(s32[4]{0:T(128)} %pad_add_fusion.slots_ref, bf16[2048,768]{1,0:T(8,128)(2,1)} %get-tuple-element.423.refs_3_.one_ref, bf16[2048,1024]{1,0:T(8,128)(2,1)} %get-tuple-element.424.refs_3_.two_ref, bf16[2048,2048]{1,0:T(8,128)(2,1)} %all-gather.7.cloned.1.call-done.rows_ref, ...), custom_call_target="tpu_custom_call" | custom-call | flops 234881024 | bytes 376832 | tf_op jit(solution)/shard_map/pallas_call | solution.py:230
  529.8 15.6 %collective-permute-done.28 = bf16[512,1024]{1,0:T(8,128)(2,1)} collective-permute-done((bf16[512,1024]{1,0:T(8,128)(2,1)}, bf16[512,1024]{1,0:T(8,128)(2,1)}, u32[]{:S(2)}, u32[]{:S(2)}) %collective-permute-start.28) | collective-permute-done | bytes 1048608 | tf_op jit(solution)/shard_map/ppermute | solution.py:637
  559.3 9.8 %collective-permute-done.30 = bf16[512,1024]{1,0:T(8,128)(2,1)} collective-permute-done((bf16[512,1024]{1,0:T(8,128)(2,1)}, bf16[512,1024]{1,0:T(8,128)(2,1)}, u32[]{:S(2)}, u32[]{:S(2)}) %collective-permute-start.30) | collective-permute-done | bytes 1048608 | tf_op jit(solution)/shard_map/ppermute | solution.py:637
  575.3 4.7 collective-permute-done.32
  582.3 10.4 %collective-permute-done.33 = bf16[256,1024]{1,0:T(8,128)(2,1)} collective-permute-done((bf16[256,1024]{1,0:T(8,128)(2,1)S(1)}, bf16[256,1024]{1,0:T(8,128)(2,1)}, u32[]{:S(2)}, u32[]{:S(2)}) %collective-permute-start.33) | collective-permute-done | bytes 524320 | tf_op jit(solution)/shard_map/ppermute | solution.py:534
  605.5 3.0 copy.97
  613.6 10.5 %reduce-scatter.8.cloned.1.call-done = bf16[256,2048]{1,0:T(8,128)(2,1)} async-done(((bf16[2048,2048]{1,0:T(8,128)(2,1)}), bf16[256,2048]{1,0:T(8,128)(2,1)}) %reduce-scatter.8.cloned.1.call-update) | async-done | bytes 1048592 | tf_op jit(solution)/shard_map/reduce_scatter | solution.py:540
  632.6 3.3 fusion.23
  (277 shorter events, 144.4 us)
Async XLA Ops:
  7.2 117.4 %all-gather.5.cloned.1.call-start = ((), (), s32[]{:S(2)}) async-start(), calls=%async_computation.3 | async-start | bytes 9437184 | tf_op jit(solution)/shard_map/all_gather | solution.py:537
  19.1 149.8 %all-gather.7.cloned.1.call-start = ((), (), s32[]{:S(2)}) async-start(), calls=%async_computation.4 | async-start | bytes 9437184 | tf_op jit(solution)/shard_map/all_gather | solution.py:537
  38.8 167.1 %all-gather.9.cloned.1.call-start = ((), (), s32[]{:S(2)}) async-start(), calls=%async_computation.5 | async-start | bytes 9437184 | tf_op jit(solution)/shard_map/all_gather | solution.py:537
  38.9 24.1 %collective-permute-start.3 = (bf16[512,1024]{1,0:T(8,128)(2,1)S(1)}, bf16[512,1024]{1,0:T(8,128)(2,1)S(1)}, u32[]{:S(2)}, u32[]{:S(2)}) collective-permute-start(bf16[512,1024]{1,0:T(8,128)(2,1)S(1)} %maximum_select_fusion.refs_0_.refs_4_), channel_id=1, source_target_pairs={{0,8},{4,12},{8,16},{12,20},{16,24},{20,28},{24,0},{28,4},{1,9},{5... | collective-permute-start | bytes 3145736 | tf_op jit(solution)/shard_map/ppermute | solution.py:611
  63.0 26.4 %collective-permute-start.5 = (bf16[512,1024]{1,0:T(8,128)(2,1)S(1)}, bf16[512,1024]{1,0:T(8,128)(2,1)S(1)}, u32[]{:S(2)}, u32[]{:S(2)}) collective-permute-start(bf16[512,1024]{1,0:T(8,128)(2,1)S(1)} %collective-permute-done.3.refs_1_.refs_5_), channel_id=1, source_target_pairs={{0,8},{4,12},{8,16},{12,20},{16,24},{20,28},{24,0},{28,4},{1,9},{5... | collective-permute-start | bytes 3145736 | tf_op jit(solution)/shard_map/ppermute | solution.py:611
  63.0 19.7 %collective-permute-start.6 = (bf16[8,704]{1,0:T(8,128)(2,1)S(1)}, bf16[8,704]{1,0:T(8,128)(2,1)S(1)}, u32[]{:S(2)}, u32[]{:S(2)}) collective-permute-start(bf16[8,704]{1,0:T(8,128)(2,1)S(1)} %maximum_select_fusion.5), channel_id=1, source_target_pairs={{0,8},{4,12},{8,0},{12,4},{16,24},{20,28},{24,16},{28,20},{1,9},{5... | collective-permute-start | bytes 33800 | tf_op jit(solution)/shard_map/ppermute | solution.py:546
  65.3 21.3 %collective-permute-start.7 = (bf16[256,1024]{1,0:T(8,128)(2,1)}, bf16[256,1024]{1,0:T(8,128)(2,1)S(1)}, u32[]{:S(2)}, u32[]{:S(2)}) collective-permute-start(bf16[256,1024]{1,0:T(8,128)(2,1)} %get-tuple-element.255), channel_id=1, source_target_pairs={{0,4},{4,0},{8,12},{12,8},{16,20},{20,16},{24,28},{28,24},{1,5},{5... | collective-permute-start | bytes 1572872 | tf_op jit(solution)/shard_map/ppermute | solution.py:534
  89.4 188.5 %all-gather.11.cloned.1.call-start = ((), (), s32[]{:S(2)}) async-start(), calls=%async_computation.6 | async-start | bytes 9437184 | tf_op jit(solution)/shard_map/all_gather | solution.py:537
  93.2 28.0 %collective-permute-start.8 = (bf16[512,1024]{1,0:T(8,128)(2,1)S(1)}, bf16[512,1024]{1,0:T(8,128)(2,1)S(1)}, u32[]{:S(2)}, u32[]{:S(2)}) collective-permute-start(bf16[512,1024]{1,0:T(8,128)(2,1)S(1)} %collective-permute-done.5.refs_2_.refs_6_), channel_id=1, source_target_pairs={{0,8},{4,12},{8,16},{12,20},{16,24},{20,28},{24,0},{28,4},{1,9},{5... | collective-permute-start | bytes 3145736 | tf_op jit(solution)/shard_map/ppermute | solution.py:611
  94.7 23.6 %collective-permute-start.10 = (bf16[256,1024]{1,0:T(8,128)(2,1)}, bf16[256,1024]{1,0:T(8,128)(2,1)}, u32[]{:S(2)}, u32[]{:S(2)}) collective-permute-start(bf16[256,1024]{1,0:T(8,128)(2,1)} %bitcast.131), channel_id=1, source_target_pairs={{0,4},{4,0},{8,12},{12,8},{16,20},{20,16},{24,28},{28,24},{1,5},{5... | collective-permute-start | bytes 1572872 | tf_op jit(solution)/shard_map/ppermute | solution.py:534
  95.3 23.0 %collective-permute-start.9 = (bf16[16,704]{1,0:T(8,128)(2,1)S(1)}, bf16[16,704]{1,0:T(8,128)(2,1)S(1)}, u32[]{:S(2)}, u32[]{:S(2)}) collective-permute-start(bf16[16,704]{1,0:T(8,128)(2,1)S(1)} %maximum_select_fusion.4), channel_id=1, source_target_pairs={{0,16},{4,20},{8,24},{12,28},{16,0},{20,4},{24,8},{28,12},{1,17},{... | collective-permute-start | bytes 67592 | tf_op jit(solution)/shard_map/ppermute | solution.py:546
  121.3 26.9 %collective-permute-start.11 = (bf16[512,1024]{1,0:T(8,128)(2,1)S(1)}, bf16[512,1024]{1,0:T(8,128)(2,1)S(1)}, u32[]{:S(2)}, u32[]{:S(2)}) collective-permute-start(bf16[512,1024]{1,0:T(8,128)(2,1)S(1)} %maximum_select_fusion.1.refs_2_.refs_4_), channel_id=1, source_target_pairs={{0,8},{4,12},{8,16},{12,20},{16,24},{20,28},{24,0},{28,4},{1,9},{5... | collective-permute-start | bytes 3145736 | tf_op jit(solution)/shard_map/ppermute | solution.py:611
  148.2 341.6 %reduce-scatter.4.cloned.1.call-start = ((), (), s32[]{:S(2)}) async-start(), calls=%async_computation.7 | async-start | bytes 18874368 | tf_op jit(solution)/shard_map/reduce_scatter | solution.py:540
  148.3 41.0 %collective-permute-start.12 = (bf16[512,1024]{1,0:T(8,128)(2,1)S(1)}, bf16[512,1024]{1,0:T(8,128)(2,1)S(1)}, u32[]{:S(2)}, u32[]{:S(2)}) collective-permute-start(bf16[512,1024]{1,0:T(8,128)(2,1)S(1)} %collective-permute-done.11.refs_3_.refs_5_), channel_id=1, source_target_pairs={{0,8},{4,12},{8,16},{12,20},{16,24},{20,28},{24,0},{28,4},{1,9},{5... | collective-permute-start | bytes 3145736 | tf_op jit(solution)/shard_map/ppermute | solution.py:611
  189.3 26.1 %collective-permute-start.13 = (bf16[512,1024]{1,0:T(8,128)(2,1)S(1)}, bf16[512,1024]{1,0:T(8,128)(2,1)S(1)}, u32[]{:S(2)}, u32[]{:S(2)}) collective-permute-start(bf16[512,1024]{1,0:T(8,128)(2,1)S(1)} %collective-permute-done.12.refs_4_.refs_6_), channel_id=1, source_target_pairs={{0,8},{4,12},{8,16},{12,20},{16,24},{20,28},{24,0},{28,4},{1,9},{5... | collective-permute-start | bytes 3145736 | tf_op jit(solution)/shard_map/ppermute | solution.py:611
  215.4 35.7 %collective-permute-start.14 = (bf16[512,1024]{1,0:T(8,128)(2,1)S(1)}, bf16[512,1024]{1,0:T(8,128)(2,1)S(1)}, u32[]{:S(2)}, u32[]{:S(2)}) collective-permute-start(bf16[512,1024]{1,0:T(8,128)(2,1)S(1)} %copy-done.9), channel_id=1, source_target_pairs={{0,8},{4,12},{8,16},{12,20},{16,24},{20,28},{24,0},{28,4},{1,9},{5... | collective-permute-start | bytes 3145736 | tf_op jit(solution)/shard_map/ppermute | solution.py:611
  251.1 25.7 %collective-permute-start.15 = (bf16[512,1024]{1,0:T(8,128)(2,1)S(1)}, bf16[512,1024]{1,0:T(8,128)(2,1)S(1)}, u32[]{:S(2)}, u32[]{:S(2)}) collective-permute-start(bf16[512,1024]{1,0:T(8,128)(2,1)S(1)} %collective-permute-done.14.refs_9_.refs_5_), channel_id=1, source_target_pairs={{0,8},{4,12},{8,16},{12,20},{16,24},{20,28},{24,0},{28,4},{1,9},{5... | collective-permute-start | bytes 3145736 | tf_op jit(solution)/shard_map/ppermute | solution.py:611
  276.8 27.8 %collective-permute-start.16 = (bf16[512,1024]{1,0:T(8,128)(2,1)S(1)}, bf16[512,1024]{1,0:T(8,128)(2,1)S(1)}, u32[]{:S(2)}, u32[]{:S(2)}) collective-permute-start(bf16[512,1024]{1,0:T(8,128)(2,1)S(1)} %collective-permute-done.15.refs_10_.refs_6_), channel_id=1, source_target_pairs={{0,8},{4,12},{8,16},{12,20},{16,24},{20,28},{24,0},{28,4},{1,9},{5... | collective-permute-start | bytes 3145736 | tf_op jit(solution)/shard_map/ppermute | solution.py:611
  304.7 31.2 %collective-permute-start.17 = (bf16[512,1024]{1,0:T(8,128)(2,1)S(1)}, bf16[512,1024]{1,0:T(8,128)(2,1)S(1)}, u32[]{:S(2)}, u32[]{:S(2)}) collective-permute-start(bf16[512,1024]{1,0:T(8,128)(2,1)S(1)} %constant_dynamic-slice_fusion.7), channel_id=1, source_target_pairs={{0,8},{4,12},{8,16},{12,20},{16,24},{20,28},{24,0},{28,4},{1,9},{5... | collective-permute-start | bytes 3145736 | tf_op jit(solution)/shard_map/ppermute | solution.py:637
  337.5 242.7 %reduce-scatter.6.cloned.1.call-start = ((), (), s32[]{:S(2)}) async-start(), calls=%async_computation.8 | async-start | bytes 9437184 | tf_op jit(solution)/shard_map/reduce_scatter | solution.py:540
  337.5 28.4 %collective-permute-start.18 = (bf16[512,1024]{1,0:T(8,128)(2,1)S(1)}, bf16[512,1024]{1,0:T(8,128)(2,1)S(1)}, u32[]{:S(2)}, u32[]{:S(2)}) collective-permute-start(bf16[512,1024]{1,0:T(8,128)(2,1)S(1)} %add_convert_fusion.5), channel_id=1, source_target_pairs={{0,8},{4,12},{8,16},{12,20},{16,24},{20,28},{24,0},{28,4},{1,9},{5... | collective-permute-start | bytes 3145736 | tf_op jit(solution)/shard_map/ppermute | solution.py:637
  367.6 28.9 %collective-permute-start.19 = (bf16[512,1024]{1,0:T(8,128)(2,1)S(1)}, bf16[512,1024]{1,0:T(8,128)(2,1)S(1)}, u32[]{:S(2)}, u32[]{:S(2)}) collective-permute-start(bf16[512,1024]{1,0:T(8,128)(2,1)S(1)} %add_convert_fusion.4), channel_id=1, source_target_pairs={{0,8},{4,12},{8,16},{12,20},{16,24},{20,28},{24,0},{28,4},{1,9},{5... | collective-permute-start | bytes 3145736 | tf_op jit(solution)/shard_map/ppermute | solution.py:637
  398.2 27.1 %collective-permute-start.20 = (bf16[512,1024]{1,0:T(8,128)(2,1)S(1)}, bf16[512,1024]{1,0:T(8,128)(2,1)S(1)}, u32[]{:S(2)}, u32[]{:S(2)}) collective-permute-start(bf16[512,1024]{1,0:T(8,128)(2,1)S(1)} %constant_dynamic-slice_fusion.6), channel_id=1, source_target_pairs={{0,8},{4,12},{8,16},{12,20},{16,24},{20,28},{24,0},{28,4},{1,9},{5... | collective-permute-start | bytes 3145736 | tf_op jit(solution)/shard_map/ppermute | solution.py:637
  399.5 27.3 %collective-permute-start.21 = (bf16[256,1024]{1,0:T(8,128)(2,1)S(1)}, bf16[256,1024]{1,0:T(8,128)(2,1)S(1)}, u32[]{:S(2)}, u32[]{:S(2)}) collective-permute-start(bf16[256,1024]{1,0:T(8,128)(2,1)S(1)} %dynamic-slice_convert_fusion.2), channel_id=1, source_target_pairs={{0,4},{4,0},{8,12},{12,8},{16,20},{20,16},{24,28},{28,24},{1,5},{5... | collective-permute-start | bytes 1572872 | tf_op jit(solution)/shard_map/ppermute | solution.py:534
  427.7 196.3 %reduce-scatter.8.cloned.1.call-start = ((), (), s32[]{:S(2)}) async-start(), calls=%async_computation.9 | async-start | bytes 9437184 | tf_op jit(solution)/shard_map/reduce_scatter | solution.py:540
  427.7 29.9 %collective-permute-start.22 = (bf16[512,1024]{1,0:T(8,128)(2,1)S(1)}, bf16[512,1024]{1,0:T(8,128)(2,1)S(1)}, u32[]{:S(2)}, u32[]{:S(2)}) collective-permute-start(bf16[512,1024]{1,0:T(8,128)(2,1)S(1)} %add_convert_fusion.3), channel_id=1, source_target_pairs={{0,8},{4,12},{8,16},{12,20},{16,24},{20,28},{24,0},{28,4},{1,9},{5... | collective-permute-start | bytes 3145736 | tf_op jit(solution)/shard_map/ppermute | solution.py:637
  458.1 31.3 %collective-permute-start.23 = (bf16[512,1024]{1,0:T(8,128)(2,1)S(1)}, bf16[512,1024]{1,0:T(8,128)(2,1)S(1)}, u32[]{:S(2)}, u32[]{:S(2)}) collective-permute-start(bf16[512,1024]{1,0:T(8,128)(2,1)S(1)} %add_convert_fusion.2), channel_id=1, source_target_pairs={{0,8},{4,12},{8,16},{12,20},{16,24},{20,28},{24,0},{28,4},{1,9},{5... | collective-permute-start | bytes 3145736 | tf_op jit(solution)/shard_map/ppermute | solution.py:637
  489.8 27.5 %collective-permute-start.24 = (bf16[512,1024]{1,0:T(8,128)(2,1)}, bf16[512,1024]{1,0:T(8,128)(2,1)S(1)}, u32[]{:S(2)}, u32[]{:S(2)}) collective-permute-start(bf16[512,1024]{1,0:T(8,128)(2,1)} %constant_dynamic-slice_fusion.5), channel_id=1, source_target_pairs={{0,8},{4,12},{8,16},{12,20},{16,24},{20,28},{24,0},{28,4},{1,9},{5... | collective-permute-start | bytes 3145736 | tf_op jit(solution)/shard_map/ppermute | solution.py:637
  492.8 27.0 %collective-permute-start.25 = (bf16[256,1024]{1,0:T(8,128)(2,1)S(1)}, bf16[256,1024]{1,0:T(8,128)(2,1)S(1)}, u32[]{:S(2)}, u32[]{:S(2)}) collective-permute-start(bf16[256,1024]{1,0:T(8,128)(2,1)S(1)} %dynamic-slice_convert_fusion.1), channel_id=1, source_target_pairs={{0,4},{4,0},{8,12},{12,8},{16,20},{20,16},{24,28},{28,24},{1,5},{5... | collective-permute-start | bytes 1572872 | tf_op jit(solution)/shard_map/ppermute | solution.py:534
  524.4 20.9 %collective-permute-start.28 = (bf16[512,1024]{1,0:T(8,128)(2,1)}, bf16[512,1024]{1,0:T(8,128)(2,1)}, u32[]{:S(2)}, u32[]{:S(2)}) collective-permute-start(bf16[512,1024]{1,0:T(8,128)(2,1)} %add_convert_fusion.1), channel_id=1, source_target_pairs={{0,8},{4,12},{8,16},{12,20},{16,24},{20,28},{24,0},{28,4},{1,9},{5... | collective-permute-start | bytes 3145736 | tf_op jit(solution)/shard_map/ppermute | solution.py:637
  548.3 20.8 %collective-permute-start.30 = (bf16[512,1024]{1,0:T(8,128)(2,1)}, bf16[512,1024]{1,0:T(8,128)(2,1)}, u32[]{:S(2)}, u32[]{:S(2)}) collective-permute-start(bf16[512,1024]{1,0:T(8,128)(2,1)} %add_convert_fusion), channel_id=1, source_target_pairs={{0,8},{4,12},{8,16},{12,20},{16,24},{20,28},{24,0},{28,4},{1,9},{5... | collective-permute-start | bytes 3145736 | tf_op jit(solution)/shard_map/ppermute | solution.py:637
  572.4 20.3 %collective-permute-start.33 = (bf16[256,1024]{1,0:T(8,128)(2,1)S(1)}, bf16[256,1024]{1,0:T(8,128)(2,1)}, u32[]{:S(2)}, u32[]{:S(2)}) collective-permute-start(bf16[256,1024]{1,0:T(8,128)(2,1)S(1)} %dynamic-slice_convert_fusion), channel_id=1, source_target_pairs={{0,4},{4,0},{8,12},{12,8},{16,20},{20,16},{24,28},{28,24},{1,5},{5... | collective-permute-start | bytes 1572872 | tf_op jit(solution)/shard_map/ppermute | solution.py:534
  (43 other events, 372.4 us)
Sparse Core Ops, SparseCore 0:
  19.2 67.5 all-gather.4
  89.2 58.6 all-gather.6
  149.8 54.3 all-gather.8
  206.6 54.3 all-gather.10
  337.6 126.5 reduce-scatter.3
  467.5 76.5 reduce-scatter.5
  547.9 76.0 reduce-scatter.7

commit v4 on v3

--- a/solution.py
+++ b/solution.py
@@ -408,13 +408,14 @@
     )[0]
 
 
-def normed_grad_rows(slots, one, one_parts, two, two_parts, rows, stats):
+def normed_grad_rows(slots, one, one_parts, two, two_parts, rows, stats, block, split):
     tokens, cols = one.shape
-    count, depth, tile = len(one_parts), one_parts[0].shape[0], 512
+    count, depth = len(one_parts), one_parts[0].shape[0]
+    tile = 2 * block
     width = count * depth
 
     def kernel(slots_ref, one_ref, two_ref, rows_ref, stat_ref, *refs):
-        out_ref, sum_ref = refs[-2:]
+        outs, sum_ref = refs[2 * count : -1], refs[-1]
 
         @pl.when(pl.program_id(0) == 0)
         def _():
@@ -425,22 +426,63 @@
             span = pl.ds(where, depth)
             total = dot_cols(one_ref[...], refs[at][:, :cols])
             total += dot_cols(two_ref[...], refs[count + at][...])
-            out_ref[:, span] = total.astype(BF)
+            if split:
+                first = slots_ref[count] == 0
+                outs[0][:, span] = jnp.where(first, total[:block], total[block:]).astype(BF)
+                outs[1][:, span] = jnp.where(first, total[block:], total[:block]).astype(BF)
+            else:
+                outs[0][:, span] = total.astype(BF)
             scaled = (rows_ref[:, span].astype(F32) - stat_ref[:, 0:1]) * stat_ref[:, 1:2]
             sum_ref[0:1, span] += jnp.sum(total * scaled, axis=0, keepdims=True)
             sum_ref[1:2, span] += jnp.sum(total, axis=0, keepdims=True)
 
+    pieces = 2 if split else 1
     return rows_call(
         kernel,
         slots,
         [one, two, rows, stats, *one_parts, *two_parts],
         [spec_rows(tile, cols), spec_rows(tile, two.shape[1]), spec_rows(tile, width), spec_rows(tile, LANES)]
         + [spec_whole(part) for part in (*one_parts, *two_parts)],
-        [jax.ShapeDtypeStruct((tokens, width), BF), jax.ShapeDtypeStruct((8, width), F32)],
+        [jax.ShapeDtypeStruct((tokens // pieces, width), BF)] * pieces + [jax.ShapeDtypeStruct((8, width), F32)],
         tile,
         estimate(2 * tokens * width * (cols + two.shape[1]), 2 * tokens * (2 * width + cols + two.shape[1])),
-        [spec_rows(tile, width), pl.BlockSpec((8, width), lambda i, s: (0, 0))],
-    )
+        [spec_rows(tile // pieces, width)] * pieces + [pl.BlockSpec((8, width), lambda i, s: (0, 0))],
+        tokens // tile,
+    )
+
+
+def norm_back(rows, cots, pieces, gain, micro, earlier=None):
+    micros, tokens, width = rows.shape
+    tile = tokens // 2
+
+    def kernel(rows_ref, cot_ref, gain_ref, *refs):
+        vals = rows_ref[0].astype(F32)
+        mean = jnp.mean(vals, axis=-1, keepdims=True)
+        centred = vals - mean
+        scale = lax.rsqrt(jnp.mean(centred * centred, axis=-1, keepdims=True) + norm_epsilon)
+        scaled = centred * scale
+        grad = refs[0][...].astype(F32)
+        for ref in refs[1 : len(pieces)]:
+            grad += ref[...].astype(F32)
+        grad *= gain_ref[...]
+        inner = jnp.mean(grad * scaled, axis=-1, keepdims=True)
+        grad = (grad - jnp.mean(grad, axis=-1, keepdims=True) - scaled * inner) * scale
+        refs[-1][0] = (cot_ref[0].astype(F32) + grad).astype(BF)
+
+    at_micro = pl.BlockSpec((1, tile, width), lambda i: (micro, i, 0))
+    given = [] if earlier is None else [earlier]
+    return pl.pallas_call(
+        kernel,
+        grid=(tokens // tile,),
+        in_specs=[at_micro, at_micro, pl.BlockSpec((1, width), lambda i: (0, 0))]
+        + [pl.BlockSpec((tile, width), lambda i: (i, 0))] * len(pieces)
+        + [pl.BlockSpec(memory_space=pl.ANY)] * len(given),
+        out_specs=at_micro,
+        out_shape=jax.ShapeDtypeStruct(rows.shape, BF),
+        input_output_aliases={3 + len(pieces): 0} if given else {},
+        compiler_params=pltpu.CompilerParams(vmem_limit_bytes=VMEM_LIMIT),
+        cost_estimate=estimate(20 * tokens * width, 10 * tokens * width),
+    )(rows, cots, gain, *pieces, *given)
 
 
 def weight_grad(groups):
@@ -539,21 +581,11 @@
     def scatter_plane(vals):
         return lax.psum_scatter(vals, both_axes, scatter_dimension=0, tiled=True, axis_index_groups=planes)
 
-    def after(vals, *others):
-        return lax.optimization_barrier((vals,) + others)[0]
-
     def doubled(cur, axis, size, at, bit):
         other = lax.ppermute(cur, axis, [(i, i ^ bit) for i in range(size)])
         upper = (at & bit) != 0
         return jnp.where(upper, jnp.concatenate([other, cur]), jnp.concatenate([cur, other]))
 
-    small = jnp.concatenate(
-        [vec.reshape(-1) for vec in (ln_gain, ln_bias, out_bias, down_bias, qkv_bias, up_bias)]
-    )
-    small_all = small[None]
-    for bit in range(tp_size.bit_length() - 1):
-        small_all = doubled(small_all, "tp", tp_size, tp_at, 1 << bit)
-    small_near = small_all
     def attn_half(half):
         qkv_part = lax.dynamic_slice_in_dim(qkv_weight, half * attn_cols, attn_cols, axis=2)
         qkv_part = qkv_part.reshape(shard_rows, 3, pairs, LANES).transpose(0, 2, 1, 3)
@@ -568,11 +600,6 @@
 
     def pair_join(own, other):
         return jnp.where(pair_at == 0, jnp.concatenate([own, other]), jnp.concatenate([other, own]))
-
-    def pair_shard(half_of, *behind):
-        own = half_of(pair_at)
-        other = swap_pair(after(half_of(1 - pair_at), *behind))
-        return pair_join(own, other)
 
     class Box:
         def __init__(self, val):
@@ -623,28 +650,31 @@
 
     class Scatter:
         def __init__(self, part):
-            self.part, self.step = part, 1
-            self.moving = Box(self.own().astype(BF))
-
-        def own(self):
+            self.part, self.step, self.came = part, 1, None
+
+        def total(self):
             at_line = lax.rem(line_at + line - self.step, line)
-            return lax.dynamic_slice_in_dim(self.part.val, at_line * line_rows, line_rows, axis=0).astype(F32)
+            own = lax.dynamic_slice_in_dim(self.part.val, at_line * line_rows, line_rows, axis=0)
+            if self.came is None:
+                return own
+            order.tie(self.came)
+            return self.came.val.astype(F32) + own.astype(F32)
 
         def move(self):
             if self.step < line:
+                sent = Box(self.total().astype(BF))
+                if self.came is None:
+                    order.tie(sent)
+                self.came = Box(lax.ppermute(sent.val, "fsdp", ring))
                 self.step += 1
-                order.tie(self.moving)
-                came = lax.ppermute(self.moving.val, "fsdp", ring).astype(F32) + self.own()
-                self.moving = Box(came.astype(BF) if self.step < line else came)
 
         def sync(self):
-            order.sync(self.moving)
+            order.sync(self.came)
 
         def swap(self):
             while self.step < line:
                 self.move()
-            order.tie(self.moving)
-            total = self.moving.val
+            total = self.total()
             self.keep = lax.dynamic_slice_in_dim(total, pair_at * shard_rows, shard_rows, axis=0)
             give = lax.dynamic_slice_in_dim(total, (1 - pair_at) * shard_rows, shard_rows, axis=0)
             self.got = Box(swap_pair(give.astype(BF)))
@@ -679,6 +709,18 @@
     micros = range(micro_count)
     plane_rows, plane_cots = [None] * micro_count, [None] * micro_count
 
+    small = jnp.concatenate(
+        [vec.reshape(-1) for vec in (ln_gain, ln_bias, out_bias, down_bias, qkv_bias, up_bias)]
+    )
+    attn_send = Box(attn_half(1 - pair_at))
+    small_all = Box(small[None])
+    order.tokens = []
+    order.tie(small_all, attn_send)
+    small_all = small_all.val
+    for bit in range(tp_size.bit_length() - 1):
+        small_all = doubled(small_all, "tp", tp_size, tp_at, 1 << bit)
+    small_near = small_all
+
     def gather_behind(rows):
         sent = Box(rows)
         order.tie(sent)
@@ -693,34 +735,37 @@
     small_all = Box(small_near)
     order.tokens = [small_all]
     plane_rows[0] = gather_behind(resid[0])
-    attn_shard = Box(pair_shard(attn_half))
-    order.tokens = [attn_shard]
-    plane_rows[1] = gather_behind(resid[1])
+    attn_shard = Box(pair_join(attn_half(pair_at), swap_pair(attn_send.val)))
+    order.tokens = [attn_shard, small_all]
     attn_ring = Gather(attn_shard)
     attn_ring.move()
+    plane_rows[1] = gather_behind(resid[1])
     small_all = small_step(small_all, 0)
+    bias_total = Box(sum(jnp.sum(cots[m].astype(F32), axis=0) for m in micros))
+    up_send = Box(up_half(1 - pair_at))
+    order.tie(up_send)
+    up_got = Box(swap_pair(up_send.val))
     attn_ring.sync()
     order.sync(small_all)
-    bias_total = Box(sum(jnp.sum(cots[m].astype(F32), axis=0) for m in micros))
+    attn_ring.move()
     order.sync(bias_total)
-    up_send = Box(up_half(1 - pair_at))
-    order.tie(up_send)
-    up_shard = Box(pair_join(up_half(pair_at), swap_pair(up_send.val)))
-    attn_ring.move()
     small_all = small_step(small_all, 1)
+    down_send = Box(down_half(1 - pair_at))
+    order.tie(down_send, up_got)
+    down_got = Box(swap_pair(down_send.val))
+    up_shard = Box(pair_join(up_half(pair_at), up_got.val))
     attn_ring.sync()
     order.sync(small_all)
-    order.sync(up_shard)
+    attn_ring.move()
     plane_cots[0] = gather_behind(cots[0])
-    down_send = Box(down_half(1 - pair_at))
-    order.tie(down_send)
-    down_shard = Box(pair_join(down_half(pair_at), swap_pair(down_send.val)))
-    attn_ring.move()
     for bit in range(2, fsdp_size.bit_length() - 1):
         small_all = small_step(small_all, bit)
+    order.sync(up_shard)
+    order.tie(down_got)
+    down_shard = Box(pair_join(down_half(pair_at), down_got.val))
     attn_ring.finish()
     order.sync(small_all)
-    order.tie()
+    order.tie(up_shard)
     small_all = small_all.val
     vec_size = ln_gain.shape[0]
     gain_vec, shift_vec, bias_out, bias_down = (
@@ -739,11 +784,12 @@
     up_b = up_b.transpose(1, 0, 2).reshape(2, mlp_cols)
     up_b = lax.dynamic_slice_in_dim(up_b, pair_at, 1, axis=0)
 
-    slots = jnp.stack([lax.rem(line_at + line - step, line) for step in range(line)]).astype(jnp.int32)
+    slots = [lax.rem(line_at + line - step, line) for step in range(line)]
+    slots = jnp.stack(slots + [tp_at & 1]).astype(jnp.int32)
     tables = rotary_tables(length, head_dim, ROT)
     gain_row, shift_row = gain_vec[None], shift_vec[None]
     normed, qkvs, stats, rots, attns, lses, acts, slopes = ([None] * micro_count for _ in range(8))
-    pre_grads, qkv_grads, qkv_sums, back, sums, attn_heads = ([None] * micro_count for _ in range(6))
+    pre_grads, qkv_grads, qkv_sums, sums, attn_heads = ([None] * micro_count for _ in range(5))
 
     def norm_piece(m):
         normed[m], qkvs[m], stats[m] = order.run(
@@ -814,16 +860,17 @@
 
         return order.run(piece, *attns, *acts)[0]
 
-    def normed_grad_piece(m):
-        back[m], sums[m] = order.run(
+    def normed_grad_piece(m, split=False):
+        *back, sums[m] = order.run(
             lambda one, two, rows, stat: normed_grad_rows(
-                slots, one, attn_ring.vals(), two, up_ring.vals(), rows, stat
+                slots, one, attn_ring.vals(), two, up_ring.vals(), rows, stat, token_rows, split
             ),
             qkv_grads[m],
             pre_grads[m],
             plane_rows[m],
             stats[m],
         )
+        return back
 
     def scatter_behind(box):
         order.tie(box)
@@ -865,26 +912,35 @@
     down_scatter.sync()
     down_scatter.swap()
     up_scatter.move()
-    normed_grad_piece(0)
-    up_scatter.sync()
-    order.sync(down_scatter.got)
-    back_sums = [scatter_behind(back[0])]
-    up_scatter.move()
     head_grad_piece(1)
     attend_back_piece(1)
     up_scatter.sync()
+    order.sync(down_scatter.got)
     up_scatter.move()
     attn_scatter = weight_piece((normed, qkv_grads), (plane_cots, attns))
     up_scatter.sync()
+    up_scatter.move()
+    (back,) = normed_grad_piece(0)
+    up_scatter.sync()
     order.sync(branch_sum)
+    back_sum = scatter_behind(back)
     up_scatter.swap()
     attn_scatter.move()
-    normed_grad_piece(1)
+    keep, give = normed_grad_piece(1, True)
+
+    def swap_core(vals):
+        return lax.ppermute(vals, "tp", [(t, t ^ 1) for t in range(tp_size)])
+
+    def swap_y(vals):
+        return lax.ppermute(vals, "tp", [(t, t ^ 2) for t in range(tp_size)])
+
+    y_at, half = tp_at >> 1, model_width // 2
     attn_scatter.sync()
     order.sync(up_scatter.got)
-    back_sums.append(scatter_behind(back[1]))
-
+    order.tie(give)
+    got = Box(swap_core(give.val))
     attn_scatter.move()
+
     up_b_grad = up_sums.val[0]
     qkv_b_grad = sum(jnp.sum(part.val.reshape(-1, 8, qkv_cols)[:, 0], axis=0) for part in qkv_sums)
     qkv_b_grad = qkv_b_grad.reshape(pairs, 3, -1).transpose(1, 0, 2).reshape(3, attn_cols)
@@ -900,12 +956,30 @@
         jnp.concatenate([gain_total, shift_total, bias_total.val]),
         jnp.concatenate([in_half(up_b_grad), in_half(qkv_b_grad).reshape(-1)]),
     )
+    order.tie(got)
+    blocks = Box((got.val.astype(F32) + keep.val.astype(F32)).astype(BF).reshape(4, token_rows, model_width))
+    order.sync(blocks)
+
+    def block(pair, y):
+        return lax.dynamic_index_in_dim(blocks.val, pair * 2 + y, 0, keepdims=False)
+
+    far = block(1 - pair_at, 1 - y_at)
+    from_pair, from_y = Box(swap_pair(far[:, :half])), Box(swap_y(far[:, half:]))
     tail.move()
     tail.move()
+    order.tie(from_pair, from_y)
+    for_y, for_pair = block(pair_at, 1 - y_at), block(1 - pair_at, y_at)
+    for_y = jnp.concatenate(
+        [(for_y[:, :half].astype(F32) + from_pair.val.astype(F32)).astype(BF), for_y[:, half:]], axis=1
+    )
+    for_pair = jnp.concatenate(
+        [for_pair[:, :half], (for_pair[:, half:].astype(F32) + from_y.val.astype(F32)).astype(BF)], axis=1
+    )
+    from_pair, from_y = Box(swap_pair(for_pair)), Box(swap_y(for_y))
     attn_scatter.sync()
     attn_scatter.move()
     tail.move()
-    down_w_grad = Box(jnp.concatenate([half.T for half in down_scatter.halves()], axis=0))
+    down_w_grad = Box(jnp.concatenate([part.T for part in down_scatter.halves()], axis=0))
     up_w_grad = Box(jnp.concatenate(up_scatter.halves(), axis=1))
     order.sync(down_w_grad)
     order.sync(up_w_grad)
@@ -914,16 +988,15 @@
     tail.move()
     tail.move()
     order.sync(tail.cur)
+    order.tie(from_pair, from_y)
+    gained = norm_back(
+        inputs[:, 0], cotangent[:, 0], [block(pair_at, y_at), from_pair.val, from_y.val], gain_row, 1,
+        norm_back(inputs[:, 0], cotangent[:, 0], [back_sum.val], gain_row, 0),
+    )
     small_sums, bias_sums = tail.split()
     attn_grads = attn_scatter.halves()
-
-    outputs, input_grads = [], []
-    for m in micros:
-        outputs.append((resid[m].astype(F32) + branch_sum.val.reshape(micro_count, token_rows, -1)[m].astype(F32) + bias_both).astype(BF))
-        order.tie(back_sums[m])
-        vals, cot = resid[m].astype(F32), cots[m].astype(F32)
-        pull_back = jax.vjp(lambda vals: layer_norm(vals, gain_vec, shift_vec), vals)[1]
-        input_grads.append((cot + pull_back(back_sums[m].val.astype(F32))[0]).astype(BF))
+    branch_sum = branch_sum.val.reshape(micro_count, token_rows, model_width)
+    output = (inputs[:, 0].astype(F32) + branch_sum.astype(F32) + bias_both).astype(BF)
 
     small_sums = small_sums.reshape(3, fsdp_size * tp_size, vec_size)
     small_sums = lax.dynamic_slice_in_dim(small_sums, fsdp_at * tp_size + tp_at, 1, axis=1)[:, 0]
@@ -941,8 +1014,8 @@
     qkv_w_grad = jnp.concatenate([qkv_columns(half) for half in attn_grads], axis=2)
     out_w_grad = jnp.concatenate([half[:, qkv_cols:].T for half in attn_grads], axis=0)
     return (
-        jnp.stack(outputs, axis=0)[:, None],
-        jnp.stack(input_grads, axis=0)[:, None],
+        output[:, None],
+        gained[:, None],
         gain_sum,
         shift_sum,
         qkv_w_grad,

time: 655 us -> 634 us (0.968)
  local copies, waits for them, and re-layouts: 60.2 us -> 44.2 us
  other arithmetic: 49.7 us -> 35.7 us
  Pallas kernels: 350 us -> 362 us
  waiting for transfers between devices: 129 us -> 117 us
  starting transfers between devices: 43.2 us -> 53.6 us
    ppermute x5, waiting for transfers between devices: 7.5 us -> 42.4 us  [move(): lax.ppermute(self.cur.val, axis, [(i, i ^ 1 << bit) for i in range(size)])]
    ppermute x9 -> x12, waiting for transfers between devices: 25.4 us -> 0.97 us  [the longest x1 0.94 us: swap_core(): return lax.ppermute(vals, 'tp', [(t, t ^ 1) for t in range(tp_size)])]
    ppermute x5, waiting for transfers between devices: 31.6 us -> 8.25 us  [doubled(): other = lax.ppermute(cur, axis, [(i, i ^ bit) for i in range(size)])]
    reduce_scatter x3 -> x2, waiting for transfers between devices: 10.5 us -> 0.02 us  [scatter_plane(): lax.psum_scatter(vals, both_axes, scatter_dimension=0, tiled=True, axis_i...]
    pallas_call x0 -> x2, Pallas kernels: none -> 8.33 us  [norm_back(): pl.pallas_call(kernel, grid=(tokens // tile,), in_specs=[at_micro, at_mic...]
    unnamed x81 -> x79, local copies, waits for them, and re-layouts: 22.2 us -> 14.9 us
    convert_element_type x6 -> x10, other arithmetic: 10.8 us -> 16.4 us  [the longest x6 8.36 us: move(): sent = Box(self.total().astype(BF))]
    ppermute x9 -> x12, starting transfers between devices: 11.2 us -> 16 us  [the longest x9 12.7 us: move(): self.came = Box(lax.ppermute(sent.val, 'fsdp', ring))]
  transfers between devices with their start and end apart: 41 -> 45, of which waited for: 18 -> 17; matrix products, arithmetic and copies ran while one was open for 12% -> 10% of each run, Pallas kernels for 54% -> 56%
where the time goes in v4:
time: 634 us; the launch traced here: 627 us
  Pallas kernels  362 us (57%)
  waiting for transfers between devices  117 us (18%)
  starting transfers between devices  53.6 us (8%)
  local copies, waits for them, and re-layouts  44.2 us (7%)
  other arithmetic  35.7 us (6%)
  between operations  15.3 us (2%)
    pallas_call x9, Pallas kernels, rows_call(): pl.pallas_call(kernel, grid_spec=pltpu.PrefetchScalarGridSpec(num_scalar_...  199 us
    pallas_call x3, Pallas kernels, weight_grad(): pl.pallas_call(kernel, grid=(micro_count * steps,), in_specs=in_specs, ou...  79.5 us
    ppermute x5, waiting for transfers between devices, move(): lax.ppermute(self.cur.val, axis, [(i, i ^ 1 << bit) for i in range(size)])  42.4 us
    pallas_call x2, Pallas kernels, attend_back(): pl.pallas_call(functools.partial(attend_back_kernel, head_dim, block), gr...  42.3 us
    ppermute x8, waiting for transfers between devices, swap_pair(): return lax.ppermute(vals, 'fsdp', [(f, f ^ 1) for f in range(fsdp_size)])  35.5 us
    pallas_call x2, Pallas kernels, attend(): pl.pallas_call(functools.partial(attend_kernel, head_dim, block), grid=(s...  32.7 us
    ppermute x9, waiting for transfers between devices, move(): self.parts.append(Box(lax.ppermute(self.parts[-1].val, 'fsdp', ring)))  24.6 us
    unnamed x79, local copies, waits for them, and re-layouts  14.9 us
  transfers between devices with their start and end apart: 45, of which 17 were waited for; matrix products, arithmetic and copies ran while one was open for 10% of the time, Pallas kernels for 56%

profile of v4, /device:TPU:0, one launch (start us, length us, event | category | flops | bytes accessed | tf_op | source)
XLA Modules:
  0.0 627.5 jit_solution(2486064208205334890)
XLA Ops:
  23.6 14.8 %collective-permute-done.2 = bf16[256,1024]{1,0:T(8,128)(2,1)S(1)} collective-permute-done((bf16[256,1024]{1,0:T(8,128)(2,1)}, bf16[256,1024]{1,0:T(8,128)(2,1)S(1)}, u32[]{:S(2)}, u32[]{:S(2)}) %collective-permute-start.2) | collective-permute-done | bytes 524320 | tf_op jit(solution)/shard_map/ppermute | solution.py:576
  46.4 17.9 %collective-permute-done.4.refs_1_.refs_5_ = bf16[512,1024]{1,0:T(8,128)(2,1)S(1)} collective-permute-done((bf16[512,1024]{1,0:T(8,128)(2,1)S(1)}, bf16[512,1024]{1,0:T(8,128)(2,1)S(1)}, u32[]{:S(2)}, u32[]{:S(2)}) %collective-permute-start.4) | collective-permute-done | bytes 1048608 | tf_op jit(solution)/shard_map/ppermute | solution.py:638
  74.3 16.1 %collective-permute-done.3 = bf16[256,1024]{1,0:T(8,128)(2,1)} collective-permute-done((bf16[256,1024]{1,0:T(8,128)(2,1)}, bf16[256,1024]{1,0:T(8,128)(2,1)}, u32[]{:S(2)}, u32[]{:S(2)}) %collective-permute-start.3) | collective-permute-done | bytes 524320 | tf_op jit(solution)/shard_map/ppermute | solution.py:576
  98.4 3.5 collective-permute-done.6
  104.5 6.8 %collective-permute-done.10 = bf16[16,704]{1,0:T(8,128)(2,1)S(1)} collective-permute-done((bf16[16,704]{1,0:T(8,128)(2,1)S(1)}, bf16[16,704]{1,0:T(8,128)(2,1)S(1)}, u32[]{:S(2)}, u32[]{:S(2)}) %collective-permute-start.10) | collective-permute-done | bytes 22560 | tf_op jit(solution)/shard_map/ppermute | solution.py:585
  115.4 20.3 %shard_map.211 = (bf16[2048,2048]{1,0:T(8,128)(2,1)}, f32[2048,768]{1,0:T(8,128)}, f32[2048,128]{1,0:T(8,128)}) custom-call(s32[5]{0:T(128)} %stack.23.slots_ref, bf16[2048,2048]{1,0:T(8,128)(2,1)} %all-gather.5.cloned.1.call-done.rows_ref, f32[1,2048]{1,0:T(1,128)} %reshape.222.gain_ref, f32[1,2048]{1,0:T(1,128)} %reshape.223.shift_ref, ...), custom_call_target="tpu_custom_call" | custom-call | flops 100663296 | bytes 360448 | tf_op jit(solution)/shard_map/pallas_call | solution.py:230
  143.6 16.4 %shard_map.212 = (bf16[2048,768]{1,0:T(8,128)(2,1)}, bf16[2048,256]{1,0:T(8,128)(2,1)}, f32[4,2,1024]{2,1,0:T(2,128)}) custom-call(f32[2048,768]{1,0:T(8,128)} %get-tuple-element.328.qkv_ref, f32[1024,128]{1,0:T(8,128)} %copy.78.cos_ref, f32[1024,128]{1,0:T(8,128)} %copy.79.low_ref, f32[1024,128]{1,0:T(8,128)} %copy.80.up_ref), custom_call_target="tpu_custom_call" | custom-call | flops 100663296 | bytes 131072 | tf_op jit(solution)/shard_map/pallas_call | solution.py:161
  160.0 20.3 %shard_map.213 = (bf16[2048,2048]{1,0:T(8,128)(2,1)}, f32[2048,768]{1,0:T(8,128)}, f32[2048,128]{1,0:T(8,128)}) custom-call(s32[5]{0:T(128)} %stack.23.slots_ref, bf16[2048,2048]{1,0:T(8,128)(2,1)} %all-gather.7.cloned.1.call-done.rows_ref, f32[1,2048]{1,0:T(1,128)} %reshape.222.gain_ref, f32[1,2048]{1,0:T(1,128)} %reshape.223.shift_ref, ...), custom_call_target="tpu_custom_call" | custom-call | flops 100663296 | bytes 360448 | tf_op jit(solution)/shard_map/pallas_call | solution.py:230
  182.8 16.4 %shard_map.214 = (bf16[2048,768]{1,0:T(8,128)(2,1)}, bf16[2048,256]{1,0:T(8,128)(2,1)}, f32[4,2,1024]{2,1,0:T(2,128)}) custom-call(f32[2048,768]{1,0:T(8,128)} %get-tuple-element.338.qkv_ref, f32[1024,128]{1,0:T(8,128)} %copy.78.cos_ref, f32[1024,128]{1,0:T(8,128)} %copy.79.low_ref, f32[1024,128]{1,0:T(8,128)} %copy.80.up_ref), custom_call_target="tpu_custom_call" | custom-call | flops 100663296 | bytes 131072 | tf_op jit(solution)/shard_map/pallas_call | solution.py:161
  199.2 5.2 all-gather.9.cloned.1.call-done.rows_ref.refs_0_.refs_4_
  204.4 7.6 %shard_map.215.grad_ref = bf16[2048,256]{1,0:T(8,128)(2,1)} custom-call(s32[5]{0:T(128)} %stack.23.slots_ref, bf16[2048,2048]{1,0:T(8,128)(2,1)} %all-gather.9.cloned.1.call-done.rows_ref.refs_0_.refs_4_, bf16[512,1024]{1,0:T(8,128)(2,1)} %copy-done, bf16[512,1024]{1,0:T(8,128)(2,1)} %copy-done.1, bf16[512,1024]{1,0:T(8,128)(2,1)} %copy-done.2, ...), custom_call_target="tpu_custom_call" | custom-call | flops 33554432 | bytes 147456 | tf_op jit(solution)/shard_map/pallas_call | solution.py:230
  214.8 34.6 %shard_map.216 = (bf16[2048,1024]{1,0:T(8,128)(2,1)}, bf16[2048,1024]{1,0:T(8,128)(2,1)}, bf16[2048,1024]{1,0:T(8,128)(2,1)}, bf16[2048,1024]{1,0:T(8,128)(2,1)}) custom-call(s32[5]{0:T(128)} %stack.23.slots_ref, f32[1,1024]{1,0:T(1,128)} %constant_dynamic-slice_fusion.8.bias_ref, bf16[2048,2048]{1,0:T(8,128)(2,1)} %get-tuple-element.421.refs_0_, ...), custom_call_target="tpu_custom_call" | custom-call | flops 268435456 | bytes 524288 | tf_op jit(solution)/shard_map/pallas_call | solution.py:230
  251.2 21.0 %shard_map.217 = (bf16[2048,768]{1,0:T(8,128)(2,1)}, f32[16,768]{1,0:T(8,128)}) custom-call(bf16[2048,768]{1,0:T(8,128)(2,1)} %get-tuple-element.362.rot_ref, bf16[2048,256]{1,0:T(8,128)(2,1)} %shard_map.215.grad_ref, bf16[2048,256]{1,0:T(8,128)(2,1)} %get-tuple-element.425.attn_ref.refs_0_.refs_6_, f32[4,2,1024]{2,1,0:T(2,128)} %get-tuple-element.364.lse_ref, ...), custom_call_target="tpu_custom_call" | custom-call | flops 201326592 | bytes 131072 | tf_op jit(solution)/shard_map/pallas_call | solution.py:186
  272.2 4.2 collective-permute-done.15.refs_10_.refs_6_
  276.8 25.4 %shard_map.218 = bf16[2048,1024]{1,0:T(8,128)(2,1)} custom-call(bf16[2048,2048]{1,0:T(8,128)(2,1)} %all-gather.9.cloned.1.call-done.rows_ref.refs_0_.refs_4_, bf16[2048,2048]{1,0:T(8,128)(2,1)} %all-gather.11.cloned.1.call-done.refs_1_.rows_ref.refs_5_, bf16[2048,1024]{1,0:T(8,128)(2,1)} %get-tuple-element.376.refs_2_, ...), custom_call_target="tpu_custom_call" | custom-call | flops 268435456 | bytes 393216 | tf_op jit(solution)/shard_map/pallas_call | solution.py:529
  304.8 30.2 %shard_map.219 = bf16[8,2,256,2048]{3,2,1,0:T(8,128)(2,1)} custom-call(s32[5]{0:T(128)} %stack.23.slots_ref, bf16[2048,256]{1,0:T(8,128)(2,1)} %get-tuple-element.425.attn_ref.refs_0_.refs_6_, bf16[2048,256]{1,0:T(8,128)(2,1)} %get-tuple-element.426.refs_1_.attn_ref.refs_7_, bf16[2048,1024]{1,0:T(8,128)(2,1)} %get-tuple-element.376.refs_2_, ...), custom_call_target="tpu_custom_call" | custom-call | flops 335544320 | bytes 294912 | tf_op jit(solution)/shard_map/pallas_call | solution.py:230
  337.9 27.1 %shard_map.220 = (bf16[2048,1024]{1,0:T(8,128)(2,1)}, bf16[2048,1024]{1,0:T(8,128)(2,1)}, f32[8,1024]{1,0:T(8,128)}) custom-call(s32[5]{0:T(128)} %stack.23.slots_ref, bf16[2048,2048]{1,0:T(8,128)(2,1)} %all-gather.9.cloned.1.call-done.rows_ref.refs_0_.refs_4_, bf16[2048,2048]{1,0:T(8,128)(2,1)} %all-gather.11.cloned.1.call-done.refs_1_.rows_ref.refs_5_, ...), custom_call_target="tpu_custom_call" | custom-call | flops 268435456 | bytes 524288 | tf_op jit(solution)/shard_map/pallas_call | solution.py:230
  366.6 3.4 collective-permute-start.19
  370.0 26.1 %shard_map.221 = bf16[2048,1024]{1,0:T(8,128)(2,1)} custom-call(bf16[2048,2048]{1,0:T(8,128)(2,1)} %get-tuple-element.421.refs_0_, bf16[2048,2048]{1,0:T(8,128)(2,1)} %get-tuple-element.422.refs_1_, bf16[2048,1024]{1,0:T(8,128)(2,1)} %get-tuple-element.431.refs_2_.two_ref, bf16[2048,1024]{1,0:T(8,128)(2,1)} %get-tuple-element.443.refs_3_.two_ref), custom_call_target="tpu_custom_call" | custom-call | flops 268435456 | bytes 393216 | tf_op jit(solution)/shard_map/pallas_call | solution.py:529
  402.0 7.7 %shard_map.222.grad_ref = bf16[2048,256]{1,0:T(8,128)(2,1)} custom-call(s32[5]{0:T(128)} %stack.23.slots_ref, bf16[2048,2048]{1,0:T(8,128)(2,1)} %all-gather.11.cloned.1.call-done.refs_1_.rows_ref.refs_5_, bf16[512,1024]{1,0:T(8,128)(2,1)} %copy-done, bf16[512,1024]{1,0:T(8,128)(2,1)} %copy-done.1, bf16[512,1024]{1,0:T(8,128)(2,1)} %copy-done.2, ...), custom_call_target="tpu_custom_call" | custom-call | flops 33554432 | bytes 147456 | tf_op jit(solution)/shard_map/pallas_call | solution.py:230
  409.7 21.2 %shard_map.223 = (bf16[2048,768]{1,0:T(8,128)(2,1)}, f32[16,768]{1,0:T(8,128)}) custom-call(bf16[2048,768]{1,0:T(8,128)(2,1)} %get-tuple-element.408.rot_ref, bf16[2048,256]{1,0:T(8,128)(2,1)} %shard_map.222.grad_ref, bf16[2048,256]{1,0:T(8,128)(2,1)} %get-tuple-element.426.refs_1_.attn_ref.refs_7_, f32[4,2,1024]{2,1,0:T(2,128)} %get-tuple-element.411.lse_ref, ...), custom_call_target="tpu_custom_call" | custom-call | flops 201326592 | bytes 131072 | tf_op jit(solution)/shard_map/pallas_call | solution.py:186
  433.8 28.0 %shard_map.224 = bf16[2048,1024]{1,0:T(8,128)(2,1)} custom-call(bf16[2048,2048]{1,0:T(8,128)(2,1)} %get-tuple-element.421.refs_0_, bf16[2048,2048]{1,0:T(8,128)(2,1)} %get-tuple-element.422.refs_1_, bf16[2048,768]{1,0:T(8,128)(2,1)} %get-tuple-element.430.refs_2_.one_ref, bf16[2048,768]{1,0:T(8,128)(2,1)} %get-tuple-element.442.refs_3_.one_ref, ...), custom_call_target="tpu_custom_call" | custom-call | flops 268435456 | bytes 655360 | tf_op jit(solution)/shard_map/pallas_call | solution.py:529
  464.5 24.0 %shard_map.225 = (bf16[2048,2048]{1,0:T(8,128)(2,1)}, f32[8,2048]{1,0:T(8,128)}) custom-call(s32[5]{0:T(128)} %stack.23.slots_ref, bf16[2048,768]{1,0:T(8,128)(2,1)} %get-tuple-element.430.refs_2_.one_ref, bf16[2048,1024]{1,0:T(8,128)(2,1)} %get-tuple-element.431.refs_2_.two_ref, bf16[2048,2048]{1,0:T(8,128)(2,1)} %all-gather.5.cloned.1.call-done.rows_ref, ...), custom_call_target="tpu_custom_call" | custom-call | flops 234881024 | bytes 376832 | tf_op jit(solution)/shard_map/pallas_call | solution.py:230
  489.8 5.3 collective-permute-start.24
  498.8 27.0 %shard_map.226 = (bf16[1024,2048]{1,0:T(8,128)(2,1)}, bf16[1024,2048]{1,0:T(8,128)(2,1)}, f32[8,2048]{1,0:T(8,128)}) custom-call(s32[5]{0:T(128)} %stack.23.slots_ref, bf16[2048,768]{1,0:T(8,128)(2,1)} %get-tuple-element.442.refs_3_.one_ref, bf16[2048,1024]{1,0:T(8,128)(2,1)} %get-tuple-element.443.refs_3_.two_ref, ...), custom_call_target="tpu_custom_call" | custom-call | flops 234881024 | bytes 376832 | tf_op jit(solution)/shard_map/pallas_call | solution.py:230
  534.3 5.5 add_convert_fusion
  546.0 16.1 %collective-permute-done.32 = f32[6144]{0:T(1024)S(1)} collective-permute-done((f32[6144]{0:T(1024)S(1)}, f32[6144]{0:T(1024)S(1)}, u32[]{:S(2)}, u32[]{:S(2)}) %collective-permute-start.32) | collective-permute-done | bytes 24608 | tf_op jit(solution)/shard_map/ppermute | solution.py:699
  569.9 20.1 %collective-permute-done.34 = f32[9728]{0:T(1024)S(1)} collective-permute-done((f32[9728]{0:T(1024)S(1)}, f32[9728]{0:T(1024)S(1)}, u32[]{:S(2)}, u32[]{:S(2)}) %collective-permute-start.34) | collective-permute-done | bytes 38944 | tf_op jit(solution)/shard_map/ppermute | solution.py:699
  590.9 3.2 collective-permute-done.36
  596.5 2.9 collective-permute-done.37
  611.6 3.8 shard_map.227.refs_3_
  615.4 4.5 shard_map.228
  (284 shorter events, 125.7 us)
Async XLA Ops:
  7.2 108.2 %all-gather.5.cloned.1.call-start = ((), (), s32[]{:S(2)}) async-start(), calls=%async_computation.2 | async-start | bytes 9437184 | tf_op jit(solution)/shard_map/all_gather | solution.py:579
  21.0 138.9 %all-gather.7.cloned.1.call-start = ((), (), s32[]{:S(2)}) async-start(), calls=%async_computation.3 | async-start | bytes 9437184 | tf_op jit(solution)/shard_map/all_gather | solution.py:579
  40.8 163.6 %all-gather.9.cloned.1.call-start = ((), (), s32[]{:S(2)}) async-start(), calls=%async_computation.4 | async-start | bytes 9437184 | tf_op jit(solution)/shard_map/all_gather | solution.py:579
  40.9 23.4 %collective-permute-start.4 = (bf16[512,1024]{1,0:T(8,128)(2,1)S(1)}, bf16[512,1024]{1,0:T(8,128)(2,1)S(1)}, u32[]{:S(2)}, u32[]{:S(2)}) collective-permute-start(bf16[512,1024]{1,0:T(8,128)(2,1)S(1)} %maximum_select_fusion.refs_0_.refs_4_), channel_id=1, source_target_pairs={{0,8},{4,12},{8,16},{12,20},{16,24},{20,28},{24,0},{28,4},{1,9},{5... | collective-permute-start | bytes 3145736 | tf_op jit(solution)/shard_map/ppermute | solution.py:638
  64.3 26.1 %collective-permute-start.7 = (bf16[512,1024]{1,0:T(8,128)(2,1)S(1)}, bf16[512,1024]{1,0:T(8,128)(2,1)S(1)}, u32[]{:S(2)}, u32[]{:S(2)}) collective-permute-start(bf16[512,1024]{1,0:T(8,128)(2,1)S(1)} %collective-permute-done.4.refs_1_.refs_5_), channel_id=1, source_target_pairs={{0,8},{4,12},{8,16},{12,20},{16,24},{20,28},{24,0},{28,4},{1,9},{5... | collective-permute-start | bytes 3145736 | tf_op jit(solution)/shard_map/ppermute | solution.py:638
  66.8 23.5 %collective-permute-start.3 = (bf16[256,1024]{1,0:T(8,128)(2,1)}, bf16[256,1024]{1,0:T(8,128)(2,1)}, u32[]{:S(2)}, u32[]{:S(2)}) collective-permute-start(bf16[256,1024]{1,0:T(8,128)(2,1)} %get-tuple-element.266), channel_id=1, source_target_pairs={{0,4},{4,0},{8,12},{12,8},{16,20},{20,16},{24,28},{28,24},{1,5},{5... | collective-permute-start | bytes 1572872 | tf_op jit(solution)/shard_map/ppermute | solution.py:576
  90.4 186.4 %all-gather.11.cloned.1.call-start = ((), (), s32[]{:S(2)}) async-start(), calls=%async_computation.5 | async-start | bytes 9437184 | tf_op jit(solution)/shard_map/all_gather | solution.py:579
  90.5 20.8 %collective-permute-start.9 = (bf16[512,1024]{1,0:T(8,128)(2,1)S(1)}, bf16[512,1024]{1,0:T(8,128)(2,1)S(1)}, u32[]{:S(2)}, u32[]{:S(2)}) collective-permute-start(bf16[512,1024]{1,0:T(8,128)(2,1)S(1)} %collective-permute-done.7.refs_2_.refs_6_), channel_id=1, source_target_pairs={{0,8},{4,12},{8,16},{12,20},{16,24},{20,28},{24,0},{28,4},{1,9},{5... | collective-permute-start | bytes 3145736 | tf_op jit(solution)/shard_map/ppermute | solution.py:638
  111.3 26.9 %collective-permute-start.11 = (bf16[512,1024]{1,0:T(8,128)(2,1)S(1)}, bf16[512,1024]{1,0:T(8,128)(2,1)S(1)}, u32[]{:S(2)}, u32[]{:S(2)}) collective-permute-start(bf16[512,1024]{1,0:T(8,128)(2,1)S(1)} %maximum_select_fusion.1.refs_2_.refs_4_), channel_id=1, source_target_pairs={{0,8},{4,12},{8,16},{12,20},{16,24},{20,28},{24,0},{28,4},{1,9},{5... | collective-permute-start | bytes 3145736 | tf_op jit(solution)/shard_map/ppermute | solution.py:638
  138.2 350.3 %reduce-scatter.3.cloned.1.call-start = ((), (), s32[]{:S(2)}) async-start(), calls=%async_computation.6 | async-start | bytes 18874368 | tf_op jit(solution)/shard_map/reduce_scatter | solution.py:582
  138.3 42.0 %collective-permute-start.12 = (bf16[512,1024]{1,0:T(8,128)(2,1)S(1)}, bf16[512,1024]{1,0:T(8,128)(2,1)S(1)}, u32[]{:S(2)}, u32[]{:S(2)}) collective-permute-start(bf16[512,1024]{1,0:T(8,128)(2,1)S(1)} %collective-permute-done.11.refs_3_.refs_5_), channel_id=1, source_target_pairs={{0,8},{4,12},{8,16},{12,20},{16,24},{20,28},{24,0},{28,4},{1,9},{5... | collective-permute-start | bytes 3145736 | tf_op jit(solution)/shard_map/ppermute | solution.py:638
  180.3 31.7 %collective-permute-start.13 = (bf16[512,1024]{1,0:T(8,128)(2,1)S(1)}, bf16[512,1024]{1,0:T(8,128)(2,1)S(1)}, u32[]{:S(2)}, u32[]{:S(2)}) collective-permute-start(bf16[512,1024]{1,0:T(8,128)(2,1)S(1)} %collective-permute-done.12.refs_4_.refs_6_), channel_id=1, source_target_pairs={{0,8},{4,12},{8,16},{12,20},{16,24},{20,28},{24,0},{28,4},{1,9},{5... | collective-permute-start | bytes 3145736 | tf_op jit(solution)/shard_map/ppermute | solution.py:638
  212.0 37.4 %collective-permute-start.14 = (bf16[512,1024]{1,0:T(8,128)(2,1)S(1)}, bf16[512,1024]{1,0:T(8,128)(2,1)S(1)}, u32[]{:S(2)}, u32[]{:S(2)}) collective-permute-start(bf16[512,1024]{1,0:T(8,128)(2,1)S(1)} %copy-done.13), channel_id=1, source_target_pairs={{0,8},{4,12},{8,16},{12,20},{16,24},{20,28},{24,0},{28,4},{1,9},{5... | collective-permute-start | bytes 3145736 | tf_op jit(solution)/shard_map/ppermute | solution.py:638
  249.4 27.0 %collective-permute-start.15 = (bf16[512,1024]{1,0:T(8,128)(2,1)S(1)}, bf16[512,1024]{1,0:T(8,128)(2,1)S(1)}, u32[]{:S(2)}, u32[]{:S(2)}) collective-permute-start(bf16[512,1024]{1,0:T(8,128)(2,1)S(1)} %collective-permute-done.14.refs_9_.refs_5_), channel_id=1, source_target_pairs={{0,8},{4,12},{8,16},{12,20},{16,24},{20,28},{24,0},{28,4},{1,9},{5... | collective-permute-start | bytes 3145736 | tf_op jit(solution)/shard_map/ppermute | solution.py:638
  276.4 27.2 %collective-permute-start.16 = (bf16[512,1024]{1,0:T(8,128)(2,1)S(1)}, bf16[512,1024]{1,0:T(8,128)(2,1)S(1)}, u32[]{:S(2)}, u32[]{:S(2)}) collective-permute-start(bf16[512,1024]{1,0:T(8,128)(2,1)S(1)} %collective-permute-done.15.refs_10_.refs_6_), channel_id=1, source_target_pairs={{0,8},{4,12},{8,16},{12,20},{16,24},{20,28},{24,0},{28,4},{1,9},{5... | collective-permute-start | bytes 3145736 | tf_op jit(solution)/shard_map/ppermute | solution.py:638
  303.6 31.5 %collective-permute-start.17 = (bf16[512,1024]{1,0:T(8,128)(2,1)S(1)}, bf16[512,1024]{1,0:T(8,128)(2,1)S(1)}, u32[]{:S(2)}, u32[]{:S(2)}) collective-permute-start(bf16[512,1024]{1,0:T(8,128)(2,1)S(1)} %constant_dynamic-slice_fusion.7), channel_id=1, source_target_pairs={{0,8},{4,12},{8,16},{12,20},{16,24},{20,28},{24,0},{28,4},{1,9},{5... | collective-permute-start | bytes 3145736 | tf_op jit(solution)/shard_map/ppermute | solution.py:668
  335.1 276.5 %reduce-scatter.5.cloned.1.call-start = ((), (), s32[]{:S(2)}) async-start(), calls=%async_computation.7 | async-start | bytes 9437184 | tf_op jit(solution)/shard_map/reduce_scatter | solution.py:582
  336.8 28.2 %collective-permute-start.18 = (bf16[512,1024]{1,0:T(8,128)(2,1)S(1)}, bf16[512,1024]{1,0:T(8,128)(2,1)S(1)}, u32[]{:S(2)}, u32[]{:S(2)}) collective-permute-start(bf16[512,1024]{1,0:T(8,128)(2,1)S(1)} %add_convert_fusion.6), channel_id=1, source_target_pairs={{0,8},{4,12},{8,16},{12,20},{16,24},{20,28},{24,0},{28,4},{1,9},{5... | collective-permute-start | bytes 3145736 | tf_op jit(solution)/shard_map/ppermute | solution.py:668
  366.6 29.5 %collective-permute-start.19 = (bf16[512,1024]{1,0:T(8,128)(2,1)S(1)}, bf16[512,1024]{1,0:T(8,128)(2,1)S(1)}, u32[]{:S(2)}, u32[]{:S(2)}) collective-permute-start(bf16[512,1024]{1,0:T(8,128)(2,1)S(1)} %add_convert_fusion.5), channel_id=1, source_target_pairs={{0,8},{4,12},{8,16},{12,20},{16,24},{20,28},{24,0},{28,4},{1,9},{5... | collective-permute-start | bytes 3145736 | tf_op jit(solution)/shard_map/ppermute | solution.py:668
  398.4 32.6 %collective-permute-start.20 = (bf16[512,1024]{1,0:T(8,128)(2,1)}, bf16[512,1024]{1,0:T(8,128)(2,1)}, u32[]{:S(2)}, u32[]{:S(2)}) collective-permute-start(bf16[512,1024]{1,0:T(8,128)(2,1)} %constant_dynamic-slice_fusion.6), channel_id=1, source_target_pairs={{0,8},{4,12},{8,16},{12,20},{16,24},{20,28},{24,0},{28,4},{1,9},{5... | collective-permute-start | bytes 3145736 | tf_op jit(solution)/shard_map/ppermute | solution.py:668
  400.3 30.6 %collective-permute-start.21 = (bf16[256,1024]{1,0:T(8,128)(2,1)S(1)}, bf16[256,1024]{1,0:T(8,128)(2,1)S(1)}, u32[]{:S(2)}, u32[]{:S(2)}) collective-permute-start(bf16[256,1024]{1,0:T(8,128)(2,1)S(1)} %dynamic-slice_convert_fusion.2), channel_id=1, source_target_pairs={{0,4},{4,0},{8,12},{12,8},{16,20},{20,16},{24,28},{28,24},{1,5},{5... | collective-permute-start | bytes 1572872 | tf_op jit(solution)/shard_map/ppermute | solution.py:576
  433.4 28.4 %collective-permute-start.22 = (bf16[512,1024]{1,0:T(8,128)(2,1)S(1)}, bf16[512,1024]{1,0:T(8,128)(2,1)}, u32[]{:S(2)}, u32[]{:S(2)}) collective-permute-start(bf16[512,1024]{1,0:T(8,128)(2,1)S(1)} %add_convert_fusion.4), channel_id=1, source_target_pairs={{0,8},{4,12},{8,16},{12,20},{16,24},{20,28},{24,0},{28,4},{1,9},{5... | collective-permute-start | bytes 3145736 | tf_op jit(solution)/shard_map/ppermute | solution.py:668
  464.5 24.0 %collective-permute-start.23 = (bf16[512,1024]{1,0:T(8,128)(2,1)}, bf16[512,1024]{1,0:T(8,128)(2,1)S(1)}, u32[]{:S(2)}, u32[]{:S(2)}) collective-permute-start(bf16[512,1024]{1,0:T(8,128)(2,1)} %add_convert_fusion.3), channel_id=1, source_target_pairs={{0,8},{4,12},{8,16},{12,20},{16,24},{20,28},{24,0},{28,4},{1,9},{5... | collective-permute-start | bytes 3145736 | tf_op jit(solution)/shard_map/ppermute | solution.py:668
  489.8 35.9 %collective-permute-start.24 = (bf16[512,1024]{1,0:T(8,128)(2,1)S(1)}, bf16[512,1024]{1,0:T(8,128)(2,1)S(1)}, u32[]{:S(2)}, u32[]{:S(2)}) collective-permute-start(bf16[512,1024]{1,0:T(8,128)(2,1)S(1)} %constant_dynamic-slice_fusion.5), channel_id=1, source_target_pairs={{0,8},{4,12},{8,16},{12,20},{16,24},{20,28},{24,0},{28,4},{1,9},{5... | collective-permute-start | bytes 3145736 | tf_op jit(solution)/shard_map/ppermute | solution.py:668
  498.2 27.6 %collective-permute-start.25 = (bf16[256,1024]{1,0:T(8,128)(2,1)S(1)}, bf16[256,1024]{1,0:T(8,128)(2,1)S(1)}, u32[]{:S(2)}, u32[]{:S(2)}) collective-permute-start(bf16[256,1024]{1,0:T(8,128)(2,1)S(1)} %dynamic-slice_convert_fusion.1), channel_id=1, source_target_pairs={{0,4},{4,0},{8,12},{12,8},{16,20},{20,16},{24,28},{28,24},{1,5},{5... | collective-permute-start | bytes 1572872 | tf_op jit(solution)/shard_map/ppermute | solution.py:576
  532.6 30.7 %collective-permute-start.33 = (bf16[512,1024]{1,0:T(8,128)(2,1)S(1)}, bf16[512,1024]{1,0:T(8,128)(2,1)S(1)}, u32[]{:S(2)}, u32[]{:S(2)}) collective-permute-start(bf16[512,1024]{1,0:T(8,128)(2,1)S(1)} %add_convert_fusion.2), channel_id=1, source_target_pairs={{0,8},{4,12},{8,16},{12,20},{16,24},{20,28},{24,0},{28,4},{1,9},{5... | collective-permute-start | bytes 3145736 | tf_op jit(solution)/shard_map/ppermute | solution.py:668
  540.1 22.0 %collective-permute-start.28 = (bf16[256,1024]{1,0:T(8,128)(2,1)S(1)}, bf16[256,1024]{1,0:T(8,128)(2,1)S(1)}, u32[]{:S(2)}, u32[]{:S(2)}) collective-permute-start(bf16[256,1024]{1,0:T(8,128)(2,1)S(1)} %get-tuple-element.550), channel_id=1, source_target_pairs={{0,2},{1,3},{2,0},{3,1},{4,6},{5,7},{6,4},{7,5},{8,10},{9,11},{10,... | collective-permute-start | bytes 1572872 | tf_op jit(solution)/shard_map/ppermute | solution.py:935
  541.5 21.9 %collective-permute-start.27 = (bf16[256,1024]{1,0:T(8,128)(2,1)S(1)}, bf16[256,1024]{1,0:T(8,128)(2,1)S(1)}, u32[]{:S(2)}, u32[]{:S(2)}) collective-permute-start(bf16[256,1024]{1,0:T(8,128)(2,1)S(1)} %get-tuple-element.551), channel_id=1, source_target_pairs={{0,4},{4,0},{8,12},{12,8},{16,20},{20,16},{24,28},{28,24},{1,5},{5... | collective-permute-start | bytes 1572872 | tf_op jit(solution)/shard_map/ppermute | solution.py:576
  563.8 26.3 %collective-permute-start.35 = (bf16[512,1024]{1,0:T(8,128)(2,1)S(1)}, bf16[512,1024]{1,0:T(8,128)(2,1)S(1)}, u32[]{:S(2)}, u32[]{:S(2)}) collective-permute-start(bf16[512,1024]{1,0:T(8,128)(2,1)S(1)} %add_convert_fusion.1), channel_id=1, source_target_pairs={{0,8},{4,12},{8,16},{12,20},{16,24},{20,28},{24,0},{28,4},{1,9},{5... | collective-permute-start | bytes 3145736 | tf_op jit(solution)/shard_map/ppermute | solution.py:668
  564.9 34.6 %collective-permute-start.30 = (bf16[256,2048]{1,0:T(8,128)(2,1)S(1)}, bf16[256,2048]{1,0:T(8,128)(2,1)}, u32[]{:S(2)}, u32[]{:S(2)}) collective-permute-start(bf16[256,2048]{1,0:T(8,128)(2,1)S(1)} %pad_maximum_fusion.3), channel_id=1, source_target_pairs={{0,4},{4,0},{8,12},{12,8},{16,20},{20,16},{24,28},{28,24},{1,5},{5... | collective-permute-start | bytes 3145736 | tf_op jit(solution)/shard_map/ppermute | solution.py:576
  565.8 33.6 %collective-permute-start.31 = (bf16[256,2048]{1,0:T(8,128)(2,1)S(1)}, bf16[256,2048]{1,0:T(8,128)(2,1)}, u32[]{:S(2)}, u32[]{:S(2)}) collective-permute-start(bf16[256,2048]{1,0:T(8,128)(2,1)S(1)} %pad_maximum_fusion.4), channel_id=1, source_target_pairs={{0,2},{1,3},{2,0},{3,1},{4,6},{5,7},{6,4},{7,5},{8,10},{9,11},{10,... | collective-permute-start | bytes 3145736 | tf_op jit(solution)/shard_map/ppermute | solution.py:935
  567.8 22.3 %collective-permute-start.34 = (f32[9728]{0:T(1024)S(1)}, f32[9728]{0:T(1024)S(1)}, u32[]{:S(2)}, u32[]{:S(2)}) collective-permute-start(f32[9728]{0:T(1024)S(1)} %pad_maximum_fusion.7), channel_id=1, source_target_pairs={{0,4},{4,0},{8,12},{12,8},{16,20},{20,16},{24,28},{28,24},{1,5},{5... | collective-permute-start | bytes 116744 | tf_op jit(solution)/shard_map/ppermute | solution.py:699
  (46 other events, 473.7 us)
Sparse Core Ops, SparseCore 0:
  21.1 68.8 all-gather.4
  92.5 55.5 all-gather.6
  149.9 54.3 all-gather.8
  206.1 54.3 all-gather.10
  335.2 127.4 reduce-scatter.2
  488.7 80.0 reduce-scatter.4

commit v5 on v4

--- a/solution.py
+++ b/solution.py
@@ -17,17 +17,6 @@
 BF = jnp.bfloat16
 F32 = jnp.float32
 VMEM_LIMIT = 56 * 1024 * 1024
-
-
-def layer_norm(resid_rows, gain_vec, shift_vec):
-    row_mean = jnp.mean(resid_rows, axis=-1, keepdims=True)
-    centred = resid_rows - row_mean
-    row_var = jnp.mean(centred * centred, axis=-1, keepdims=True)
-    return centred * lax.rsqrt(row_var + norm_epsilon) * gain_vec + shift_vec
-
-
-def gelu_tanh(inner):
-    return 0.5 * inner * (1.0 + jnp.tanh(gelu_factor * (inner + 0.044715 * inner * inner * inner)))
 
 
 def rotary_tables(length, head_dim, rot_dim):
@@ -241,20 +230,37 @@
     )(slots, *ins)
 
 
-def norm_qkv(slots, rows, gain, shift, parts, bias):
-    tokens, width = rows.shape
-    cols, tile = bias.shape[1], 256
-
-    def kernel(slots_ref, rows_ref, gain_ref, shift_ref, bias_ref, *refs):
-        parts, (normed_ref, qkv_ref, stat_ref) = refs[:-3], refs[-3:]
-        vals = rows_ref[...].astype(F32)
+def normalise(rows):
+    micros, tokens, width = rows.shape
+
+    def kernel(rows_ref, out_ref):
+        vals = rows_ref[0].astype(F32)
         mean = jnp.mean(vals, axis=-1, keepdims=True)
         centred = vals - mean
         var = jnp.mean(centred * centred, axis=-1, keepdims=True)
-        scale = lax.rsqrt(var + norm_epsilon)
-        normed_ref[...] = (centred * scale * gain_ref[...] + shift_ref[...]).astype(BF)
-        lane_ids = lax.broadcasted_iota(jnp.int32, (tile, LANES), 1)
-        stat_ref[...] = jnp.where(lane_ids == 0, mean, scale)
+        out_ref[...] = (centred * lax.rsqrt(var + norm_epsilon)).astype(BF)
+
+    def one(micro):
+        return pl.pallas_call(
+            kernel,
+            grid=(2,),
+            in_specs=[pl.BlockSpec((1, tokens // 2, width), lambda i: (micro, i, 0))],
+            out_specs=pl.BlockSpec((tokens // 2, width), lambda i: (i, 0)),
+            out_shape=jax.ShapeDtypeStruct((tokens, width), BF),
+            compiler_params=pltpu.CompilerParams(vmem_limit_bytes=VMEM_LIMIT),
+            cost_estimate=estimate(10 * tokens * width, 4 * tokens * width),
+        )(rows)
+
+    return [one(micro) for micro in range(micros)]
+
+
+def norm_qkv(slots, rows, gain, shift, parts, bias):
+    tokens, width = rows.shape
+    cols, tile = bias.shape[1], 512
+
+    def kernel(slots_ref, rows_ref, gain_ref, shift_ref, bias_ref, *refs):
+        parts, (normed_ref, qkv_ref) = refs[:-2], refs[-2:]
+        normed_ref[...] = (rows_ref[...].astype(F32) * gain_ref[...] + shift_ref[...]).astype(BF)
         qkv_ref[...] = lined_dot(slots_ref, normed_ref, parts, slice(0, cols)) + bias_ref[...]
 
     return rows_call(
@@ -262,11 +268,7 @@
         slots,
         [rows, gain, shift, bias, *parts],
         [spec_rows(tile, width)] + [spec_whole(array) for array in (gain, shift, bias, *parts)],
-        [
-            jax.ShapeDtypeStruct((tokens, width), BF),
-            jax.ShapeDtypeStruct((tokens, cols), F32),
-            jax.ShapeDtypeStruct((tokens, LANES), F32),
-        ],
+        [jax.ShapeDtypeStruct((tokens, width), BF), jax.ShapeDtypeStruct((tokens, cols), F32)],
         tile,
         estimate(2 * tokens * width * cols, tokens * (4 * width + 4 * cols)),
     )
@@ -292,12 +294,12 @@
                     span = slice(at, at + chunk)
                     pre = lined_dot(slots_ref, ins[micro], parts, span) + bias_ref[:, span]
                     square = pre * pre
-                    tanh = jnp.tanh(gelu_factor * (pre * (1.0 + 0.044715 * square)))
-                    half = 0.5 * (1.0 + tanh)
-                    outs[micro][:, span] = (pre * half).astype(BF)
-                    inner = gelu_factor * (1.0 + 3 * 0.044715 * square)
-                    slope = half + 0.5 * pre * (1.0 - tanh * tanh) * inner
-                    outs[count + micro][:, span] = slope.astype(BF)
+                    tanh = jnp.tanh(pre * (gelu_factor + (gelu_factor * 0.044715) * square))
+                    half = 0.5 + 0.5 * tanh
+                    act = pre * half
+                    outs[micro][:, span] = act.astype(BF)
+                    inner = 2 * gelu_factor + (6 * 0.044715 * gelu_factor) * square
+                    outs[count + micro][:, span] = (half + (act - act * half) * inner).astype(BF)
 
     outs = rows_call(
         kernel,
@@ -408,13 +410,13 @@
     )[0]
 
 
-def normed_grad_rows(slots, one, one_parts, two, two_parts, rows, stats, block, split):
+def normed_grad_rows(slots, one, one_parts, two, two_parts, rows, block, split):
     tokens, cols = one.shape
     count, depth = len(one_parts), one_parts[0].shape[0]
     tile = 2 * block
     width = count * depth
 
-    def kernel(slots_ref, one_ref, two_ref, rows_ref, stat_ref, *refs):
+    def kernel(slots_ref, one_ref, two_ref, rows_ref, *refs):
         outs, sum_ref = refs[2 * count : -1], refs[-1]
 
         @pl.when(pl.program_id(0) == 0)
@@ -432,16 +434,15 @@
                 outs[1][:, span] = jnp.where(first, total[block:], total[:block]).astype(BF)
             else:
                 outs[0][:, span] = total.astype(BF)
-            scaled = (rows_ref[:, span].astype(F32) - stat_ref[:, 0:1]) * stat_ref[:, 1:2]
-            sum_ref[0:1, span] += jnp.sum(total * scaled, axis=0, keepdims=True)
+            sum_ref[0:1, span] += jnp.sum(total * rows_ref[:, span].astype(F32), axis=0, keepdims=True)
             sum_ref[1:2, span] += jnp.sum(total, axis=0, keepdims=True)
 
     pieces = 2 if split else 1
     return rows_call(
         kernel,
         slots,
-        [one, two, rows, stats, *one_parts, *two_parts],
-        [spec_rows(tile, cols), spec_rows(tile, two.shape[1]), spec_rows(tile, width), spec_rows(tile, LANES)]
+        [one, two, rows, *one_parts, *two_parts],
+        [spec_rows(tile, cols), spec_rows(tile, two.shape[1]), spec_rows(tile, width)]
         + [spec_whole(part) for part in (*one_parts, *two_parts)],
         [jax.ShapeDtypeStruct((tokens // pieces, width), BF)] * pieces + [jax.ShapeDtypeStruct((8, width), F32)],
         tile,
@@ -453,7 +454,7 @@
 
 def norm_back(rows, cots, pieces, gain, micro, earlier=None):
     micros, tokens, width = rows.shape
-    tile = tokens // 2
+    tile = tokens // 4
 
     def kernel(rows_ref, cot_ref, gain_ref, *refs):
         vals = rows_ref[0].astype(F32)
@@ -485,16 +486,15 @@
     )(rows, cots, gain, *pieces, *given)
 
 
-def weight_grad(groups):
+def weight_grad(lefts, rights):
     tile, chunk = 512, 512
-    micro_count = len(groups[0][0])
-    tokens, width = groups[0][0][0].shape
-    widths = [rights[0].shape[1] for _, rights in groups]
+    micro_count = len(lefts)
+    tokens, width = lefts[0].shape
+    widths = [right[0].shape[1] for right in rights]
     cols, steps = sum(widths), tokens // tile
-    arrays = [array for lefts, rights in groups for array in (*lefts, *rights)]
 
     def kernel(*refs):
-        ins, out_ref, acc_ref = refs[: len(arrays)], refs[-2], refs[-1]
+        out_ref, acc_ref = refs[-2:]
         step = pl.program_id(0)
 
         @pl.when(step == 0)
@@ -507,11 +507,10 @@
             def _():
                 first = 0
                 for at, span in enumerate(widths):
-                    left = ins[2 * micro_count * at + micro]
-                    right = ins[2 * micro_count * at + micro_count + micro]
+                    right = refs[(1 + at) * micro_count + micro]
                     for row in range(0, width, chunk):
                         acc_ref[row : row + chunk, first : first + span] += dot_rows(
-                            left[:, row : row + chunk], right[...]
+                            refs[micro][:, row : row + chunk], right[...]
                         )
                     first += span
 
@@ -522,22 +521,18 @@
     def side(micro, span):
         return pl.BlockSpec((tile, span), lambda i: (jnp.clip(i - micro * steps, 0, steps - 1), 0))
 
-    in_specs = []
-    for span in widths:
-        in_specs += [side(micro, width) for micro in range(micro_count)]
-        in_specs += [side(micro, span) for micro in range(micro_count)]
     return pl.pallas_call(
         kernel,
         grid=(micro_count * steps,),
-        in_specs=in_specs,
+        in_specs=[side(micro, span) for span in (width, *widths) for micro in range(micro_count)],
         out_specs=pl.BlockSpec((width, cols), lambda i: (0, 0)),
         out_shape=jax.ShapeDtypeStruct((width, cols), BF),
         scratch_shapes=[pltpu.VMEM((width, cols), F32)],
         compiler_params=pltpu.CompilerParams(vmem_limit_bytes=VMEM_LIMIT),
         cost_estimate=estimate(
-            2 * micro_count * tokens * width * cols, 2 * micro_count * tokens * (len(groups) * width + cols)
+            2 * micro_count * tokens * width * cols, 2 * micro_count * tokens * (width + cols)
         ),
-    )(*arrays)
+    )(*lefts, *(array for right in rights for array in right))
 
 
 def shards(
@@ -704,27 +699,30 @@
                 self.move()
             return self.cur.val[: self.size], self.cur.val[self.size :]
 
-    resid = [inputs[m].reshape(token_rows, model_width) for m in range(micro_count)]
+    plain = normalise(inputs[:, 0])
     cots = [cotangent[m].reshape(token_rows, model_width) for m in range(micro_count)]
     micros = range(micro_count)
     plane_rows, plane_cots = [None] * micro_count, [None] * micro_count
+
+    def gather_behind(rows):
+        sent = Box(rows)
+        order.tie(sent)
+        return Box(gather_plane(sent.val))
 
     small = jnp.concatenate(
         [vec.reshape(-1) for vec in (ln_gain, ln_bias, out_bias, down_bias, qkv_bias, up_bias)]
     )
     attn_send = Box(attn_half(1 - pair_at))
+    order.tokens = [attn_send]
+    plane_rows[0] = gather_behind(plain[0])
+    attn_shard = Box(pair_join(attn_half(pair_at), swap_pair(attn_send.val)))
     small_all = Box(small[None])
-    order.tokens = []
-    order.tie(small_all, attn_send)
+    order.tokens = [attn_shard]
+    order.tie(small_all)
     small_all = small_all.val
     for bit in range(tp_size.bit_length() - 1):
         small_all = doubled(small_all, "tp", tp_size, tp_at, 1 << bit)
     small_near = small_all
-
-    def gather_behind(rows):
-        sent = Box(rows)
-        order.tie(sent)
-        return Box(gather_plane(sent.val))
 
     def small_step(small_all, bit):
         if bit < fsdp_size.bit_length() - 1:
@@ -733,13 +731,10 @@
         return small_all
 
     small_all = Box(small_near)
-    order.tokens = [small_all]
-    plane_rows[0] = gather_behind(resid[0])
-    attn_shard = Box(pair_join(attn_half(pair_at), swap_pair(attn_send.val)))
-    order.tokens = [attn_shard, small_all]
     attn_ring = Gather(attn_shard)
     attn_ring.move()
-    plane_rows[1] = gather_behind(resid[1])
+    plane_rows[1] = gather_behind(plain[1])
+    order.sync(small_all)
     small_all = small_step(small_all, 0)
     bias_total = Box(sum(jnp.sum(cots[m].astype(F32), axis=0) for m in micros))
     up_send = Box(up_half(1 - pair_at))
@@ -788,11 +783,11 @@
     slots = jnp.stack(slots + [tp_at & 1]).astype(jnp.int32)
     tables = rotary_tables(length, head_dim, ROT)
     gain_row, shift_row = gain_vec[None], shift_vec[None]
-    normed, qkvs, stats, rots, attns, lses, acts, slopes = ([None] * micro_count for _ in range(8))
+    normed, qkvs, rots, attns, lses, acts, slopes = ([None] * micro_count for _ in range(7))
     pre_grads, qkv_grads, qkv_sums, sums, attn_heads = ([None] * micro_count for _ in range(5))
 
     def norm_piece(m):
-        normed[m], qkvs[m], stats[m] = order.run(
+        normed[m], qkvs[m] = order.run(
             lambda rows: norm_qkv(slots, rows, gain_row, shift_row, attn_ring.vals(), qkv_b), plane_rows[m]
         )
 
@@ -829,21 +824,12 @@
         *pre_grads[:], up_sums = order.run(piece, *plane_cots, *slopes)
         return up_sums
 
-    def weight_piece(*groups):
-        flat = [box for lefts, rights in groups for box in (*lefts, *rights)]
-
+    def weight_piece(lefts, *rights):
         def piece(*flat):
-            count = 2 * micro_count
-            return [
-                weight_grad(
-                    [
-                        (flat[at : at + micro_count], flat[at + micro_count : at + count])
-                        for at in range(0, len(flat), count)
-                    ]
-                )
-            ]
-
-        return Scatter(order.run(piece, *flat)[0])
+            sets = [flat[at : at + micro_count] for at in range(0, len(flat), micro_count)]
+            return [weight_grad(sets[0], sets[1:])]
+
+        return Scatter(order.run(piece, *lefts, *(box for right in rights for box in right))[0])
 
     def branch_piece():
         def piece(*vals):
@@ -862,13 +848,12 @@
 
     def normed_grad_piece(m, split=False):
         *back, sums[m] = order.run(
-            lambda one, two, rows, stat: normed_grad_rows(
-                slots, one, attn_ring.vals(), two, up_ring.vals(), rows, stat, token_rows, split
+            lambda one, two, rows: normed_grad_rows(
+                slots, one, attn_ring.vals(), two, up_ring.vals(), rows, token_rows, split
             ),
             qkv_grads[m],
             pre_grads[m],
             plane_rows[m],
-            stats[m],
         )
         return back
 
@@ -898,7 +883,7 @@
     down_ring.sync()
     down_ring.move()
 
-    down_scatter = weight_piece((plane_cots, acts))
+    down_scatter = weight_piece(plane_cots, acts, attns)
     down_ring.finish()
     down_scatter.move()
     branch = branch_piece()
@@ -908,7 +893,7 @@
     up_sums = pre_grad_piece()
     down_scatter.sync()
     down_scatter.move()
-    up_scatter = weight_piece((normed, pre_grads))
+    up_scatter = weight_piece(normed, pre_grads)
     down_scatter.sync()
     down_scatter.swap()
     up_scatter.move()
@@ -917,15 +902,15 @@
     up_scatter.sync()
     order.sync(down_scatter.got)
     up_scatter.move()
-    attn_scatter = weight_piece((normed, qkv_grads), (plane_cots, attns))
-    up_scatter.sync()
-    up_scatter.move()
     (back,) = normed_grad_piece(0)
     up_scatter.sync()
     order.sync(branch_sum)
     back_sum = scatter_behind(back)
+    up_scatter.move()
+    qkv_scatter = weight_piece(normed, qkv_grads)
+    up_scatter.sync()
     up_scatter.swap()
-    attn_scatter.move()
+    qkv_scatter.move()
     keep, give = normed_grad_piece(1, True)
 
     def swap_core(vals):
@@ -935,12 +920,6 @@
         return lax.ppermute(vals, "tp", [(t, t ^ 2) for t in range(tp_size)])
 
     y_at, half = tp_at >> 1, model_width // 2
-    attn_scatter.sync()
-    order.sync(up_scatter.got)
-    order.tie(give)
-    got = Box(swap_core(give.val))
-    attn_scatter.move()
-
     up_b_grad = up_sums.val[0]
     qkv_b_grad = sum(jnp.sum(part.val.reshape(-1, 8, qkv_cols)[:, 0], axis=0) for part in qkv_sums)
     qkv_b_grad = qkv_b_grad.reshape(pairs, 3, -1).transpose(1, 0, 2).reshape(3, attn_cols)
@@ -956,17 +935,31 @@
         jnp.concatenate([gain_total, shift_total, bias_total.val]),
         jnp.concatenate([in_half(up_b_grad), in_half(qkv_b_grad).reshape(-1)]),
     )
+    qkv_scatter.sync()
+    order.sync(up_scatter.got)
+    order.tie(give, tail.cur)
+    tail.move()
+    got = Box(swap_core(give.val))
+    qkv_scatter.move()
+    order.sync(tail.cur)
     order.tie(got)
     blocks = Box((got.val.astype(F32) + keep.val.astype(F32)).astype(BF).reshape(4, token_rows, model_width))
-    order.sync(blocks)
+    tail.move()
 
     def block(pair, y):
         return lax.dynamic_index_in_dim(blocks.val, pair * 2 + y, 0, keepdims=False)
 
+    order.sync(blocks)
+    order.sync(tail.cur)
+    order.tie(tail.cur)
     far = block(1 - pair_at, 1 - y_at)
+    tail.move()
     from_pair, from_y = Box(swap_pair(far[:, :half])), Box(swap_y(far[:, half:]))
+    qkv_scatter.sync()
+    order.sync(tail.cur)
+    order.tie(tail.cur)
     tail.move()
-    tail.move()
+    qkv_scatter.move()
     order.tie(from_pair, from_y)
     for_y, for_pair = block(pair_at, 1 - y_at), block(1 - pair_at, y_at)
     for_y = jnp.concatenate(
@@ -975,26 +968,26 @@
     for_pair = jnp.concatenate(
         [for_pair[:, :half], (for_pair[:, half:].astype(F32) + from_y.val.astype(F32)).astype(BF)], axis=1
     )
-    from_pair, from_y = Box(swap_pair(for_pair)), Box(swap_y(for_y))
-    attn_scatter.sync()
-    attn_scatter.move()
+    for_pair, for_y = Box(for_pair), Box(for_y)
+    from_pair, from_y = Box(swap_pair(for_pair.val)), Box(swap_y(for_y.val))
+    order.sync(for_pair)
+    order.sync(for_y)
+    order.tie(back_sum)
+    gained = Box(norm_back(inputs[:, 0], cotangent[:, 0], [back_sum.val], gain_row, 0))
+    halves = down_scatter.halves()
+    down_w_grad = Box(jnp.concatenate([part[:, :mlp_cols].T for part in halves], axis=0))
+    out_w_grad = Box(jnp.concatenate([part[:, mlp_cols:].T for part in halves], axis=0))
+    up_w_grad = Box(jnp.concatenate(up_scatter.halves(), axis=1))
+    for box in (gained, down_w_grad, out_w_grad, up_w_grad, tail.cur):
+        order.sync(box)
+    qkv_scatter.sync()
+    order.tie(tail.cur)
     tail.move()
-    down_w_grad = Box(jnp.concatenate([part.T for part in down_scatter.halves()], axis=0))
-    up_w_grad = Box(jnp.concatenate(up_scatter.halves(), axis=1))
-    order.sync(down_w_grad)
-    order.sync(up_w_grad)
-    attn_scatter.sync()
-    attn_scatter.swap()
-    tail.move()
-    tail.move()
-    order.sync(tail.cur)
+    qkv_scatter.swap()
     order.tie(from_pair, from_y)
-    gained = norm_back(
-        inputs[:, 0], cotangent[:, 0], [block(pair_at, y_at), from_pair.val, from_y.val], gain_row, 1,
-        norm_back(inputs[:, 0], cotangent[:, 0], [back_sum.val], gain_row, 0),
-    )
+    last_pieces = [block(pair_at, y_at), from_pair.val, from_y.val]
+    gained = norm_back(inputs[:, 0], cotangent[:, 0], last_pieces, gain_row, 1, gained.val)
     small_sums, bias_sums = tail.split()
-    attn_grads = attn_scatter.halves()
     branch_sum = branch_sum.val.reshape(micro_count, token_rows, model_width)
     output = (inputs[:, 0].astype(F32) + branch_sum.astype(F32) + bias_both).astype(BF)
 
@@ -1007,12 +1000,11 @@
     qkv_b_sum = lax.dynamic_slice_in_dim(qkv_b_sum, fsdp_at * qkv_bias.shape[2], qkv_bias.shape[2], axis=2)
 
     def qkv_columns(vals):
-        return vals[:, :qkv_cols].reshape(shard_rows, pairs, 3, LANES).transpose(0, 2, 1, 3).reshape(
+        return vals.reshape(shard_rows, pairs, 3, LANES).transpose(0, 2, 1, 3).reshape(
             shard_rows, 3, attn_cols
         )
 
-    qkv_w_grad = jnp.concatenate([qkv_columns(half) for half in attn_grads], axis=2)
-    out_w_grad = jnp.concatenate([half[:, qkv_cols:].T for half in attn_grads], axis=0)
+    qkv_w_grad = jnp.concatenate([qkv_columns(part) for part in qkv_scatter.halves()], axis=2)
     return (
         output[:, None],
         gained[:, None],
@@ -1020,7 +1012,7 @@
         shift_sum,
         qkv_w_grad,
         qkv_b_sum,
-        out_w_grad,
+        out_w_grad.val,
         bias_sum,
         up_w_grad.val,
         up_b_sum,

time: 634 us -> 620 us (0.978)
  starting transfers between devices: 53.6 us -> 42.8 us
  Pallas kernels: 362 us -> 354 us
  local copies, waits for them, and re-layouts: 44.2 us -> 36.7 us
  other arithmetic: 35.7 us -> 42.4 us
    ppermute x5, waiting for transfers between devices: 42.4 us -> 16.5 us  [move(): lax.ppermute(self.cur.val, axis, [(i, i ^ 1 << bit) for i in range(size)])]
    ppermute x9, waiting for transfers between devices: 0.02 us -> 18.7 us  [move(): self.came = Box(lax.ppermute(sent.val, 'fsdp', ring))]
    pallas_call x9, Pallas kernels: 199 us -> 186 us  [rows_call(): pl.pallas_call(kernel, grid_spec=pltpu.PrefetchScalarGridSpec(num_scalar_...]
    ppermute x9, starting transfers between devices: 12.7 us -> 6.21 us  [move(): self.came = Box(lax.ppermute(sent.val, 'fsdp', ring))]
    ppermute x5, waiting for transfers between devices: 8.25 us -> 14.8 us  [doubled(): other = lax.ppermute(cur, axis, [(i, i ^ bit) for i in range(size)])]
    pallas_call x3 -> x5, Pallas kernels: 79.5 us -> 83.2 us  [the longest x3 78.1 us: weight_grad(): pl.pallas_call(kernel, grid=(micro_count * steps,), in_specs=[side(micro,...]
    unnamed x79 -> x85, local copies, waits for them, and re-layouts: 14.9 us -> 12.1 us
  transfers between devices with their start and end apart: 45 -> 45, of which waited for: 17 -> 20; matrix products, arithmetic and copies ran while one was open for 10% -> 11% of each run, Pallas kernels for 56% -> 58%
where the time goes in v5:
time: 620 us; the launch traced here: 612 us
  Pallas kernels  354 us (57%)
  waiting for transfers between devices  120 us (19%)
  starting transfers between devices  42.8 us (7%)
  other arithmetic  42.4 us (7%)
  local copies, waits for them, and re-layouts  36.7 us (6%)
  between operations  15.4 us (2%)
    pallas_call x9, Pallas kernels, rows_call(): pl.pallas_call(kernel, grid_spec=pltpu.PrefetchScalarGridSpec(num_scalar_...  186 us
    pallas_call x3, Pallas kernels, weight_grad(): pl.pallas_call(kernel, grid=(micro_count * steps,), in_specs=[side(micro,...  78.1 us
    pallas_call x2, Pallas kernels, attend_back(): pl.pallas_call(functools.partial(attend_back_kernel, head_dim, block), gr...  42.2 us
    ppermute x8, waiting for transfers between devices, swap_pair(): return lax.ppermute(vals, 'fsdp', [(f, f ^ 1) for f in range(fsdp_size)])  34.3 us
    pallas_call x2, Pallas kernels, attend(): pl.pallas_call(functools.partial(attend_kernel, head_dim, block), grid=(s...  32.8 us
    ppermute x9, waiting for transfers between devices, move(): self.parts.append(Box(lax.ppermute(self.parts[-1].val, 'fsdp', ring)))  24.5 us
    ppermute x9, waiting for transfers between devices, move(): self.came = Box(lax.ppermute(sent.val, 'fsdp', ring))  18.7 us
    ppermute x5, waiting for transfers between devices, move(): lax.ppermute(self.cur.val, axis, [(i, i ^ 1 << bit) for i in range(size)])  16.5 us
  transfers between devices with their start and end apart: 45, of which 20 were waited for; matrix products, arithmetic and copies ran while one was open for 11% of the time, Pallas kernels for 58%

profile of v5, /device:TPU:0, one launch (start us, length us, event | category | flops | bytes accessed | tf_op | source)
XLA Modules:
  0.0 612.0 jit_solution(7615094341008759224)
XLA Ops:
  19.2 11.8 %collective-permute-done = bf16[256,1024]{1,0:T(8,128)(2,1)S(1)} collective-permute-done((bf16[256,1024]{1,0:T(8,128)(2,1)S(1)}, bf16[256,1024]{1,0:T(8,128)(2,1)S(1)}, u32[]{:S(2)}, u32[]{:S(2)}) %collective-permute-start) | collective-permute-done | bytes 524320 | tf_op jit(solution)/shard_map/ppermute | solution.py:571
  43.9 13.3 %collective-permute-done.4.refs_1_.refs_5_ = bf16[512,1024]{1,0:T(8,128)(2,1)S(1)} collective-permute-done((bf16[512,1024]{1,0:T(8,128)(2,1)S(1)}, bf16[512,1024]{1,0:T(8,128)(2,1)S(1)}, u32[]{:S(2)}, u32[]{:S(2)}) %collective-permute-start.4) | collective-permute-done | bytes 1048608 | tf_op jit(solution)/shard_map/ppermute | solution.py:633
  66.8 15.0 %collective-permute-done.3 = bf16[256,1024]{1,0:T(8,128)(2,1)} collective-permute-done((bf16[256,1024]{1,0:T(8,128)(2,1)}, bf16[256,1024]{1,0:T(8,128)(2,1)}, u32[]{:S(2)}, u32[]{:S(2)}) %collective-permute-start.3) | collective-permute-done | bytes 524320 | tf_op jit(solution)/shard_map/ppermute | solution.py:571
  89.6 4.9 collective-permute-done.6
  97.2 11.0 %collective-permute-done.10 = bf16[16,704]{1,0:T(8,128)(2,1)S(1)} collective-permute-done((bf16[16,704]{1,0:T(8,128)(2,1)S(1)}, bf16[16,704]{1,0:T(8,128)(2,1)S(1)}, u32[]{:S(2)}, u32[]{:S(2)}) %collective-permute-start.10) | collective-permute-done | bytes 22560 | tf_op jit(solution)/shard_map/ppermute | solution.py:580
  111.7 16.6 %shard_map.213 = (bf16[2048,2048]{1,0:T(8,128)(2,1)}, f32[2048,768]{1,0:T(8,128)}) custom-call(s32[5]{0:T(128)} %stack.23.slots_ref, bf16[2048,2048]{1,0:T(8,128)(2,1)} %all-gather.5.cloned.1.call-done.rows_ref, f32[1,2048]{1,0:T(1,128)} %reshape.216.gain_ref, f32[1,2048]{1,0:T(1,128)} %reshape.217.shift_ref, f32[1,768]{1,0:T(1,128)} %reshape.202.bias_ref, ...), custom_call_target="tpu_custom_call" | custom-call | flops 100663296 | bytes 360448 | tf_op jit(solution)/shard_map/pallas_call | solution.py:219
  128.3 6.9 %collective-permute-done.11.refs_3_.refs_5_ = bf16[512,1024]{1,0:T(8,128)(2,1)S(1)} collective-permute-done((bf16[512,1024]{1,0:T(8,128)(2,1)S(1)}, bf16[512,1024]{1,0:T(8,128)(2,1)S(1)}, u32[]{:S(2)}, u32[]{:S(2)}) %collective-permute-start.11) | collective-permute-done | bytes 1048608 | tf_op jit(solution)/shard_map/ppermute | solution.py:633
  139.4 16.3 %shard_map.214 = (bf16[2048,768]{1,0:T(8,128)(2,1)}, bf16[2048,256]{1,0:T(8,128)(2,1)}, f32[4,2,1024]{2,1,0:T(2,128)}) custom-call(f32[2048,768]{1,0:T(8,128)} %get-tuple-element.349.qkv_ref, f32[1024,128]{1,0:T(8,128)} %copy.78.cos_ref, f32[1024,128]{1,0:T(8,128)} %copy.79.low_ref, f32[1024,128]{1,0:T(8,128)} %copy.80.up_ref), custom_call_target="tpu_custom_call" | custom-call | flops 100663296 | bytes 131072 | tf_op jit(solution)/shard_map/pallas_call | solution.py:150
  155.6 16.1 %shard_map.215 = (bf16[2048,2048]{1,0:T(8,128)(2,1)}, f32[2048,768]{1,0:T(8,128)}) custom-call(s32[5]{0:T(128)} %stack.23.slots_ref, bf16[2048,2048]{1,0:T(8,128)(2,1)} %all-gather.7.cloned.1.call-done.rows_ref, f32[1,2048]{1,0:T(1,128)} %reshape.216.gain_ref, f32[1,2048]{1,0:T(1,128)} %reshape.217.shift_ref, f32[1,768]{1,0:T(1,128)} %reshape.202.bias_ref, ...), custom_call_target="tpu_custom_call" | custom-call | flops 100663296 | bytes 360448 | tf_op jit(solution)/shard_map/pallas_call | solution.py:219
  171.8 16.6 %shard_map.216 = (bf16[2048,768]{1,0:T(8,128)(2,1)}, bf16[2048,256]{1,0:T(8,128)(2,1)}, f32[4,2,1024]{2,1,0:T(2,128)}) custom-call(f32[2048,768]{1,0:T(8,128)} %get-tuple-element.359.qkv_ref, f32[1024,128]{1,0:T(8,128)} %copy.78.cos_ref, f32[1024,128]{1,0:T(8,128)} %copy.79.low_ref, f32[1024,128]{1,0:T(8,128)} %copy.80.up_ref), custom_call_target="tpu_custom_call" | custom-call | flops 100663296 | bytes 131072 | tf_op jit(solution)/shard_map/pallas_call | solution.py:150
  188.4 6.7 %all-gather.9.cloned.1.call-done.rows_ref.refs_0_ = bf16[2048,2048]{1,0:T(8,128)(2,1)} async-done(((bf16[256,2048]{1,0:T(8,128)(2,1)}), bf16[2048,2048]{1,0:T(8,128)(2,1)}) %all-gather.9.cloned.1.call-update) | async-done | bytes 8388624 | tf_op jit(solution)/shard_map/all_gather | solution.py:574
  195.1 7.6 %shard_map.217.grad_ref = bf16[2048,256]{1,0:T(8,128)(2,1)} custom-call(s32[5]{0:T(128)} %stack.23.slots_ref, bf16[2048,2048]{1,0:T(8,128)(2,1)} %all-gather.9.cloned.1.call-done.rows_ref.refs_0_, bf16[512,1024]{1,0:T(8,128)(2,1)} %copy-done, bf16[512,1024]{1,0:T(8,128)(2,1)} %copy-done.2, bf16[512,1024]{1,0:T(8,128)(2,1)} %copy-done.3, ...), custom_call_target="tpu_custom_call" | custom-call | flops 33554432 | bytes 147456 | tf_op jit(solution)/shard_map/pallas_call | solution.py:219
  205.7 32.4 %shard_map.218 = (bf16[2048,1024]{1,0:T(8,128)(2,1)}, bf16[2048,1024]{1,0:T(8,128)(2,1)}, bf16[2048,1024]{1,0:T(8,128)(2,1)}, bf16[2048,1024]{1,0:T(8,128)(2,1)}) custom-call(s32[5]{0:T(128)} %stack.23.slots_ref, f32[1,1024]{1,0:T(1,128)} %constant_dynamic-slice_fusion.8.bias_ref, bf16[2048,2048]{1,0:T(8,128)(2,1)} %get-tuple-element.452.refs_0_, ...), custom_call_target="tpu_custom_call" | custom-call | flops 268435456 | bytes 524288 | tf_op jit(solution)/shard_map/pallas_call | solution.py:219
  239.7 21.0 %shard_map.219 = (bf16[2048,768]{1,0:T(8,128)(2,1)}, f32[16,768]{1,0:T(8,128)}) custom-call(bf16[2048,768]{1,0:T(8,128)(2,1)} %get-tuple-element.383.rot_ref, bf16[2048,256]{1,0:T(8,128)(2,1)} %shard_map.217.grad_ref, bf16[2048,256]{1,0:T(8,128)(2,1)} %get-tuple-element.397.attn_ref.refs_4_.refs_0_, f32[4,2,1024]{2,1,0:T(2,128)} %get-tuple-element.385.lse_ref, ...), custom_call_target="tpu_custom_call" | custom-call | flops 201326592 | bytes 131072 | tf_op jit(solution)/shard_map/pallas_call | solution.py:175
  260.7 4.3 collective-permute-done.15.refs_10_.refs_6_
  265.3 30.7 %shard_map.220 = bf16[2048,1280]{1,0:T(8,128)(2,1)} custom-call(bf16[2048,2048]{1,0:T(8,128)(2,1)} %all-gather.9.cloned.1.call-done.rows_ref.refs_0_, bf16[2048,2048]{1,0:T(8,128)(2,1)} %all-gather.11.cloned.1.call-done.refs_1_.rows_ref, bf16[2048,1024]{1,0:T(8,128)(2,1)} %get-tuple-element.399.refs_2_, bf16[2048,1024]{1,0:T(8,128)(2,1)} %get-tuple-element.400.refs_3_, ...), custom_call_target="tpu_custom_call" | custom-call | flops 335544320 | bytes 425984 | tf_op jit(solution)/shard_map/pallas_call | solution.py:524
  298.5 30.3 %shard_map.221 = bf16[8,2,256,2048]{3,2,1,0:T(8,128)(2,1)} custom-call(s32[5]{0:T(128)} %stack.23.slots_ref, bf16[2048,256]{1,0:T(8,128)(2,1)} %get-tuple-element.397.attn_ref.refs_4_.refs_0_, bf16[2048,256]{1,0:T(8,128)(2,1)} %get-tuple-element.433.refs_5_.refs_1_.attn_ref, bf16[2048,1024]{1,0:T(8,128)(2,1)} %get-tuple-element.399.refs_2_, ...), custom_call_target="tpu_custom_call" | custom-call | flops 335544320 | bytes 294912 | tf_op jit(solution)/shard_map/pallas_call | solution.py:219
  331.6 27.0 %shard_map.222 = (bf16[2048,1024]{1,0:T(8,128)(2,1)}, bf16[2048,1024]{1,0:T(8,128)(2,1)}, f32[8,1024]{1,0:T(8,128)}) custom-call(s32[5]{0:T(128)} %stack.23.slots_ref, bf16[2048,2048]{1,0:T(8,128)(2,1)} %all-gather.9.cloned.1.call-done.rows_ref.refs_0_, bf16[2048,2048]{1,0:T(8,128)(2,1)} %all-gather.11.cloned.1.call-done.refs_1_.rows_ref, ...), custom_call_target="tpu_custom_call" | custom-call | flops 268435456 | bytes 524288 | tf_op jit(solution)/shard_map/pallas_call | solution.py:219
  358.6 3.6 collective-permute-done.18
  364.0 26.1 %shard_map.223 = bf16[2048,1024]{1,0:T(8,128)(2,1)} custom-call(bf16[2048,2048]{1,0:T(8,128)(2,1)} %get-tuple-element.452.refs_0_, bf16[2048,2048]{1,0:T(8,128)(2,1)} %get-tuple-element.453.refs_1_, bf16[2048,1024]{1,0:T(8,128)(2,1)} %get-tuple-element.441.refs_2_.two_ref, bf16[2048,1024]{1,0:T(8,128)(2,1)} %get-tuple-element.459.refs_3_.two_ref), custom_call_target="tpu_custom_call" | custom-call | flops 268435456 | bytes 393216 | tf_op jit(solution)/shard_map/pallas_call | solution.py:524
  390.0 4.2 collective-permute-done.19
  400.4 7.7 %shard_map.224.grad_ref = bf16[2048,256]{1,0:T(8,128)(2,1)} custom-call(s32[5]{0:T(128)} %stack.23.slots_ref, bf16[2048,2048]{1,0:T(8,128)(2,1)} %all-gather.11.cloned.1.call-done.refs_1_.rows_ref, bf16[512,1024]{1,0:T(8,128)(2,1)} %copy-done, bf16[512,1024]{1,0:T(8,128)(2,1)} %copy-done.2, bf16[512,1024]{1,0:T(8,128)(2,1)} %copy-done.3, ...), custom_call_target="tpu_custom_call" | custom-call | flops 33554432 | bytes 147456 | tf_op jit(solution)/shard_map/pallas_call | solution.py:219
  408.1 21.1 %shard_map.225 = (bf16[2048,768]{1,0:T(8,128)(2,1)}, f32[16,768]{1,0:T(8,128)}) custom-call(bf16[2048,768]{1,0:T(8,128)(2,1)} %get-tuple-element.431.rot_ref, bf16[2048,256]{1,0:T(8,128)(2,1)} %shard_map.224.grad_ref, bf16[2048,256]{1,0:T(8,128)(2,1)} %get-tuple-element.433.refs_5_.refs_1_.attn_ref, f32[4,2,1024]{2,1,0:T(2,128)} %get-tuple-element.434.lse_ref, ...), custom_call_target="tpu_custom_call" | custom-call | flops 201326592 | bytes 131072 | tf_op jit(solution)/shard_map/pallas_call | solution.py:175
  430.9 23.9 %shard_map.226 = (bf16[2048,2048]{1,0:T(8,128)(2,1)}, f32[8,2048]{1,0:T(8,128)}) custom-call(s32[5]{0:T(128)} %stack.23.slots_ref, bf16[2048,768]{1,0:T(8,128)(2,1)} %get-tuple-element.454.one_ref.refs_2_, bf16[2048,1024]{1,0:T(8,128)(2,1)} %get-tuple-element.441.refs_2_.two_ref, bf16[2048,2048]{1,0:T(8,128)(2,1)} %all-gather.5.cloned.1.call-done.rows_ref, ...), custom_call_target="tpu_custom_call" | custom-call | flops 234881024 | bytes 376832 | tf_op jit(solution)/shard_map/pallas_call | solution.py:219
  461.8 21.3 %shard_map.227 = bf16[2048,768]{1,0:T(8,128)(2,1)} custom-call(bf16[2048,2048]{1,0:T(8,128)(2,1)} %get-tuple-element.452.refs_0_, bf16[2048,2048]{1,0:T(8,128)(2,1)} %get-tuple-element.453.refs_1_, bf16[2048,768]{1,0:T(8,128)(2,1)} %get-tuple-element.454.one_ref.refs_2_, bf16[2048,768]{1,0:T(8,128)(2,1)} %get-tuple-element.458.refs_3_.one_ref), custom_call_target="tpu_custom_call" | custom-call | flops 201326592 | bytes 360448 | tf_op jit(solution)/shard_map/pallas_call | solution.py:524
  483.2 3.8 collective-permute-done.23
  492.8 24.7 %shard_map.228 = (bf16[1024,2048]{1,0:T(8,128)(2,1)}, bf16[1024,2048]{1,0:T(8,128)(2,1)}, f32[8,2048]{1,0:T(8,128)}) custom-call(s32[5]{0:T(128)} %stack.23.slots_ref, bf16[2048,768]{1,0:T(8,128)(2,1)} %get-tuple-element.458.refs_3_.one_ref, bf16[2048,1024]{1,0:T(8,128)(2,1)} %get-tuple-element.459.refs_3_.two_ref, ...), custom_call_target="tpu_custom_call" | custom-call | flops 234881024 | bytes 376832 | tf_op jit(solution)/shard_map/pallas_call | solution.py:219
  528.5 4.6 add_convert_fusion
  537.9 16.5 %collective-permute-done.31 = f32[9728]{0:T(1024)S(1)} collective-permute-done((f32[9728]{0:T(1024)S(1)}, f32[9728]{0:T(1024)S(1)}, u32[]{:S(2)}, u32[]{:S(2)}) %collective-permute-start.31) | collective-permute-done | bytes 38944 | tf_op jit(solution)/shard_map/ppermute | solution.py:694
  565.0 4.7 shard_map.229.refs_3_
  571.6 6.7 %collective-permute-done.36 = bf16[512,768]{1,0:T(8,128)(2,1)} collective-permute-done((bf16[512,768]{1,0:T(8,128)(2,1)}, bf16[512,768]{1,0:T(8,128)(2,1)}, u32[]{:S(2)}, u32[]{:S(2)}) %collective-permute-start.36) | collective-permute-done | bytes 786464 | tf_op jit(solution)/shard_map/ppermute | solution.py:663
  590.5 5.2 shard_map.230
  (291 shorter events, 133.8 us)
Async XLA Ops:
  7.2 104.5 %all-gather.5.cloned.1.call-start = ((), (), s32[]{:S(2)}) async-start(), calls=%async_computation.2 | async-start | bytes 9437184 | tf_op jit(solution)/shard_map/all_gather | solution.py:574
  12.6 143.0 %all-gather.7.cloned.1.call-start = ((), (), s32[]{:S(2)}) async-start(), calls=%async_computation.3 | async-start | bytes 9437184 | tf_op jit(solution)/shard_map/all_gather | solution.py:574
  33.3 161.8 %all-gather.9.cloned.1.call-start = ((), (), s32[]{:S(2)}) async-start(), calls=%async_computation.4 | async-start | bytes 9437184 | tf_op jit(solution)/shard_map/all_gather | solution.py:574
  33.4 23.8 %collective-permute-start.4 = (bf16[512,1024]{1,0:T(8,128)(2,1)S(1)}, bf16[512,1024]{1,0:T(8,128)(2,1)S(1)}, u32[]{:S(2)}, u32[]{:S(2)}) collective-permute-start(bf16[512,1024]{1,0:T(8,128)(2,1)S(1)} %maximum_select_fusion.refs_0_.refs_4_), channel_id=1, source_target_pairs={{0,8},{4,12},{8,16},{12,20},{16,24},{20,28},{24,0},{28,4},{1,9},{5... | collective-permute-start | bytes 3145736 | tf_op jit(solution)/shard_map/ppermute | solution.py:633
  57.2 24.6 %collective-permute-start.7 = (bf16[512,1024]{1,0:T(8,128)(2,1)S(1)}, bf16[512,1024]{1,0:T(8,128)(2,1)S(1)}, u32[]{:S(2)}, u32[]{:S(2)}) collective-permute-start(bf16[512,1024]{1,0:T(8,128)(2,1)S(1)} %collective-permute-done.4.refs_1_.refs_5_), channel_id=1, source_target_pairs={{0,8},{4,12},{8,16},{12,20},{16,24},{20,28},{24,0},{28,4},{1,9},{5... | collective-permute-start | bytes 3145736 | tf_op jit(solution)/shard_map/ppermute | solution.py:633
  59.6 22.3 %collective-permute-start.3 = (bf16[256,1024]{1,0:T(8,128)(2,1)}, bf16[256,1024]{1,0:T(8,128)(2,1)}, u32[]{:S(2)}, u32[]{:S(2)}) collective-permute-start(bf16[256,1024]{1,0:T(8,128)(2,1)} %get-tuple-element.287), channel_id=1, source_target_pairs={{0,4},{4,0},{8,12},{12,8},{16,20},{20,16},{24,28},{28,24},{1,5},{5... | collective-permute-start | bytes 1572872 | tf_op jit(solution)/shard_map/ppermute | solution.py:571
  81.9 183.4 %all-gather.11.cloned.1.call-start = ((), (), s32[]{:S(2)}) async-start(), calls=%async_computation.5 | async-start | bytes 9437184 | tf_op jit(solution)/shard_map/all_gather | solution.py:574
  81.9 26.3 %collective-permute-start.9 = (bf16[512,1024]{1,0:T(8,128)(2,1)S(1)}, bf16[512,1024]{1,0:T(8,128)(2,1)S(1)}, u32[]{:S(2)}, u32[]{:S(2)}) collective-permute-start(bf16[512,1024]{1,0:T(8,128)(2,1)S(1)} %collective-permute-done.7.refs_2_.refs_6_), channel_id=1, source_target_pairs={{0,8},{4,12},{8,16},{12,20},{16,24},{20,28},{24,0},{28,4},{1,9},{5... | collective-permute-start | bytes 3145736 | tf_op jit(solution)/shard_map/ppermute | solution.py:633
  87.1 21.1 %collective-permute-start.10 = (bf16[16,704]{1,0:T(8,128)(2,1)S(1)}, bf16[16,704]{1,0:T(8,128)(2,1)S(1)}, u32[]{:S(2)}, u32[]{:S(2)}) collective-permute-start(bf16[16,704]{1,0:T(8,128)(2,1)S(1)} %maximum_select_fusion.4), channel_id=1, source_target_pairs={{0,16},{4,20},{8,24},{12,28},{16,0},{20,4},{24,8},{28,12},{1,17},{... | collective-permute-start | bytes 67592 | tf_op jit(solution)/shard_map/ppermute | solution.py:580
  108.3 26.9 %collective-permute-start.11 = (bf16[512,1024]{1,0:T(8,128)(2,1)S(1)}, bf16[512,1024]{1,0:T(8,128)(2,1)S(1)}, u32[]{:S(2)}, u32[]{:S(2)}) collective-permute-start(bf16[512,1024]{1,0:T(8,128)(2,1)S(1)} %maximum_select_fusion.1.refs_2_.refs_4_), channel_id=1, source_target_pairs={{0,8},{4,12},{8,16},{12,20},{16,24},{20,28},{24,0},{28,4},{1,9},{5... | collective-permute-start | bytes 3145736 | tf_op jit(solution)/shard_map/ppermute | solution.py:633
  135.2 323.0 %reduce-scatter.3.cloned.1.call-start = ((), (), s32[]{:S(2)}) async-start(), calls=%async_computation.6 | async-start | bytes 18874368 | tf_op jit(solution)/shard_map/reduce_scatter | solution.py:577
  135.3 36.5 %collective-permute-start.12 = (bf16[512,1024]{1,0:T(8,128)(2,1)S(1)}, bf16[512,1024]{1,0:T(8,128)(2,1)S(1)}, u32[]{:S(2)}, u32[]{:S(2)}) collective-permute-start(bf16[512,1024]{1,0:T(8,128)(2,1)S(1)} %collective-permute-done.11.refs_3_.refs_5_), channel_id=1, source_target_pairs={{0,8},{4,12},{8,16},{12,20},{16,24},{20,28},{24,0},{28,4},{1,9},{5... | collective-permute-start | bytes 3145736 | tf_op jit(solution)/shard_map/ppermute | solution.py:633
  171.8 30.9 %collective-permute-start.13 = (bf16[512,1024]{1,0:T(8,128)(2,1)S(1)}, bf16[512,1024]{1,0:T(8,128)(2,1)S(1)}, u32[]{:S(2)}, u32[]{:S(2)}) collective-permute-start(bf16[512,1024]{1,0:T(8,128)(2,1)S(1)} %collective-permute-done.12.refs_4_.refs_6_), channel_id=1, source_target_pairs={{0,8},{4,12},{8,16},{12,20},{16,24},{20,28},{24,0},{28,4},{1,9},{5... | collective-permute-start | bytes 3145736 | tf_op jit(solution)/shard_map/ppermute | solution.py:633
  202.7 35.4 %collective-permute-start.14 = (bf16[512,1024]{1,0:T(8,128)(2,1)S(1)}, bf16[512,1024]{1,0:T(8,128)(2,1)S(1)}, u32[]{:S(2)}, u32[]{:S(2)}) collective-permute-start(bf16[512,1024]{1,0:T(8,128)(2,1)S(1)} %copy-done.9), channel_id=1, source_target_pairs={{0,8},{4,12},{8,16},{12,20},{16,24},{20,28},{24,0},{28,4},{1,9},{5... | collective-permute-start | bytes 3145736 | tf_op jit(solution)/shard_map/ppermute | solution.py:633
  238.1 27.0 %collective-permute-start.15 = (bf16[512,1024]{1,0:T(8,128)(2,1)S(1)}, bf16[512,1024]{1,0:T(8,128)(2,1)S(1)}, u32[]{:S(2)}, u32[]{:S(2)}) collective-permute-start(bf16[512,1024]{1,0:T(8,128)(2,1)S(1)} %collective-permute-done.14.refs_9_.refs_5_), channel_id=1, source_target_pairs={{0,8},{4,12},{8,16},{12,20},{16,24},{20,28},{24,0},{28,4},{1,9},{5... | collective-permute-start | bytes 3145736 | tf_op jit(solution)/shard_map/ppermute | solution.py:633
  265.1 32.3 %collective-permute-start.16 = (bf16[512,1024]{1,0:T(8,128)(2,1)S(1)}, bf16[512,1024]{1,0:T(8,128)(2,1)S(1)}, u32[]{:S(2)}, u32[]{:S(2)}) collective-permute-start(bf16[512,1024]{1,0:T(8,128)(2,1)S(1)} %collective-permute-done.15.refs_10_.refs_6_), channel_id=1, source_target_pairs={{0,8},{4,12},{8,16},{12,20},{16,24},{20,28},{24,0},{28,4},{1,9},{5... | collective-permute-start | bytes 3145736 | tf_op jit(solution)/shard_map/ppermute | solution.py:633
  297.4 31.7 %collective-permute-start.17 = (bf16[512,1280]{1,0:T(8,128)(2,1)S(1)}, bf16[512,1280]{1,0:T(8,128)(2,1)S(1)}, u32[]{:S(2)}, u32[]{:S(2)}) collective-permute-start(bf16[512,1280]{1,0:T(8,128)(2,1)S(1)} %constant_dynamic-slice_fusion.7), channel_id=1, source_target_pairs={{0,8},{4,12},{8,16},{12,20},{16,24},{20,28},{24,0},{28,4},{1,9},{5... | collective-permute-start | bytes 3932168 | tf_op jit(solution)/shard_map/ppermute | solution.py:663
  329.1 235.8 %reduce-scatter.5.cloned.1.call-start = ((), (), s32[]{:S(2)}) async-start(), calls=%async_computation.7 | async-start | bytes 9437184 | tf_op jit(solution)/shard_map/reduce_scatter | solution.py:577
  330.8 31.5 %collective-permute-start.18 = (bf16[512,1280]{1,0:T(8,128)(2,1)S(1)}, bf16[512,1280]{1,0:T(8,128)(2,1)S(1)}, u32[]{:S(2)}, u32[]{:S(2)}) collective-permute-start(bf16[512,1280]{1,0:T(8,128)(2,1)S(1)} %add_convert_fusion.2), channel_id=1, source_target_pairs={{0,8},{4,12},{8,16},{12,20},{16,24},{20,28},{24,0},{28,4},{1,9},{5... | collective-permute-start | bytes 3932168 | tf_op jit(solution)/shard_map/ppermute | solution.py:663
  363.9 30.3 %collective-permute-start.19 = (bf16[512,1280]{1,0:T(8,128)(2,1)S(1)}, bf16[512,1280]{1,0:T(8,128)(2,1)S(1)}, u32[]{:S(2)}, u32[]{:S(2)}) collective-permute-start(bf16[512,1280]{1,0:T(8,128)(2,1)S(1)} %add_convert_fusion.1), channel_id=1, source_target_pairs={{0,8},{4,12},{8,16},{12,20},{16,24},{20,28},{24,0},{28,4},{1,9},{5... | collective-permute-start | bytes 3932168 | tf_op jit(solution)/shard_map/ppermute | solution.py:663
  396.0 33.2 %collective-permute-start.20 = (bf16[512,1024]{1,0:T(8,128)(2,1)S(1)}, bf16[512,1024]{1,0:T(8,128)(2,1)S(1)}, u32[]{:S(2)}, u32[]{:S(2)}) collective-permute-start(bf16[512,1024]{1,0:T(8,128)(2,1)S(1)} %constant_dynamic-slice_fusion.6), channel_id=1, source_target_pairs={{0,8},{4,12},{8,16},{12,20},{16,24},{20,28},{24,0},{28,4},{1,9},{5... | collective-permute-start | bytes 3145736 | tf_op jit(solution)/shard_map/ppermute | solution.py:663
  398.8 30.4 %collective-permute-start.21 = (bf16[256,1280]{1,0:T(8,128)(2,1)S(1)}, bf16[256,1280]{1,0:T(8,128)(2,1)S(1)}, u32[]{:S(2)}, u32[]{:S(2)}) collective-permute-start(bf16[256,1280]{1,0:T(8,128)(2,1)S(1)} %dynamic-slice_convert_fusion), channel_id=1, source_target_pairs={{0,4},{4,0},{8,12},{12,8},{16,20},{20,16},{24,28},{28,24},{1,5},{5... | collective-permute-start | bytes 1966088 | tf_op jit(solution)/shard_map/ppermute | solution.py:571
  430.9 24.0 %collective-permute-start.22 = (bf16[512,1024]{1,0:T(8,128)(2,1)S(1)}, bf16[512,1024]{1,0:T(8,128)(2,1)}, u32[]{:S(2)}, u32[]{:S(2)}) collective-permute-start(bf16[512,1024]{1,0:T(8,128)(2,1)S(1)} %add_convert_fusion.4), channel_id=1, source_target_pairs={{0,8},{4,12},{8,16},{12,20},{16,24},{20,28},{24,0},{28,4},{1,9},{5... | collective-permute-start | bytes 3145736 | tf_op jit(solution)/shard_map/ppermute | solution.py:663
  460.1 26.9 %collective-permute-start.23 = (bf16[512,1024]{1,0:T(8,128)(2,1)S(1)}, bf16[512,1024]{1,0:T(8,128)(2,1)S(1)}, u32[]{:S(2)}, u32[]{:S(2)}) collective-permute-start(bf16[512,1024]{1,0:T(8,128)(2,1)S(1)} %add_convert_fusion.3), channel_id=1, source_target_pairs={{0,8},{4,12},{8,16},{12,20},{16,24},{20,28},{24,0},{28,4},{1,9},{5... | collective-permute-start | bytes 3145736 | tf_op jit(solution)/shard_map/ppermute | solution.py:663
  488.2 30.3 %collective-permute-start.24 = (bf16[512,768]{1,0:T(8,128)(2,1)S(1)}, bf16[512,768]{1,0:T(8,128)(2,1)}, u32[]{:S(2)}, u32[]{:S(2)}) collective-permute-start(bf16[512,768]{1,0:T(8,128)(2,1)S(1)} %constant_dynamic-slice_fusion.5), channel_id=1, source_target_pairs={{0,8},{4,12},{8,16},{12,20},{16,24},{20,28},{24,0},{28,4},{1,9},{5... | collective-permute-start | bytes 2359304 | tf_op jit(solution)/shard_map/ppermute | solution.py:663
  491.3 27.2 %collective-permute-start.25 = (bf16[256,1024]{1,0:T(8,128)(2,1)S(1)}, bf16[256,1024]{1,0:T(8,128)(2,1)S(1)}, u32[]{:S(2)}, u32[]{:S(2)}) collective-permute-start(bf16[256,1024]{1,0:T(8,128)(2,1)S(1)} %dynamic-slice_convert_fusion.1), channel_id=1, source_target_pairs={{0,4},{4,0},{8,12},{12,8},{16,20},{20,16},{24,28},{28,24},{1,5},{5... | collective-permute-start | bytes 1572872 | tf_op jit(solution)/shard_map/ppermute | solution.py:571
  526.6 27.9 %collective-permute-start.32 = (bf16[512,768]{1,0:T(8,128)(2,1)S(1)}, bf16[512,768]{1,0:T(8,128)(2,1)S(1)}, u32[]{:S(2)}, u32[]{:S(2)}) collective-permute-start(bf16[512,768]{1,0:T(8,128)(2,1)S(1)} %add_convert_fusion.6), channel_id=1, source_target_pairs={{0,8},{4,12},{8,16},{12,20},{16,24},{20,28},{24,0},{28,4},{1,9},{5... | collective-permute-start | bytes 2359304 | tf_op jit(solution)/shard_map/ppermute | solution.py:663
  533.4 24.5 %collective-permute-start.30 = (bf16[256,1024]{1,0:T(8,128)(2,1)S(1)}, bf16[256,1024]{1,0:T(8,128)(2,1)S(1)}, u32[]{:S(2)}, u32[]{:S(2)}) collective-permute-start(bf16[256,1024]{1,0:T(8,128)(2,1)S(1)} %get-tuple-element.585), channel_id=1, source_target_pairs={{0,2},{1,3},{2,0},{3,1},{4,6},{5,7},{6,4},{7,5},{8,10},{9,11},{10,... | collective-permute-start | bytes 1572872 | tf_op jit(solution)/shard_map/ppermute | solution.py:920
  535.1 22.8 %collective-permute-start.29 = (bf16[256,1024]{1,0:T(8,128)(2,1)S(1)}, bf16[256,1024]{1,0:T(8,128)(2,1)S(1)}, u32[]{:S(2)}, u32[]{:S(2)}) collective-permute-start(bf16[256,1024]{1,0:T(8,128)(2,1)S(1)} %get-tuple-element.586), channel_id=1, source_target_pairs={{0,4},{4,0},{8,12},{12,8},{16,20},{20,16},{24,28},{28,24},{1,5},{5... | collective-permute-start | bytes 1572872 | tf_op jit(solution)/shard_map/ppermute | solution.py:571
  557.1 21.1 %collective-permute-start.36 = (bf16[512,768]{1,0:T(8,128)(2,1)}, bf16[512,768]{1,0:T(8,128)(2,1)}, u32[]{:S(2)}, u32[]{:S(2)}) collective-permute-start(bf16[512,768]{1,0:T(8,128)(2,1)} %add_convert_fusion.5), channel_id=1, source_target_pairs={{0,8},{4,12},{8,16},{12,20},{16,24},{20,28},{24,0},{28,4},{1,9},{5... | collective-permute-start | bytes 2359304 | tf_op jit(solution)/shard_map/ppermute | solution.py:663
  559.4 24.5 %collective-permute-start.33 = (bf16[256,2048]{1,0:T(8,128)(2,1)}, bf16[256,2048]{1,0:T(8,128)(2,1)}, u32[]{:S(2)}, u32[]{:S(2)}) collective-permute-start(bf16[256,2048]{1,0:T(8,128)(2,1)} %pad_maximum_fusion.3), channel_id=1, source_target_pairs={{0,4},{4,0},{8,12},{12,8},{16,20},{20,16},{24,28},{28,24},{1,5},{5... | collective-permute-start | bytes 3145736 | tf_op jit(solution)/shard_map/ppermute | solution.py:571
  561.1 24.2 %collective-permute-start.34 = (bf16[256,2048]{1,0:T(8,128)(2,1)}, bf16[256,2048]{1,0:T(8,128)(2,1)}, u32[]{:S(2)}, u32[]{:S(2)}) collective-permute-start(bf16[256,2048]{1,0:T(8,128)(2,1)} %pad_maximum_fusion.4), channel_id=1, source_target_pairs={{0,2},{1,3},{2,0},{3,1},{4,6},{5,7},{6,4},{7,5},{8,10},{9,11},{10,... | collective-permute-start | bytes 3145736 | tf_op jit(solution)/shard_map/ppermute | solution.py:920
  (49 other events, 468.9 us)
Sparse Core Ops, SparseCore 0:
  12.7 69.2 all-gather.4
  84.5 54.2 all-gather.6
  140.7 54.3 all-gather.8
  196.9 54.3 all-gather.10
  329.2 128.8 reduce-scatter.2
  461.5 88.8 reduce-scatter.4

commit v6 on v5

--- a/solution.py
+++ b/solution.py
@@ -683,16 +683,19 @@
             self.cur, self.rest = Box(everywhere), over_fsdp
             self.size = everywhere.shape[0]
             bits = [("tp", tp_size, bit) for bit in range(tp_size.bit_length() - 1)]
-            self.steps = bits + [("fsdp", fsdp_size, bit) for bit in range(fsdp_size.bit_length() - 1)]
+            self.steps = bits + [("fsdp", fsdp_size, 0), ("line", 0, 0)]
 
         def move(self):
             if self.steps:
                 axis, size, bit = self.steps.pop(0)
-                if axis == "fsdp" and bit == 0:
+                if axis == "fsdp":
                     self.cur = Box(jnp.concatenate([self.cur.val, self.rest]))
                 order.tie(self.cur)
-                other = lax.ppermute(self.cur.val, axis, [(i, i ^ (1 << bit)) for i in range(size)])
-                self.cur = Box(self.cur.val + other)
+                if axis == "line":
+                    others = along_line(self.cur.val)
+                else:
+                    others = [lax.ppermute(self.cur.val, axis, [(i, i ^ (1 << bit)) for i in range(size)])]
+                self.cur = Box(sum(others, self.cur.val))
 
         def split(self):
             while self.steps:
@@ -724,11 +727,18 @@
         small_all = doubled(small_all, "tp", tp_size, tp_at, 1 << bit)
     small_near = small_all
 
-    def small_step(small_all, bit):
-        if bit < fsdp_size.bit_length() - 1:
-            order.tie(small_all)
-            return Box(doubled(small_all.val, "fsdp", fsdp_size, fsdp_at, 1 << bit))
-        return small_all
+    def along_line(vals):
+        return [lax.ppermute(vals, "fsdp", [(f, f ^ (far << 1)) for f in range(fsdp_size)]) for far in range(1, line)]
+
+    def small_step(small_all, step):
+        order.tie(small_all)
+        if step == 0:
+            return Box(doubled(small_all.val, "fsdp", fsdp_size, fsdp_at, 1))
+        held = [small_all.val] + along_line(small_all.val)
+        for bit in range(line.bit_length() - 1):
+            other = (line_at & (1 << bit)) != 0
+            held = [jnp.where(other, held[i ^ (1 << bit)], held[i]) for i in range(line)]
+        return Box(jnp.concatenate(held))
 
     small_all = Box(small_near)
     attn_ring = Gather(attn_shard)
@@ -753,8 +763,6 @@
     order.sync(small_all)
     attn_ring.move()
     plane_cots[0] = gather_behind(cots[0])
-    for bit in range(2, fsdp_size.bit_length() - 1):
-        small_all = small_step(small_all, bit)
     order.sync(up_shard)
     order.tie(down_got)
     down_shard = Box(pair_join(down_half(pair_at), down_got.val))
@@ -904,11 +912,11 @@
     up_scatter.move()
     (back,) = normed_grad_piece(0)
     up_scatter.sync()
-    order.sync(branch_sum)
     back_sum = scatter_behind(back)
     up_scatter.move()
     qkv_scatter = weight_piece(normed, qkv_grads)
     up_scatter.sync()
+    order.sync(branch_sum)
     up_scatter.swap()
     qkv_scatter.move()
     keep, give = normed_grad_piece(1, True)
@@ -953,12 +961,10 @@
     order.sync(tail.cur)
     order.tie(tail.cur)
     far = block(1 - pair_at, 1 - y_at)
+    from_pair, from_y = Box(swap_pair(far[:, :half])), Box(swap_y(far[:, half:]))
     tail.move()
-    from_pair, from_y = Box(swap_pair(far[:, :half])), Box(swap_y(far[:, half:]))
     qkv_scatter.sync()
-    order.sync(tail.cur)
-    order.tie(tail.cur)
-    tail.move()
+    order.tie()
     qkv_scatter.move()
     order.tie(from_pair, from_y)
     for_y, for_pair = block(pair_at, 1 - y_at), block(1 - pair_at, y_at)
@@ -978,15 +984,24 @@
     down_w_grad = Box(jnp.concatenate([part[:, :mlp_cols].T for part in halves], axis=0))
     out_w_grad = Box(jnp.concatenate([part[:, mlp_cols:].T for part in halves], axis=0))
     up_w_grad = Box(jnp.concatenate(up_scatter.halves(), axis=1))
-    for box in (gained, down_w_grad, out_w_grad, up_w_grad, tail.cur):
-        order.sync(box)
+    order.sync(gained)
     qkv_scatter.sync()
+    order.sync(tail.cur)
     order.tie(tail.cur)
     tail.move()
     qkv_scatter.swap()
+    for box in (down_w_grad, out_w_grad, up_w_grad):
+        order.sync(box)
+
+    def qkv_columns(vals):
+        return vals.reshape(shard_rows, pairs, 3, LANES).transpose(0, 2, 1, 3).reshape(shard_rows, 3, attn_cols)
+
     order.tie(from_pair, from_y)
     last_pieces = [block(pair_at, y_at), from_pair.val, from_y.val]
-    gained = norm_back(inputs[:, 0], cotangent[:, 0], last_pieces, gain_row, 1, gained.val)
+    gained = Box(norm_back(inputs[:, 0], cotangent[:, 0], last_pieces, gain_row, 1, gained.val))
+    order.tokens = [gained]
+    order.tie(qkv_scatter.got, tail.cur)
+    qkv_w_grad = Box(jnp.concatenate([qkv_columns(part) for part in qkv_scatter.halves()], axis=2))
     small_sums, bias_sums = tail.split()
     branch_sum = branch_sum.val.reshape(micro_count, token_rows, model_width)
     output = (inputs[:, 0].astype(F32) + branch_sum.astype(F32) + bias_both).astype(BF)
@@ -999,18 +1014,12 @@
     qkv_b_sum = bias_sums[2 * mlp_cols :].reshape(3, qkv_bias.shape[1], -1)
     qkv_b_sum = lax.dynamic_slice_in_dim(qkv_b_sum, fsdp_at * qkv_bias.shape[2], qkv_bias.shape[2], axis=2)
 
-    def qkv_columns(vals):
-        return vals.reshape(shard_rows, pairs, 3, LANES).transpose(0, 2, 1, 3).reshape(
-            shard_rows, 3, attn_cols
-        )
-
-    qkv_w_grad = jnp.concatenate([qkv_columns(part) for part in qkv_scatter.halves()], axis=2)
     return (
         output[:, None],
-        gained[:, None],
+        gained.val[:, None],
         gain_sum,
         shift_sum,
-        qkv_w_grad,
+        qkv_w_grad.val,
         qkv_b_sum,
         out_w_grad.val,
         bias_sum,

time: 620 us -> 611 us (0.985)
  waiting for transfers between devices: 120 us -> 108 us
    ppermute x5 -> x3, waiting for transfers between devices: 16.5 us -> 2.25 us  [move(): lax.ppermute(self.cur.val, axis, [(i, i ^ 1 << bit) for i in range(size)])]
    ppermute x5 -> x3, waiting for transfers between devices: 14.8 us -> 3.74 us  [doubled(): other = lax.ppermute(cur, axis, [(i, i ^ bit) for i in range(size)])]
    ppermute x0 -> x6, starting transfers between devices: none -> 9.28 us  [along_line(): lax.ppermute(vals, 'fsdp', [(f, f ^ far << 1) for f in range(fsdp_size)])]
    ppermute x9, waiting for transfers between devices: 18.7 us -> 26.1 us  [move(): self.came = Box(lax.ppermute(sent.val, 'fsdp', ring))]
    unnamed x85 -> x87, local copies, waits for them, and re-layouts: 12.1 us -> 15.1 us
  transfers between devices with their start and end apart: 45 -> 47, of which waited for: 20 -> 21; matrix products, arithmetic and copies ran while one was open for 11% -> 10% of each run, Pallas kernels for 58% -> 59%
where the time goes in v6:
time: 611 us; the launch traced here: 604 us
  Pallas kernels  356 us (58%)
  waiting for transfers between devices  108 us (18%)
  starting transfers between devices  44.7 us (7%)
  other arithmetic  41.2 us (7%)
  local copies, waits for them, and re-layouts  38.8 us (6%)
  between operations  15.4 us (3%)
    pallas_call x9, Pallas kernels, rows_call(): pl.pallas_call(kernel, grid_spec=pltpu.PrefetchScalarGridSpec(num_scalar_...  187 us
    pallas_call x3, Pallas kernels, weight_grad(): pl.pallas_call(kernel, grid=(micro_count * steps,), in_specs=[side(micro,...  78.1 us
    pallas_call x2, Pallas kernels, attend_back(): pl.pallas_call(functools.partial(attend_back_kernel, head_dim, block), gr...  42.1 us
    ppermute x8, waiting for transfers between devices, swap_pair(): return lax.ppermute(vals, 'fsdp', [(f, f ^ 1) for f in range(fsdp_size)])  38.7 us
    pallas_call x2, Pallas kernels, attend(): pl.pallas_call(functools.partial(attend_kernel, head_dim, block), grid=(s...  33.7 us
    ppermute x9, waiting for transfers between devices, move(): self.parts.append(Box(lax.ppermute(self.parts[-1].val, 'fsdp', ring)))  26.1 us
    ppermute x9, waiting for transfers between devices, move(): self.came = Box(lax.ppermute(sent.val, 'fsdp', ring))  26.1 us
    unnamed x87, local copies, waits for them, and re-layouts  15.1 us
  transfers between devices with their start and end apart: 47, of which 21 were waited for; matrix products, arithmetic and copies ran while one was open for 10% of the time, Pallas kernels for 59%

profile of v6, /device:TPU:0, one launch (start us, length us, event | category | flops | bytes accessed | tf_op | source)
XLA Modules:
  0.0 603.5 jit_solution(18182650438960240687)
XLA Ops:
  19.2 11.8 %collective-permute-done = bf16[256,1024]{1,0:T(8,128)(2,1)S(1)} collective-permute-done((bf16[256,1024]{1,0:T(8,128)(2,1)S(1)}, bf16[256,1024]{1,0:T(8,128)(2,1)S(1)}, u32[]{:S(2)}, u32[]{:S(2)}) %collective-permute-start) | collective-permute-done | bytes 524320 | tf_op jit(solution)/shard_map/ppermute | solution.py:571
  43.9 13.3 %collective-permute-done.4.refs_1_.refs_5_ = bf16[512,1024]{1,0:T(8,128)(2,1)S(1)} collective-permute-done((bf16[512,1024]{1,0:T(8,128)(2,1)S(1)}, bf16[512,1024]{1,0:T(8,128)(2,1)S(1)}, u32[]{:S(2)}, u32[]{:S(2)}) %collective-permute-start.4) | collective-permute-done | bytes 1048608 | tf_op jit(solution)/shard_map/ppermute | solution.py:633
  69.5 12.3 %collective-permute-done.3 = bf16[256,1024]{1,0:T(8,128)(2,1)} collective-permute-done((bf16[256,1024]{1,0:T(8,128)(2,1)}, bf16[256,1024]{1,0:T(8,128)(2,1)}, u32[]{:S(2)}, u32[]{:S(2)}) %collective-permute-start.3) | collective-permute-done | bytes 524320 | tf_op jit(solution)/shard_map/ppermute | solution.py:571
  87.4 12.3 %collective-permute-done.6 = bf16[256,1024]{1,0:T(8,128)(2,1)} collective-permute-done((bf16[256,1024]{1,0:T(8,128)(2,1)}, bf16[256,1024]{1,0:T(8,128)(2,1)}, u32[]{:S(2)}, u32[]{:S(2)}) %collective-permute-start.6) | collective-permute-done | bytes 524320 | tf_op jit(solution)/shard_map/ppermute | solution.py:571
  102.4 4.8 collective-permute-done.11.refs_3_.refs_7_
  110.3 17.5 %shard_map.213 = (bf16[2048,2048]{1,0:T(8,128)(2,1)}, f32[2048,768]{1,0:T(8,128)}) custom-call(s32[5]{0:T(128)} %stack.23.slots_ref, bf16[2048,2048]{1,0:T(8,128)(2,1)} %all-gather.5.cloned.1.call-done.rows_ref, f32[1,2048]{1,0:T(1,128)} %reshape.222.gain_ref, f32[1,2048]{1,0:T(1,128)} %reshape.223.shift_ref, f32[1,768]{1,0:T(1,128)} %reshape.206.bias_ref, ...), custom_call_target="tpu_custom_call" | custom-call | flops 100663296 | bytes 360448 | tf_op jit(solution)/shard_map/pallas_call | solution.py:219
  127.9 3.6 collective-permute-done.12.refs_3_.refs_5_
  135.6 16.3 %shard_map.214 = (bf16[2048,768]{1,0:T(8,128)(2,1)}, bf16[2048,256]{1,0:T(8,128)(2,1)}, f32[4,2,1024]{2,1,0:T(2,128)}) custom-call(f32[2048,768]{1,0:T(8,128)} %get-tuple-element.327.qkv_ref, f32[1024,128]{1,0:T(8,128)} %copy.78.cos_ref, f32[1024,128]{1,0:T(8,128)} %copy.79.low_ref, f32[1024,128]{1,0:T(8,128)} %copy.80.up_ref), custom_call_target="tpu_custom_call" | custom-call | flops 100663296 | bytes 131072 | tf_op jit(solution)/shard_map/pallas_call | solution.py:150
  151.9 16.1 %shard_map.215 = (bf16[2048,2048]{1,0:T(8,128)(2,1)}, f32[2048,768]{1,0:T(8,128)}) custom-call(s32[5]{0:T(128)} %stack.23.slots_ref, bf16[2048,2048]{1,0:T(8,128)(2,1)} %all-gather.7.cloned.1.call-done.rows_ref, f32[1,2048]{1,0:T(1,128)} %reshape.222.gain_ref, f32[1,2048]{1,0:T(1,128)} %reshape.223.shift_ref, f32[1,768]{1,0:T(1,128)} %reshape.206.bias_ref, ...), custom_call_target="tpu_custom_call" | custom-call | flops 100663296 | bytes 360448 | tf_op jit(solution)/shard_map/pallas_call | solution.py:219
  168.1 17.4 %shard_map.216 = (bf16[2048,768]{1,0:T(8,128)(2,1)}, bf16[2048,256]{1,0:T(8,128)(2,1)}, f32[4,2,1024]{2,1,0:T(2,128)}) custom-call(f32[2048,768]{1,0:T(8,128)} %get-tuple-element.337.qkv_ref, f32[1024,128]{1,0:T(8,128)} %copy.78.cos_ref, f32[1024,128]{1,0:T(8,128)} %copy.79.low_ref, f32[1024,128]{1,0:T(8,128)} %copy.80.up_ref), custom_call_target="tpu_custom_call" | custom-call | flops 100663296 | bytes 131072 | tf_op jit(solution)/shard_map/pallas_call | solution.py:150
  185.5 9.6 %all-gather.9.cloned.1.call-done.rows_ref.refs_0_ = bf16[2048,2048]{1,0:T(8,128)(2,1)} async-done(((bf16[256,2048]{1,0:T(8,128)(2,1)}), bf16[2048,2048]{1,0:T(8,128)(2,1)}) %all-gather.9.cloned.1.call-update) | async-done | bytes 8388624 | tf_op jit(solution)/shard_map/all_gather | solution.py:574
  195.1 7.6 %shard_map.217.grad_ref = bf16[2048,256]{1,0:T(8,128)(2,1)} custom-call(s32[5]{0:T(128)} %stack.23.slots_ref, bf16[2048,2048]{1,0:T(8,128)(2,1)} %all-gather.9.cloned.1.call-done.rows_ref.refs_0_, bf16[512,1024]{1,0:T(8,128)(2,1)} %copy-done, bf16[512,1024]{1,0:T(8,128)(2,1)} %copy-done.2, bf16[512,1024]{1,0:T(8,128)(2,1)} %copy-done.3, ...), custom_call_target="tpu_custom_call" | custom-call | flops 33554432 | bytes 147456 | tf_op jit(solution)/shard_map/pallas_call | solution.py:219
  205.6 32.4 %shard_map.218 = (bf16[2048,1024]{1,0:T(8,128)(2,1)}, bf16[2048,1024]{1,0:T(8,128)(2,1)}, bf16[2048,1024]{1,0:T(8,128)(2,1)}, bf16[2048,1024]{1,0:T(8,128)(2,1)}) custom-call(s32[5]{0:T(128)} %stack.23.slots_ref, f32[1,1024]{1,0:T(1,128)} %constant_dynamic-slice_fusion.8.bias_ref, bf16[2048,2048]{1,0:T(8,128)(2,1)} %get-tuple-element.427.refs_0_, ...), custom_call_target="tpu_custom_call" | custom-call | flops 268435456 | bytes 524288 | tf_op jit(solution)/shard_map/pallas_call | solution.py:219
  239.7 21.0 %shard_map.219 = (bf16[2048,768]{1,0:T(8,128)(2,1)}, f32[16,768]{1,0:T(8,128)}) custom-call(bf16[2048,768]{1,0:T(8,128)(2,1)} %get-tuple-element.361.rot_ref, bf16[2048,256]{1,0:T(8,128)(2,1)} %shard_map.217.grad_ref, bf16[2048,256]{1,0:T(8,128)(2,1)} %get-tuple-element.375.attn_ref.refs_4_.refs_0_, f32[4,2,1024]{2,1,0:T(2,128)} %get-tuple-element.363.lse_ref, ...), custom_call_target="tpu_custom_call" | custom-call | flops 201326592 | bytes 131072 | tf_op jit(solution)/shard_map/pallas_call | solution.py:175
  260.7 4.4 collective-permute-done.16.refs_10_.refs_6_
  265.3 30.7 %shard_map.220 = bf16[2048,1280]{1,0:T(8,128)(2,1)} custom-call(bf16[2048,2048]{1,0:T(8,128)(2,1)} %all-gather.9.cloned.1.call-done.rows_ref.refs_0_, bf16[2048,2048]{1,0:T(8,128)(2,1)} %all-gather.11.cloned.1.call-done.refs_1_.rows_ref, bf16[2048,1024]{1,0:T(8,128)(2,1)} %get-tuple-element.377.refs_2_, bf16[2048,1024]{1,0:T(8,128)(2,1)} %get-tuple-element.378.refs_3_, ...), custom_call_target="tpu_custom_call" | custom-call | flops 335544320 | bytes 425984 | tf_op jit(solution)/shard_map/pallas_call | solution.py:524
  298.5 30.2 %shard_map.221 = bf16[8,2,256,2048]{3,2,1,0:T(8,128)(2,1)} custom-call(s32[5]{0:T(128)} %stack.23.slots_ref, bf16[2048,256]{1,0:T(8,128)(2,1)} %get-tuple-element.375.attn_ref.refs_4_.refs_0_, bf16[2048,256]{1,0:T(8,128)(2,1)} %get-tuple-element.411.refs_5_.refs_1_.attn_ref, bf16[2048,1024]{1,0:T(8,128)(2,1)} %get-tuple-element.377.refs_2_, ...), custom_call_target="tpu_custom_call" | custom-call | flops 335544320 | bytes 294912 | tf_op jit(solution)/shard_map/pallas_call | solution.py:219
  331.7 27.0 %shard_map.222 = (bf16[2048,1024]{1,0:T(8,128)(2,1)}, bf16[2048,1024]{1,0:T(8,128)(2,1)}, f32[8,1024]{1,0:T(8,128)}) custom-call(s32[5]{0:T(128)} %stack.23.slots_ref, bf16[2048,2048]{1,0:T(8,128)(2,1)} %all-gather.9.cloned.1.call-done.rows_ref.refs_0_, bf16[2048,2048]{1,0:T(8,128)(2,1)} %all-gather.11.cloned.1.call-done.refs_1_.rows_ref, ...), custom_call_target="tpu_custom_call" | custom-call | flops 268435456 | bytes 524288 | tf_op jit(solution)/shard_map/pallas_call | solution.py:219
  358.6 3.6 collective-permute-done.19
  364.0 26.1 %shard_map.223 = bf16[2048,1024]{1,0:T(8,128)(2,1)} custom-call(bf16[2048,2048]{1,0:T(8,128)(2,1)} %get-tuple-element.427.refs_0_, bf16[2048,2048]{1,0:T(8,128)(2,1)} %get-tuple-element.428.refs_1_, bf16[2048,1024]{1,0:T(8,128)(2,1)} %get-tuple-element.419.refs_2_.two_ref, bf16[2048,1024]{1,0:T(8,128)(2,1)} %get-tuple-element.437.refs_3_.two_ref), custom_call_target="tpu_custom_call" | custom-call | flops 268435456 | bytes 393216 | tf_op jit(solution)/shard_map/pallas_call | solution.py:524
  390.0 4.2 collective-permute-done.20
  400.3 7.7 %shard_map.224.grad_ref = bf16[2048,256]{1,0:T(8,128)(2,1)} custom-call(s32[5]{0:T(128)} %stack.23.slots_ref, bf16[2048,2048]{1,0:T(8,128)(2,1)} %all-gather.11.cloned.1.call-done.refs_1_.rows_ref, bf16[512,1024]{1,0:T(8,128)(2,1)} %copy-done, bf16[512,1024]{1,0:T(8,128)(2,1)} %copy-done.2, bf16[512,1024]{1,0:T(8,128)(2,1)} %copy-done.3, ...), custom_call_target="tpu_custom_call" | custom-call | flops 33554432 | bytes 147456 | tf_op jit(solution)/shard_map/pallas_call | solution.py:219
  408.0 21.1 %shard_map.225 = (bf16[2048,768]{1,0:T(8,128)(2,1)}, f32[16,768]{1,0:T(8,128)}) custom-call(bf16[2048,768]{1,0:T(8,128)(2,1)} %get-tuple-element.409.rot_ref, bf16[2048,256]{1,0:T(8,128)(2,1)} %shard_map.224.grad_ref, bf16[2048,256]{1,0:T(8,128)(2,1)} %get-tuple-element.411.refs_5_.refs_1_.attn_ref, f32[4,2,1024]{2,1,0:T(2,128)} %get-tuple-element.412.lse_ref, ...), custom_call_target="tpu_custom_call" | custom-call | flops 201326592 | bytes 131072 | tf_op jit(solution)/shard_map/pallas_call | solution.py:175
  430.8 24.0 %shard_map.226 = (bf16[2048,2048]{1,0:T(8,128)(2,1)}, f32[8,2048]{1,0:T(8,128)}) custom-call(s32[5]{0:T(128)} %stack.23.slots_ref, bf16[2048,768]{1,0:T(8,128)(2,1)} %get-tuple-element.429.one_ref.refs_2_, bf16[2048,1024]{1,0:T(8,128)(2,1)} %get-tuple-element.419.refs_2_.two_ref, bf16[2048,2048]{1,0:T(8,128)(2,1)} %all-gather.5.cloned.1.call-done.rows_ref, ...), custom_call_target="tpu_custom_call" | custom-call | flops 234881024 | bytes 376832 | tf_op jit(solution)/shard_map/pallas_call | solution.py:219
  458.5 21.4 %shard_map.227 = bf16[2048,768]{1,0:T(8,128)(2,1)} custom-call(bf16[2048,2048]{1,0:T(8,128)(2,1)} %get-tuple-element.427.refs_0_, bf16[2048,2048]{1,0:T(8,128)(2,1)} %get-tuple-element.428.refs_1_, bf16[2048,768]{1,0:T(8,128)(2,1)} %get-tuple-element.429.one_ref.refs_2_, bf16[2048,768]{1,0:T(8,128)(2,1)} %get-tuple-element.436.refs_3_.one_ref), custom_call_target="tpu_custom_call" | custom-call | flops 201326592 | bytes 360448 | tf_op jit(solution)/shard_map/pallas_call | solution.py:524
  488.2 24.5 %shard_map.228 = (bf16[1024,2048]{1,0:T(8,128)(2,1)}, bf16[1024,2048]{1,0:T(8,128)(2,1)}, f32[8,2048]{1,0:T(8,128)}) custom-call(s32[5]{0:T(128)} %stack.23.slots_ref, bf16[2048,768]{1,0:T(8,128)(2,1)} %get-tuple-element.436.refs_3_.one_ref, bf16[2048,1024]{1,0:T(8,128)(2,1)} %get-tuple-element.437.refs_3_.two_ref, ...), custom_call_target="tpu_custom_call" | custom-call | flops 234881024 | bytes 376832 | tf_op jit(solution)/shard_map/pallas_call | solution.py:219
  524.9 4.1 add_convert_fusion
  534.9 9.7 %collective-permute-done.33 = bf16[512,768]{1,0:T(8,128)(2,1)S(1)} collective-permute-done((bf16[512,768]{1,0:T(8,128)(2,1)S(1)}, bf16[512,768]{1,0:T(8,128)(2,1)S(1)}, u32[]{:S(2)}, u32[]{:S(2)}) %collective-permute-start.33) | collective-permute-done | bytes 786464 | tf_op jit(solution)/shard_map/ppermute | solution.py:663
  554.0 4.7 shard_map.229.refs_3_
  560.6 7.2 %collective-permute-done.34 = bf16[512,768]{1,0:T(8,128)(2,1)} collective-permute-done((bf16[512,768]{1,0:T(8,128)(2,1)}, bf16[512,768]{1,0:T(8,128)(2,1)}, u32[]{:S(2)}, u32[]{:S(2)}) %collective-permute-start.34) | collective-permute-done | bytes 786464 | tf_op jit(solution)/shard_map/ppermute | solution.py:663
  567.8 4.4 collective-permute-start.36
  580.3 5.1 shard_map.230
  (299 shorter events, 132.1 us)
Async XLA Ops:
  7.2 103.2 %all-gather.5.cloned.1.call-start = ((), (), s32[]{:S(2)}) async-start(), calls=%async_computation.2 | async-start | bytes 9437184 | tf_op jit(solution)/shard_map/all_gather | solution.py:574
  12.6 139.3 %all-gather.7.cloned.1.call-start = ((), (), s32[]{:S(2)}) async-start(), calls=%async_computation.3 | async-start | bytes 9437184 | tf_op jit(solution)/shard_map/all_gather | solution.py:574
  33.3 161.8 %all-gather.9.cloned.1.call-start = ((), (), s32[]{:S(2)}) async-start(), calls=%async_computation.4 | async-start | bytes 9437184 | tf_op jit(solution)/shard_map/all_gather | solution.py:574
  33.4 23.8 %collective-permute-start.4 = (bf16[512,1024]{1,0:T(8,128)(2,1)S(1)}, bf16[512,1024]{1,0:T(8,128)(2,1)S(1)}, u32[]{:S(2)}, u32[]{:S(2)}) collective-permute-start(bf16[512,1024]{1,0:T(8,128)(2,1)S(1)} %maximum_select_fusion.refs_0_.refs_4_), channel_id=1, source_target_pairs={{0,8},{4,12},{8,16},{12,20},{16,24},{20,28},{24,0},{28,4},{1,9},{5... | collective-permute-start | bytes 3145736 | tf_op jit(solution)/shard_map/ppermute | solution.py:633
  57.2 24.7 %collective-permute-start.7 = (bf16[512,1024]{1,0:T(8,128)(2,1)S(1)}, bf16[512,1024]{1,0:T(8,128)(2,1)S(1)}, u32[]{:S(2)}, u32[]{:S(2)}) collective-permute-start(bf16[512,1024]{1,0:T(8,128)(2,1)S(1)} %collective-permute-done.4.refs_1_.refs_5_), channel_id=1, source_target_pairs={{0,8},{4,12},{8,16},{12,20},{16,24},{20,28},{24,0},{28,4},{1,9},{5... | collective-permute-start | bytes 3145736 | tf_op jit(solution)/shard_map/ppermute | solution.py:633
  59.6 22.3 %collective-permute-start.3 = (bf16[256,1024]{1,0:T(8,128)(2,1)}, bf16[256,1024]{1,0:T(8,128)(2,1)}, u32[]{:S(2)}, u32[]{:S(2)}) collective-permute-start(bf16[256,1024]{1,0:T(8,128)(2,1)} %get-tuple-element.269), channel_id=1, source_target_pairs={{0,4},{4,0},{8,12},{12,8},{16,20},{20,16},{24,28},{28,24},{1,5},{5... | collective-permute-start | bytes 1572872 | tf_op jit(solution)/shard_map/ppermute | solution.py:571
  63.5 18.3 %collective-permute-start.10 = (bf16[8,704]{1,0:T(8,128)(2,1)S(1)}, bf16[8,704]{1,0:T(8,128)(2,1)S(1)}, u32[]{:S(2)}, u32[]{:S(2)}) collective-permute-start(bf16[8,704]{1,0:T(8,128)(2,1)S(1)} %maximum_select_fusion.3), channel_id=1, source_target_pairs={{0,8},{4,12},{8,0},{12,4},{16,24},{20,28},{24,16},{28,20},{1,9},{5... | collective-permute-start | bytes 33800 | tf_op jit(solution)/shard_map/ppermute | solution.py:731
  81.9 183.3 %all-gather.11.cloned.1.call-start = ((), (), s32[]{:S(2)}) async-start(), calls=%async_computation.5 | async-start | bytes 9437184 | tf_op jit(solution)/shard_map/all_gather | solution.py:574
  82.0 25.2 %collective-permute-start.11 = (bf16[512,1024]{1,0:T(8,128)(2,1)S(1)}, bf16[512,1024]{1,0:T(8,128)(2,1)S(1)}, u32[]{:S(2)}, u32[]{:S(2)}) collective-permute-start(bf16[512,1024]{1,0:T(8,128)(2,1)S(1)} %collective-permute-done.7.refs_2_.refs_6_), channel_id=1, source_target_pairs={{0,8},{4,12},{8,16},{12,20},{16,24},{20,28},{24,0},{28,4},{1,9},{5... | collective-permute-start | bytes 3145736 | tf_op jit(solution)/shard_map/ppermute | solution.py:633
  107.2 24.3 %collective-permute-start.12 = (bf16[512,1024]{1,0:T(8,128)(2,1)S(1)}, bf16[512,1024]{1,0:T(8,128)(2,1)S(1)}, u32[]{:S(2)}, u32[]{:S(2)}) collective-permute-start(bf16[512,1024]{1,0:T(8,128)(2,1)S(1)} %maximum_select_fusion.1.refs_2_.refs_4_), channel_id=1, source_target_pairs={{0,8},{4,12},{8,16},{12,20},{16,24},{20,28},{24,0},{28,4},{1,9},{5... | collective-permute-start | bytes 3145736 | tf_op jit(solution)/shard_map/ppermute | solution.py:633
  131.5 349.3 %reduce-scatter.3.cloned.1.call-start = ((), (), s32[]{:S(2)}) async-start(), calls=%async_computation.6 | async-start | bytes 18874368 | tf_op jit(solution)/shard_map/reduce_scatter | solution.py:577
  131.5 36.5 %collective-permute-start.13 = (bf16[512,1024]{1,0:T(8,128)(2,1)S(1)}, bf16[512,1024]{1,0:T(8,128)(2,1)S(1)}, u32[]{:S(2)}, u32[]{:S(2)}) collective-permute-start(bf16[512,1024]{1,0:T(8,128)(2,1)S(1)} %collective-permute-done.12.refs_3_.refs_5_), channel_id=1, source_target_pairs={{0,8},{4,12},{8,16},{12,20},{16,24},{20,28},{24,0},{28,4},{1,9},{5... | collective-permute-start | bytes 3145736 | tf_op jit(solution)/shard_map/ppermute | solution.py:633
  168.0 34.7 %collective-permute-start.14 = (bf16[512,1024]{1,0:T(8,128)(2,1)S(1)}, bf16[512,1024]{1,0:T(8,128)(2,1)S(1)}, u32[]{:S(2)}, u32[]{:S(2)}) collective-permute-start(bf16[512,1024]{1,0:T(8,128)(2,1)S(1)} %collective-permute-done.13.refs_4_.refs_6_), channel_id=1, source_target_pairs={{0,8},{4,12},{8,16},{12,20},{16,24},{20,28},{24,0},{28,4},{1,9},{5... | collective-permute-start | bytes 3145736 | tf_op jit(solution)/shard_map/ppermute | solution.py:633
  202.7 35.4 %collective-permute-start.15 = (bf16[512,1024]{1,0:T(8,128)(2,1)S(1)}, bf16[512,1024]{1,0:T(8,128)(2,1)S(1)}, u32[]{:S(2)}, u32[]{:S(2)}) collective-permute-start(bf16[512,1024]{1,0:T(8,128)(2,1)S(1)} %copy-done.9), channel_id=1, source_target_pairs={{0,8},{4,12},{8,16},{12,20},{16,24},{20,28},{24,0},{28,4},{1,9},{5... | collective-permute-start | bytes 3145736 | tf_op jit(solution)/shard_map/ppermute | solution.py:633
  238.1 27.0 %collective-permute-start.16 = (bf16[512,1024]{1,0:T(8,128)(2,1)S(1)}, bf16[512,1024]{1,0:T(8,128)(2,1)S(1)}, u32[]{:S(2)}, u32[]{:S(2)}) collective-permute-start(bf16[512,1024]{1,0:T(8,128)(2,1)S(1)} %collective-permute-done.15.refs_9_.refs_5_), channel_id=1, source_target_pairs={{0,8},{4,12},{8,16},{12,20},{16,24},{20,28},{24,0},{28,4},{1,9},{5... | collective-permute-start | bytes 3145736 | tf_op jit(solution)/shard_map/ppermute | solution.py:633
  265.1 32.3 %collective-permute-start.17 = (bf16[512,1024]{1,0:T(8,128)(2,1)S(1)}, bf16[512,1024]{1,0:T(8,128)(2,1)S(1)}, u32[]{:S(2)}, u32[]{:S(2)}) collective-permute-start(bf16[512,1024]{1,0:T(8,128)(2,1)S(1)} %collective-permute-done.16.refs_10_.refs_6_), channel_id=1, source_target_pairs={{0,8},{4,12},{8,16},{12,20},{16,24},{20,28},{24,0},{28,4},{1,9},{5... | collective-permute-start | bytes 3145736 | tf_op jit(solution)/shard_map/ppermute | solution.py:633
  297.4 31.7 %collective-permute-start.18 = (bf16[512,1280]{1,0:T(8,128)(2,1)S(1)}, bf16[512,1280]{1,0:T(8,128)(2,1)S(1)}, u32[]{:S(2)}, u32[]{:S(2)}) collective-permute-start(bf16[512,1280]{1,0:T(8,128)(2,1)S(1)} %constant_dynamic-slice_fusion.7), channel_id=1, source_target_pairs={{0,8},{4,12},{8,16},{12,20},{16,24},{20,28},{24,0},{28,4},{1,9},{5... | collective-permute-start | bytes 3932168 | tf_op jit(solution)/shard_map/ppermute | solution.py:663
  329.2 224.9 %reduce-scatter.5.cloned.1.call-start = ((), (), s32[]{:S(2)}) async-start(), calls=%async_computation.7 | async-start | bytes 9437184 | tf_op jit(solution)/shard_map/reduce_scatter | solution.py:577
  330.9 31.4 %collective-permute-start.19 = (bf16[512,1280]{1,0:T(8,128)(2,1)S(1)}, bf16[512,1280]{1,0:T(8,128)(2,1)S(1)}, u32[]{:S(2)}, u32[]{:S(2)}) collective-permute-start(bf16[512,1280]{1,0:T(8,128)(2,1)S(1)} %add_convert_fusion.2), channel_id=1, source_target_pairs={{0,8},{4,12},{8,16},{12,20},{16,24},{20,28},{24,0},{28,4},{1,9},{5... | collective-permute-start | bytes 3932168 | tf_op jit(solution)/shard_map/ppermute | solution.py:663
  363.9 30.3 %collective-permute-start.20 = (bf16[512,1280]{1,0:T(8,128)(2,1)S(1)}, bf16[512,1280]{1,0:T(8,128)(2,1)S(1)}, u32[]{:S(2)}, u32[]{:S(2)}) collective-permute-start(bf16[512,1280]{1,0:T(8,128)(2,1)S(1)} %add_convert_fusion.1), channel_id=1, source_target_pairs={{0,8},{4,12},{8,16},{12,20},{16,24},{20,28},{24,0},{28,4},{1,9},{5... | collective-permute-start | bytes 3932168 | tf_op jit(solution)/shard_map/ppermute | solution.py:663
  396.0 33.1 %collective-permute-start.21 = (bf16[512,1024]{1,0:T(8,128)(2,1)S(1)}, bf16[512,1024]{1,0:T(8,128)(2,1)S(1)}, u32[]{:S(2)}, u32[]{:S(2)}) collective-permute-start(bf16[512,1024]{1,0:T(8,128)(2,1)S(1)} %constant_dynamic-slice_fusion.6), channel_id=1, source_target_pairs={{0,8},{4,12},{8,16},{12,20},{16,24},{20,28},{24,0},{28,4},{1,9},{5... | collective-permute-start | bytes 3145736 | tf_op jit(solution)/shard_map/ppermute | solution.py:663
  398.8 30.3 %collective-permute-start.22 = (bf16[256,1280]{1,0:T(8,128)(2,1)S(1)}, bf16[256,1280]{1,0:T(8,128)(2,1)S(1)}, u32[]{:S(2)}, u32[]{:S(2)}) collective-permute-start(bf16[256,1280]{1,0:T(8,128)(2,1)S(1)} %dynamic-slice_convert_fusion), channel_id=1, source_target_pairs={{0,4},{4,0},{8,12},{12,8},{16,20},{20,16},{24,28},{28,24},{1,5},{5... | collective-permute-start | bytes 1966088 | tf_op jit(solution)/shard_map/ppermute | solution.py:571
  430.7 24.1 %collective-permute-start.23 = (bf16[512,1024]{1,0:T(8,128)(2,1)S(1)}, bf16[512,1024]{1,0:T(8,128)(2,1)}, u32[]{:S(2)}, u32[]{:S(2)}) collective-permute-start(bf16[512,1024]{1,0:T(8,128)(2,1)S(1)} %add_convert_fusion.4), channel_id=1, source_target_pairs={{0,8},{4,12},{8,16},{12,20},{16,24},{20,28},{24,0},{28,4},{1,9},{5... | collective-permute-start | bytes 3145736 | tf_op jit(solution)/shard_map/ppermute | solution.py:663
  456.9 23.9 %collective-permute-start.24 = (bf16[512,1024]{1,0:T(8,128)(2,1)S(1)}, bf16[512,1024]{1,0:T(8,128)(2,1)}, u32[]{:S(2)}, u32[]{:S(2)}) collective-permute-start(bf16[512,1024]{1,0:T(8,128)(2,1)S(1)} %add_convert_fusion.3), channel_id=1, source_target_pairs={{0,8},{4,12},{8,16},{12,20},{16,24},{20,28},{24,0},{28,4},{1,9},{5... | collective-permute-start | bytes 3145736 | tf_op jit(solution)/shard_map/ppermute | solution.py:663
  482.0 31.7 %collective-permute-start.25 = (bf16[512,768]{1,0:T(8,128)(2,1)S(1)}, bf16[512,768]{1,0:T(8,128)(2,1)}, u32[]{:S(2)}, u32[]{:S(2)}) collective-permute-start(bf16[512,768]{1,0:T(8,128)(2,1)S(1)} %constant_dynamic-slice_fusion.5), channel_id=1, source_target_pairs={{0,8},{4,12},{8,16},{12,20},{16,24},{20,28},{24,0},{28,4},{1,9},{5... | collective-permute-start | bytes 2359304 | tf_op jit(solution)/shard_map/ppermute | solution.py:663
  487.2 26.5 %collective-permute-start.26 = (bf16[256,1024]{1,0:T(8,128)(2,1)S(1)}, bf16[256,1024]{1,0:T(8,128)(2,1)S(1)}, u32[]{:S(2)}, u32[]{:S(2)}) collective-permute-start(bf16[256,1024]{1,0:T(8,128)(2,1)S(1)} %dynamic-slice_convert_fusion.1), channel_id=1, source_target_pairs={{0,4},{4,0},{8,12},{12,8},{16,20},{20,16},{24,28},{28,24},{1,5},{5... | collective-permute-start | bytes 1572872 | tf_op jit(solution)/shard_map/ppermute | solution.py:571
  522.6 22.0 %collective-permute-start.33 = (bf16[512,768]{1,0:T(8,128)(2,1)S(1)}, bf16[512,768]{1,0:T(8,128)(2,1)S(1)}, u32[]{:S(2)}, u32[]{:S(2)}) collective-permute-start(bf16[512,768]{1,0:T(8,128)(2,1)S(1)} %add_convert_fusion.6), channel_id=1, source_target_pairs={{0,8},{4,12},{8,16},{12,20},{16,24},{20,28},{24,0},{28,4},{1,9},{5... | collective-permute-start | bytes 2359304 | tf_op jit(solution)/shard_map/ppermute | solution.py:663
  529.3 19.8 %collective-permute-start.32 = (bf16[256,1024]{1,0:T(8,128)(2,1)S(1)}, bf16[256,1024]{1,0:T(8,128)(2,1)S(1)}, u32[]{:S(2)}, u32[]{:S(2)}) collective-permute-start(bf16[256,1024]{1,0:T(8,128)(2,1)S(1)} %get-tuple-element.556), channel_id=1, source_target_pairs={{0,2},{1,3},{2,0},{3,1},{4,6},{5,7},{6,4},{7,5},{8,10},{9,11},{10,... | collective-permute-start | bytes 1572872 | tf_op jit(solution)/shard_map/ppermute | solution.py:928
  530.0 19.0 %collective-permute-start.31 = (bf16[256,1024]{1,0:T(8,128)(2,1)S(1)}, bf16[256,1024]{1,0:T(8,128)(2,1)S(1)}, u32[]{:S(2)}, u32[]{:S(2)}) collective-permute-start(bf16[256,1024]{1,0:T(8,128)(2,1)S(1)} %get-tuple-element.557), channel_id=1, source_target_pairs={{0,4},{4,0},{8,12},{12,8},{16,20},{20,16},{24,28},{28,24},{1,5},{5... | collective-permute-start | bytes 1572872 | tf_op jit(solution)/shard_map/ppermute | solution.py:571
  546.8 21.0 %collective-permute-start.34 = (bf16[512,768]{1,0:T(8,128)(2,1)}, bf16[512,768]{1,0:T(8,128)(2,1)}, u32[]{:S(2)}, u32[]{:S(2)}) collective-permute-start(bf16[512,768]{1,0:T(8,128)(2,1)} %add_convert_fusion.5), channel_id=1, source_target_pairs={{0,8},{4,12},{8,16},{12,20},{16,24},{20,28},{24,0},{28,4},{1,9},{5... | collective-permute-start | bytes 2359304 | tf_op jit(solution)/shard_map/ppermute | solution.py:663
  550.7 26.4 %collective-permute-start.39 = (bf16[256,2048]{1,0:T(8,128)(2,1)}, bf16[256,2048]{1,0:T(8,128)(2,1)}, u32[]{:S(2)}, u32[]{:S(2)}) collective-permute-start(bf16[256,2048]{1,0:T(8,128)(2,1)} %pad_maximum_fusion.3), channel_id=1, source_target_pairs={{0,4},{4,0},{8,12},{12,8},{16,20},{20,16},{24,28},{28,24},{1,5},{5... | collective-permute-start | bytes 3145736 | tf_op jit(solution)/shard_map/ppermute | solution.py:571
  553.1 24.9 %collective-permute-start.40 = (bf16[256,2048]{1,0:T(8,128)(2,1)}, bf16[256,2048]{1,0:T(8,128)(2,1)}, u32[]{:S(2)}, u32[]{:S(2)}) collective-permute-start(bf16[256,2048]{1,0:T(8,128)(2,1)} %pad_maximum_fusion.4), channel_id=1, source_target_pairs={{0,2},{1,3},{2,0},{3,1},{4,6},{5,7},{6,4},{7,5},{8,10},{9,11},{10,... | collective-permute-start | bytes 3145736 | tf_op jit(solution)/shard_map/ppermute | solution.py:928
  (55 other events, 473.7 us)
Sparse Core Ops, SparseCore 0:
  12.7 69.2 all-gather.4
  84.5 54.2 all-gather.6
  140.7 54.3 all-gather.8
  196.8 54.3 all-gather.10
  329.3 128.7 reduce-scatter.2
  461.4 82.9 reduce-scatter.4

commit v7 on v6

--- a/solution.py
+++ b/solution.py
@@ -5,6 +5,7 @@
 import jax.numpy as jnp
 from jax import lax
 from jax.experimental import pallas as pl
+from jax.experimental.layout import Layout, with_layout_constraint
 from jax.experimental.pallas import tpu as pltpu
 from jax.sharding import PartitionSpec as P
 
@@ -21,15 +22,15 @@
 
 def rotary_tables(length, head_dim, rot_dim):
     half_rot = rot_dim // 2
-    inv_freq = 10000.0 ** (-2.0 * jnp.arange(half_rot, dtype=F32) / rot_dim)
-    angles = jnp.arange(length, dtype=F32)[:, None] * inv_freq[None, :]
-    cos, sin = jnp.cos(angles), jnp.sin(angles)
-    rest = jnp.ones((length, head_dim - rot_dim), F32)
-    cosine = jnp.concatenate([cos, cos, rest], axis=1)
-    lower = jnp.concatenate([-sin, 0.0 * sin, 0.0 * rest], axis=1)
-    upper = jnp.concatenate([0.0 * sin, sin, 0.0 * rest], axis=1)
-    copies = LANES // head_dim
-    return tuple(jnp.tile(table, (1, copies)) for table in (cosine, lower, upper))
+    places = lax.broadcasted_iota(jnp.int32, (length, LANES), 0).astype(F32)
+    lanes = lax.rem(lax.broadcasted_iota(jnp.int32, (length, LANES), 1), head_dim)
+    inv_freq = 10000.0 ** (-2.0 * lax.rem(lanes, half_rot).astype(F32) / rot_dim)
+    angles = places * inv_freq
+    sine = jnp.sin(angles)
+    cosine = jnp.where(lanes < rot_dim, jnp.cos(angles), 1.0)
+    lower = jnp.where(lanes < half_rot, -sine, 0.0)
+    upper = jnp.where((lanes >= half_rot) & (lanes < rot_dim), sine, 0.0)
+    return cosine, lower, upper
 
 
 def turn(vals, cosine, lower, upper):
@@ -666,17 +667,24 @@
         def sync(self):
             order.sync(self.came)
 
+        def rows_at(self, half):
+            own = lax.dynamic_slice_in_dim(
+                self.part.val, line_at * line_rows + half * shard_rows, shard_rows, axis=0
+            )
+            came = lax.dynamic_slice_in_dim(self.came.val, half * shard_rows, shard_rows, axis=0)
+            return came.astype(F32) + own.astype(F32)
+
         def swap(self):
             while self.step < line:
                 self.move()
-            total = self.total()
-            self.keep = lax.dynamic_slice_in_dim(total, pair_at * shard_rows, shard_rows, axis=0)
-            give = lax.dynamic_slice_in_dim(total, (1 - pair_at) * shard_rows, shard_rows, axis=0)
-            self.got = Box(swap_pair(give.astype(BF)))
+            order.tie(self.came)
+            self.sent = Box(self.rows_at(1 - pair_at).astype(BF))
+            self.got = Box(swap_pair(self.sent.val))
 
         def halves(self):
-            got = self.got.val.astype(F32)
-            return jnp.where(pair_at == 0, self.keep, got), jnp.where(pair_at == 0, got, self.keep)
+            order.tie(self.came)
+            keep, got = self.rows_at(pair_at), self.got.val.astype(F32)
+            return jnp.where(pair_at == 0, keep, got), jnp.where(pair_at == 0, got, keep)
 
     class SmallSum:
         def __init__(self, everywhere, over_fsdp):
@@ -764,11 +772,7 @@
     attn_ring.move()
     plane_cots[0] = gather_behind(cots[0])
     order.sync(up_shard)
-    order.tie(down_got)
-    down_shard = Box(pair_join(down_half(pair_at), down_got.val))
-    attn_ring.finish()
-    order.sync(small_all)
-    order.tie(up_shard)
+    order.tie(small_all)
     small_all = small_all.val
     vec_size = ln_gain.shape[0]
     gain_vec, shift_vec, bias_out, bias_down = (
@@ -790,7 +794,15 @@
     slots = [lax.rem(line_at + line - step, line) for step in range(line)]
     slots = jnp.stack(slots + [tp_at & 1]).astype(jnp.int32)
     tables = rotary_tables(length, head_dim, ROT)
-    gain_row, shift_row = gain_vec[None], shift_vec[None]
+    prepared = [Box(val) for val in (gain_vec[None], shift_vec[None], qkv_b, up_b, slots, *tables)]
+    for box in prepared:
+        order.sync(box)
+    order.tie(down_got)
+    down_shard = Box(pair_join(down_half(pair_at), down_got.val))
+    order.tokens = [down_shard]
+    attn_ring.finish()
+    order.tie(up_shard, *prepared)
+    gain_row, shift_row, qkv_b, up_b, slots, *tables = (box.val for box in prepared)
     normed, qkvs, rots, attns, lses, acts, slopes = ([None] * micro_count for _ in range(7))
     pre_grads, qkv_grads, qkv_sums, sums, attn_heads = ([None] * micro_count for _ in range(5))
 
@@ -881,12 +893,12 @@
     up_ring.sync()
     up_ring.move()
     attend_piece(1)
-    head_grad_piece(0)
     up_ring.finish()
     down_ring.move()
     up_piece()
     down_ring.sync()
     down_ring.move()
+    head_grad_piece(0)
     attend_back_piece(0)
     down_ring.sync()
     down_ring.move()
@@ -963,6 +975,15 @@
     far = block(1 - pair_at, 1 - y_at)
     from_pair, from_y = Box(swap_pair(far[:, :half])), Box(swap_y(far[:, half:]))
     tail.move()
+    row_major = Layout(major_to_minor=(0, 1))
+    halves = [with_layout_constraint(part, row_major) for part in down_scatter.halves()]
+    down_w_grad = jnp.concatenate([part[:, :mlp_cols].T for part in halves], axis=0)
+    down_w_grad = Box(with_layout_constraint(down_w_grad, row_major))
+    out_w_grad = jnp.concatenate([part[:, mlp_cols:].T for part in halves], axis=0)
+    out_w_grad = Box(with_layout_constraint(out_w_grad, row_major))
+    for box in (down_w_grad, out_w_grad):
+        order.sync(box)
+
     qkv_scatter.sync()
     order.tie()
     qkv_scatter.move()
@@ -976,32 +997,37 @@
     )
     for_pair, for_y = Box(for_pair), Box(for_y)
     from_pair, from_y = Box(swap_pair(for_pair.val)), Box(swap_y(for_y.val))
-    order.sync(for_pair)
-    order.sync(for_y)
+    own_block = Box(block(pair_at, y_at))
+    for box in (for_pair, for_y, own_block):
+        order.sync(box)
     order.tie(back_sum)
     gained = Box(norm_back(inputs[:, 0], cotangent[:, 0], [back_sum.val], gain_row, 0))
-    halves = down_scatter.halves()
-    down_w_grad = Box(jnp.concatenate([part[:, :mlp_cols].T for part in halves], axis=0))
-    out_w_grad = Box(jnp.concatenate([part[:, mlp_cols:].T for part in halves], axis=0))
-    up_w_grad = Box(jnp.concatenate(up_scatter.halves(), axis=1))
     order.sync(gained)
     qkv_scatter.sync()
     order.sync(tail.cur)
     order.tie(tail.cur)
     tail.move()
     qkv_scatter.swap()
-    for box in (down_w_grad, out_w_grad, up_w_grad):
-        order.sync(box)
-
-    def qkv_columns(vals):
-        return vals.reshape(shard_rows, pairs, 3, LANES).transpose(0, 2, 1, 3).reshape(shard_rows, 3, attn_cols)
-
+    up_w_grad = Box(jnp.concatenate(up_scatter.halves(), axis=1))
+    order.sync(up_w_grad)
     order.tie(from_pair, from_y)
-    last_pieces = [block(pair_at, y_at), from_pair.val, from_y.val]
+    last_pieces = [own_block.val, from_pair.val, from_y.val]
     gained = Box(norm_back(inputs[:, 0], cotangent[:, 0], last_pieces, gain_row, 1, gained.val))
     order.tokens = [gained]
     order.tie(qkv_scatter.got, tail.cur)
-    qkv_w_grad = Box(jnp.concatenate([qkv_columns(part) for part in qkv_scatter.halves()], axis=2))
+    halves = qkv_scatter.halves()
+    planes = [
+        jnp.concatenate(
+            [
+                part[:, (pair * 3 + plane) * LANES : (pair * 3 + plane + 1) * LANES]
+                for part in halves
+                for pair in range(pairs)
+            ],
+            axis=1,
+        )
+        for plane in range(3)
+    ]
+    qkv_w_grad = jnp.stack(planes, axis=0).transpose(1, 0, 2)
     small_sums, bias_sums = tail.split()
     branch_sum = branch_sum.val.reshape(micro_count, token_rows, model_width)
     output = (inputs[:, 0].astype(F32) + branch_sum.astype(F32) + bias_both).astype(BF)
@@ -1019,7 +1045,7 @@
         gained.val[:, None],
         gain_sum,
         shift_sum,
-        qkv_w_grad.val,
+        qkv_w_grad,
         qkv_b_sum,
         out_w_grad.val,
         bias_sum,

time: 611 us -> 599 us (0.980)
  waiting for transfers between devices: 108 us -> 91.4 us
  other arithmetic: 41.2 us -> 50.9 us
  local copies, waits for them, and re-layouts: 38.8 us -> 31.5 us
    all_gather x4, waiting for transfers between devices: 9.59 us -> 0.06 us  [gather_plane(): lax.all_gather(vals, both_axes, axis=0, tiled=True, axis_index_groups=pla...]
    ppermute x9, waiting for transfers between devices: 26.1 us -> 17.3 us  [move(): self.came = Box(lax.ppermute(sent.val, 'fsdp', ring))]
    select_n x3 -> x4, other arithmetic: 0.63 us -> 8.15 us  [the longest x3 4.97 us: halves(): jnp.where(pair_at == 0, keep, got)]
    unnamed x87 -> x90, local copies, waits for them, and re-layouts: 15.1 us -> 11.5 us
  transfers between devices with their start and end apart: 47 -> 47, of which waited for: 21 -> 18; matrix products, arithmetic and copies ran while one was open for 10% -> 12% of each run, Pallas kernels for 59% -> 60%
where the time goes in v7:
time: 599 us; the launch traced here: 590 us
  Pallas kernels  356 us (59%)
  waiting for transfers between devices  91.4 us (15%)
  other arithmetic  50.9 us (8%)
  starting transfers between devices  44.8 us (7%)
  local copies, waits for them, and re-layouts  31.5 us (5%)
  between operations  15.3 us (3%)
    pallas_call x9, Pallas kernels, rows_call(): pl.pallas_call(kernel, grid_spec=pltpu.PrefetchScalarGridSpec(num_scalar_...  188 us
    pallas_call x3, Pallas kernels, weight_grad(): pl.pallas_call(kernel, grid=(micro_count * steps,), in_specs=[side(micro,...  77.7 us
    ppermute x8, waiting for transfers between devices, swap_pair(): return lax.ppermute(vals, 'fsdp', [(f, f ^ 1) for f in range(fsdp_size)])  43.2 us
    pallas_call x2, Pallas kernels, attend_back(): pl.pallas_call(functools.partial(attend_back_kernel, head_dim, block), gr...  42.2 us
    pallas_call x2, Pallas kernels, attend(): pl.pallas_call(functools.partial(attend_kernel, head_dim, block), grid=(s...  32.9 us
    ppermute x9, waiting for transfers between devices, move(): self.parts.append(Box(lax.ppermute(self.parts[-1].val, 'fsdp', ring)))  23.8 us
    ppermute x9, waiting for transfers between devices, move(): self.came = Box(lax.ppermute(sent.val, 'fsdp', ring))  17.3 us
  transfers between devices with their start and end apart: 47, of which 18 were waited for; matrix products, arithmetic and copies ran while one was open for 12% of the time, Pallas kernels for 60%

profile of v7, /device:TPU:0, one launch (start us, length us, event | category | flops | bytes accessed | tf_op | source)
XLA Modules:
  0.0 589.7 jit_solution(11809553287586759981)
XLA Ops:
  19.2 11.8 %collective-permute-done = bf16[256,1024]{1,0:T(8,128)(2,1)S(1)} collective-permute-done((bf16[256,1024]{1,0:T(8,128)(2,1)S(1)}, bf16[256,1024]{1,0:T(8,128)(2,1)S(1)}, u32[]{:S(2)}, u32[]{:S(2)}) %collective-permute-start) | collective-permute-done | bytes 524320 | tf_op jit(solution)/shard_map/ppermute | solution.py:572
  42.6 12.7 %collective-permute-done.4.refs_1_.refs_5_ = bf16[512,1024]{1,0:T(8,128)(2,1)S(1)} collective-permute-done((bf16[512,1024]{1,0:T(8,128)(2,1)S(1)}, bf16[512,1024]{1,0:T(8,128)(2,1)S(1)}, u32[]{:S(2)}, u32[]{:S(2)}) %collective-permute-start.4) | collective-permute-done | bytes 1048608 | tf_op jit(solution)/shard_map/ppermute | solution.py:634
  67.5 14.4 %collective-permute-done.3 = bf16[256,1024]{1,0:T(8,128)(2,1)} collective-permute-done((bf16[256,1024]{1,0:T(8,128)(2,1)}, bf16[256,1024]{1,0:T(8,128)(2,1)}, u32[]{:S(2)}, u32[]{:S(2)}) %collective-permute-start.3) | collective-permute-done | bytes 524320 | tf_op jit(solution)/shard_map/ppermute | solution.py:572
  85.3 3.2 fusion.2
  94.5 13.2 %collective-permute-done.6 = bf16[256,1024]{1,0:T(8,128)(2,1)} collective-permute-done((bf16[256,1024]{1,0:T(8,128)(2,1)}, bf16[256,1024]{1,0:T(8,128)(2,1)}, u32[]{:S(2)}, u32[]{:S(2)}) %collective-permute-start.6) | collective-permute-done | bytes 524320 | tf_op jit(solution)/shard_map/ppermute | solution.py:572
  111.6 16.1 %shard_map.213 = (bf16[2048,2048]{1,0:T(8,128)(2,1)}, f32[2048,768]{1,0:T(8,128)}) custom-call(s32[5]{0:T(128)} %stack.35.slots_ref, bf16[2048,2048]{1,0:T(8,128)(2,1)} %all-gather.5.cloned.1.call-done.rows_ref, f32[1,2048]{1,0:T(1,128)} %reshape.189.gain_ref, f32[1,2048]{1,0:T(1,128)} %reshape.190.shift_ref, f32[1,768]{1,0:T(1,128)} %reshape.177.bias_ref, ...), custom_call_target="tpu_custom_call" | custom-call | flops 100663296 | bytes 360448 | tf_op jit(solution)/shard_map/pallas_call | solution.py:220
  127.8 4.9 collective-permute-done.12.refs_3_.refs_5_
  133.9 16.3 %shard_map.214 = (bf16[2048,768]{1,0:T(8,128)(2,1)}, bf16[2048,256]{1,0:T(8,128)(2,1)}, f32[4,2,1024]{2,1,0:T(2,128)}) custom-call(f32[2048,768]{1,0:T(8,128)} %get-tuple-element.369.qkv_ref, f32[1024,128]{1,0:T(8,128)} %get-tuple-element.370.cos_ref, f32[1024,128]{1,0:T(8,128)} %get-tuple-element.371.low_ref, f32[1024,128]{1,0:T(8,128)} %get-tuple-element.372.up_ref), custom_call_target="tpu_custom_call" | custom-call | flops 100663296 | bytes 131072 | tf_op jit(solution)/shard_map/pallas_call | solution.py:151
  150.2 16.8 %shard_map.215 = (bf16[2048,2048]{1,0:T(8,128)(2,1)}, f32[2048,768]{1,0:T(8,128)}) custom-call(s32[5]{0:T(128)} %stack.35.slots_ref, bf16[2048,2048]{1,0:T(8,128)(2,1)} %all-gather.7.cloned.1.call-done.rows_ref, f32[1,2048]{1,0:T(1,128)} %reshape.189.gain_ref, f32[1,2048]{1,0:T(1,128)} %reshape.190.shift_ref, f32[1,768]{1,0:T(1,128)} %reshape.177.bias_ref, ...), custom_call_target="tpu_custom_call" | custom-call | flops 100663296 | bytes 360448 | tf_op jit(solution)/shard_map/pallas_call | solution.py:220
  167.1 16.7 %shard_map.216 = (bf16[2048,768]{1,0:T(8,128)(2,1)}, bf16[2048,256]{1,0:T(8,128)(2,1)}, f32[4,2,1024]{2,1,0:T(2,128)}) custom-call(f32[2048,768]{1,0:T(8,128)} %get-tuple-element.381.qkv_ref, f32[1024,128]{1,0:T(8,128)} %get-tuple-element.370.cos_ref, f32[1024,128]{1,0:T(8,128)} %get-tuple-element.371.low_ref, f32[1024,128]{1,0:T(8,128)} %get-tuple-element.372.up_ref), custom_call_target="tpu_custom_call" | custom-call | flops 100663296 | bytes 131072 | tf_op jit(solution)/shard_map/pallas_call | solution.py:151
  183.7 6.3 %collective-permute-done.14.refs_5_.refs_7_ = bf16[512,1024]{1,0:T(8,128)(2,1)S(1)} collective-permute-done((bf16[512,1024]{1,0:T(8,128)(2,1)S(1)}, bf16[512,1024]{1,0:T(8,128)(2,1)S(1)}, u32[]{:S(2)}, u32[]{:S(2)}) %collective-permute-start.14) | collective-permute-done | bytes 1048608 | tf_op jit(solution)/shard_map/ppermute | solution.py:634
  191.0 32.6 %shard_map.217 = (bf16[2048,1024]{1,0:T(8,128)(2,1)}, bf16[2048,1024]{1,0:T(8,128)(2,1)}, bf16[2048,1024]{1,0:T(8,128)(2,1)}, bf16[2048,1024]{1,0:T(8,128)(2,1)}) custom-call(s32[5]{0:T(128)} %stack.35.slots_ref, f32[1,1024]{1,0:T(1,128)} %constant_dynamic-slice_fusion.9.bias_ref, bf16[2048,2048]{1,0:T(8,128)(2,1)} %get-tuple-element.472.refs_0_, ...), custom_call_target="tpu_custom_call" | custom-call | flops 268435456 | bytes 524288 | tf_op jit(solution)/shard_map/pallas_call | solution.py:220
  223.7 7.8 %shard_map.218.grad_ref = bf16[2048,256]{1,0:T(8,128)(2,1)} custom-call(s32[5]{0:T(128)} %stack.35.slots_ref, bf16[2048,2048]{1,0:T(8,128)(2,1)} %all-gather.9.cloned.1.call-done.rows_ref.refs_0_, bf16[512,1024]{1,0:T(8,128)(2,1)} %copy-done, bf16[512,1024]{1,0:T(8,128)(2,1)} %copy-done.2, bf16[512,1024]{1,0:T(8,128)(2,1)} %copy-done.3, ...), custom_call_target="tpu_custom_call" | custom-call | flops 33554432 | bytes 147456 | tf_op jit(solution)/shard_map/pallas_call | solution.py:220
  231.5 21.1 %shard_map.219 = (bf16[2048,768]{1,0:T(8,128)(2,1)}, f32[16,768]{1,0:T(8,128)}) custom-call(bf16[2048,768]{1,0:T(8,128)(2,1)} %get-tuple-element.405.rot_ref, bf16[2048,256]{1,0:T(8,128)(2,1)} %shard_map.218.grad_ref, bf16[2048,256]{1,0:T(8,128)(2,1)} %get-tuple-element.419.attn_ref.refs_4_.refs_0_, f32[4,2,1024]{2,1,0:T(2,128)} %get-tuple-element.407.lse_ref, ...), custom_call_target="tpu_custom_call" | custom-call | flops 201326592 | bytes 131072 | tf_op jit(solution)/shard_map/pallas_call | solution.py:176
  252.7 3.3 collective-permute-start.17
  256.0 30.5 %shard_map.220 = bf16[2048,1280]{1,0:T(8,128)(2,1)} custom-call(bf16[2048,2048]{1,0:T(8,128)(2,1)} %all-gather.9.cloned.1.call-done.rows_ref.refs_0_, bf16[2048,2048]{1,0:T(8,128)(2,1)} %all-gather.11.cloned.1.call-done.refs_1_.rows_ref, bf16[2048,1024]{1,0:T(8,128)(2,1)} %get-tuple-element.421.refs_2_, bf16[2048,1024]{1,0:T(8,128)(2,1)} %get-tuple-element.422.refs_3_, ...), custom_call_target="tpu_custom_call" | custom-call | flops 335544320 | bytes 425984 | tf_op jit(solution)/shard_map/pallas_call | solution.py:525
  290.3 30.2 %shard_map.221 = bf16[8,2,256,2048]{3,2,1,0:T(8,128)(2,1)} custom-call(s32[5]{0:T(128)} %stack.35.slots_ref, bf16[2048,256]{1,0:T(8,128)(2,1)} %get-tuple-element.419.attn_ref.refs_4_.refs_0_, bf16[2048,256]{1,0:T(8,128)(2,1)} %get-tuple-element.456.refs_5_.refs_1_.attn_ref, bf16[2048,1024]{1,0:T(8,128)(2,1)} %get-tuple-element.421.refs_2_, ...), custom_call_target="tpu_custom_call" | custom-call | flops 335544320 | bytes 294912 | tf_op jit(solution)/shard_map/pallas_call | solution.py:220
  323.4 27.7 %shard_map.222 = (bf16[2048,1024]{1,0:T(8,128)(2,1)}, bf16[2048,1024]{1,0:T(8,128)(2,1)}, f32[8,1024]{1,0:T(8,128)}) custom-call(s32[5]{0:T(128)} %stack.35.slots_ref, bf16[2048,2048]{1,0:T(8,128)(2,1)} %all-gather.9.cloned.1.call-done.rows_ref.refs_0_, bf16[2048,2048]{1,0:T(8,128)(2,1)} %all-gather.11.cloned.1.call-done.refs_1_.rows_ref, ...), custom_call_target="tpu_custom_call" | custom-call | flops 268435456 | bytes 524288 | tf_op jit(solution)/shard_map/pallas_call | solution.py:220
  354.9 26.0 %shard_map.223 = bf16[2048,1024]{1,0:T(8,128)(2,1)} custom-call(bf16[2048,2048]{1,0:T(8,128)(2,1)} %get-tuple-element.472.refs_0_, bf16[2048,2048]{1,0:T(8,128)(2,1)} %get-tuple-element.473.refs_1_, bf16[2048,1024]{1,0:T(8,128)(2,1)} %get-tuple-element.464.refs_2_.two_ref, bf16[2048,1024]{1,0:T(8,128)(2,1)} %get-tuple-element.483.refs_3_.two_ref), custom_call_target="tpu_custom_call" | custom-call | flops 268435456 | bytes 393216 | tf_op jit(solution)/shard_map/pallas_call | solution.py:525
  381.0 3.8 collective-permute-done.20
  389.2 7.7 %shard_map.224.grad_ref = bf16[2048,256]{1,0:T(8,128)(2,1)} custom-call(s32[5]{0:T(128)} %stack.35.slots_ref, bf16[2048,2048]{1,0:T(8,128)(2,1)} %all-gather.11.cloned.1.call-done.refs_1_.rows_ref, bf16[512,1024]{1,0:T(8,128)(2,1)} %copy-done, bf16[512,1024]{1,0:T(8,128)(2,1)} %copy-done.2, bf16[512,1024]{1,0:T(8,128)(2,1)} %copy-done.3, ...), custom_call_target="tpu_custom_call" | custom-call | flops 33554432 | bytes 147456 | tf_op jit(solution)/shard_map/pallas_call | solution.py:220
  396.9 21.1 %shard_map.225 = (bf16[2048,768]{1,0:T(8,128)(2,1)}, f32[16,768]{1,0:T(8,128)}) custom-call(bf16[2048,768]{1,0:T(8,128)(2,1)} %get-tuple-element.454.rot_ref, bf16[2048,256]{1,0:T(8,128)(2,1)} %shard_map.224.grad_ref, bf16[2048,256]{1,0:T(8,128)(2,1)} %get-tuple-element.456.refs_5_.refs_1_.attn_ref, f32[4,2,1024]{2,1,0:T(2,128)} %get-tuple-element.457.lse_ref, ...), custom_call_target="tpu_custom_call" | custom-call | flops 201326592 | bytes 131072 | tf_op jit(solution)/shard_map/pallas_call | solution.py:176
  421.7 24.2 %shard_map.226 = (bf16[2048,2048]{1,0:T(8,128)(2,1)}, f32[8,2048]{1,0:T(8,128)}) custom-call(s32[5]{0:T(128)} %stack.35.slots_ref, bf16[2048,768]{1,0:T(8,128)(2,1)} %get-tuple-element.474.one_ref.refs_2_, bf16[2048,1024]{1,0:T(8,128)(2,1)} %get-tuple-element.464.refs_2_.two_ref, bf16[2048,2048]{1,0:T(8,128)(2,1)} %all-gather.5.cloned.1.call-done.rows_ref, ...), custom_call_target="tpu_custom_call" | custom-call | flops 234881024 | bytes 376832 | tf_op jit(solution)/shard_map/pallas_call | solution.py:220
  448.7 21.1 %shard_map.227 = bf16[2048,768]{1,0:T(8,128)(2,1)} custom-call(bf16[2048,2048]{1,0:T(8,128)(2,1)} %get-tuple-element.472.refs_0_, bf16[2048,2048]{1,0:T(8,128)(2,1)} %get-tuple-element.473.refs_1_, bf16[2048,768]{1,0:T(8,128)(2,1)} %get-tuple-element.474.one_ref.refs_2_, bf16[2048,768]{1,0:T(8,128)(2,1)} %get-tuple-element.482.refs_3_.one_ref), custom_call_target="tpu_custom_call" | custom-call | flops 201326592 | bytes 360448 | tf_op jit(solution)/shard_map/pallas_call | solution.py:525
  476.6 25.0 %shard_map.228 = (bf16[1024,2048]{1,0:T(8,128)(2,1)}, bf16[1024,2048]{1,0:T(8,128)(2,1)}, f32[8,2048]{1,0:T(8,128)}) custom-call(s32[5]{0:T(128)} %stack.35.slots_ref, bf16[2048,768]{1,0:T(8,128)(2,1)} %get-tuple-element.482.refs_3_.one_ref, bf16[2048,1024]{1,0:T(8,128)(2,1)} %get-tuple-element.483.refs_3_.two_ref, ...), custom_call_target="tpu_custom_call" | custom-call | flops 234881024 | bytes 376832 | tf_op jit(solution)/shard_map/pallas_call | solution.py:220
  506.1 3.9 fusion.1
  514.2 4.7 add_convert_fusion
  537.1 3.2 collective-permute-done.31
  547.3 4.7 shard_map.229.refs_3_
  551.9 6.1 %collective-permute-done.36 = bf16[512,768]{1,0:T(8,128)(2,1)} collective-permute-done((bf16[512,768]{1,0:T(8,128)(2,1)}, bf16[512,768]{1,0:T(8,128)(2,1)}, u32[]{:S(2)}, u32[]{:S(2)}) %collective-permute-start.36) | collective-permute-done | bytes 786464 | tf_op jit(solution)/shard_map/ppermute | solution.py:664
  558.4 4.0 collective-permute-start.38
  569.7 5.1 shard_map.230
  (291 shorter events, 128.4 us)
Async XLA Ops:
  7.2 103.5 %all-gather.5.cloned.1.call-start = ((), (), s32[]{:S(2)}) async-start(), calls=%async_computation.2 | async-start | bytes 9437184 | tf_op jit(solution)/shard_map/all_gather | solution.py:575
  12.6 137.5 %all-gather.7.cloned.1.call-start = ((), (), s32[]{:S(2)}) async-start(), calls=%async_computation.3 | async-start | bytes 9437184 | tf_op jit(solution)/shard_map/all_gather | solution.py:575
  12.7 18.3 %collective-permute-start = (bf16[256,1024]{1,0:T(8,128)(2,1)S(1)}, bf16[256,1024]{1,0:T(8,128)(2,1)S(1)}, u32[]{:S(2)}, u32[]{:S(2)}) collective-permute-start(bf16[256,1024]{1,0:T(8,128)(2,1)S(1)} %pad_maximum_fusion.4), channel_id=1, source_target_pairs={{0,4},{4,0},{8,12},{12,8},{16,20},{20,16},{24,28},{28,24},{1,5},{5... | collective-permute-start | bytes 1572872 | tf_op jit(solution)/shard_map/ppermute | solution.py:572
  31.4 192.3 %all-gather.9.cloned.1.call-start = ((), (), s32[]{:S(2)}) async-start(), calls=%async_computation.4 | async-start | bytes 9437184 | tf_op jit(solution)/shard_map/all_gather | solution.py:575
  31.5 23.8 %collective-permute-start.4 = (bf16[512,1024]{1,0:T(8,128)(2,1)S(1)}, bf16[512,1024]{1,0:T(8,128)(2,1)S(1)}, u32[]{:S(2)}, u32[]{:S(2)}) collective-permute-start(bf16[512,1024]{1,0:T(8,128)(2,1)S(1)} %maximum_select_fusion.refs_0_.refs_4_), channel_id=1, source_target_pairs={{0,8},{4,12},{8,16},{12,20},{16,24},{20,28},{24,0},{28,4},{1,9},{5... | collective-permute-start | bytes 3145736 | tf_op jit(solution)/shard_map/ppermute | solution.py:634
  55.3 26.6 %collective-permute-start.7 = (bf16[512,1024]{1,0:T(8,128)(2,1)S(1)}, bf16[512,1024]{1,0:T(8,128)(2,1)S(1)}, u32[]{:S(2)}, u32[]{:S(2)}) collective-permute-start(bf16[512,1024]{1,0:T(8,128)(2,1)S(1)} %collective-permute-done.4.refs_1_.refs_5_), channel_id=1, source_target_pairs={{0,8},{4,12},{8,16},{12,20},{16,24},{20,28},{24,0},{28,4},{1,9},{5... | collective-permute-start | bytes 3145736 | tf_op jit(solution)/shard_map/ppermute | solution.py:634
  57.7 24.2 %collective-permute-start.3 = (bf16[256,1024]{1,0:T(8,128)(2,1)}, bf16[256,1024]{1,0:T(8,128)(2,1)}, u32[]{:S(2)}, u32[]{:S(2)}) collective-permute-start(bf16[256,1024]{1,0:T(8,128)(2,1)} %get-tuple-element.305), channel_id=1, source_target_pairs={{0,4},{4,0},{8,12},{12,8},{16,20},{20,16},{24,28},{28,24},{1,5},{5... | collective-permute-start | bytes 1572872 | tf_op jit(solution)/shard_map/ppermute | solution.py:572
  61.7 20.2 %collective-permute-start.10 = (bf16[8,704]{1,0:T(8,128)(2,1)S(1)}, bf16[8,704]{1,0:T(8,128)(2,1)S(1)}, u32[]{:S(2)}, u32[]{:S(2)}) collective-permute-start(bf16[8,704]{1,0:T(8,128)(2,1)S(1)} %maximum_select_fusion.3), channel_id=1, source_target_pairs={{0,8},{4,12},{8,0},{12,4},{16,24},{20,28},{24,16},{28,20},{1,9},{5... | collective-permute-start | bytes 33800 | tf_op jit(solution)/shard_map/ppermute | solution.py:739
  81.9 174.1 %all-gather.11.cloned.1.call-start = ((), (), s32[]{:S(2)}) async-start(), calls=%async_computation.5 | async-start | bytes 9437184 | tf_op jit(solution)/shard_map/all_gather | solution.py:575
  83.8 26.9 %collective-permute-start.11 = (bf16[512,1024]{1,0:T(8,128)(2,1)S(1)}, bf16[512,1024]{1,0:T(8,128)(2,1)S(1)}, u32[]{:S(2)}, u32[]{:S(2)}) collective-permute-start(bf16[512,1024]{1,0:T(8,128)(2,1)S(1)} %collective-permute-done.7.refs_2_.refs_6_), channel_id=1, source_target_pairs={{0,8},{4,12},{8,16},{12,20},{16,24},{20,28},{24,0},{28,4},{1,9},{5... | collective-permute-start | bytes 3145736 | tf_op jit(solution)/shard_map/ppermute | solution.py:634
  88.5 19.3 %collective-permute-start.6 = (bf16[256,1024]{1,0:T(8,128)(2,1)}, bf16[256,1024]{1,0:T(8,128)(2,1)}, u32[]{:S(2)}, u32[]{:S(2)}) collective-permute-start(bf16[256,1024]{1,0:T(8,128)(2,1)} %bitcast), channel_id=1, source_target_pairs={{0,4},{4,0},{8,12},{12,8},{16,20},{20,16},{24,28},{28,24},{1,5},{5... | collective-permute-start | bytes 1572872 | tf_op jit(solution)/shard_map/ppermute | solution.py:572
  110.7 22.0 %collective-permute-start.12 = (bf16[512,1024]{1,0:T(8,128)(2,1)S(1)}, bf16[512,1024]{1,0:T(8,128)(2,1)S(1)}, u32[]{:S(2)}, u32[]{:S(2)}) collective-permute-start(bf16[512,1024]{1,0:T(8,128)(2,1)S(1)} %maximum_select_fusion.1.refs_2_.refs_4_), channel_id=1, source_target_pairs={{0,8},{4,12},{8,16},{12,20},{16,24},{20,28},{24,0},{28,4},{1,9},{5... | collective-permute-start | bytes 3145736 | tf_op jit(solution)/shard_map/ppermute | solution.py:634
  132.7 340.0 %reduce-scatter.3.cloned.1.call-start = ((), (), s32[]{:S(2)}) async-start(), calls=%async_computation.6 | async-start | bytes 18874368 | tf_op jit(solution)/shard_map/reduce_scatter | solution.py:578
  132.7 34.3 %collective-permute-start.13 = (bf16[512,1024]{1,0:T(8,128)(2,1)S(1)}, bf16[512,1024]{1,0:T(8,128)(2,1)S(1)}, u32[]{:S(2)}, u32[]{:S(2)}) collective-permute-start(bf16[512,1024]{1,0:T(8,128)(2,1)S(1)} %collective-permute-done.12.refs_3_.refs_5_), channel_id=1, source_target_pairs={{0,8},{4,12},{8,16},{12,20},{16,24},{20,28},{24,0},{28,4},{1,9},{5... | collective-permute-start | bytes 3145736 | tf_op jit(solution)/shard_map/ppermute | solution.py:634
  167.0 23.0 %collective-permute-start.14 = (bf16[512,1024]{1,0:T(8,128)(2,1)S(1)}, bf16[512,1024]{1,0:T(8,128)(2,1)S(1)}, u32[]{:S(2)}, u32[]{:S(2)}) collective-permute-start(bf16[512,1024]{1,0:T(8,128)(2,1)S(1)} %collective-permute-done.13.refs_4_.refs_6_), channel_id=1, source_target_pairs={{0,8},{4,12},{8,16},{12,20},{16,24},{20,28},{24,0},{28,4},{1,9},{5... | collective-permute-start | bytes 3145736 | tf_op jit(solution)/shard_map/ppermute | solution.py:634
  190.0 33.6 %collective-permute-start.15 = (bf16[512,1024]{1,0:T(8,128)(2,1)S(1)}, bf16[512,1024]{1,0:T(8,128)(2,1)S(1)}, u32[]{:S(2)}, u32[]{:S(2)}) collective-permute-start(bf16[512,1024]{1,0:T(8,128)(2,1)S(1)} %copy-done.10), channel_id=1, source_target_pairs={{0,8},{4,12},{8,16},{12,20},{16,24},{20,28},{24,0},{28,4},{1,9},{5... | collective-permute-start | bytes 3145736 | tf_op jit(solution)/shard_map/ppermute | solution.py:634
  223.6 29.0 %collective-permute-start.16 = (bf16[512,1024]{1,0:T(8,128)(2,1)S(1)}, bf16[512,1024]{1,0:T(8,128)(2,1)S(1)}, u32[]{:S(2)}, u32[]{:S(2)}) collective-permute-start(bf16[512,1024]{1,0:T(8,128)(2,1)S(1)} %collective-permute-done.15.refs_9_.refs_5_), channel_id=1, source_target_pairs={{0,8},{4,12},{8,16},{12,20},{16,24},{20,28},{24,0},{28,4},{1,9},{5... | collective-permute-start | bytes 3145736 | tf_op jit(solution)/shard_map/ppermute | solution.py:634
  252.7 35.3 %collective-permute-start.17 = (bf16[512,1024]{1,0:T(8,128)(2,1)S(1)}, bf16[512,1024]{1,0:T(8,128)(2,1)S(1)}, u32[]{:S(2)}, u32[]{:S(2)}) collective-permute-start(bf16[512,1024]{1,0:T(8,128)(2,1)S(1)} %collective-permute-done.16.refs_10_.refs_6_), channel_id=1, source_target_pairs={{0,8},{4,12},{8,16},{12,20},{16,24},{20,28},{24,0},{28,4},{1,9},{5... | collective-permute-start | bytes 3145736 | tf_op jit(solution)/shard_map/ppermute | solution.py:634
  288.0 32.5 %collective-permute-start.18 = (bf16[512,1280]{1,0:T(8,128)(2,1)S(1)}, bf16[512,1280]{1,0:T(8,128)(2,1)S(1)}, u32[]{:S(2)}, u32[]{:S(2)}) collective-permute-start(bf16[512,1280]{1,0:T(8,128)(2,1)S(1)} %constant_dynamic-slice_fusion.7), channel_id=1, source_target_pairs={{0,8},{4,12},{8,16},{12,20},{16,24},{20,28},{24,0},{28,4},{1,9},{5... | collective-permute-start | bytes 3932168 | tf_op jit(solution)/shard_map/ppermute | solution.py:664
  320.5 226.7 %reduce-scatter.5.cloned.1.call-start = ((), (), s32[]{:S(2)}) async-start(), calls=%async_computation.7 | async-start | bytes 9437184 | tf_op jit(solution)/shard_map/reduce_scatter | solution.py:578
  322.2 31.0 %collective-permute-start.19 = (bf16[512,1280]{1,0:T(8,128)(2,1)S(1)}, bf16[512,1280]{1,0:T(8,128)(2,1)S(1)}, u32[]{:S(2)}, u32[]{:S(2)}) collective-permute-start(bf16[512,1280]{1,0:T(8,128)(2,1)S(1)} %add_convert_fusion.2), channel_id=1, source_target_pairs={{0,8},{4,12},{8,16},{12,20},{16,24},{20,28},{24,0},{28,4},{1,9},{5... | collective-permute-start | bytes 3932168 | tf_op jit(solution)/shard_map/ppermute | solution.py:664
  354.9 29.9 %collective-permute-start.20 = (bf16[512,1280]{1,0:T(8,128)(2,1)S(1)}, bf16[512,1280]{1,0:T(8,128)(2,1)S(1)}, u32[]{:S(2)}, u32[]{:S(2)}) collective-permute-start(bf16[512,1280]{1,0:T(8,128)(2,1)S(1)} %add_convert_fusion.1), channel_id=1, source_target_pairs={{0,8},{4,12},{8,16},{12,20},{16,24},{20,28},{24,0},{28,4},{1,9},{5... | collective-permute-start | bytes 3932168 | tf_op jit(solution)/shard_map/ppermute | solution.py:664
  386.1 31.9 %collective-permute-start.21 = (bf16[512,1024]{1,0:T(8,128)(2,1)S(1)}, bf16[512,1024]{1,0:T(8,128)(2,1)S(1)}, u32[]{:S(2)}, u32[]{:S(2)}) collective-permute-start(bf16[512,1024]{1,0:T(8,128)(2,1)S(1)} %constant_dynamic-slice_fusion.6), channel_id=1, source_target_pairs={{0,8},{4,12},{8,16},{12,20},{16,24},{20,28},{24,0},{28,4},{1,9},{5... | collective-permute-start | bytes 3145736 | tf_op jit(solution)/shard_map/ppermute | solution.py:664
  387.9 30.2 %collective-permute-start.22 = (bf16[256,1280]{1,0:T(8,128)(2,1)S(1)}, bf16[256,1280]{1,0:T(8,128)(2,1)S(1)}, u32[]{:S(2)}, u32[]{:S(2)}) collective-permute-start(bf16[256,1280]{1,0:T(8,128)(2,1)S(1)} %add_convert_fusion.7), channel_id=1, source_target_pairs={{0,4},{4,0},{8,12},{12,8},{16,20},{20,16},{24,28},{28,24},{1,5},{5... | collective-permute-start | bytes 1966088 | tf_op jit(solution)/shard_map/ppermute | solution.py:572
  420.5 25.4 %collective-permute-start.23 = (bf16[512,1024]{1,0:T(8,128)(2,1)S(1)}, bf16[512,1024]{1,0:T(8,128)(2,1)S(1)}, u32[]{:S(2)}, u32[]{:S(2)}) collective-permute-start(bf16[512,1024]{1,0:T(8,128)(2,1)S(1)} %add_convert_fusion.4), channel_id=1, source_target_pairs={{0,8},{4,12},{8,16},{12,20},{16,24},{20,28},{24,0},{28,4},{1,9},{5... | collective-permute-start | bytes 3145736 | tf_op jit(solution)/shard_map/ppermute | solution.py:664
  447.7 25.0 %collective-permute-start.24 = (bf16[512,1024]{1,0:T(8,128)(2,1)S(1)}, bf16[512,1024]{1,0:T(8,128)(2,1)S(1)}, u32[]{:S(2)}, u32[]{:S(2)}) collective-permute-start(bf16[512,1024]{1,0:T(8,128)(2,1)S(1)} %add_convert_fusion.3), channel_id=1, source_target_pairs={{0,8},{4,12},{8,16},{12,20},{16,24},{20,28},{24,0},{28,4},{1,9},{5... | collective-permute-start | bytes 3145736 | tf_op jit(solution)/shard_map/ppermute | solution.py:664
  474.3 28.3 %collective-permute-start.25 = (bf16[512,768]{1,0:T(8,128)(2,1)S(1)}, bf16[512,768]{1,0:T(8,128)(2,1)}, u32[]{:S(2)}, u32[]{:S(2)}) collective-permute-start(bf16[512,768]{1,0:T(8,128)(2,1)S(1)} %constant_dynamic-slice_fusion.5), channel_id=1, source_target_pairs={{0,8},{4,12},{8,16},{12,20},{16,24},{20,28},{24,0},{28,4},{1,9},{5... | collective-permute-start | bytes 2359304 | tf_op jit(solution)/shard_map/ppermute | solution.py:664
  475.6 27.0 %collective-permute-start.26 = (bf16[256,1024]{1,0:T(8,128)(2,1)S(1)}, bf16[256,1024]{1,0:T(8,128)(2,1)S(1)}, u32[]{:S(2)}, u32[]{:S(2)}) collective-permute-start(bf16[256,1024]{1,0:T(8,128)(2,1)S(1)} %add_convert_fusion.10), channel_id=1, source_target_pairs={{0,4},{4,0},{8,12},{12,8},{16,20},{20,16},{24,28},{28,24},{1,5},{5... | collective-permute-start | bytes 1572872 | tf_op jit(solution)/shard_map/ppermute | solution.py:572
  513.0 21.9 %collective-permute-start.32 = (bf16[512,768]{1,0:T(8,128)(2,1)}, bf16[512,768]{1,0:T(8,128)(2,1)}, u32[]{:S(2)}, u32[]{:S(2)}) collective-permute-start(bf16[512,768]{1,0:T(8,128)(2,1)} %add_convert_fusion.6), channel_id=1, source_target_pairs={{0,8},{4,12},{8,16},{12,20},{16,24},{20,28},{24,0},{28,4},{1,9},{5... | collective-permute-start | bytes 2359304 | tf_op jit(solution)/shard_map/ppermute | solution.py:664
  537.1 21.0 %collective-permute-start.36 = (bf16[512,768]{1,0:T(8,128)(2,1)}, bf16[512,768]{1,0:T(8,128)(2,1)}, u32[]{:S(2)}, u32[]{:S(2)}) collective-permute-start(bf16[512,768]{1,0:T(8,128)(2,1)} %add_convert_fusion.5), channel_id=1, source_target_pairs={{0,8},{4,12},{8,16},{12,20},{16,24},{20,28},{24,0},{28,4},{1,9},{5... | collective-permute-start | bytes 2359304 | tf_op jit(solution)/shard_map/ppermute | solution.py:664
  544.0 25.2 %collective-permute-start.33 = (bf16[256,2048]{1,0:T(8,128)(2,1)}, bf16[256,2048]{1,0:T(8,128)(2,1)}, u32[]{:S(2)}, u32[]{:S(2)}) collective-permute-start(bf16[256,2048]{1,0:T(8,128)(2,1)} %pad_maximum_fusion.2), channel_id=1, source_target_pairs={{0,4},{4,0},{8,12},{12,8},{16,20},{20,16},{24,28},{28,24},{1,5},{5... | collective-permute-start | bytes 3145736 | tf_op jit(solution)/shard_map/ppermute | solution.py:572
  546.0 23.7 %collective-permute-start.34 = (bf16[256,2048]{1,0:T(8,128)(2,1)}, bf16[256,2048]{1,0:T(8,128)(2,1)}, u32[]{:S(2)}, u32[]{:S(2)}) collective-permute-start(bf16[256,2048]{1,0:T(8,128)(2,1)} %pad_maximum_fusion.3), channel_id=1, source_target_pairs={{0,2},{1,3},{2,0},{3,1},{4,6},{5,7},{6,4},{7,5},{8,10},{9,11},{10,... | collective-permute-start | bytes 3145736 | tf_op jit(solution)/shard_map/ppermute | solution.py:940
  (56 other events, 521.2 us)
Sparse Core Ops, SparseCore 0:
  12.7 70.1 all-gather.4
  84.8 57.6 all-gather.6
  144.5 54.3 all-gather.8
  200.6 54.3 all-gather.10
  320.7 128.8 reduce-scatter.2
  452.8 78.7 reduce-scatter.4

commit v8 on v7

--- a/solution.py
+++ b/solution.py
@@ -5,7 +5,6 @@
 import jax.numpy as jnp
 from jax import lax
 from jax.experimental import pallas as pl
-from jax.experimental.layout import Layout, with_layout_constraint
 from jax.experimental.pallas import tpu as pltpu
 from jax.sharding import PartitionSpec as P
 
@@ -487,12 +486,13 @@
     )(rows, cots, gain, *pieces, *given)
 
 
-def weight_grad(lefts, rights):
+def weight_grad(lefts, rights, turned=False):
     tile, chunk = 512, 512
     micro_count = len(lefts)
     tokens, width = lefts[0].shape
     widths = [right[0].shape[1] for right in rights]
     cols, steps = sum(widths), tokens // tile
+    shape = (cols, width) if turned else (width, cols)
 
     def kernel(*refs):
         out_ref, acc_ref = refs[-2:]
@@ -509,10 +509,15 @@
                 first = 0
                 for at, span in enumerate(widths):
                     right = refs[(1 + at) * micro_count + micro]
-                    for row in range(0, width, chunk):
-                        acc_ref[row : row + chunk, first : first + span] += dot_rows(
-                            refs[micro][:, row : row + chunk], right[...]
-                        )
+                    if turned:
+                        for row in range(0, span, min(chunk, span)):
+                            rows = slice(row, row + min(chunk, span))
+                            acc_ref[first + row : first + rows.stop, :] += dot_rows(right[:, rows], refs[micro][...])
+                    else:
+                        for row in range(0, width, chunk):
+                            acc_ref[row : row + chunk, first : first + span] += dot_rows(
+                                refs[micro][:, row : row + chunk], right[...]
+                            )
                     first += span
 
         @pl.when(step == micro_count * steps - 1)
@@ -526,9 +531,9 @@
         kernel,
         grid=(micro_count * steps,),
         in_specs=[side(micro, span) for span in (width, *widths) for micro in range(micro_count)],
-        out_specs=pl.BlockSpec((width, cols), lambda i: (0, 0)),
-        out_shape=jax.ShapeDtypeStruct((width, cols), BF),
-        scratch_shapes=[pltpu.VMEM((width, cols), F32)],
+        out_specs=pl.BlockSpec(shape, lambda i: (0, 0)),
+        out_shape=jax.ShapeDtypeStruct(shape, BF),
+        scratch_shapes=[pltpu.VMEM(shape, F32)],
         compiler_params=pltpu.CompilerParams(vmem_limit_bytes=VMEM_LIMIT),
         cost_estimate=estimate(
             2 * micro_count * tokens * width * cols, 2 * micro_count * tokens * (width + cols)
@@ -645,12 +650,12 @@
             return [part.val for part in self.parts]
 
     class Scatter:
-        def __init__(self, part):
-            self.part, self.step, self.came = part, 1, None
+        def __init__(self, part, axis):
+            self.part, self.step, self.came, self.axis = part, 1, None, axis
 
         def total(self):
             at_line = lax.rem(line_at + line - self.step, line)
-            own = lax.dynamic_slice_in_dim(self.part.val, at_line * line_rows, line_rows, axis=0)
+            own = lax.dynamic_slice_in_dim(self.part.val, at_line * line_rows, line_rows, axis=self.axis)
             if self.came is None:
                 return own
             order.tie(self.came)
@@ -669,9 +674,9 @@
 
         def rows_at(self, half):
             own = lax.dynamic_slice_in_dim(
-                self.part.val, line_at * line_rows + half * shard_rows, shard_rows, axis=0
+                self.part.val, line_at * line_rows + half * shard_rows, shard_rows, axis=self.axis
             )
-            came = lax.dynamic_slice_in_dim(self.came.val, half * shard_rows, shard_rows, axis=0)
+            came = lax.dynamic_slice_in_dim(self.came.val, half * shard_rows, shard_rows, axis=self.axis)
             return came.astype(F32) + own.astype(F32)
 
         def swap(self):
@@ -844,12 +849,13 @@
         *pre_grads[:], up_sums = order.run(piece, *plane_cots, *slopes)
         return up_sums
 
-    def weight_piece(lefts, *rights):
+    def weight_piece(lefts, *rights, turned=False):
         def piece(*flat):
             sets = [flat[at : at + micro_count] for at in range(0, len(flat), micro_count)]
-            return [weight_grad(sets[0], sets[1:])]
-
-        return Scatter(order.run(piece, *lefts, *(box for right in rights for box in right))[0])
+            return [weight_grad(sets[0], sets[1:], turned)]
+
+        part = order.run(piece, *lefts, *(box for right in rights for box in right))[0]
+        return Scatter(part, 1 if turned else 0)
 
     def branch_piece():
         def piece(*vals):
@@ -903,7 +909,7 @@
     down_ring.sync()
     down_ring.move()
 
-    down_scatter = weight_piece(plane_cots, acts, attns)
+    down_scatter = weight_piece(plane_cots, acts, attns, turned=True)
     down_ring.finish()
     down_scatter.move()
     branch = branch_piece()
@@ -975,12 +981,9 @@
     far = block(1 - pair_at, 1 - y_at)
     from_pair, from_y = Box(swap_pair(far[:, :half])), Box(swap_y(far[:, half:]))
     tail.move()
-    row_major = Layout(major_to_minor=(0, 1))
-    halves = [with_layout_constraint(part, row_major) for part in down_scatter.halves()]
-    down_w_grad = jnp.concatenate([part[:, :mlp_cols].T for part in halves], axis=0)
-    down_w_grad = Box(with_layout_constraint(down_w_grad, row_major))
-    out_w_grad = jnp.concatenate([part[:, mlp_cols:].T for part in halves], axis=0)
-    out_w_grad = Box(with_layout_constraint(out_w_grad, row_major))
+    halves = down_scatter.halves()
+    down_w_grad = Box(jnp.concatenate([part[:mlp_cols] for part in halves], axis=0))
+    out_w_grad = Box(jnp.concatenate([part[mlp_cols:] for part in halves], axis=0))
     for box in (down_w_grad, out_w_grad):
         order.sync(box)
 

time: 599 us -> 597 us (level)
  waiting for transfers between devices: 91.4 us -> 99 us
  transfers between devices with their start and end apart: 47 -> 47, of which waited for: 18 -> 18; matrix products, arithmetic and copies ran while one was open for 12% -> 10% of each run, Pallas kernels for 60% -> 60%
where the time goes in v8:
time: 597 us; the launch traced here: 588 us
  Pallas kernels  355 us (59%)
  waiting for transfers between devices  99 us (17%)
  other arithmetic  45.9 us (8%)
  starting transfers between devices  44.9 us (8%)
  local copies, waits for them, and re-layouts  27.9 us (5%)
  between operations  15.3 us (3%)
    pallas_call x9, Pallas kernels, rows_call(): pl.pallas_call(kernel, grid_spec=pltpu.PrefetchScalarGridSpec(num_scalar_...  188 us
    pallas_call x3, Pallas kernels, weight_grad(): pl.pallas_call(kernel, grid=(micro_count * steps,), in_specs=[side(micro,...  77.5 us
    ppermute x8, waiting for transfers between devices, swap_pair(): return lax.ppermute(vals, 'fsdp', [(f, f ^ 1) for f in range(fsdp_size)])  43.5 us
    pallas_call x2, Pallas kernels, attend_back(): pl.pallas_call(functools.partial(attend_back_kernel, head_dim, block), gr...  42.2 us
    pallas_call x2, Pallas kernels, attend(): pl.pallas_call(functools.partial(attend_kernel, head_dim, block), grid=(s...  32.9 us
    ppermute x9, waiting for transfers between devices, move(): self.parts.append(Box(lax.ppermute(self.parts[-1].val, 'fsdp', ring)))  23.8 us
    ppermute x9, waiting for transfers between devices, move(): self.came = Box(lax.ppermute(sent.val, 'fsdp', ring))  22.5 us
  transfers between devices with their start and end apart: 47, of which 18 were waited for; matrix products, arithmetic and copies ran while one was open for 10% of the time, Pallas kernels for 60%

profile of v8, /device:TPU:0, one launch (start us, length us, event | category | flops | bytes accessed | tf_op | source)
XLA Modules:
  0.0 588.2 jit_solution(15921980392895936123)
XLA Ops:
  19.2 11.8 %collective-permute-done = bf16[256,1024]{1,0:T(8,128)(2,1)S(1)} collective-permute-done((bf16[256,1024]{1,0:T(8,128)(2,1)S(1)}, bf16[256,1024]{1,0:T(8,128)(2,1)S(1)}, u32[]{:S(2)}, u32[]{:S(2)}) %collective-permute-start) | collective-permute-done | bytes 524320 | tf_op jit(solution)/shard_map/ppermute | solution.py:577
  42.6 12.7 %collective-permute-done.4.refs_1_.refs_5_ = bf16[512,1024]{1,0:T(8,128)(2,1)S(1)} collective-permute-done((bf16[512,1024]{1,0:T(8,128)(2,1)S(1)}, bf16[512,1024]{1,0:T(8,128)(2,1)S(1)}, u32[]{:S(2)}, u32[]{:S(2)}) %collective-permute-start.4) | collective-permute-done | bytes 1048608 | tf_op jit(solution)/shard_map/ppermute | solution.py:639
  67.5 14.3 %collective-permute-done.3 = bf16[256,1024]{1,0:T(8,128)(2,1)} collective-permute-done((bf16[256,1024]{1,0:T(8,128)(2,1)}, bf16[256,1024]{1,0:T(8,128)(2,1)}, u32[]{:S(2)}, u32[]{:S(2)}) %collective-permute-start.3) | collective-permute-done | bytes 524320 | tf_op jit(solution)/shard_map/ppermute | solution.py:577
  94.5 13.2 %collective-permute-done.6 = bf16[256,1024]{1,0:T(8,128)(2,1)} collective-permute-done((bf16[256,1024]{1,0:T(8,128)(2,1)}, bf16[256,1024]{1,0:T(8,128)(2,1)}, u32[]{:S(2)}, u32[]{:S(2)}) %collective-permute-start.6) | collective-permute-done | bytes 524320 | tf_op jit(solution)/shard_map/ppermute | solution.py:577
  111.7 16.1 %shard_map.213 = (bf16[2048,2048]{1,0:T(8,128)(2,1)}, f32[2048,768]{1,0:T(8,128)}) custom-call(s32[5]{0:T(128)} %stack.35.slots_ref, bf16[2048,2048]{1,0:T(8,128)(2,1)} %all-gather.5.cloned.1.call-done.rows_ref, f32[1,2048]{1,0:T(1,128)} %reshape.189.gain_ref, f32[1,2048]{1,0:T(1,128)} %reshape.190.shift_ref, f32[1,768]{1,0:T(1,128)} %reshape.177.bias_ref, ...), custom_call_target="tpu_custom_call" | custom-call | flops 100663296 | bytes 360448 | tf_op jit(solution)/shard_map/pallas_call | solution.py:219
  127.8 4.9 collective-permute-done.12.refs_3_.refs_5_
  133.9 16.3 %shard_map.214 = (bf16[2048,768]{1,0:T(8,128)(2,1)}, bf16[2048,256]{1,0:T(8,128)(2,1)}, f32[4,2,1024]{2,1,0:T(2,128)}) custom-call(f32[2048,768]{1,0:T(8,128)} %get-tuple-element.369.qkv_ref, f32[1024,128]{1,0:T(8,128)} %get-tuple-element.370.cos_ref, f32[1024,128]{1,0:T(8,128)} %get-tuple-element.371.low_ref, f32[1024,128]{1,0:T(8,128)} %get-tuple-element.372.up_ref), custom_call_target="tpu_custom_call" | custom-call | flops 100663296 | bytes 131072 | tf_op jit(solution)/shard_map/pallas_call | solution.py:150
  150.2 16.8 %shard_map.215 = (bf16[2048,2048]{1,0:T(8,128)(2,1)}, f32[2048,768]{1,0:T(8,128)}) custom-call(s32[5]{0:T(128)} %stack.35.slots_ref, bf16[2048,2048]{1,0:T(8,128)(2,1)} %all-gather.7.cloned.1.call-done.rows_ref, f32[1,2048]{1,0:T(1,128)} %reshape.189.gain_ref, f32[1,2048]{1,0:T(1,128)} %reshape.190.shift_ref, f32[1,768]{1,0:T(1,128)} %reshape.177.bias_ref, ...), custom_call_target="tpu_custom_call" | custom-call | flops 100663296 | bytes 360448 | tf_op jit(solution)/shard_map/pallas_call | solution.py:219
  167.1 16.7 %shard_map.216 = (bf16[2048,768]{1,0:T(8,128)(2,1)}, bf16[2048,256]{1,0:T(8,128)(2,1)}, f32[4,2,1024]{2,1,0:T(2,128)}) custom-call(f32[2048,768]{1,0:T(8,128)} %get-tuple-element.381.qkv_ref, f32[1024,128]{1,0:T(8,128)} %get-tuple-element.370.cos_ref, f32[1024,128]{1,0:T(8,128)} %get-tuple-element.371.low_ref, f32[1024,128]{1,0:T(8,128)} %get-tuple-element.372.up_ref), custom_call_target="tpu_custom_call" | custom-call | flops 100663296 | bytes 131072 | tf_op jit(solution)/shard_map/pallas_call | solution.py:150
  183.8 6.2 %collective-permute-done.14.refs_5_.refs_7_ = bf16[512,1024]{1,0:T(8,128)(2,1)S(1)} collective-permute-done((bf16[512,1024]{1,0:T(8,128)(2,1)S(1)}, bf16[512,1024]{1,0:T(8,128)(2,1)S(1)}, u32[]{:S(2)}, u32[]{:S(2)}) %collective-permute-start.14) | collective-permute-done | bytes 1048608 | tf_op jit(solution)/shard_map/ppermute | solution.py:639
  191.0 32.6 %shard_map.217 = (bf16[2048,1024]{1,0:T(8,128)(2,1)}, bf16[2048,1024]{1,0:T(8,128)(2,1)}, bf16[2048,1024]{1,0:T(8,128)(2,1)}, bf16[2048,1024]{1,0:T(8,128)(2,1)}) custom-call(s32[5]{0:T(128)} %stack.35.slots_ref, f32[1,1024]{1,0:T(1,128)} %constant_dynamic-slice_fusion.9.bias_ref, bf16[2048,2048]{1,0:T(8,128)(2,1)} %get-tuple-element.472.refs_0_, ...), custom_call_target="tpu_custom_call" | custom-call | flops 268435456 | bytes 524288 | tf_op jit(solution)/shard_map/pallas_call | solution.py:219
  223.8 7.9 %shard_map.218.grad_ref = bf16[2048,256]{1,0:T(8,128)(2,1)} custom-call(s32[5]{0:T(128)} %stack.35.slots_ref, bf16[2048,2048]{1,0:T(8,128)(2,1)} %all-gather.9.cloned.1.call-done.rows_ref.refs_0_, bf16[512,1024]{1,0:T(8,128)(2,1)} %copy-done, bf16[512,1024]{1,0:T(8,128)(2,1)} %copy-done.2, bf16[512,1024]{1,0:T(8,128)(2,1)} %copy-done.3, ...), custom_call_target="tpu_custom_call" | custom-call | flops 33554432 | bytes 147456 | tf_op jit(solution)/shard_map/pallas_call | solution.py:219
  231.6 21.1 %shard_map.219 = (bf16[2048,768]{1,0:T(8,128)(2,1)}, f32[16,768]{1,0:T(8,128)}) custom-call(bf16[2048,768]{1,0:T(8,128)(2,1)} %get-tuple-element.405.rot_ref, bf16[2048,256]{1,0:T(8,128)(2,1)} %shard_map.218.grad_ref, bf16[2048,256]{1,0:T(8,128)(2,1)} %get-tuple-element.419.attn_ref.refs_4_.refs_0_, f32[4,2,1024]{2,1,0:T(2,128)} %get-tuple-element.407.lse_ref, ...), custom_call_target="tpu_custom_call" | custom-call | flops 201326592 | bytes 131072 | tf_op jit(solution)/shard_map/pallas_call | solution.py:175
  252.8 3.5 collective-permute-start.17
  256.3 30.4 %shard_map.220 = bf16[1280,2048]{1,0:T(8,128)(2,1)} custom-call(bf16[2048,2048]{1,0:T(8,128)(2,1)} %all-gather.9.cloned.1.call-done.rows_ref.refs_0_, bf16[2048,2048]{1,0:T(8,128)(2,1)} %all-gather.11.cloned.1.call-done.refs_1_.rows_ref, bf16[2048,1024]{1,0:T(8,128)(2,1)} %get-tuple-element.421.refs_2_, bf16[2048,1024]{1,0:T(8,128)(2,1)} %get-tuple-element.422.refs_3_, ...), custom_call_target="tpu_custom_call" | custom-call | flops 335544320 | bytes 425984 | tf_op jit(solution)/shard_map/pallas_call | solution.py:530
  290.2 30.2 %shard_map.221 = bf16[8,2,256,2048]{3,2,1,0:T(8,128)(2,1)} custom-call(s32[5]{0:T(128)} %stack.35.slots_ref, bf16[2048,256]{1,0:T(8,128)(2,1)} %get-tuple-element.419.attn_ref.refs_4_.refs_0_, bf16[2048,256]{1,0:T(8,128)(2,1)} %get-tuple-element.456.refs_5_.refs_1_.attn_ref, bf16[2048,1024]{1,0:T(8,128)(2,1)} %get-tuple-element.421.refs_2_, ...), custom_call_target="tpu_custom_call" | custom-call | flops 335544320 | bytes 294912 | tf_op jit(solution)/shard_map/pallas_call | solution.py:219
  323.3 27.7 %shard_map.222 = (bf16[2048,1024]{1,0:T(8,128)(2,1)}, bf16[2048,1024]{1,0:T(8,128)(2,1)}, f32[8,1024]{1,0:T(8,128)}) custom-call(s32[5]{0:T(128)} %stack.35.slots_ref, bf16[2048,2048]{1,0:T(8,128)(2,1)} %all-gather.9.cloned.1.call-done.rows_ref.refs_0_, bf16[2048,2048]{1,0:T(8,128)(2,1)} %all-gather.11.cloned.1.call-done.refs_1_.rows_ref, ...), custom_call_target="tpu_custom_call" | custom-call | flops 268435456 | bytes 524288 | tf_op jit(solution)/shard_map/pallas_call | solution.py:219
  354.9 26.0 %shard_map.223 = bf16[2048,1024]{1,0:T(8,128)(2,1)} custom-call(bf16[2048,2048]{1,0:T(8,128)(2,1)} %get-tuple-element.472.refs_0_, bf16[2048,2048]{1,0:T(8,128)(2,1)} %get-tuple-element.473.refs_1_, bf16[2048,1024]{1,0:T(8,128)(2,1)} %get-tuple-element.464.refs_2_.two_ref, bf16[2048,1024]{1,0:T(8,128)(2,1)} %get-tuple-element.483.refs_3_.two_ref), custom_call_target="tpu_custom_call" | custom-call | flops 268435456 | bytes 393216 | tf_op jit(solution)/shard_map/pallas_call | solution.py:530
  380.9 3.8 collective-permute-done.20
  389.1 7.7 %shard_map.224.grad_ref = bf16[2048,256]{1,0:T(8,128)(2,1)} custom-call(s32[5]{0:T(128)} %stack.35.slots_ref, bf16[2048,2048]{1,0:T(8,128)(2,1)} %all-gather.11.cloned.1.call-done.refs_1_.rows_ref, bf16[512,1024]{1,0:T(8,128)(2,1)} %copy-done, bf16[512,1024]{1,0:T(8,128)(2,1)} %copy-done.2, bf16[512,1024]{1,0:T(8,128)(2,1)} %copy-done.3, ...), custom_call_target="tpu_custom_call" | custom-call | flops 33554432 | bytes 147456 | tf_op jit(solution)/shard_map/pallas_call | solution.py:219
  396.8 21.1 %shard_map.225 = (bf16[2048,768]{1,0:T(8,128)(2,1)}, f32[16,768]{1,0:T(8,128)}) custom-call(bf16[2048,768]{1,0:T(8,128)(2,1)} %get-tuple-element.454.rot_ref, bf16[2048,256]{1,0:T(8,128)(2,1)} %shard_map.224.grad_ref, bf16[2048,256]{1,0:T(8,128)(2,1)} %get-tuple-element.456.refs_5_.refs_1_.attn_ref, f32[4,2,1024]{2,1,0:T(2,128)} %get-tuple-element.457.lse_ref, ...), custom_call_target="tpu_custom_call" | custom-call | flops 201326592 | bytes 131072 | tf_op jit(solution)/shard_map/pallas_call | solution.py:175
  421.7 24.0 %shard_map.226 = (bf16[2048,2048]{1,0:T(8,128)(2,1)}, f32[8,2048]{1,0:T(8,128)}) custom-call(s32[5]{0:T(128)} %stack.35.slots_ref, bf16[2048,768]{1,0:T(8,128)(2,1)} %get-tuple-element.474.one_ref.refs_2_, bf16[2048,1024]{1,0:T(8,128)(2,1)} %get-tuple-element.464.refs_2_.two_ref, bf16[2048,2048]{1,0:T(8,128)(2,1)} %all-gather.5.cloned.1.call-done.rows_ref, ...), custom_call_target="tpu_custom_call" | custom-call | flops 234881024 | bytes 376832 | tf_op jit(solution)/shard_map/pallas_call | solution.py:219
  448.6 21.0 %shard_map.227 = bf16[2048,768]{1,0:T(8,128)(2,1)} custom-call(bf16[2048,2048]{1,0:T(8,128)(2,1)} %get-tuple-element.472.refs_0_, bf16[2048,2048]{1,0:T(8,128)(2,1)} %get-tuple-element.473.refs_1_, bf16[2048,768]{1,0:T(8,128)(2,1)} %get-tuple-element.474.one_ref.refs_2_, bf16[2048,768]{1,0:T(8,128)(2,1)} %get-tuple-element.482.refs_3_.one_ref), custom_call_target="tpu_custom_call" | custom-call | flops 201326592 | bytes 360448 | tf_op jit(solution)/shard_map/pallas_call | solution.py:530
  476.4 24.8 %shard_map.228 = (bf16[1024,2048]{1,0:T(8,128)(2,1)}, bf16[1024,2048]{1,0:T(8,128)(2,1)}, f32[8,2048]{1,0:T(8,128)}) custom-call(s32[5]{0:T(128)} %stack.35.slots_ref, bf16[2048,768]{1,0:T(8,128)(2,1)} %get-tuple-element.482.refs_3_.one_ref, bf16[2048,1024]{1,0:T(8,128)(2,1)} %get-tuple-element.483.refs_3_.two_ref, ...), custom_call_target="tpu_custom_call" | custom-call | flops 234881024 | bytes 376832 | tf_op jit(solution)/shard_map/pallas_call | solution.py:219
  505.7 3.9 fusion.1
  513.6 4.6 add_convert_fusion
  524.6 8.6 %collective-permute-done.32 = bf16[512,768]{1,0:T(8,128)(2,1)S(1)} collective-permute-done((bf16[512,768]{1,0:T(8,128)(2,1)S(1)}, bf16[512,768]{1,0:T(8,128)(2,1)S(1)}, u32[]{:S(2)}, u32[]{:S(2)}) %collective-permute-start.32) | collective-permute-done | bytes 786464 | tf_op jit(solution)/shard_map/ppermute | solution.py:669
  534.3 5.6 collective-permute-done.31
  545.7 4.7 shard_map.229.refs_3_
  550.3 5.0 collective-permute-done.36
  555.3 4.4 collective-permute-start.38
  570.4 5.1 shard_map.230
  (272 shorter events, 120.4 us)
Async XLA Ops:
  7.2 103.6 %all-gather.5.cloned.1.call-start = ((), (), s32[]{:S(2)}) async-start(), calls=%async_computation.2 | async-start | bytes 9437184 | tf_op jit(solution)/shard_map/all_gather | solution.py:580
  12.6 137.6 %all-gather.7.cloned.1.call-start = ((), (), s32[]{:S(2)}) async-start(), calls=%async_computation.3 | async-start | bytes 9437184 | tf_op jit(solution)/shard_map/all_gather | solution.py:580
  31.4 192.4 %all-gather.9.cloned.1.call-start = ((), (), s32[]{:S(2)}) async-start(), calls=%async_computation.4 | async-start | bytes 9437184 | tf_op jit(solution)/shard_map/all_gather | solution.py:580
  31.5 23.8 %collective-permute-start.4 = (bf16[512,1024]{1,0:T(8,128)(2,1)S(1)}, bf16[512,1024]{1,0:T(8,128)(2,1)S(1)}, u32[]{:S(2)}, u32[]{:S(2)}) collective-permute-start(bf16[512,1024]{1,0:T(8,128)(2,1)S(1)} %maximum_select_fusion.refs_0_.refs_4_), channel_id=1, source_target_pairs={{0,8},{4,12},{8,16},{12,20},{16,24},{20,28},{24,0},{28,4},{1,9},{5... | collective-permute-start | bytes 3145736 | tf_op jit(solution)/shard_map/ppermute | solution.py:639
  55.3 26.6 %collective-permute-start.7 = (bf16[512,1024]{1,0:T(8,128)(2,1)S(1)}, bf16[512,1024]{1,0:T(8,128)(2,1)S(1)}, u32[]{:S(2)}, u32[]{:S(2)}) collective-permute-start(bf16[512,1024]{1,0:T(8,128)(2,1)S(1)} %collective-permute-done.4.refs_1_.refs_5_), channel_id=1, source_target_pairs={{0,8},{4,12},{8,16},{12,20},{16,24},{20,28},{24,0},{28,4},{1,9},{5... | collective-permute-start | bytes 3145736 | tf_op jit(solution)/shard_map/ppermute | solution.py:639
  57.7 24.2 %collective-permute-start.3 = (bf16[256,1024]{1,0:T(8,128)(2,1)}, bf16[256,1024]{1,0:T(8,128)(2,1)}, u32[]{:S(2)}, u32[]{:S(2)}) collective-permute-start(bf16[256,1024]{1,0:T(8,128)(2,1)} %get-tuple-element.305), channel_id=1, source_target_pairs={{0,4},{4,0},{8,12},{12,8},{16,20},{20,16},{24,28},{28,24},{1,5},{5... | collective-permute-start | bytes 1572872 | tf_op jit(solution)/shard_map/ppermute | solution.py:577
  61.7 20.1 %collective-permute-start.10 = (bf16[8,704]{1,0:T(8,128)(2,1)S(1)}, bf16[8,704]{1,0:T(8,128)(2,1)S(1)}, u32[]{:S(2)}, u32[]{:S(2)}) collective-permute-start(bf16[8,704]{1,0:T(8,128)(2,1)S(1)} %maximum_select_fusion.3), channel_id=1, source_target_pairs={{0,8},{4,12},{8,0},{12,4},{16,24},{20,28},{24,16},{28,20},{1,9},{5... | collective-permute-start | bytes 33800 | tf_op jit(solution)/shard_map/ppermute | solution.py:744
  81.9 174.3 %all-gather.11.cloned.1.call-start = ((), (), s32[]{:S(2)}) async-start(), calls=%async_computation.5 | async-start | bytes 9437184 | tf_op jit(solution)/shard_map/all_gather | solution.py:580
  83.8 26.9 %collective-permute-start.11 = (bf16[512,1024]{1,0:T(8,128)(2,1)S(1)}, bf16[512,1024]{1,0:T(8,128)(2,1)S(1)}, u32[]{:S(2)}, u32[]{:S(2)}) collective-permute-start(bf16[512,1024]{1,0:T(8,128)(2,1)S(1)} %collective-permute-done.7.refs_2_.refs_6_), channel_id=1, source_target_pairs={{0,8},{4,12},{8,16},{12,20},{16,24},{20,28},{24,0},{28,4},{1,9},{5... | collective-permute-start | bytes 3145736 | tf_op jit(solution)/shard_map/ppermute | solution.py:639
  88.5 19.3 %collective-permute-start.6 = (bf16[256,1024]{1,0:T(8,128)(2,1)}, bf16[256,1024]{1,0:T(8,128)(2,1)}, u32[]{:S(2)}, u32[]{:S(2)}) collective-permute-start(bf16[256,1024]{1,0:T(8,128)(2,1)} %bitcast), channel_id=1, source_target_pairs={{0,4},{4,0},{8,12},{12,8},{16,20},{20,16},{24,28},{28,24},{1,5},{5... | collective-permute-start | bytes 1572872 | tf_op jit(solution)/shard_map/ppermute | solution.py:577
  110.7 22.0 %collective-permute-start.12 = (bf16[512,1024]{1,0:T(8,128)(2,1)S(1)}, bf16[512,1024]{1,0:T(8,128)(2,1)S(1)}, u32[]{:S(2)}, u32[]{:S(2)}) collective-permute-start(bf16[512,1024]{1,0:T(8,128)(2,1)S(1)} %maximum_select_fusion.1.refs_2_.refs_4_), channel_id=1, source_target_pairs={{0,8},{4,12},{8,16},{12,20},{16,24},{20,28},{24,0},{28,4},{1,9},{5... | collective-permute-start | bytes 3145736 | tf_op jit(solution)/shard_map/ppermute | solution.py:639
  132.7 339.8 %reduce-scatter.3.cloned.1.call-start = ((), (), s32[]{:S(2)}) async-start(), calls=%async_computation.6 | async-start | bytes 18874368 | tf_op jit(solution)/shard_map/reduce_scatter | solution.py:583
  132.8 34.3 %collective-permute-start.13 = (bf16[512,1024]{1,0:T(8,128)(2,1)S(1)}, bf16[512,1024]{1,0:T(8,128)(2,1)S(1)}, u32[]{:S(2)}, u32[]{:S(2)}) collective-permute-start(bf16[512,1024]{1,0:T(8,128)(2,1)S(1)} %collective-permute-done.12.refs_3_.refs_5_), channel_id=1, source_target_pairs={{0,8},{4,12},{8,16},{12,20},{16,24},{20,28},{24,0},{28,4},{1,9},{5... | collective-permute-start | bytes 3145736 | tf_op jit(solution)/shard_map/ppermute | solution.py:639
  167.1 23.0 %collective-permute-start.14 = (bf16[512,1024]{1,0:T(8,128)(2,1)S(1)}, bf16[512,1024]{1,0:T(8,128)(2,1)S(1)}, u32[]{:S(2)}, u32[]{:S(2)}) collective-permute-start(bf16[512,1024]{1,0:T(8,128)(2,1)S(1)} %collective-permute-done.13.refs_4_.refs_6_), channel_id=1, source_target_pairs={{0,8},{4,12},{8,16},{12,20},{16,24},{20,28},{24,0},{28,4},{1,9},{5... | collective-permute-start | bytes 3145736 | tf_op jit(solution)/shard_map/ppermute | solution.py:639
  190.1 33.6 %collective-permute-start.15 = (bf16[512,1024]{1,0:T(8,128)(2,1)S(1)}, bf16[512,1024]{1,0:T(8,128)(2,1)S(1)}, u32[]{:S(2)}, u32[]{:S(2)}) collective-permute-start(bf16[512,1024]{1,0:T(8,128)(2,1)S(1)} %copy-done.8), channel_id=1, source_target_pairs={{0,8},{4,12},{8,16},{12,20},{16,24},{20,28},{24,0},{28,4},{1,9},{5... | collective-permute-start | bytes 3145736 | tf_op jit(solution)/shard_map/ppermute | solution.py:639
  223.6 29.1 %collective-permute-start.16 = (bf16[512,1024]{1,0:T(8,128)(2,1)S(1)}, bf16[512,1024]{1,0:T(8,128)(2,1)S(1)}, u32[]{:S(2)}, u32[]{:S(2)}) collective-permute-start(bf16[512,1024]{1,0:T(8,128)(2,1)S(1)} %collective-permute-done.15.refs_9_.refs_5_), channel_id=1, source_target_pairs={{0,8},{4,12},{8,16},{12,20},{16,24},{20,28},{24,0},{28,4},{1,9},{5... | collective-permute-start | bytes 3145736 | tf_op jit(solution)/shard_map/ppermute | solution.py:639
  252.8 35.4 %collective-permute-start.17 = (bf16[512,1024]{1,0:T(8,128)(2,1)S(1)}, bf16[512,1024]{1,0:T(8,128)(2,1)S(1)}, u32[]{:S(2)}, u32[]{:S(2)}) collective-permute-start(bf16[512,1024]{1,0:T(8,128)(2,1)S(1)} %collective-permute-done.16.refs_10_.refs_6_), channel_id=1, source_target_pairs={{0,8},{4,12},{8,16},{12,20},{16,24},{20,28},{24,0},{28,4},{1,9},{5... | collective-permute-start | bytes 3145736 | tf_op jit(solution)/shard_map/ppermute | solution.py:639
  288.1 32.2 %collective-permute-start.18 = (bf16[1280,512]{1,0:T(8,128)(2,1)S(1)}, bf16[1280,512]{1,0:T(8,128)(2,1)S(1)}, u32[]{:S(2)}, u32[]{:S(2)}) collective-permute-start(bf16[1280,512]{1,0:T(8,128)(2,1)S(1)} %constant_dynamic-slice_fusion.7), channel_id=1, source_target_pairs={{0,8},{4,12},{8,16},{12,20},{16,24},{20,28},{24,0},{28,4},{1,9},{5... | collective-permute-start | bytes 3932168 | tf_op jit(solution)/shard_map/ppermute | solution.py:669
  320.4 225.3 %reduce-scatter.5.cloned.1.call-start = ((), (), s32[]{:S(2)}) async-start(), calls=%async_computation.7 | async-start | bytes 9437184 | tf_op jit(solution)/shard_map/reduce_scatter | solution.py:583
  322.1 31.0 %collective-permute-start.19 = (bf16[1280,512]{1,0:T(8,128)(2,1)S(1)}, bf16[1280,512]{1,0:T(8,128)(2,1)S(1)}, u32[]{:S(2)}, u32[]{:S(2)}) collective-permute-start(bf16[1280,512]{1,0:T(8,128)(2,1)S(1)} %add_convert_fusion.2), channel_id=1, source_target_pairs={{0,8},{4,12},{8,16},{12,20},{16,24},{20,28},{24,0},{28,4},{1,9},{5... | collective-permute-start | bytes 3932168 | tf_op jit(solution)/shard_map/ppermute | solution.py:669
  354.8 29.9 %collective-permute-start.20 = (bf16[1280,512]{1,0:T(8,128)(2,1)S(1)}, bf16[1280,512]{1,0:T(8,128)(2,1)S(1)}, u32[]{:S(2)}, u32[]{:S(2)}) collective-permute-start(bf16[1280,512]{1,0:T(8,128)(2,1)S(1)} %add_convert_fusion.1), channel_id=1, source_target_pairs={{0,8},{4,12},{8,16},{12,20},{16,24},{20,28},{24,0},{28,4},{1,9},{5... | collective-permute-start | bytes 3932168 | tf_op jit(solution)/shard_map/ppermute | solution.py:669
  386.1 31.9 %collective-permute-start.21 = (bf16[512,1024]{1,0:T(8,128)(2,1)S(1)}, bf16[512,1024]{1,0:T(8,128)(2,1)S(1)}, u32[]{:S(2)}, u32[]{:S(2)}) collective-permute-start(bf16[512,1024]{1,0:T(8,128)(2,1)S(1)} %constant_dynamic-slice_fusion.6), channel_id=1, source_target_pairs={{0,8},{4,12},{8,16},{12,20},{16,24},{20,28},{24,0},{28,4},{1,9},{5... | collective-permute-start | bytes 3145736 | tf_op jit(solution)/shard_map/ppermute | solution.py:669
  387.8 30.1 %collective-permute-start.22 = (bf16[1280,256]{1,0:T(8,128)(2,1)S(1)}, bf16[1280,256]{1,0:T(8,128)(2,1)S(1)}, u32[]{:S(2)}, u32[]{:S(2)}) collective-permute-start(bf16[1280,256]{1,0:T(8,128)(2,1)S(1)} %add_convert_fusion.7), channel_id=1, source_target_pairs={{0,4},{4,0},{8,12},{12,8},{16,20},{20,16},{24,28},{28,24},{1,5},{5... | collective-permute-start | bytes 1966088 | tf_op jit(solution)/shard_map/ppermute | solution.py:577
  420.4 25.3 %collective-permute-start.23 = (bf16[512,1024]{1,0:T(8,128)(2,1)S(1)}, bf16[512,1024]{1,0:T(8,128)(2,1)S(1)}, u32[]{:S(2)}, u32[]{:S(2)}) collective-permute-start(bf16[512,1024]{1,0:T(8,128)(2,1)S(1)} %add_convert_fusion.4), channel_id=1, source_target_pairs={{0,8},{4,12},{8,16},{12,20},{16,24},{20,28},{24,0},{28,4},{1,9},{5... | collective-permute-start | bytes 3145736 | tf_op jit(solution)/shard_map/ppermute | solution.py:669
  447.4 25.1 %collective-permute-start.24 = (bf16[512,1024]{1,0:T(8,128)(2,1)S(1)}, bf16[512,1024]{1,0:T(8,128)(2,1)S(1)}, u32[]{:S(2)}, u32[]{:S(2)}) collective-permute-start(bf16[512,1024]{1,0:T(8,128)(2,1)S(1)} %add_convert_fusion.3), channel_id=1, source_target_pairs={{0,8},{4,12},{8,16},{12,20},{16,24},{20,28},{24,0},{28,4},{1,9},{5... | collective-permute-start | bytes 3145736 | tf_op jit(solution)/shard_map/ppermute | solution.py:669
  474.1 28.1 %collective-permute-start.25 = (bf16[512,768]{1,0:T(8,128)(2,1)S(1)}, bf16[512,768]{1,0:T(8,128)(2,1)}, u32[]{:S(2)}, u32[]{:S(2)}) collective-permute-start(bf16[512,768]{1,0:T(8,128)(2,1)S(1)} %constant_dynamic-slice_fusion.5), channel_id=1, source_target_pairs={{0,8},{4,12},{8,16},{12,20},{16,24},{20,28},{24,0},{28,4},{1,9},{5... | collective-permute-start | bytes 2359304 | tf_op jit(solution)/shard_map/ppermute | solution.py:669
  475.4 26.8 %collective-permute-start.26 = (bf16[256,1024]{1,0:T(8,128)(2,1)S(1)}, bf16[256,1024]{1,0:T(8,128)(2,1)S(1)}, u32[]{:S(2)}, u32[]{:S(2)}) collective-permute-start(bf16[256,1024]{1,0:T(8,128)(2,1)S(1)} %add_convert_fusion.10), channel_id=1, source_target_pairs={{0,4},{4,0},{8,12},{12,8},{16,20},{20,16},{24,28},{28,24},{1,5},{5... | collective-permute-start | bytes 1572872 | tf_op jit(solution)/shard_map/ppermute | solution.py:577
  511.5 21.7 %collective-permute-start.32 = (bf16[512,768]{1,0:T(8,128)(2,1)S(1)}, bf16[512,768]{1,0:T(8,128)(2,1)S(1)}, u32[]{:S(2)}, u32[]{:S(2)}) collective-permute-start(bf16[512,768]{1,0:T(8,128)(2,1)S(1)} %add_convert_fusion.6), channel_id=1, source_target_pairs={{0,8},{4,12},{8,16},{12,20},{16,24},{20,28},{24,0},{28,4},{1,9},{5... | collective-permute-start | bytes 2359304 | tf_op jit(solution)/shard_map/ppermute | solution.py:669
  521.6 19.1 %collective-permute-start.30 = (bf16[256,1024]{1,0:T(8,128)(2,1)S(1)}, bf16[256,1024]{1,0:T(8,128)(2,1)S(1)}, u32[]{:S(2)}, u32[]{:S(2)}) collective-permute-start(bf16[256,1024]{1,0:T(8,128)(2,1)S(1)} %get-tuple-element.629), channel_id=1, source_target_pairs={{0,4},{4,0},{8,12},{12,8},{16,20},{20,16},{24,28},{28,24},{1,5},{5... | collective-permute-start | bytes 1572872 | tf_op jit(solution)/shard_map/ppermute | solution.py:577
  534.3 21.0 %collective-permute-start.36 = (bf16[512,768]{1,0:T(8,128)(2,1)}, bf16[512,768]{1,0:T(8,128)(2,1)}, u32[]{:S(2)}, u32[]{:S(2)}) collective-permute-start(bf16[512,768]{1,0:T(8,128)(2,1)} %add_convert_fusion.5), channel_id=1, source_target_pairs={{0,8},{4,12},{8,16},{12,20},{16,24},{20,28},{24,0},{28,4},{1,9},{5... | collective-permute-start | bytes 2359304 | tf_op jit(solution)/shard_map/ppermute | solution.py:669
  542.3 26.1 %collective-permute-start.33 = (bf16[256,2048]{1,0:T(8,128)(2,1)S(1)}, bf16[256,2048]{1,0:T(8,128)(2,1)S(1)}, u32[]{:S(2)}, u32[]{:S(2)}) collective-permute-start(bf16[256,2048]{1,0:T(8,128)(2,1)S(1)} %pad_maximum_fusion.2), channel_id=1, source_target_pairs={{0,4},{4,0},{8,12},{12,8},{16,20},{20,16},{24,28},{28,24},{1,5},{5... | collective-permute-start | bytes 3145736 | tf_op jit(solution)/shard_map/ppermute | solution.py:577
  544.2 24.4 %collective-permute-start.34 = (bf16[256,2048]{1,0:T(8,128)(2,1)}, bf16[256,2048]{1,0:T(8,128)(2,1)S(1)}, u32[]{:S(2)}, u32[]{:S(2)}) collective-permute-start(bf16[256,2048]{1,0:T(8,128)(2,1)} %pad_maximum_fusion.3), channel_id=1, source_target_pairs={{0,2},{1,3},{2,0},{3,1},{4,6},{5,7},{6,4},{7,5},{8,10},{9,11},{10,... | collective-permute-start | bytes 3145736 | tf_op jit(solution)/shard_map/ppermute | solution.py:946
  (47 other events, 479.5 us)
Sparse Core Ops, SparseCore 0:
  12.7 70.1 all-gather.4
  84.8 57.6 all-gather.6
  144.5 54.3 all-gather.8
  200.6 54.3 all-gather.10
  320.5 128.4 reduce-scatter.2
  452.3 84.0 reduce-scatter.4

commit v9 on v8

--- a/solution.py
+++ b/solution.py
@@ -1006,6 +1006,10 @@
     order.tie(back_sum)
     gained = Box(norm_back(inputs[:, 0], cotangent[:, 0], [back_sum.val], gain_row, 0))
     order.sync(gained)
+    order.tie(branch_sum)
+    branch_rows_sum = branch_sum.val.reshape(micro_count, token_rows, model_width).astype(F32)
+    output = Box((inputs[:, 0].astype(F32) + branch_rows_sum + bias_both).astype(BF))
+    order.sync(output)
     qkv_scatter.sync()
     order.sync(tail.cur)
     order.tie(tail.cur)
@@ -1032,8 +1036,6 @@
     ]
     qkv_w_grad = jnp.stack(planes, axis=0).transpose(1, 0, 2)
     small_sums, bias_sums = tail.split()
-    branch_sum = branch_sum.val.reshape(micro_count, token_rows, model_width)
-    output = (inputs[:, 0].astype(F32) + branch_sum.astype(F32) + bias_both).astype(BF)
 
     small_sums = small_sums.reshape(3, fsdp_size * tp_size, vec_size)
     small_sums = lax.dynamic_slice_in_dim(small_sums, fsdp_at * tp_size + tp_at, 1, axis=1)[:, 0]
@@ -1044,7 +1046,7 @@
     qkv_b_sum = lax.dynamic_slice_in_dim(qkv_b_sum, fsdp_at * qkv_bias.shape[2], qkv_bias.shape[2], axis=2)
 
     return (
-        output[:, None],
+        output.val[:, None],
         gained.val[:, None],
         gain_sum,
         shift_sum,

time: 597 us -> 599 us (level)
    ppermute x9, waiting for transfers between devices: 22.5 us -> 13.6 us  [move(): self.came = Box(lax.ppermute(sent.val, 'fsdp', ring))]
  transfers between devices with their start and end apart: 47 -> 47, of which waited for: 18 -> 19; matrix products, arithmetic and copies ran while one was open for 10% -> 10% of each run, Pallas kernels for 60% -> 60%
where the time goes in v9:
time: 599 us; the launch traced here: 590 us
  Pallas kernels  355 us (59%)
  waiting for transfers between devices  101 us (17%)
  other arithmetic  47.4 us (8%)
  starting transfers between devices  45.2 us (8%)
  local copies, waits for them, and re-layouts  26 us (4%)
  between operations  15.3 us (3%)
    pallas_call x9, Pallas kernels, rows_call(): pl.pallas_call(kernel, grid_spec=pltpu.PrefetchScalarGridSpec(num_scalar_...  188 us
    pallas_call x3, Pallas kernels, weight_grad(): pl.pallas_call(kernel, grid=(micro_count * steps,), in_specs=[side(micro,...  77.6 us
    ppermute x8, waiting for transfers between devices, swap_pair(): return lax.ppermute(vals, 'fsdp', [(f, f ^ 1) for f in range(fsdp_size)])  48.1 us
    pallas_call x2, Pallas kernels, attend_back(): pl.pallas_call(functools.partial(attend_back_kernel, head_dim, block), gr...  42.2 us
    pallas_call x2, Pallas kernels, attend(): pl.pallas_call(functools.partial(attend_kernel, head_dim, block), grid=(s...  32.9 us
    ppermute x9, waiting for transfers between devices, move(): self.parts.append(Box(lax.ppermute(self.parts[-1].val, 'fsdp', ring)))  23.8 us
    ppermute x9, waiting for transfers between devices, move(): self.came = Box(lax.ppermute(sent.val, 'fsdp', ring))  13.6 us
  transfers between devices with their start and end apart: 47, of which 19 were waited for; matrix products, arithmetic and copies ran while one was open for 10% of the time, Pallas kernels for 60%

profile of v9, /device:TPU:0, one launch (start us, length us, event | category | flops | bytes accessed | tf_op | source)
XLA Modules:
  0.0 590.1 jit_solution(14120264605970237849)
XLA Ops:
  19.2 11.8 %collective-permute-done = bf16[256,1024]{1,0:T(8,128)(2,1)S(1)} collective-permute-done((bf16[256,1024]{1,0:T(8,128)(2,1)S(1)}, bf16[256,1024]{1,0:T(8,128)(2,1)S(1)}, u32[]{:S(2)}, u32[]{:S(2)}) %collective-permute-start) | collective-permute-done | bytes 524320 | tf_op jit(solution)/shard_map/ppermute | solution.py:577
  42.6 12.7 %collective-permute-done.4.refs_1_.refs_5_ = bf16[512,1024]{1,0:T(8,128)(2,1)S(1)} collective-permute-done((bf16[512,1024]{1,0:T(8,128)(2,1)S(1)}, bf16[512,1024]{1,0:T(8,128)(2,1)S(1)}, u32[]{:S(2)}, u32[]{:S(2)}) %collective-permute-start.4) | collective-permute-done | bytes 1048608 | tf_op jit(solution)/shard_map/ppermute | solution.py:639
  67.5 14.3 %collective-permute-done.3 = bf16[256,1024]{1,0:T(8,128)(2,1)} collective-permute-done((bf16[256,1024]{1,0:T(8,128)(2,1)}, bf16[256,1024]{1,0:T(8,128)(2,1)}, u32[]{:S(2)}, u32[]{:S(2)}) %collective-permute-start.3) | collective-permute-done | bytes 524320 | tf_op jit(solution)/shard_map/ppermute | solution.py:577
  85.3 3.2 fusion.2
  94.5 13.3 %collective-permute-done.6 = bf16[256,1024]{1,0:T(8,128)(2,1)} collective-permute-done((bf16[256,1024]{1,0:T(8,128)(2,1)}, bf16[256,1024]{1,0:T(8,128)(2,1)}, u32[]{:S(2)}, u32[]{:S(2)}) %collective-permute-start.6) | collective-permute-done | bytes 524320 | tf_op jit(solution)/shard_map/ppermute | solution.py:577
  111.7 16.1 %shard_map.213 = (bf16[2048,2048]{1,0:T(8,128)(2,1)}, f32[2048,768]{1,0:T(8,128)}) custom-call(s32[5]{0:T(128)} %stack.35.slots_ref, bf16[2048,2048]{1,0:T(8,128)(2,1)} %all-gather.5.cloned.1.call-done.rows_ref, f32[1,2048]{1,0:T(1,128)} %reshape.179.gain_ref, f32[1,2048]{1,0:T(1,128)} %reshape.180.shift_ref, f32[1,768]{1,0:T(1,128)} %reshape.167.bias_ref, ...), custom_call_target="tpu_custom_call" | custom-call | flops 100663296 | bytes 360448 | tf_op jit(solution)/shard_map/pallas_call | solution.py:219
  127.8 4.9 collective-permute-done.12.refs_3_.refs_5_
  133.9 16.3 %shard_map.214 = (bf16[2048,768]{1,0:T(8,128)(2,1)}, bf16[2048,256]{1,0:T(8,128)(2,1)}, f32[4,2,1024]{2,1,0:T(2,128)}) custom-call(f32[2048,768]{1,0:T(8,128)} %get-tuple-element.380.qkv_ref, f32[1024,128]{1,0:T(8,128)} %get-tuple-element.381.cos_ref, f32[1024,128]{1,0:T(8,128)} %get-tuple-element.382.low_ref, f32[1024,128]{1,0:T(8,128)} %get-tuple-element.383.up_ref), custom_call_target="tpu_custom_call" | custom-call | flops 100663296 | bytes 131072 | tf_op jit(solution)/shard_map/pallas_call | solution.py:150
  150.2 16.8 %shard_map.215 = (bf16[2048,2048]{1,0:T(8,128)(2,1)}, f32[2048,768]{1,0:T(8,128)}) custom-call(s32[5]{0:T(128)} %stack.35.slots_ref, bf16[2048,2048]{1,0:T(8,128)(2,1)} %all-gather.7.cloned.1.call-done.rows_ref, f32[1,2048]{1,0:T(1,128)} %reshape.179.gain_ref, f32[1,2048]{1,0:T(1,128)} %reshape.180.shift_ref, f32[1,768]{1,0:T(1,128)} %reshape.167.bias_ref, ...), custom_call_target="tpu_custom_call" | custom-call | flops 100663296 | bytes 360448 | tf_op jit(solution)/shard_map/pallas_call | solution.py:219
  167.1 16.7 %shard_map.216 = (bf16[2048,768]{1,0:T(8,128)(2,1)}, bf16[2048,256]{1,0:T(8,128)(2,1)}, f32[4,2,1024]{2,1,0:T(2,128)}) custom-call(f32[2048,768]{1,0:T(8,128)} %get-tuple-element.392.qkv_ref, f32[1024,128]{1,0:T(8,128)} %get-tuple-element.381.cos_ref, f32[1024,128]{1,0:T(8,128)} %get-tuple-element.382.low_ref, f32[1024,128]{1,0:T(8,128)} %get-tuple-element.383.up_ref), custom_call_target="tpu_custom_call" | custom-call | flops 100663296 | bytes 131072 | tf_op jit(solution)/shard_map/pallas_call | solution.py:150
  183.8 6.2 %collective-permute-done.14.refs_5_.refs_7_ = bf16[512,1024]{1,0:T(8,128)(2,1)S(1)} collective-permute-done((bf16[512,1024]{1,0:T(8,128)(2,1)S(1)}, bf16[512,1024]{1,0:T(8,128)(2,1)S(1)}, u32[]{:S(2)}, u32[]{:S(2)}) %collective-permute-start.14) | collective-permute-done | bytes 1048608 | tf_op jit(solution)/shard_map/ppermute | solution.py:639
  191.0 32.6 %shard_map.217 = (bf16[2048,1024]{1,0:T(8,128)(2,1)}, bf16[2048,1024]{1,0:T(8,128)(2,1)}, bf16[2048,1024]{1,0:T(8,128)(2,1)}, bf16[2048,1024]{1,0:T(8,128)(2,1)}) custom-call(s32[5]{0:T(128)} %stack.35.slots_ref, f32[1,1024]{1,0:T(1,128)} %constant_dynamic-slice_fusion.9.bias_ref, bf16[2048,2048]{1,0:T(8,128)(2,1)} %get-tuple-element.483.refs_0_, ...), custom_call_target="tpu_custom_call" | custom-call | flops 268435456 | bytes 524288 | tf_op jit(solution)/shard_map/pallas_call | solution.py:219
  223.8 7.8 %shard_map.218.grad_ref = bf16[2048,256]{1,0:T(8,128)(2,1)} custom-call(s32[5]{0:T(128)} %stack.35.slots_ref, bf16[2048,2048]{1,0:T(8,128)(2,1)} %all-gather.9.cloned.1.call-done.rows_ref.refs_0_, bf16[512,1024]{1,0:T(8,128)(2,1)} %copy-done, bf16[512,1024]{1,0:T(8,128)(2,1)} %copy-done.2, bf16[512,1024]{1,0:T(8,128)(2,1)} %copy-done.3, ...), custom_call_target="tpu_custom_call" | custom-call | flops 33554432 | bytes 147456 | tf_op jit(solution)/shard_map/pallas_call | solution.py:219
  231.6 21.1 %shard_map.219 = (bf16[2048,768]{1,0:T(8,128)(2,1)}, f32[16,768]{1,0:T(8,128)}) custom-call(bf16[2048,768]{1,0:T(8,128)(2,1)} %get-tuple-element.416.rot_ref, bf16[2048,256]{1,0:T(8,128)(2,1)} %shard_map.218.grad_ref, bf16[2048,256]{1,0:T(8,128)(2,1)} %get-tuple-element.430.attn_ref.refs_4_.refs_0_, f32[4,2,1024]{2,1,0:T(2,128)} %get-tuple-element.418.lse_ref, ...), custom_call_target="tpu_custom_call" | custom-call | flops 201326592 | bytes 131072 | tf_op jit(solution)/shard_map/pallas_call | solution.py:175
  252.7 3.4 collective-permute-start.17
  256.1 30.5 %shard_map.220 = bf16[1280,2048]{1,0:T(8,128)(2,1)} custom-call(bf16[2048,2048]{1,0:T(8,128)(2,1)} %all-gather.9.cloned.1.call-done.rows_ref.refs_0_, bf16[2048,2048]{1,0:T(8,128)(2,1)} %all-gather.11.cloned.1.call-done.refs_1_.rows_ref, bf16[2048,1024]{1,0:T(8,128)(2,1)} %get-tuple-element.432.refs_2_, bf16[2048,1024]{1,0:T(8,128)(2,1)} %get-tuple-element.433.refs_3_, ...), custom_call_target="tpu_custom_call" | custom-call | flops 335544320 | bytes 425984 | tf_op jit(solution)/shard_map/pallas_call | solution.py:530
  290.2 30.2 %shard_map.221 = bf16[8,2,256,2048]{3,2,1,0:T(8,128)(2,1)} custom-call(s32[5]{0:T(128)} %stack.35.slots_ref, bf16[2048,256]{1,0:T(8,128)(2,1)} %get-tuple-element.430.attn_ref.refs_4_.refs_0_, bf16[2048,256]{1,0:T(8,128)(2,1)} %get-tuple-element.467.refs_5_.refs_1_.attn_ref, bf16[2048,1024]{1,0:T(8,128)(2,1)} %get-tuple-element.432.refs_2_, ...), custom_call_target="tpu_custom_call" | custom-call | flops 335544320 | bytes 294912 | tf_op jit(solution)/shard_map/pallas_call | solution.py:219
  323.3 27.8 %shard_map.222 = (bf16[2048,1024]{1,0:T(8,128)(2,1)}, bf16[2048,1024]{1,0:T(8,128)(2,1)}, f32[8,1024]{1,0:T(8,128)}) custom-call(s32[5]{0:T(128)} %stack.35.slots_ref, bf16[2048,2048]{1,0:T(8,128)(2,1)} %all-gather.9.cloned.1.call-done.rows_ref.refs_0_, bf16[2048,2048]{1,0:T(8,128)(2,1)} %all-gather.11.cloned.1.call-done.refs_1_.rows_ref, ...), custom_call_target="tpu_custom_call" | custom-call | flops 268435456 | bytes 524288 | tf_op jit(solution)/shard_map/pallas_call | solution.py:219
  355.0 26.0 %shard_map.223 = bf16[2048,1024]{1,0:T(8,128)(2,1)} custom-call(bf16[2048,2048]{1,0:T(8,128)(2,1)} %get-tuple-element.483.refs_0_, bf16[2048,2048]{1,0:T(8,128)(2,1)} %get-tuple-element.484.refs_1_, bf16[2048,1024]{1,0:T(8,128)(2,1)} %get-tuple-element.475.refs_2_.two_ref, bf16[2048,1024]{1,0:T(8,128)(2,1)} %get-tuple-element.493.refs_3_.two_ref), custom_call_target="tpu_custom_call" | custom-call | flops 268435456 | bytes 393216 | tf_op jit(solution)/shard_map/pallas_call | solution.py:530
  381.0 3.9 collective-permute-done.20
  389.7 7.7 %shard_map.224.grad_ref = bf16[2048,256]{1,0:T(8,128)(2,1)} custom-call(s32[5]{0:T(128)} %stack.35.slots_ref, bf16[2048,2048]{1,0:T(8,128)(2,1)} %all-gather.11.cloned.1.call-done.refs_1_.rows_ref, bf16[512,1024]{1,0:T(8,128)(2,1)} %copy-done, bf16[512,1024]{1,0:T(8,128)(2,1)} %copy-done.2, bf16[512,1024]{1,0:T(8,128)(2,1)} %copy-done.3, ...), custom_call_target="tpu_custom_call" | custom-call | flops 33554432 | bytes 147456 | tf_op jit(solution)/shard_map/pallas_call | solution.py:219
  397.4 21.1 %shard_map.225 = (bf16[2048,768]{1,0:T(8,128)(2,1)}, f32[16,768]{1,0:T(8,128)}) custom-call(bf16[2048,768]{1,0:T(8,128)(2,1)} %get-tuple-element.465.rot_ref, bf16[2048,256]{1,0:T(8,128)(2,1)} %shard_map.224.grad_ref, bf16[2048,256]{1,0:T(8,128)(2,1)} %get-tuple-element.467.refs_5_.refs_1_.attn_ref, f32[4,2,1024]{2,1,0:T(2,128)} %get-tuple-element.468.lse_ref, ...), custom_call_target="tpu_custom_call" | custom-call | flops 201326592 | bytes 131072 | tf_op jit(solution)/shard_map/pallas_call | solution.py:175
  421.6 23.9 %shard_map.226 = (bf16[2048,2048]{1,0:T(8,128)(2,1)}, f32[8,2048]{1,0:T(8,128)}) custom-call(s32[5]{0:T(128)} %stack.35.slots_ref, bf16[2048,768]{1,0:T(8,128)(2,1)} %get-tuple-element.485.one_ref.refs_2_, bf16[2048,1024]{1,0:T(8,128)(2,1)} %get-tuple-element.475.refs_2_.two_ref, bf16[2048,2048]{1,0:T(8,128)(2,1)} %all-gather.5.cloned.1.call-done.rows_ref, ...), custom_call_target="tpu_custom_call" | custom-call | flops 234881024 | bytes 376832 | tf_op jit(solution)/shard_map/pallas_call | solution.py:219
  448.3 21.1 %shard_map.227 = bf16[2048,768]{1,0:T(8,128)(2,1)} custom-call(bf16[2048,2048]{1,0:T(8,128)(2,1)} %get-tuple-element.483.refs_0_, bf16[2048,2048]{1,0:T(8,128)(2,1)} %get-tuple-element.484.refs_1_, bf16[2048,768]{1,0:T(8,128)(2,1)} %get-tuple-element.485.one_ref.refs_2_, bf16[2048,768]{1,0:T(8,128)(2,1)} %get-tuple-element.492.refs_3_.one_ref), custom_call_target="tpu_custom_call" | custom-call | flops 201326592 | bytes 360448 | tf_op jit(solution)/shard_map/pallas_call | solution.py:530
  476.3 24.8 %shard_map.228 = (bf16[1024,2048]{1,0:T(8,128)(2,1)}, bf16[1024,2048]{1,0:T(8,128)(2,1)}, f32[8,2048]{1,0:T(8,128)}) custom-call(s32[5]{0:T(128)} %stack.35.slots_ref, bf16[2048,768]{1,0:T(8,128)(2,1)} %get-tuple-element.492.refs_3_.one_ref, bf16[2048,1024]{1,0:T(8,128)(2,1)} %get-tuple-element.493.refs_3_.two_ref, ...), custom_call_target="tpu_custom_call" | custom-call | flops 234881024 | bytes 376832 | tf_op jit(solution)/shard_map/pallas_call | solution.py:219
  512.1 5.8 add_convert_fusion
  524.3 4.7 collective-permute-done.32
  530.2 9.4 %collective-permute-done.31 = bf16[256,1024]{1,0:T(8,128)(2,1)S(1)} collective-permute-done((bf16[256,1024]{1,0:T(8,128)(2,1)S(1)}, bf16[256,1024]{1,0:T(8,128)(2,1)S(1)}, u32[]{:S(2)}, u32[]{:S(2)}) %collective-permute-start.31) | collective-permute-done | bytes 524320 | tf_op jit(solution)/shard_map/ppermute | solution.py:946
  546.5 4.7 shard_map.229.refs_3_
  553.5 3.3 collective-permute-start.40
  563.4 6.2 %collective-permute-done.33.refs_1_ = bf16[256,2048]{1,0:T(8,128)(2,1)} collective-permute-done((bf16[256,2048]{1,0:T(8,128)(2,1)}, bf16[256,2048]{1,0:T(8,128)(2,1)}, u32[]{:S(2)}, u32[]{:S(2)}) %collective-permute-start.33) | collective-permute-done | bytes 1048608 | tf_op jit(solution)/shard_map/ppermute | solution.py:577
  569.7 5.2 shard_map.230
  (279 shorter events, 121.6 us)
Async XLA Ops:
  7.2 103.6 %all-gather.5.cloned.1.call-start = ((), (), s32[]{:S(2)}) async-start(), calls=%async_computation.2 | async-start | bytes 9437184 | tf_op jit(solution)/shard_map/all_gather | solution.py:580
  12.6 137.6 %all-gather.7.cloned.1.call-start = ((), (), s32[]{:S(2)}) async-start(), calls=%async_computation.3 | async-start | bytes 9437184 | tf_op jit(solution)/shard_map/all_gather | solution.py:580
  31.4 192.3 %all-gather.9.cloned.1.call-start = ((), (), s32[]{:S(2)}) async-start(), calls=%async_computation.4 | async-start | bytes 9437184 | tf_op jit(solution)/shard_map/all_gather | solution.py:580
  31.5 23.8 %collective-permute-start.4 = (bf16[512,1024]{1,0:T(8,128)(2,1)S(1)}, bf16[512,1024]{1,0:T(8,128)(2,1)S(1)}, u32[]{:S(2)}, u32[]{:S(2)}) collective-permute-start(bf16[512,1024]{1,0:T(8,128)(2,1)S(1)} %maximum_select_fusion.refs_0_.refs_4_), channel_id=1, source_target_pairs={{0,8},{4,12},{8,16},{12,20},{16,24},{20,28},{24,0},{28,4},{1,9},{5... | collective-permute-start | bytes 3145736 | tf_op jit(solution)/shard_map/ppermute | solution.py:639
  55.3 26.6 %collective-permute-start.7 = (bf16[512,1024]{1,0:T(8,128)(2,1)S(1)}, bf16[512,1024]{1,0:T(8,128)(2,1)S(1)}, u32[]{:S(2)}, u32[]{:S(2)}) collective-permute-start(bf16[512,1024]{1,0:T(8,128)(2,1)S(1)} %collective-permute-done.4.refs_1_.refs_5_), channel_id=1, source_target_pairs={{0,8},{4,12},{8,16},{12,20},{16,24},{20,28},{24,0},{28,4},{1,9},{5... | collective-permute-start | bytes 3145736 | tf_op jit(solution)/shard_map/ppermute | solution.py:639
  57.7 24.2 %collective-permute-start.3 = (bf16[256,1024]{1,0:T(8,128)(2,1)}, bf16[256,1024]{1,0:T(8,128)(2,1)}, u32[]{:S(2)}, u32[]{:S(2)}) collective-permute-start(bf16[256,1024]{1,0:T(8,128)(2,1)} %get-tuple-element.316), channel_id=1, source_target_pairs={{0,4},{4,0},{8,12},{12,8},{16,20},{20,16},{24,28},{28,24},{1,5},{5... | collective-permute-start | bytes 1572872 | tf_op jit(solution)/shard_map/ppermute | solution.py:577
  61.7 20.2 %collective-permute-start.10 = (bf16[8,704]{1,0:T(8,128)(2,1)S(1)}, bf16[8,704]{1,0:T(8,128)(2,1)S(1)}, u32[]{:S(2)}, u32[]{:S(2)}) collective-permute-start(bf16[8,704]{1,0:T(8,128)(2,1)S(1)} %maximum_select_fusion.3), channel_id=1, source_target_pairs={{0,8},{4,12},{8,0},{12,4},{16,24},{20,28},{24,16},{28,20},{1,9},{5... | collective-permute-start | bytes 33800 | tf_op jit(solution)/shard_map/ppermute | solution.py:744
  81.9 174.2 %all-gather.11.cloned.1.call-start = ((), (), s32[]{:S(2)}) async-start(), calls=%async_computation.5 | async-start | bytes 9437184 | tf_op jit(solution)/shard_map/all_gather | solution.py:580
  83.8 26.9 %collective-permute-start.11 = (bf16[512,1024]{1,0:T(8,128)(2,1)S(1)}, bf16[512,1024]{1,0:T(8,128)(2,1)S(1)}, u32[]{:S(2)}, u32[]{:S(2)}) collective-permute-start(bf16[512,1024]{1,0:T(8,128)(2,1)S(1)} %collective-permute-done.7.refs_2_.refs_6_), channel_id=1, source_target_pairs={{0,8},{4,12},{8,16},{12,20},{16,24},{20,28},{24,0},{28,4},{1,9},{5... | collective-permute-start | bytes 3145736 | tf_op jit(solution)/shard_map/ppermute | solution.py:639
  88.5 19.3 %collective-permute-start.6 = (bf16[256,1024]{1,0:T(8,128)(2,1)}, bf16[256,1024]{1,0:T(8,128)(2,1)}, u32[]{:S(2)}, u32[]{:S(2)}) collective-permute-start(bf16[256,1024]{1,0:T(8,128)(2,1)} %bitcast), channel_id=1, source_target_pairs={{0,4},{4,0},{8,12},{12,8},{16,20},{20,16},{24,28},{28,24},{1,5},{5... | collective-permute-start | bytes 1572872 | tf_op jit(solution)/shard_map/ppermute | solution.py:577
  110.7 22.0 %collective-permute-start.12 = (bf16[512,1024]{1,0:T(8,128)(2,1)S(1)}, bf16[512,1024]{1,0:T(8,128)(2,1)S(1)}, u32[]{:S(2)}, u32[]{:S(2)}) collective-permute-start(bf16[512,1024]{1,0:T(8,128)(2,1)S(1)} %maximum_select_fusion.1.refs_2_.refs_4_), channel_id=1, source_target_pairs={{0,8},{4,12},{8,16},{12,20},{16,24},{20,28},{24,0},{28,4},{1,9},{5... | collective-permute-start | bytes 3145736 | tf_op jit(solution)/shard_map/ppermute | solution.py:639
  132.7 339.6 %reduce-scatter.3.cloned.1.call-start = ((), (), s32[]{:S(2)}) async-start(), calls=%async_computation.6 | async-start | bytes 18874368 | tf_op jit(solution)/shard_map/reduce_scatter | solution.py:583
  132.7 34.3 %collective-permute-start.13 = (bf16[512,1024]{1,0:T(8,128)(2,1)S(1)}, bf16[512,1024]{1,0:T(8,128)(2,1)S(1)}, u32[]{:S(2)}, u32[]{:S(2)}) collective-permute-start(bf16[512,1024]{1,0:T(8,128)(2,1)S(1)} %collective-permute-done.12.refs_3_.refs_5_), channel_id=1, source_target_pairs={{0,8},{4,12},{8,16},{12,20},{16,24},{20,28},{24,0},{28,4},{1,9},{5... | collective-permute-start | bytes 3145736 | tf_op jit(solution)/shard_map/ppermute | solution.py:639
  167.0 23.0 %collective-permute-start.14 = (bf16[512,1024]{1,0:T(8,128)(2,1)S(1)}, bf16[512,1024]{1,0:T(8,128)(2,1)S(1)}, u32[]{:S(2)}, u32[]{:S(2)}) collective-permute-start(bf16[512,1024]{1,0:T(8,128)(2,1)S(1)} %collective-permute-done.13.refs_4_.refs_6_), channel_id=1, source_target_pairs={{0,8},{4,12},{8,16},{12,20},{16,24},{20,28},{24,0},{28,4},{1,9},{5... | collective-permute-start | bytes 3145736 | tf_op jit(solution)/shard_map/ppermute | solution.py:639
  190.0 33.6 %collective-permute-start.15 = (bf16[512,1024]{1,0:T(8,128)(2,1)S(1)}, bf16[512,1024]{1,0:T(8,128)(2,1)S(1)}, u32[]{:S(2)}, u32[]{:S(2)}) collective-permute-start(bf16[512,1024]{1,0:T(8,128)(2,1)S(1)} %copy-done.8), channel_id=1, source_target_pairs={{0,8},{4,12},{8,16},{12,20},{16,24},{20,28},{24,0},{28,4},{1,9},{5... | collective-permute-start | bytes 3145736 | tf_op jit(solution)/shard_map/ppermute | solution.py:639
  223.7 29.0 %collective-permute-start.16 = (bf16[512,1024]{1,0:T(8,128)(2,1)S(1)}, bf16[512,1024]{1,0:T(8,128)(2,1)S(1)}, u32[]{:S(2)}, u32[]{:S(2)}) collective-permute-start(bf16[512,1024]{1,0:T(8,128)(2,1)S(1)} %collective-permute-done.15.refs_9_.refs_5_), channel_id=1, source_target_pairs={{0,8},{4,12},{8,16},{12,20},{16,24},{20,28},{24,0},{28,4},{1,9},{5... | collective-permute-start | bytes 3145736 | tf_op jit(solution)/shard_map/ppermute | solution.py:639
  252.7 35.4 %collective-permute-start.17 = (bf16[512,1024]{1,0:T(8,128)(2,1)S(1)}, bf16[512,1024]{1,0:T(8,128)(2,1)S(1)}, u32[]{:S(2)}, u32[]{:S(2)}) collective-permute-start(bf16[512,1024]{1,0:T(8,128)(2,1)S(1)} %collective-permute-done.16.refs_10_.refs_6_), channel_id=1, source_target_pairs={{0,8},{4,12},{8,16},{12,20},{16,24},{20,28},{24,0},{28,4},{1,9},{5... | collective-permute-start | bytes 3145736 | tf_op jit(solution)/shard_map/ppermute | solution.py:639
  288.0 32.4 %collective-permute-start.18 = (bf16[1280,512]{1,0:T(8,128)(2,1)S(1)}, bf16[1280,512]{1,0:T(8,128)(2,1)S(1)}, u32[]{:S(2)}, u32[]{:S(2)}) collective-permute-start(bf16[1280,512]{1,0:T(8,128)(2,1)S(1)} %constant_dynamic-slice_fusion.7), channel_id=1, source_target_pairs={{0,8},{4,12},{8,16},{12,20},{16,24},{20,28},{24,0},{28,4},{1,9},{5... | collective-permute-start | bytes 3932168 | tf_op jit(solution)/shard_map/ppermute | solution.py:669
  320.4 226.0 %reduce-scatter.5.cloned.1.call-start = ((), (), s32[]{:S(2)}) async-start(), calls=%async_computation.7 | async-start | bytes 9437184 | tf_op jit(solution)/shard_map/reduce_scatter | solution.py:583
  322.1 31.1 %collective-permute-start.19 = (bf16[1280,512]{1,0:T(8,128)(2,1)S(1)}, bf16[1280,512]{1,0:T(8,128)(2,1)S(1)}, u32[]{:S(2)}, u32[]{:S(2)}) collective-permute-start(bf16[1280,512]{1,0:T(8,128)(2,1)S(1)} %add_convert_fusion.2), channel_id=1, source_target_pairs={{0,8},{4,12},{8,16},{12,20},{16,24},{20,28},{24,0},{28,4},{1,9},{5... | collective-permute-start | bytes 3932168 | tf_op jit(solution)/shard_map/ppermute | solution.py:669
  354.9 29.9 %collective-permute-start.20 = (bf16[1280,512]{1,0:T(8,128)(2,1)S(1)}, bf16[1280,512]{1,0:T(8,128)(2,1)S(1)}, u32[]{:S(2)}, u32[]{:S(2)}) collective-permute-start(bf16[1280,512]{1,0:T(8,128)(2,1)S(1)} %add_convert_fusion.1), channel_id=1, source_target_pairs={{0,8},{4,12},{8,16},{12,20},{16,24},{20,28},{24,0},{28,4},{1,9},{5... | collective-permute-start | bytes 3932168 | tf_op jit(solution)/shard_map/ppermute | solution.py:669
  386.6 31.9 %collective-permute-start.21 = (bf16[512,1024]{1,0:T(8,128)(2,1)S(1)}, bf16[512,1024]{1,0:T(8,128)(2,1)S(1)}, u32[]{:S(2)}, u32[]{:S(2)}) collective-permute-start(bf16[512,1024]{1,0:T(8,128)(2,1)S(1)} %constant_dynamic-slice_fusion.6), channel_id=1, source_target_pairs={{0,8},{4,12},{8,16},{12,20},{16,24},{20,28},{24,0},{28,4},{1,9},{5... | collective-permute-start | bytes 3145736 | tf_op jit(solution)/shard_map/ppermute | solution.py:669
  388.5 30.0 %collective-permute-start.22 = (bf16[1280,256]{1,0:T(8,128)(2,1)S(1)}, bf16[1280,256]{1,0:T(8,128)(2,1)S(1)}, u32[]{:S(2)}, u32[]{:S(2)}) collective-permute-start(bf16[1280,256]{1,0:T(8,128)(2,1)S(1)} %add_convert_fusion.7), channel_id=1, source_target_pairs={{0,4},{4,0},{8,12},{12,8},{16,20},{20,16},{24,28},{28,24},{1,5},{5... | collective-permute-start | bytes 1966088 | tf_op jit(solution)/shard_map/ppermute | solution.py:577
  420.4 25.2 %collective-permute-start.23 = (bf16[512,1024]{1,0:T(8,128)(2,1)S(1)}, bf16[512,1024]{1,0:T(8,128)(2,1)S(1)}, u32[]{:S(2)}, u32[]{:S(2)}) collective-permute-start(bf16[512,1024]{1,0:T(8,128)(2,1)S(1)} %add_convert_fusion.4), channel_id=1, source_target_pairs={{0,8},{4,12},{8,16},{12,20},{16,24},{20,28},{24,0},{28,4},{1,9},{5... | collective-permute-start | bytes 3145736 | tf_op jit(solution)/shard_map/ppermute | solution.py:669
  447.3 25.0 %collective-permute-start.24 = (bf16[512,1024]{1,0:T(8,128)(2,1)S(1)}, bf16[512,1024]{1,0:T(8,128)(2,1)S(1)}, u32[]{:S(2)}, u32[]{:S(2)}) collective-permute-start(bf16[512,1024]{1,0:T(8,128)(2,1)S(1)} %add_convert_fusion.3), channel_id=1, source_target_pairs={{0,8},{4,12},{8,16},{12,20},{16,24},{20,28},{24,0},{28,4},{1,9},{5... | collective-permute-start | bytes 3145736 | tf_op jit(solution)/shard_map/ppermute | solution.py:669
  473.9 28.2 %collective-permute-start.25 = (bf16[512,768]{1,0:T(8,128)(2,1)S(1)}, bf16[512,768]{1,0:T(8,128)(2,1)}, u32[]{:S(2)}, u32[]{:S(2)}) collective-permute-start(bf16[512,768]{1,0:T(8,128)(2,1)S(1)} %constant_dynamic-slice_fusion.5), channel_id=1, source_target_pairs={{0,8},{4,12},{8,16},{12,20},{16,24},{20,28},{24,0},{28,4},{1,9},{5... | collective-permute-start | bytes 2359304 | tf_op jit(solution)/shard_map/ppermute | solution.py:669
  475.2 26.9 %collective-permute-start.26 = (bf16[256,1024]{1,0:T(8,128)(2,1)S(1)}, bf16[256,1024]{1,0:T(8,128)(2,1)S(1)}, u32[]{:S(2)}, u32[]{:S(2)}) collective-permute-start(bf16[256,1024]{1,0:T(8,128)(2,1)S(1)} %add_convert_fusion.10), channel_id=1, source_target_pairs={{0,4},{4,0},{8,12},{12,8},{16,20},{20,16},{24,28},{28,24},{1,5},{5... | collective-permute-start | bytes 1572872 | tf_op jit(solution)/shard_map/ppermute | solution.py:577
  507.5 21.5 %collective-permute-start.32 = (bf16[512,768]{1,0:T(8,128)(2,1)S(1)}, bf16[512,768]{1,0:T(8,128)(2,1)S(1)}, u32[]{:S(2)}, u32[]{:S(2)}) collective-permute-start(bf16[512,768]{1,0:T(8,128)(2,1)S(1)} %add_convert_fusion.6), channel_id=1, source_target_pairs={{0,8},{4,12},{8,16},{12,20},{16,24},{20,28},{24,0},{28,4},{1,9},{5... | collective-permute-start | bytes 2359304 | tf_op jit(solution)/shard_map/ppermute | solution.py:669
  520.4 19.2 %collective-permute-start.31 = (bf16[256,1024]{1,0:T(8,128)(2,1)S(1)}, bf16[256,1024]{1,0:T(8,128)(2,1)S(1)}, u32[]{:S(2)}, u32[]{:S(2)}) collective-permute-start(bf16[256,1024]{1,0:T(8,128)(2,1)S(1)} %get-tuple-element.649), channel_id=1, source_target_pairs={{0,2},{1,3},{2,0},{3,1},{4,6},{5,7},{6,4},{7,5},{8,10},{9,11},{10,... | collective-permute-start | bytes 1572872 | tf_op jit(solution)/shard_map/ppermute | solution.py:946
  530.0 23.4 %collective-permute-start.36 = (bf16[512,768]{1,0:T(8,128)(2,1)}, bf16[512,768]{1,0:T(8,128)(2,1)}, u32[]{:S(2)}, u32[]{:S(2)}) collective-permute-start(bf16[512,768]{1,0:T(8,128)(2,1)} %add_convert_fusion.5), channel_id=1, source_target_pairs={{0,8},{4,12},{8,16},{12,20},{16,24},{20,28},{24,0},{28,4},{1,9},{5... | collective-permute-start | bytes 2359304 | tf_op jit(solution)/shard_map/ppermute | solution.py:669
  543.2 26.4 %collective-permute-start.33 = (bf16[256,2048]{1,0:T(8,128)(2,1)}, bf16[256,2048]{1,0:T(8,128)(2,1)}, u32[]{:S(2)}, u32[]{:S(2)}) collective-permute-start(bf16[256,2048]{1,0:T(8,128)(2,1)} %pad_maximum_fusion.2), channel_id=1, source_target_pairs={{0,4},{4,0},{8,12},{12,8},{16,20},{20,16},{24,28},{28,24},{1,5},{5... | collective-permute-start | bytes 3145736 | tf_op jit(solution)/shard_map/ppermute | solution.py:577
  545.0 24.7 %collective-permute-start.34 = (bf16[256,2048]{1,0:T(8,128)(2,1)}, bf16[256,2048]{1,0:T(8,128)(2,1)}, u32[]{:S(2)}, u32[]{:S(2)}) collective-permute-start(bf16[256,2048]{1,0:T(8,128)(2,1)} %pad_maximum_fusion.3), channel_id=1, source_target_pairs={{0,2},{1,3},{2,0},{3,1},{4,6},{5,7},{6,4},{7,5},{8,10},{9,11},{10,... | collective-permute-start | bytes 3145736 | tf_op jit(solution)/shard_map/ppermute | solution.py:946
  (52 other events, 528.4 us)
Sparse Core Ops, SparseCore 0:
  12.7 70.1 all-gather.4
  84.8 57.6 all-gather.6
  144.5 54.3 all-gather.8
  200.6 54.3 all-gather.10
  320.5 128.2 reduce-scatter.2
  452.2 83.8 reduce-scatter.4
